TPU v7x, 32 devices: a whole 2x2x4 slice. The times are simulated.
32 devices in a mesh: dp: 8 (over y, x, core), tensor: 4 (over z).
Axes of the slice: x: 2, y: 2, z: 4, core: 2. Of those that a mesh axis runs over, the one named last changes fastest.
Arguments:
- tokens: bfloat16 [16384, 1024], P(('dp', 'tensor')), may hold values from -6 to 6
- enc_states: bfloat16 [4096, 1024], P(('dp', 'tensor')), may hold values from -6 to 6
- enc_len: int32 [8], P('dp'), may hold values from 1 to 512, 3072 in all
- cont_lengths: int32 [8, 8], P('dp'), may hold values from 1 to 256, 1024 in all within a row
- cotangent: bfloat16 [16384, 1024], P(('dp', 'tensor')), may hold values from -6 to 6
- self_qkv: bfloat16 [3, 1024, 1024], P(None, 'dp', 'tensor'), may hold values from -0.1875 to 0.1875
- self_out: bfloat16 [1024, 1024], P('tensor', 'dp'), may hold values from -1.5 to 1.5
- cross_qkv: bfloat16 [3, 1024, 1024], P(None, 'dp', 'tensor'), may hold values from -0.1875 to 0.1875
- cross_out: bfloat16 [1024, 1024], P('tensor', 'dp'), may hold values from -1.5 to 1.5
- ff_in: bfloat16 [1024, 8192], P('dp', 'tensor'), may hold values from -0.1875 to 0.1875
- ff_out: bfloat16 [8192, 1024], P('tensor', 'dp'), may hold values from -0.25 to 0.25
- head_bias: bfloat16 [4, 1024], P(None, ('tensor', 'dp')), may hold values from -1.796875 to 1.796875
- ff_bias: bfloat16 [8192], P(('tensor', 'dp')), may hold values from -1.796875 to 1.796875
- vec_params: bfloat16 [9, 1024], P(None, 'dp'), may hold values from -0.9 to 1.9, as said below
Outputs:
- layer_out: bfloat16 [16384, 1024], P(('dp', 'tensor'))
- input_grad: float32 [16384, 1024], P(('dp', 'tensor'))
- enc_grad: float32 [4096, 1024], P(('dp', 'tensor'))
- self_qkv_grad: float32 [3, 1024, 1024], P(None, 'dp', 'tensor')
- self_out_grad: float32 [1024, 1024], P('tensor', 'dp')
- cross_qkv_grad: float32 [3, 1024, 1024], P(None, 'dp', 'tensor')
- cross_out_grad: float32 [1024, 1024], P('tensor', 'dp')
- ff_in_grad: float32 [1024, 8192], P('dp', 'tensor')
- ff_out_grad: float32 [8192, 1024], P('tensor', 'dp')
- head_bias_grad: float32 [4, 1024], P(None, ('tensor', 'dp'))
- ff_bias_grad: float32 [8192], P(('tensor', 'dp'))
- vec_params_grad: float32 [9, 1024], P(None, 'dp')
Inputs may be any that keep to these rules, and one draw needn't show every extreme that they name: `cont_lengths`: each row sums to 1024. `vec_params`: rows 0 to 2 lie near one, rows 3 to 8 near zero.
All inputs are finite; a program needn't handle non-finite values. No bound on the sum of `enc_len` on one device may be relied on, other than what follows from the above.
Results may differ from a plain program's by a relative error of at most 0.025.
Values may be sent and summed in bfloat16 or wider, within the bound.
A program may use at most 256 MiB of HBM per device.

v0:
```python
import math

import jax
import jax.numpy as jnp
from jax import lax
from jax.sharding import PartitionSpec as P

HD = 64
PROMPT = 1024
CONT_TOK = 1024
ENC = 512


EPSILON = 1e-05
MASKED = 1e30
GELU_C = math.sqrt(2.0 / math.pi)
GELU_A = 0.044715


def gelu_value(values):
    inner = jnp.tanh(GELU_C * (values + GELU_A * values * values * values))
    return 0.5 * values * (1.0 + inner)


def gelu_slope(values):
    inner = jnp.tanh(GELU_C * (values + GELU_A * values * values * values))
    return 0.5 * (1.0 + inner) + 0.5 * values * (1.0 - inner * inner) * GELU_C * (
        1.0 + 3.0 * GELU_A * values * values
    )


def norm_forward(values, gain_vec, shift_vec):
    row_mean = jnp.mean(values, axis=1, keepdims=True)
    centred = values - row_mean
    inverse = lax.rsqrt(jnp.mean(centred * centred, axis=1, keepdims=True) + EPSILON)
    normed = centred * inverse
    return (normed * gain_vec + shift_vec, normed, inverse)


def norm_backward(gradient, normed, inverse, gain_vec):
    scaled = gradient * gain_vec
    inner = (
        scaled
        - jnp.mean(scaled, axis=1, keepdims=True)
        - normed * jnp.mean(scaled * normed, axis=1, keepdims=True)
    )
    return (inner * inverse, jnp.sum(gradient * normed, axis=0), jnp.sum(gradient, axis=0))


def product(left, right):
    return jnp.dot(left, right, preferred_element_type=jnp.float32)


def product_left_t(left, right):
    return lax.dot_general(
        left, right, (((0,), (0,)), ((), ())), preferred_element_type=jnp.float32
    )


def product_right_t(left, right):
    return lax.dot_general(
        left, right, (((1,), (1,)), ((), ())), preferred_element_type=jnp.float32
    )


def attend_forward(queries, key_rows, value_rows, rule, block_rows):
    seq_rows, local_width = queries.shape
    local_heads = local_width // HD
    query_blocks = queries.reshape(seq_rows // block_rows, block_rows, local_heads, HD)
    key_heads = key_rows.reshape(-1, local_heads, HD)
    value_heads = value_rows.reshape(-1, local_heads, HD)
    block_starts = jnp.arange(seq_rows // block_rows, dtype=jnp.int32) * block_rows

    def attend_block(pieces):
        query_block, offset = pieces
        scores = jnp.einsum(
            "qhd,khd->hqk", query_block, key_heads, preferred_element_type=jnp.float32
        )
        scores = jnp.where(rule(offset, block_rows)[None], scores, -MASKED)
        row_max = jnp.max(scores, axis=2, keepdims=True)
        exponent = jnp.exp(scores - row_max)
        row_total = jnp.sum(exponent, axis=2, keepdims=True)
        probs_low = (exponent / row_total).astype(jnp.bfloat16)
        mixed = jnp.einsum(
            "hqk,khd->qhd", probs_low, value_heads, preferred_element_type=jnp.float32
        )
        return (
            mixed.astype(jnp.bfloat16).reshape(block_rows, local_width),
            (row_max + jnp.log(row_total))[:, :, 0],
        )

    outputs, log_total = lax.map(attend_block, (query_blocks, block_starts))
    return (outputs.reshape(seq_rows, local_width), log_total)


def attend_backward(queries, key_rows, value_rows, out_grad, log_total, rule, block_rows):
    seq_rows, local_width = queries.shape
    local_heads = local_width // HD
    key_count = key_rows.shape[0]
    query_blocks = queries.reshape(seq_rows // block_rows, block_rows, local_heads, HD)
    grad_blocks = out_grad.reshape(seq_rows // block_rows, block_rows, local_heads, HD)
    key_heads = key_rows.reshape(key_count, local_heads, HD)
    value_heads = value_rows.reshape(key_count, local_heads, HD)
    block_starts = jnp.arange(seq_rows // block_rows, dtype=jnp.int32) * block_rows

    def back_block(running, pieces):
        key_sum, value_sum = running
        query_block, grad_block, block_total, offset = pieces
        scores = jnp.einsum(
            "qhd,khd->hqk", query_block, key_heads, preferred_element_type=jnp.float32
        )
        probs = jnp.where(
            rule(offset, block_rows)[None], jnp.exp(scores - block_total[:, :, None]), 0.0
        )
        probs_low = probs.astype(jnp.bfloat16)
        prob_grad = jnp.einsum(
            "qhd,khd->hqk", grad_block, value_heads, preferred_element_type=jnp.float32
        )
        row_delta = jnp.sum(probs * prob_grad, axis=2, keepdims=True)
        score_grad = (probs * (prob_grad - row_delta)).astype(jnp.bfloat16)
        query_grad = jnp.einsum(
            "hqk,khd->qhd", score_grad, key_heads, preferred_element_type=jnp.float32
        )
        key_sum = key_sum + jnp.einsum(
            "hqk,qhd->khd", score_grad, query_block, preferred_element_type=jnp.float32
        )
        value_sum = value_sum + jnp.einsum(
            "hqk,qhd->khd", probs_low, grad_block, preferred_element_type=jnp.float32
        )
        return (
            (key_sum, value_sum),
            query_grad.astype(jnp.bfloat16).reshape(block_rows, local_width),
        )

    zero_sum = jnp.zeros((key_count, local_heads, HD), jnp.float32)
    (key_sum, value_sum), query_grads = lax.scan(
        back_block, (zero_sum, zero_sum), (query_blocks, grad_blocks, log_total, block_starts)
    )
    return (
        query_grads.reshape(seq_rows, local_width),
        key_sum.astype(jnp.bfloat16).reshape(key_count, local_width),
        value_sum.astype(jnp.bfloat16).reshape(key_count, local_width),
    )


def attend_groups(queries, key_rows, value_rows, rules, block_rows):
    results, totals = ([], [])
    for which_group, rule in enumerate(rules):
        mixed, log_total = attend_forward(queries, key_rows, value_rows, rule, block_rows)
        results.append(mixed)
        totals.append(log_total)
    return (results[0], totals)


def back_groups(queries, key_rows, value_rows, out_grad, totals, rules, block_rows):
    query_list, key_list, value_list = ([], [], [])
    for which_group, rule in enumerate(rules):
        query_grad, key_grad, value_grad = attend_backward(
            queries, key_rows, value_rows, out_grad, totals[which_group], rule, block_rows
        )
        query_list.append(query_grad)
        key_list.append(key_grad)
        value_list.append(value_grad)
    return (query_list[0], key_list[0], value_list[0])


def shards(
    tokens,
    enc_states,
    enc_len,
    cont_lengths,
    cotangent,
    self_qkv,
    self_out,
    cross_qkv,
    cross_out,
    ff_in,
    ff_out,
    head_bias,
    ff_bias,
    vec_params,
):
    gathered = (
        lax.all_gather(self_qkv, "dp", axis=1, tiled=True),
        lax.all_gather(self_out, "dp", axis=1, tiled=True),
        lax.all_gather(cross_qkv, "dp", axis=1, tiled=True),
        lax.all_gather(cross_out, "dp", axis=1, tiled=True),
        lax.all_gather(ff_in, "dp", axis=0, tiled=True),
        lax.all_gather(ff_out, "dp", axis=1, tiled=True),
        lax.all_gather(head_bias, "dp", axis=1, tiled=True),
        lax.all_gather(ff_bias, "dp", axis=0, tiled=True),
        lax.all_gather(vec_params, "dp", axis=1, tiled=True),
    )
    (
        w_self,
        w_self_out,
        w_cross,
        w_cross_out,
        w_hidden_in,
        w_hidden_out,
        bias_heads,
        bias_hidden,
        vectors,
    ) = gathered
    vectors = vectors.astype(jnp.float32)
    bias_heads = bias_heads.astype(jnp.float32)
    bias_hidden = bias_hidden.astype(jnp.float32)
    seq_rows = PROMPT + CONT_TOK
    block_rows = min(512, seq_rows)
    scaling = HD ** (-0.5)
    rows_dev = tokens.shape[0]

    def self_rule(which_group):
        bounds = PROMPT + jnp.cumsum(cont_lengths[which_group])
        positions = jnp.arange(seq_rows, dtype=jnp.int32)
        segment = jnp.sum((positions[:, None] >= bounds[None, :]).astype(jnp.int32), axis=1)

        def self_allowed(offset, number):
            row_ids = offset + jnp.arange(number, dtype=jnp.int32)
            row_segment = lax.dynamic_slice_in_dim(segment, offset, number)
            return (positions[None, :] <= row_ids[:, None]) & (
                (positions[None, :] < PROMPT) | (segment[None, :] == row_segment[:, None])
            )

        return self_allowed

    def cross_rule(which_group):
        usable = jnp.arange(ENC, dtype=jnp.int32) < enc_len[which_group]

        def cross_allowed(offset, number):
            return jnp.broadcast_to(usable[None, :], (number, ENC))

        return cross_allowed

    def spread(low_rows):
        return lax.all_gather(low_rows, "tensor", axis=0, tiled=True)

    def head_branch(values, weight):

        def term(offset, number):
            return product(values, weight)

        return lax.psum_scatter(
            term(jnp.int32(0), rows_dev * lax.axis_size("tensor")),
            "tensor",
            scatter_dimension=0,
            tiled=True,
        )

    def widen(low_rows):
        return lax.all_gather(low_rows, "tensor", axis=0, tiled=True)

    def narrow(term):
        return lax.psum_scatter(
            term(jnp.int32(0), rows_dev * lax.axis_size("tensor")),
            "tensor",
            scatter_dimension=0,
            tiled=True,
        )

    self_rules = [self_rule(0)]
    cross_rules = [cross_rule(0)]
    resid = tokens.astype(jnp.float32)
    enc_full = lax.all_gather(enc_states, "tensor", axis=0, tiled=True)
    normed_in, hat_one, inv_one = norm_forward(resid, vectors[0], vectors[3])
    attn_low = normed_in.astype(jnp.bfloat16)
    attn_full = spread(attn_low)
    queries = ((product(attn_full, w_self[0]) + bias_heads[0]) * scaling).astype(jnp.bfloat16)
    key_rows = product(attn_full, w_self[1]).astype(jnp.bfloat16)
    value_rows = (product(attn_full, w_self[2]) + bias_heads[1]).astype(jnp.bfloat16)
    mixed, self_totals = attend_groups(queries, key_rows, value_rows, self_rules, block_rows)
    after_one = resid + (head_branch(mixed, w_self_out) + vectors[6])
    normed_mid, hat_two, inv_two = norm_forward(after_one, vectors[1], vectors[4])
    cross_low = normed_mid.astype(jnp.bfloat16)
    cross_full = spread(cross_low)
    cross_queries = ((product(cross_full, w_cross[0]) + bias_heads[2]) * scaling).astype(
        jnp.bfloat16
    )
    cross_keys = product(enc_full, w_cross[1]).astype(jnp.bfloat16)
    cross_values = (product(enc_full, w_cross[2]) + bias_heads[3]).astype(jnp.bfloat16)
    cross_mixed, cross_totals = attend_groups(
        cross_queries, cross_keys, cross_values, cross_rules, block_rows
    )
    after_two = after_one + (head_branch(cross_mixed, w_cross_out) + vectors[7])
    normed_out, hat_three, inv_three = norm_forward(after_two, vectors[2], vectors[5])
    hidden_low = normed_out.astype(jnp.bfloat16)
    hidden_full = spread(hidden_low)
    pre_act = product(hidden_full, w_hidden_in) + bias_hidden
    activation = gelu_value(pre_act).astype(jnp.bfloat16)

    def term(offset, number):
        return product(activation, w_hidden_out)

    after_three = after_two + (
        lax.psum_scatter(
            term(jnp.int32(0), rows_dev * lax.axis_size("tensor")),
            "tensor",
            scatter_dimension=0,
            tiled=True,
        )
        + vectors[8]
    )
    layer_out = after_three.astype(jnp.bfloat16)
    gradient = cotangent.astype(jnp.float32)
    grad_low = gradient.astype(jnp.bfloat16)
    bias_out_three = jnp.sum(grad_low.astype(jnp.float32), axis=0)
    grad_full = widen(grad_low)
    act_grad = (product_right_t(grad_full, w_hidden_out) * gelu_slope(pre_act)).astype(jnp.bfloat16)
    grad_hidden_out = product_left_t(activation, grad_full)
    grad_hidden_in = product_left_t(hidden_full, act_grad)
    grad_bias_hidden = jnp.sum(act_grad.astype(jnp.float32), axis=0)

    def hidden_term(offset, number):
        return product_right_t(act_grad, w_hidden_in)

    input_part, gain_three, shift_three = norm_backward(
        narrow(hidden_term), hat_three, inv_three, vectors[2]
    )
    gradient = gradient + input_part
    grad_low = gradient.astype(jnp.bfloat16)
    bias_out_two = jnp.sum(grad_low.astype(jnp.float32), axis=0)
    grad_full = widen(grad_low)
    grad_cross_out = product_left_t(cross_mixed, grad_full)
    mixed_grad = product_right_t(grad_full, w_cross_out).astype(jnp.bfloat16)
    cross_query_grad, cross_key_grad, cross_value_grad = back_groups(
        cross_queries, cross_keys, cross_values, mixed_grad, cross_totals, cross_rules, block_rows
    )
    grad_cross = jnp.stack(
        [
            product_left_t(cross_full, cross_query_grad) * scaling,
            product_left_t(enc_full, cross_key_grad),
            product_left_t(enc_full, cross_value_grad),
        ]
    )
    bias_cross_query = jnp.sum(cross_query_grad.astype(jnp.float32), axis=0) * scaling
    bias_cross_value = jnp.sum(cross_value_grad.astype(jnp.float32), axis=0)
    enc_grad = lax.psum_scatter(
        product_right_t(cross_key_grad, w_cross[1]) + product_right_t(cross_value_grad, w_cross[2]),
        "tensor",
        scatter_dimension=0,
        tiled=True,
    )

    def cross_term(offset, number):
        return product_right_t(cross_query_grad, w_cross[0]) * scaling

    input_part, gain_two, shift_two = norm_backward(
        narrow(cross_term), hat_two, inv_two, vectors[1]
    )
    gradient = gradient + input_part
    grad_low = gradient.astype(jnp.bfloat16)
    bias_out_one = jnp.sum(grad_low.astype(jnp.float32), axis=0)
    grad_full = widen(grad_low)
    grad_self_out = product_left_t(mixed, grad_full)
    self_mixed_grad = product_right_t(grad_full, w_self_out).astype(jnp.bfloat16)
    query_grad, key_grad, value_grad = back_groups(
        queries, key_rows, value_rows, self_mixed_grad, self_totals, self_rules, block_rows
    )
    grad_self = jnp.stack(
        [
            product_left_t(attn_full, query_grad) * scaling,
            product_left_t(attn_full, key_grad),
            product_left_t(attn_full, value_grad),
        ]
    )
    bias_self_query = jnp.sum(query_grad.astype(jnp.float32), axis=0) * scaling
    bias_self_value = jnp.sum(value_grad.astype(jnp.float32), axis=0)

    def self_term(offset, number):
        return (
            product_right_t(query_grad, w_self[0]) * scaling
            + product_right_t(key_grad, w_self[1])
            + product_right_t(value_grad, w_self[2])
        )

    input_part, gain_one, shift_one = norm_backward(narrow(self_term), hat_one, inv_one, vectors[0])
    input_grad = gradient + input_part
    vector_grads = jnp.stack(
        [
            gain_one,
            gain_two,
            gain_three,
            shift_one,
            shift_two,
            shift_three,
            bias_out_one,
            bias_out_two,
            bias_out_three,
        ]
    )
    head_grads = jnp.stack([bias_self_query, bias_self_value, bias_cross_query, bias_cross_value])
    results = (
        lax.psum_scatter(grad_self, "dp", scatter_dimension=1, tiled=True),
        lax.psum_scatter(grad_self_out, "dp", scatter_dimension=1, tiled=True),
        lax.psum_scatter(grad_cross, "dp", scatter_dimension=1, tiled=True),
        lax.psum_scatter(grad_cross_out, "dp", scatter_dimension=1, tiled=True),
        lax.psum_scatter(grad_hidden_in, "dp", scatter_dimension=0, tiled=True),
        lax.psum_scatter(grad_hidden_out, "dp", scatter_dimension=1, tiled=True),
        lax.psum_scatter(head_grads, "dp", scatter_dimension=1, tiled=True),
        lax.psum_scatter(grad_bias_hidden, "dp", scatter_dimension=0, tiled=True),
        lax.psum_scatter(vector_grads, "dp", scatter_dimension=1, tiled=True),
    )
    vector_total = lax.psum(results[8], "tensor")
    return (
        layer_out,
        input_grad,
        enc_grad,
        results[0],
        results[1],
        results[2],
        results[3],
        results[4],
        results[5],
        results[6],
        results[7],
        vector_total,
    )


def solution(mesh):
    in_specs = (
        P(("dp", "tensor"), None),
        P(("dp", "tensor"), None),
        P("dp"),
        P("dp", None),
        P(("dp", "tensor"), None),
        P(None, "dp", "tensor"),
        P("tensor", "dp"),
        P(None, "dp", "tensor"),
        P("tensor", "dp"),
        P("dp", "tensor"),
        P("tensor", "dp"),
        P(None, ("tensor", "dp")),
        P(("tensor", "dp")),
        P(None, "dp"),
    )
    out_specs = (
        P(("dp", "tensor"), None),
        P(("dp", "tensor"), None),
        P(("dp", "tensor"), None),
        P(None, "dp", "tensor"),
        P("tensor", "dp"),
        P(None, "dp", "tensor"),
        P("tensor", "dp"),
        P("dp", "tensor"),
        P("tensor", "dp"),
        P(None, ("tensor", "dp")),
        P(("tensor", "dp")),
        P(None, "dp"),
    )
    return jax.shard_map(shards, mesh=mesh, in_specs=in_specs, out_specs=out_specs, check_vma=False)
```

profile of v0, /device:TPU:0, one launch (start us, length us, event | category | flops | bytes accessed | tf_op | source)
XLA Modules:
  0.0 2444.9 jit_solution(13503522162828489254)
XLA Ops:
  45.4 75.9 %all-gather.14.cloned.1.call-done = bf16[2048,1024]{1,0:T(8,128)(2,1)} async-done(((bf16[512,1024]{1,0:T(8,128)(2,1)}), bf16[2048,1024]{1,0:T(8,128)(2,1)}) %all-gather.14.cloned.1.call-update) | async-done | bytes 4194320 | tf_op jit(solution)/shard_map/all_gather | solution.py:236
  134.7 74.9 %while.59 = (s32[]{:T(128)}, bf16[4,512,256]{2,1,0:T(8,128)(2,1)}, f32[4,4,512]{2,1,0:T(4,128)S(1)}, s32[4]{0:T(128)S(1)}, s32[2048]{0:T(1024)S(1)}, /*index=5*/...) while((s32[]{:T(128)}, bf16[4,512,256]{2,1,0:T(8,128)(2,1)}, ...), condition=%wide.region_7.8_spmd.clone.clone, body=%wide.region_4.7_spmd.clone.clone.sunk | while | flops 1115816448 | bytes 58284216 | solution.py:92
  218.2 141.8 %reduce-scatter.18.cloned.1.call-done = f32[512,1024]{1,0:T(8,128)} async-done(((f32[2048,1024]{1,0:T(8,128)}), f32[512,1024]{1,0:T(8,128)}) %reduce-scatter.18.cloned.1.call-update) | async-done | bytes 2097168 | tf_op jit(solution)/shard_map/reduce_scatter | solution.py:243
  374.8 15.3 all-gather.22.cloned.1.call-done
  390.1 27.0 %all-gather.20.cloned.1.call-done = bf16[3,1024,256]{2,1,0:T(8,128)(2,1)} async-done(((bf16[3,128,256]{2,1,0:T(8,128)(2,1)}), bf16[3,1024,256]{2,1,0:T(8,128)(2,1)}) %all-gather.20.cloned.1.call-update) | async-done | bytes 1572880 | tf_op jit(solution)/shard_map/all_gather | solution.py:186
  420.7 79.1 %all-gather.18.cloned.1.call-done = bf16[2048,1024]{1,0:T(8,128)(2,1)} async-done(((bf16[512,1024]{1,0:T(8,128)(2,1)}), bf16[2048,1024]{1,0:T(8,128)(2,1)}) %all-gather.18.cloned.1.call-update) | async-done | bytes 4194320 | tf_op jit(solution)/shard_map/all_gather | solution.py:236
  513.8 21.1 while.58
  541.8 142.3 %reduce-scatter.20.cloned.1.call-done = f32[512,1024]{1,0:T(8,128)} async-done(((f32[2048,1024]{1,0:T(8,128)}), f32[512,1024]{1,0:T(8,128)}) %reduce-scatter.20.cloned.1.call-update) | async-done | bytes 2097168 | tf_op jit(solution)/shard_map/reduce_scatter | solution.py:243
  699.3 24.2 all-gather.26.cloned.1.call-done
  723.5 82.9 %all-gather.24.cloned.1.call-done = bf16[2048,1024]{1,0:T(8,128)(2,1)} async-done(((bf16[512,1024]{1,0:T(8,128)(2,1)}), bf16[2048,1024]{1,0:T(8,128)(2,1)}) %all-gather.24.cloned.1.call-update) | async-done | bytes 4194320 | tf_op jit(solution)/shard_map/all_gather | solution.py:236
  806.5 20.4 multiply_convert_fusion.2
  826.9 60.3 %all-gather.30.cloned.1.call-done = bf16[2048,1024]{1,0:T(8,128)(2,1)} async-done(((bf16[512,1024]{1,0:T(8,128)(2,1)}), bf16[2048,1024]{1,0:T(8,128)(2,1)}) %all-gather.30.cloned.1.call-update) | async-done | bytes 4194320 | tf_op jit(solution)/shard_map/all_gather | solution.py:251
  887.2 37.9 %all-gather.28.cloned.1.call-done = bf16[2048,1024]{1,0:T(8,128)(2,1)} async-done(((bf16[2048,128]{1,0:T(8,128)(2,1)}), bf16[2048,1024]{1,0:T(8,128)(2,1)}) %all-gather.28.cloned.1.call-update) | async-done | bytes 4194320 | tf_op jit(solution)/shard_map/all_gather | solution.py:189
  925.1 27.4 %convert_reduce_fusion = (f32[2048]{0:T(1024)}, bf16[2048,2048]{1,0:T(8,128)(2,1)}) fusion(f32[2048,2048]{1,0:T(8,128)} %get-tuple-element.693, f32[2048]{0:T(1024)S(1)} %bitcast.356, bf16[2048,1024]{1,0:T(8,128)(2,1)} %all-gather.30.cloned.1.call-done, bf16[2048,1024]{1,0:T(8,128)(2,1)} %all-gather.28.cloned.1.call-done), kind=kOutput, calls=%fused_computation.109 | convolution fusion | flops 8682207232 | bytes 33570816 | tf_op jit(solution)/shard_map/dot_general | solution.py:61
  966.4 14.5 fusion.120
  980.9 130.0 %reduce-scatter.24.cloned.1.call-done = f32[512,1024]{1,0:T(8,128)} async-done(((f32[2048,1024]{1,0:T(8,128)}), f32[512,1024]{1,0:T(8,128)}) %reduce-scatter.24.cloned.1.call-update) | async-done | bytes 2097168 | tf_op jit(solution)/shard_map/reduce_scatter | solution.py:254
  1114.0 144.5 %reduce-scatter.22.cloned.1.call-done = f32[512,1024]{1,0:T(8,128)} async-done(((f32[2048,1024]{1,0:T(8,128)}), f32[512,1024]{1,0:T(8,128)}) %reduce-scatter.22.cloned.1.call-update) | async-done | bytes 2097168 | tf_op jit(solution)/shard_map/reduce_scatter | solution.py:295
  1263.6 81.6 %all-gather.32.cloned.1.call-done = bf16[2048,1024]{1,0:T(8,128)(2,1)} async-done(((bf16[512,1024]{1,0:T(8,128)(2,1)}), bf16[2048,1024]{1,0:T(8,128)(2,1)}) %all-gather.32.cloned.1.call-update) | async-done | bytes 4194320 | tf_op jit(solution)/shard_map/all_gather | solution.py:251
  1353.7 33.4 %while.60 = (s32[]{:T(128)}, f32[512,4,64]{0,2,1:T(8,128)S(1)}, f32[512,4,64]{0,2,1:T(8,128)S(1)}, bf16[4,512,256]{1,2,0:T(8,128)(2,1)S(1)}, bf16[4,512,4,64]{1,...) while((s32[]{:T(128)}, f32[512,4,64]{0,2,1:T(8,128)S(1)}, ...), condition=%wide.region_24.25_spmd.clone, body=%wide.region_22.24_spmd.clone.sunk | while | flops 684325376 | bytes 37284028 | solution.py:136
  1393.8 143.1 %reduce-scatter.26.cloned.1.call-done = f32[512,1024]{1,0:T(8,128)} async-done(((f32[2048,1024]{1,0:T(8,128)}), f32[512,1024]{1,0:T(8,128)}) %reduce-scatter.26.cloned.1.call-update) | async-done | bytes 2097168 | tf_op jit(solution)/shard_map/reduce_scatter | solution.py:254
  1543.3 81.6 %all-gather.34.cloned.1.call-done = bf16[2048,1024]{1,0:T(8,128)(2,1)} async-done(((bf16[512,1024]{1,0:T(8,128)(2,1)}), bf16[2048,1024]{1,0:T(8,128)(2,1)}) %all-gather.34.cloned.1.call-update) | async-done | bytes 4194320 | tf_op jit(solution)/shard_map/all_gather | solution.py:251
  1636.1 195.4 %while.61 = (s32[]{:T(128)}, f32[2048,4,64]{0,2,1:T(8,128)}, f32[2048,4,64]{0,2,1:T(8,128)}, bf16[4,512,256]{1,2,0:T(8,128)(2,1)}, bf16[4,512,4,64]{1,3,2,0:T(8,...) while((s32[]{:T(128)}, f32[2048,4,64]{0,2,1:T(8,128)}, ...), condition=%wide.region_30.31_spmd.clone.clone, body=%wide.region_28.30_spmd.clone.clone.sunk | while | flops 2741109248 | bytes 177060112 | solution.py:136
  1849.9 139.3 %reduce-scatter.28.cloned.1.call-done = f32[512,1024]{1,0:T(8,128)} async-done(((f32[2048,1024]{1,0:T(8,128)}), f32[512,1024]{1,0:T(8,128)}) %reduce-scatter.28.cloned.1.call-update) | async-done | bytes 2097168 | tf_op jit(solution)/shard_map/reduce_scatter | solution.py:254
  1993.2 14.6 fusion.124
  2007.9 14.7 fusion.125
  2085.2 50.9 %reduce-scatter.40.cloned.1.call-done = f32[128,2048]{1,0:T(8,128)} async-done(((f32[1024,2048]{1,0:T(8,128)}), f32[128,2048]{1,0:T(8,128)}) %reduce-scatter.40.cloned.1.call-update) | async-done | bytes 1048592 | tf_op jit(solution)/shard_map/reduce_scatter | solution.py:397
  2136.2 75.7 %reduce-scatter.42.cloned.1.call-done = f32[2048,128]{1,0:T(8,128)} async-done(((f32[2048,1024]{1,0:T(8,128)}), f32[2048,128]{1,0:T(8,128)}) %reduce-scatter.42.cloned.1.call-update) | async-done | bytes 1048592 | tf_op jit(solution)/shard_map/reduce_scatter | solution.py:398
  2211.9 39.8 %reduce-scatter.38.cloned.1.call-done = f32[256,128]{1,0:T(8,128)} async-done(((f32[256,1024]{1,0:T(8,128)}), f32[256,128]{1,0:T(8,128)}) %reduce-scatter.38.cloned.1.call-update) | async-done | bytes 131088 | tf_op jit(solution)/shard_map/reduce_scatter | solution.py:396
  2251.7 46.8 %reduce-scatter.30.cloned.1.call-done = f32[128,1024]{1,0:T(8,128)} async-done(((f32[512,1024]{1,0:T(8,128)}), f32[128,1024]{1,0:T(8,128)}) %reduce-scatter.30.cloned.1.call-update) | async-done | bytes 524304 | tf_op jit(solution)/shard_map/reduce_scatter | solution.py:337
  2298.5 49.8 %reduce-scatter.36.cloned.1.call-done = f32[3,128,256]{2,1,0:T(8,128)} async-done(((f32[3,1024,256]{2,1,0:T(8,128)}), f32[3,128,256]{2,1,0:T(8,128)}) %reduce-scatter.36.cloned.1.call-update) | async-done | bytes 393232 | tf_op jit(solution)/shard_map/reduce_scatter | solution.py:395
  2348.2 39.8 %reduce-scatter.34.cloned.1.call-done = f32[256,128]{1,0:T(8,128)} async-done(((f32[256,1024]{1,0:T(8,128)}), f32[256,128]{1,0:T(8,128)}) %reduce-scatter.34.cloned.1.call-update) | async-done | bytes 131088 | tf_op jit(solution)/shard_map/reduce_scatter | solution.py:394
  2388.0 50.0 %reduce-scatter.32.cloned.1.call-done = f32[3,128,256]{2,1,0:T(8,128)} async-done(((f32[3,1024,256]{2,1,0:T(8,128)}), f32[3,128,256]{2,1,0:T(8,128)}) %reduce-scatter.32.cloned.1.call-update) | async-done | bytes 393232 | tf_op jit(solution)/shard_map/reduce_scatter | solution.py:393
  (499 shorter events, 560.5 us)
Async XLA Ops:
  7.2 38.2 %all-gather.16.cloned.1.call-start = ((), (), s32[]{:S(2)}) async-start(), calls=%async_computation.16 | async-start | bytes 1769472 | tf_op jit(solution)/shard_map/all_gather | solution.py:184
  7.9 113.4 %all-gather.14.cloned.1.call-start = ((), (), s32[]{:S(2)}) async-start(), calls=%async_computation.15 | async-start | bytes 5242880 | tf_op jit(solution)/shard_map/all_gather | solution.py:236
  25.5 334.4 %reduce-scatter.18.cloned.1.call-start = ((), (), s32[]{:S(2)}) async-start(), calls=%async_computation.17 | async-start | bytes 10485760 | tf_op jit(solution)/shard_map/reduce_scatter | solution.py:243
  216.8 173.3 %all-gather.22.cloned.1.call-start = ((), (), s32[]{:S(2)}) async-start(), calls=%async_computation.20 | async-start | bytes 1310720 | tf_op jit(solution)/shard_map/all_gather | solution.py:264
  217.4 199.7 %all-gather.20.cloned.1.call-start = ((), (), s32[]{:S(2)}) async-start(), calls=%async_computation.19 | async-start | bytes 1769472 | tf_op jit(solution)/shard_map/all_gather | solution.py:186
  217.9 281.9 %all-gather.18.cloned.1.call-start = ((), (), s32[]{:S(2)}) async-start(), calls=%async_computation.18 | async-start | bytes 5242880 | tf_op jit(solution)/shard_map/all_gather | solution.py:236
  361.9 322.3 %copy-start.2 = (f32[512,1024]{1,0:T(8,128)}, f32[512,1024]{1,0:T(8,128)S(1)}, u32[]{:S(2)}) copy-start(f32[512,1024]{1,0:T(8,128)S(1)} %get-tuple-element.668) | copy-start | bytes 6291460
  363.7 320.4 %reduce-scatter.20.cloned.1.call-start = ((), (), s32[]{:S(2)}) async-start(), calls=%async_computation.21 | async-start | bytes 10485760 | tf_op jit(solution)/shard_map/reduce_scatter | solution.py:243
  541.0 182.5 %all-gather.26.cloned.1.call-start = ((), (), s32[]{:S(2)}) async-start(), calls=%async_computation.23 | async-start | bytes 4718592 | tf_op jit(solution)/shard_map/all_gather | solution.py:188
  541.8 264.7 %all-gather.24.cloned.1.call-start = ((), (), s32[]{:S(2)}) async-start(), calls=%async_computation.22 | async-start | bytes 5242880 | tf_op jit(solution)/shard_map/all_gather | solution.py:236
  688.8 198.4 %all-gather.30.cloned.1.call-start = ((), (), s32[]{:S(2)}) async-start(), calls=%async_computation.26 | async-start | bytes 5242880 | tf_op jit(solution)/shard_map/all_gather | solution.py:251
  689.4 235.7 %all-gather.28.cloned.1.call-start = ((), (), s32[]{:S(2)}) async-start(), calls=%async_computation.24 | async-start | bytes 4718592 | tf_op jit(solution)/shard_map/all_gather | solution.py:189
  690.1 420.8 %reduce-scatter.24.cloned.1.call-start = ((), (), s32[]{:S(2)}) async-start(), calls=%async_computation.27 | async-start | bytes 10485760 | tf_op jit(solution)/shard_map/reduce_scatter | solution.py:254
  966.3 292.2 %reduce-scatter.22.cloned.1.call-start = ((), (), s32[]{:S(2)}) async-start(), calls=%async_computation.25 | async-start | bytes 10485760 | tf_op jit(solution)/shard_map/reduce_scatter | solution.py:295
  980.9 277.7 %copy-start.29 = (bf16[512,1024]{1,0:T(8,128)(2,1)S(1)}, bf16[512,1024]{1,0:T(8,128)(2,1)}, u32[]{:S(2)}) copy-start(bf16[512,1024]{1,0:T(8,128)(2,1)} %param.26) | copy-start | bytes 3145732
  980.9 277.7 %copy-start.55 = (f32[1,1024]{1,0:T(1,128)S(1)}, f32[1,1024]{1,0:T(1,128)}, u32[]{:S(2)}) copy-start(f32[1,1024]{1,0:T(1,128)} %get-tuple-element.679) | copy-start | bytes 12292
  980.9 364.2 %all-gather.32.cloned.1.call-start = ((), (), s32[]{:S(2)}) async-start(), calls=%async_computation.28 | async-start | bytes 5242880 | tf_op jit(solution)/shard_map/all_gather | solution.py:251
  1263.5 273.4 %reduce-scatter.26.cloned.1.call-start = ((), (), s32[]{:S(2)}) async-start(), calls=%async_computation.29 | async-start | bytes 10485760 | tf_op jit(solution)/shard_map/reduce_scatter | solution.py:254
  1393.7 231.1 %all-gather.34.cloned.1.call-start = ((), (), s32[]{:S(2)}) async-start(), calls=%async_computation.30 | async-start | bytes 5242880 | tf_op jit(solution)/shard_map/all_gather | solution.py:251
  1543.2 446.0 %reduce-scatter.28.cloned.1.call-start = ((), (), s32[]{:S(2)}) async-start(), calls=%async_computation.31 | async-start | bytes 10485760 | tf_op jit(solution)/shard_map/reduce_scatter | solution.py:254
  1846.1 145.7 %copy-start.56 = (f32[1024]{0:T(1024)S(1)}, f32[1024]{0:T(1024)}, u32[]{:S(2)}) copy-start(f32[1024]{0:T(1024)} %get-tuple-element.655) | copy-start | bytes 12292
  1846.1 145.7 %copy-start.57 = (f32[1024]{0:T(1024)S(1)}, f32[1024]{0:T(1024)}, u32[]{:S(2)}) copy-start(f32[1024]{0:T(1024)} %get-tuple-element.678) | copy-start | bytes 12292
  1846.1 145.7 %copy-start.58 = (f32[1024]{0:T(1024)S(1)}, f32[1024]{0:T(1024)}, u32[]{:S(2)}) copy-start(f32[1024]{0:T(1024)} %get-tuple-element.571) | copy-start | bytes 12292
  1846.1 221.6 %reduce-scatter.46.cloned.1.call-start = ((), (), s32[]{:S(2)}) async-start(), calls=%async_computation.40 | async-start | bytes 147456
  1849.9 223.3 %reduce-scatter.44.cloned.1.call-start = ((), (), s32[]{:S(2)}) async-start(), calls=%async_computation.39 | async-start | bytes 73728 | tf_op jit(solution)/shard_map/reduce_scatter | solution.py:401
  1993.1 143.1 %reduce-scatter.40.cloned.1.call-start = ((), (), s32[]{:S(2)}) async-start(), calls=%async_computation.37 | async-start | bytes 9437184 | tf_op jit(solution)/shard_map/reduce_scatter | solution.py:397
  2007.8 204.1 %reduce-scatter.42.cloned.1.call-start = ((), (), s32[]{:S(2)}) async-start(), calls=%async_computation.38 | async-start | bytes 9437184 | tf_op jit(solution)/shard_map/reduce_scatter | solution.py:398
  2022.7 229.1 %reduce-scatter.38.cloned.1.call-start = ((), (), s32[]{:S(2)}) async-start(), calls=%async_computation.36 | async-start | bytes 1179648 | tf_op jit(solution)/shard_map/reduce_scatter | solution.py:396
  2028.3 270.1 %reduce-scatter.30.cloned.1.call-start = ((), (), s32[]{:S(2)}) async-start(), calls=%async_computation.32 | async-start | bytes 2621440 | tf_op jit(solution)/shard_map/reduce_scatter | solution.py:337
  2033.1 315.1 %reduce-scatter.36.cloned.1.call-start = ((), (), s32[]{:S(2)}) async-start(), calls=%async_computation.35 | async-start | bytes 3538944 | tf_op jit(solution)/shard_map/reduce_scatter | solution.py:395
  2038.9 349.1 %reduce-scatter.34.cloned.1.call-start = ((), (), s32[]{:S(2)}) async-start(), calls=%async_computation.34 | async-start | bytes 1179648 | tf_op jit(solution)/shard_map/reduce_scatter | solution.py:394
  2043.6 394.5 %reduce-scatter.32.cloned.1.call-start = ((), (), s32[]{:S(2)}) async-start(), calls=%async_computation.33 | async-start | bytes 3538944 | tf_op jit(solution)/shard_map/reduce_scatter | solution.py:393
  (83 other events, 3257.6 us)
Sparse Core Ops, SparseCore 0:
  9.9 28.3 all-gather.15
  40.5 80.7 all-gather.13
  216.9 143.0 reduce-scatter.17
  361.4 28.6 all-gather.21
  391.8 25.1 all-gather.19
  419.0 80.7 all-gather.17
  541.1 142.9 reduce-scatter.19
  686.0 37.4 all-gather.25
  725.7 80.7 all-gather.23
  807.9 79.2 all-gather.29
  889.1 35.9 all-gather.27
  966.4 144.4 reduce-scatter.23
  1113.3 145.1 reduce-scatter.21
  1263.6 81.4 all-gather.31
  1393.9 142.9 reduce-scatter.25
  1543.3 81.4 all-gather.33
  1846.2 142.9 reduce-scatter.27
  1992.1 34.0 reduce-scatter.45
  2029.5 31.4 reduce-scatter.43
  2064.8 71.2 reduce-scatter.39
  2140.6 71.2 reduce-scatter.41
  2215.6 36.0 reduce-scatter.37
  2254.6 43.8 reduce-scatter.29
  2302.7 45.5 reduce-scatter.35
  2352.0 36.0 reduce-scatter.33
  2391.9 46.1 reduce-scatter.31
where the time goes:
time: 2450 us; the launch traced here: 2440 us
  waiting for transfers between devices  1760 us (72%)
  matrix products  380 us (16%)
  other arithmetic  132 us (5%)
  blocking collectives  75.2 us (3%)
  local copies, waits for them, and re-layouts  59.2 us (2%)
    reduce_scatter x3, waiting for transfers between devices, narrow(): lax.psum_scatter(term(jnp.int32(0), rows_dev * lax.axis_size('tensor')),...  412 us
    reduce_scatter x2, waiting for transfers between devices, head_branch(): lax.psum_scatter(term(jnp.int32(0), rows_dev * lax.axis_size('tensor')),...  284 us
    all_gather x3, waiting for transfers between devices, spread(): return lax.all_gather(low_rows, 'tensor', axis=0, tiled=True)  238 us
    all_gather x3, waiting for transfers between devices, widen(): return lax.all_gather(low_rows, 'tensor', axis=0, tiled=True)  224 us
    reduce_scatter x1, waiting for transfers between devices, shards(): lax.psum_scatter(term(jnp.int32(0), rows_dev * lax.axis_size('tensor')),...  145 us
    reduce_scatter x1, waiting for transfers between devices, shards(): lax.psum_scatter(grad_hidden_out, 'dp', scatter_dimension=1, tiled=True)  75.7 us
    dot_general x10, matrix products, product_right_t(): lax.dot_general(left, right, (((1,), (1,)), ((), ())), preferred_element_...  68.5 us
    dot_general x10, matrix products, product(): return jnp.dot(left, right, preferred_element_type=jnp.float32)  65.7 us
  transfers between devices with their start and end apart: 26, of which 23 were waited for; matrix products, arithmetic and copies ran while one was open for 5% of the time, Pallas kernels for 0%

commit v1 on v0

--- a/solution.py
+++ b/solution.py
@@ -1,14 +1,231 @@
+import functools
 import math
 
 import jax
 import jax.numpy as jnp
 from jax import lax
+from jax.experimental import pallas as pl
+from jax.experimental.pallas import tpu as pltpu
+from jax.sharding import Mesh
 from jax.sharding import PartitionSpec as P
 
 HD = 64
 PROMPT = 1024
 CONT_TOK = 1024
 ENC = 512
+BLOCK = 256
+PAIR = 2 * HD
+AXES = ("y", "x", "core", "zhi", "zlo")
+
+
+def lane_half():
+    return lax.broadcasted_iota(jnp.int32, (1, PAIR), 1) < HD
+
+
+def one_head(rows, head):
+    keep = lane_half() if head == 0 else jnp.logical_not(lane_half())
+    return rows * jnp.where(keep, 1.0, 0.0).astype(rows.dtype)
+
+
+def dot_nt(left, right):
+    return lax.dot_general(left, right, (((1,), (1,)), ((), ())), preferred_element_type=jnp.float32)
+
+
+def dot_nn(left, right):
+    return jnp.dot(left, right, preferred_element_type=jnp.float32)
+
+
+def dot_tn(left, right):
+    return lax.dot_general(left, right, (((0,), (0,)), ((), ())), preferred_element_type=jnp.float32)
+
+
+def self_sections(meta_ref, segments):
+    def at(block):
+        return pl.multiple_of(meta_ref[block], 512)
+
+    def place(index):
+        return pl.multiple_of(meta_ref[index >> 1] + (index & 1) * BLOCK, BLOCK)
+
+    def causal(row, col):
+        return col <= row
+
+    def banded(row, col):
+        start = jnp.full(row.shape, meta_ref[4], jnp.int32)
+        for segment in range(1, segments):
+            bound = meta_ref[4 + segment]
+            start = jnp.where(row >= bound, bound, start)
+        return (col <= row) & (col >= start)
+
+    def early(index):
+        return [(at(0), 512, 0, causal)]
+
+    def middle(index):
+        return [(at(0), 512, 0, None), (at(1), 512, 512, causal)]
+
+    def late(index):
+        return [
+            (at(0), 512, 0, None),
+            (at(1), 512, 512, None),
+            (place(index - 1), BLOCK, (index - 1) * BLOCK, banded),
+            (place(index), BLOCK, index * BLOCK, banded),
+        ]
+
+    return place, ((0, 2, early), (2, 4, middle), (4, 8, late))
+
+
+def cross_sections(meta_ref, blocks):
+    def place(index):
+        return pl.multiple_of(index * BLOCK, BLOCK)
+
+    def usable(row, col):
+        return col < meta_ref[0]
+
+    def every(index):
+        return [(0, ENC, 0, usable)]
+
+    return place, ((0, blocks, every),)
+
+
+def forward_kernel(sections, meta_ref, q_ref, k_ref, v_ref, o_ref, lse_ref):
+    place, ranges = sections(meta_ref)
+
+    for low, high, parts_of in ranges:
+
+        def step(index, carry, parts_of=parts_of):
+            rows = pl.ds(place(index), BLOCK)
+            parts = parts_of(index)
+            queries = q_ref[rows, :]
+            row = index * BLOCK + lax.broadcasted_iota(jnp.int32, (BLOCK, 1), 0)
+            allowed = [
+                None if rule is None else rule(row, first + lax.broadcasted_iota(jnp.int32, (1, size), 1))
+                for _, size, first, rule in parts
+            ]
+            outs, totals = [], []
+            for head in range(2):
+                query = one_head(queries, head)
+                scores = []
+                for (where, size, _, _), ok in zip(parts, allowed):
+                    score = dot_nt(query, k_ref[pl.ds(where, size), :])
+                    scores.append(score if ok is None else jnp.where(ok, score, -1e30))
+                top = functools.reduce(jnp.maximum, [jnp.max(s, axis=1, keepdims=True) for s in scores])
+                exps = [jnp.exp(s - top) for s in scores]
+                total = sum(jnp.sum(e, axis=1, keepdims=True) for e in exps)
+                mixed = sum(
+                    dot_nn(e.astype(jnp.bfloat16), v_ref[pl.ds(where, size), :])
+                    for (where, size, _, _), e in zip(parts, exps)
+                )
+                outs.append(mixed * (1.0 / total))
+                totals.append(top + jnp.log(total))
+            o_ref[rows, :] = jnp.where(lane_half(), outs[0], outs[1]).astype(o_ref.dtype)
+            lse_ref[rows, :] = jnp.where(lane_half(), totals[0], totals[1])
+            return carry
+
+        lax.fori_loop(low, high, step, 0)
+
+
+def backward_kernel(
+    sections, meta_ref, q_ref, k_ref, v_ref, o_ref, do_ref, lse_ref, dq_ref, dk_ref, dv_ref, dk_sum, dv_sum
+):
+    place, ranges = sections(meta_ref)
+    dk_sum[...] = jnp.zeros_like(dk_sum)
+    dv_sum[...] = jnp.zeros_like(dv_sum)
+
+    for low, high, parts_of in ranges:
+
+        def step(index, carry, parts_of=parts_of):
+            rows = pl.ds(place(index), BLOCK)
+            parts = parts_of(index)
+            queries, grads = q_ref[rows, :], do_ref[rows, :]
+            row = index * BLOCK + lax.broadcasted_iota(jnp.int32, (1, BLOCK), 1)
+            allowed = [
+                None if rule is None else rule(row, first + lax.broadcasted_iota(jnp.int32, (size, 1), 0))
+                for _, size, first, rule in parts
+            ]
+            logs = jnp.transpose(lse_ref[rows, :])
+            spread = jnp.transpose(grads.astype(jnp.float32) * o_ref[rows, :].astype(jnp.float32))
+            key_parts = [k_ref[pl.ds(where, size), :] for where, size, _, _ in parts]
+            value_parts = [v_ref[pl.ds(where, size), :] for where, size, _, _ in parts]
+            query_grads = []
+            for head in range(2):
+                query, grad = one_head(queries, head), one_head(grads, head)
+                log = logs[head * HD : head * HD + 1, :]
+                delta = jnp.sum(spread[head * HD : (head + 1) * HD, :], axis=0, keepdims=True)
+                query_grad = None
+                for (where, size, _, _), ok, keys, values in zip(parts, allowed, key_parts, value_parts):
+                    score = dot_nt(keys, query)
+                    if ok is not None:
+                        score = jnp.where(ok, score, -1e30)
+                    probs = jnp.exp(score - log)
+                    score_grad = (probs * (dot_nt(values, grad) - delta)).astype(jnp.bfloat16)
+                    dv_sum[pl.ds(where, size), :] += dot_nn(probs.astype(jnp.bfloat16), grad)
+                    dk_sum[pl.ds(where, size), :] += dot_nn(score_grad, query)
+                    term = dot_tn(score_grad, keys)
+                    query_grad = term if query_grad is None else query_grad + term
+                query_grads.append(query_grad)
+            both = jnp.where(lane_half(), query_grads[0], query_grads[1])
+            dq_ref[rows, :] = both.astype(jnp.bfloat16) * jnp.asarray(HD**-0.5, jnp.bfloat16)
+            return carry
+
+        lax.fori_loop(low, high, step, 0)
+    dk_ref[...] = dk_sum[...].astype(dk_ref.dtype)
+    dv_ref[...] = dv_sum[...].astype(dv_ref.dtype)
+
+
+def columns(rows, first):
+    return pl.BlockSpec((rows, PAIR), lambda pair, meta: (0, first + pair))
+
+
+def attend(sections, meta, q, q_at, keys, k_at, v_at, pairs, weight):
+    count, key_rows = q.shape[0], keys.shape[0]
+    return pl.pallas_call(
+        functools.partial(forward_kernel, sections),
+        grid_spec=pltpu.PrefetchScalarGridSpec(
+            num_scalar_prefetch=1,
+            grid=(pairs,),
+            in_specs=[columns(count, q_at), columns(key_rows, k_at), columns(key_rows, v_at)],
+            out_specs=[columns(count, 0), columns(count, 0)],
+        ),
+        out_shape=[
+            jax.ShapeDtypeStruct((count, pairs * PAIR), jnp.bfloat16),
+            jax.ShapeDtypeStruct((count, pairs * PAIR), jnp.float32),
+        ],
+        cost_estimate=pl.CostEstimate(
+            flops=2 * 4 * 4 * count * weight * pairs * PAIR,
+            bytes_accessed=10 * count * pairs * PAIR,
+            transcendentals=2 * pairs * count * weight,
+        ),
+    )(meta, q, keys, keys)
+
+
+def attend_back(sections, meta, q, q_at, keys, k_at, v_at, out, out_grad, lse, pairs, weight):
+    count, key_rows = q.shape[0], keys.shape[0]
+    return pl.pallas_call(
+        functools.partial(backward_kernel, sections),
+        grid_spec=pltpu.PrefetchScalarGridSpec(
+            num_scalar_prefetch=1,
+            grid=(pairs,),
+            in_specs=[
+                columns(count, q_at),
+                columns(key_rows, k_at),
+                columns(key_rows, v_at),
+                columns(count, 0),
+                columns(count, 0),
+                columns(count, 0),
+            ],
+            out_specs=[columns(count, 0), columns(key_rows, 0), columns(key_rows, 0)],
+            scratch_shapes=[pltpu.VMEM((key_rows, PAIR), jnp.float32)] * 2,
+        ),
+        out_shape=[
+            jax.ShapeDtypeStruct((count, pairs * PAIR), jnp.bfloat16),
+            jax.ShapeDtypeStruct((key_rows, pairs * PAIR), jnp.bfloat16),
+            jax.ShapeDtypeStruct((key_rows, pairs * PAIR), jnp.bfloat16),
+        ],
+        cost_estimate=pl.CostEstimate(
+            flops=5 * 4 * 4 * count * weight * pairs * PAIR,
+            bytes_accessed=20 * count * pairs * PAIR,
+            transcendentals=2 * pairs * count * weight,
+        ),
+    )(meta, q, keys, keys, out, out_grad, lse)
 
 
 EPSILON = 1e-05
@@ -417,35 +634,354 @@
     )
 
 
+def trade(rows, axis):
+    return lax.ppermute(rows, axis, [(0, 1), (1, 0)])
+
+
+def regroup(rows):
+    return lax.ppermute(rows, ("core", "zhi"), [(0, 0), (1, 2), (2, 1), (3, 3)])
+
+
+def in_order(index, own, other, axis):
+    return jnp.concatenate(
+        [jnp.where(index == 0, own, other), jnp.where(index == 0, other, own)], axis=axis
+    )
+
+
+def low(values):
+    return values.astype(jnp.bfloat16)
+
+
+def half_of(values, index, axis):
+    size = values.shape[axis] // 2
+    return lax.dynamic_slice_in_dim(values, index * size, size, axis)
+
+
+def over_chips(rows):
+    return lax.all_gather(rows, ("y", "x"), axis=0, tiled=True)
+
+
+def sum_over_chips(partial):
+    return lax.psum_scatter(partial, ("y", "x"), scatter_dimension=0, tiled=True)
+
+
+def spread_rows(rows):
+    beyond = trade(rows, "zlo")
+    return (
+        jnp.concatenate([rows, trade(rows, "core")], axis=0),
+        jnp.concatenate([beyond, trade(beyond, "core")], axis=0),
+    )
+
+
+def sum_rows(near, far, term):
+    size = near.shape[0] // 2
+    far_sum = term(far[:size]) + trade(low(term(far[size:])), "core")
+    from_far = trade(low(far_sum), "zlo")
+    near_other = trade(low(term(near[size:])), "core")
+    return term(near[:size]) + near_other + from_far
+
+
+def fast_layer(
+    tokens,
+    enc_states,
+    enc_len,
+    cont_lengths,
+    cotangent,
+    self_qkv,
+    self_out,
+    cross_qkv,
+    cross_out,
+    ff_in,
+    ff_out,
+    head_bias,
+    ff_bias,
+    vec_params,
+):
+    core, zhi, zlo = lax.axis_index("core"), lax.axis_index("zhi"), lax.axis_index("zlo")
+    scaling = HD**-0.5
+    model = tokens.shape[1]
+    segments = cont_lengths.shape[1]
+
+    flat = jnp.concatenate([vec_params.reshape(-1), head_bias.reshape(-1), ff_bias])
+    sizes = (vec_params.size, head_bias.size, ff_bias.size)
+    small = lax.all_gather(flat, AXES, axis=0).reshape(8, 4, -1).astype(jnp.float32)
+    vec_part, head_part, ff_part = jnp.split(small, [sizes[0], sizes[0] + sizes[1]], axis=2)
+    vectors = vec_part[:, 0].reshape(8, 9, -1).transpose(1, 0, 2).reshape(9, model)
+    heads = head_part.reshape(8, 4, 4, -1).transpose(2, 1, 0, 3).reshape(4, 2, 2, 2, -1)
+    self_bias = lax.dynamic_index_in_dim(
+        lax.dynamic_index_in_dim(heads[:2], zlo, 2, False), core, 2, False
+    ).reshape(2, -1)
+    cross_bias = lax.dynamic_index_in_dim(heads[2:], core, 3, False).reshape(2, -1)
+    hidden_bias = ff_part.transpose(1, 0, 2).reshape(2, 2, 2, -1)
+    hidden_bias = lax.dynamic_index_in_dim(
+        lax.dynamic_index_in_dim(hidden_bias, zlo, 1, False), core, 1, False
+    ).reshape(-1)
+
+    token_rows = regroup(tokens)
+    grad_rows = regroup(cotangent)
+    lengths = regroup(jnp.concatenate([cont_lengths[0], enc_len]))
+    places = jnp.stack(
+        [512 * ((core != block // 2) + 2 * (zlo != block % 2)) for block in range(4)]
+    ).astype(jnp.int32)
+    bounds = PROMPT + jnp.concatenate(
+        [jnp.zeros((1,), jnp.int32), jnp.cumsum(lengths[:segments]).astype(jnp.int32)]
+    )
+    self_meta = jnp.concatenate([places, bounds])
+    cross_meta = lengths[segments:]
+
+    attention = jnp.concatenate([self_qkv, self_out.T[None], cross_qkv, cross_out.T[None]], axis=0)
+    mine, theirs = half_of(attention, core, 2), half_of(attention, 1 - core, 2)
+    attention = in_order(core, mine, trade(theirs, "core"), 1)
+    rows_of = attention.shape[1]
+    own = attention[:4].transpose(1, 0, 2)[:, :, None]
+    own = in_order(zhi, own, trade(own, "zhi"), 2)
+    w_self = over_chips(own.reshape(rows_of, -1))
+    own = attention[4:].transpose(1, 0, 2)[:, :, None]
+    own = in_order(zlo, own, trade(own, "zlo"), 2)[:, :, None]
+    own = in_order(zhi, own, trade(own, "zhi"), 2)
+    w_cross = over_chips(own.reshape(rows_of, -1))
+    hidden = jnp.stack([ff_in, ff_out.T])
+    mine, theirs = half_of(hidden, core, 2), half_of(hidden, 1 - core, 2)
+    hidden = in_order(core, mine, trade(theirs, "core"), 1)
+    hidden = in_order(zhi, hidden, trade(hidden, "zhi"), 2)
+    w_in = over_chips(hidden[0])
+    w_out = over_chips(hidden[1])
+    width = w_self.shape[1] // 4
+    pairs = width // PAIR
+    cross_width = w_cross.shape[1] // 4
+    cross_pairs = cross_width // PAIR
+
+    enc_rows = regroup(enc_states)
+    enc_both = in_order(zlo, enc_rows, trade(enc_rows, "zlo"), 0)
+    enc_full = in_order(core, enc_both, trade(enc_both, "core"), 0)
+
+    resid = token_rows.astype(jnp.float32)
+    normed_in, hat_one, inv_one = norm_forward(resid, vectors[0], vectors[3])
+    attn_near, attn_far = spread_rows(low(normed_in))
+    qkv_bias = jnp.concatenate([self_bias[0], jnp.zeros((width,), jnp.float32), self_bias[1]])
+    qkv_scale = jnp.concatenate([jnp.full((width,), scaling), jnp.ones((2 * width,))]).astype(jnp.float32)
+    w_qkv, w_so = w_self[:, : 3 * width], w_self[:, 3 * width :]
+
+    def project(rows):
+        return low((product(rows, w_qkv) + qkv_bias) * qkv_scale)
+
+    qkv = jnp.concatenate([project(attn_near), project(attn_far)], axis=0)
+    count = qkv.shape[0]
+    self_plan = functools.partial(self_sections, segments=segments)
+    mixed, self_lse = attend(self_plan, self_meta, qkv, 0, qkv, pairs, 2 * pairs, pairs, 1152)
+    near, far = mixed[: count // 2], mixed[count // 2 :]
+    branch = sum_rows(near, far, lambda rows: product_right_t(rows, w_so))
+    after_one = resid + (branch + vectors[6])
+
+    normed_mid, hat_two, inv_two = norm_forward(after_one, vectors[1], vectors[4])
+    cross_low = low(normed_mid)
+    cross_rows = jnp.concatenate([cross_low, trade(cross_low, "core")], axis=0)
+    own_rows = cross_low.shape[0]
+    w_cq = w_cross[:, :cross_width]
+    w_ckv = w_cross[:, cross_width : 3 * cross_width]
+    w_co = w_cross[:, 3 * cross_width :]
+    cross_kv = low(
+        product(enc_full, w_ckv)
+        + jnp.concatenate([jnp.zeros((cross_width,), jnp.float32), cross_bias[1]])
+    )
+    cross_q = low((product(cross_rows, w_cq) + cross_bias[0]) * scaling)
+    cross_plan = functools.partial(cross_sections, blocks=cross_q.shape[0] // BLOCK)
+    cross_mixed, cross_lse = attend(
+        cross_plan, cross_meta, cross_q, 0, cross_kv, 0, cross_pairs, cross_pairs, ENC
+    )
+    other = trade(low(product_right_t(cross_mixed[own_rows:], w_co)), "core")
+    branch = product_right_t(cross_mixed[:own_rows], w_co) + other
+    after_two = after_one + (branch + vectors[7])
+
+    normed_out, hat_three, inv_three = norm_forward(after_two, vectors[2], vectors[5])
+    mlp_near, mlp_far = spread_rows(low(normed_out))
+    grad_near, grad_far = spread_rows(grad_rows)
+    pre_near = product(mlp_near, w_in) + hidden_bias
+    pre_far = product(mlp_far, w_in) + hidden_bias
+    act_near, act_far = low(gelu_value(pre_near)), low(gelu_value(pre_far))
+    dpre_near = low(product(grad_near, w_out) * gelu_slope(pre_near))
+    dpre_far = low(product(grad_far, w_out) * gelu_slope(pre_far))
+    gradient = grad_rows.astype(jnp.float32)
+    bias_out_three = jnp.sum(gradient, axis=0)
+    mlp_term = sum_rows(dpre_near, dpre_far, lambda rows: product_right_t(rows, w_in))
+    branch = sum_rows(act_near, act_far, lambda rows: product_right_t(rows, w_out))
+    layer_out = regroup(low(after_two + (branch + vectors[8])))
+    grad_w_out = product_left_t(grad_near, act_near) + product_left_t(grad_far, act_far)
+    grad_w_in = product_left_t(mlp_near, dpre_near) + product_left_t(mlp_far, dpre_far)
+    grad_hidden_bias = jnp.sum(dpre_near.astype(jnp.float32), axis=0) + jnp.sum(
+        dpre_far.astype(jnp.float32), axis=0
+    )
+    part, gain_three, shift_three = norm_backward(mlp_term, hat_three, inv_three, vectors[2])
+    gradient = gradient + part
+
+    grad_low = low(gradient)
+    bias_out_two = jnp.sum(grad_low.astype(jnp.float32), axis=0)
+    grad_both = jnp.concatenate([grad_low, trade(grad_low, "core")], axis=0)
+    cross_mixed_grad = low(product(grad_both, w_co))
+    cross_dq, cross_dk, cross_dv = attend_back(
+        cross_plan,
+        cross_meta,
+        cross_q,
+        0,
+        cross_kv,
+        0,
+        cross_pairs,
+        cross_mixed,
+        cross_mixed_grad,
+        cross_lse,
+        cross_pairs,
+        ENC,
+    )
+    other = trade(low(product_right_t(cross_dq[own_rows:], w_cq)), "core")
+    part, gain_two, shift_two = norm_backward(
+        product_right_t(cross_dq[:own_rows], w_cq) + other, hat_two, inv_two, vectors[1]
+    )
+    gradient = gradient + part
+    grad_cross = jnp.concatenate(
+        [
+            low(product_left_t(cross_rows, cross_dq)),
+            low(product_left_t(enc_full, cross_dk)),
+            low(product_left_t(enc_full, cross_dv)),
+            low(product_left_t(grad_both, cross_mixed)),
+        ],
+        axis=1,
+    )
+    bias_cross_query = jnp.sum(cross_dq.astype(jnp.float32), axis=0)
+    bias_cross_value = jnp.sum(cross_dv.astype(jnp.float32), axis=0)
+
+    def enc_term(rows):
+        return product_right_t(half_of(cross_dk, rows, 0), w_ckv[:, :cross_width]) + product_right_t(
+            half_of(cross_dv, rows, 0), w_ckv[:, cross_width:]
+        )
+
+    enc_half = enc_term(core) + trade(low(enc_term(1 - core)), "core")
+    enc_sum = half_of(enc_half, zlo, 0) + trade(low(half_of(enc_half, 1 - zlo, 0)), "zlo")
+    enc_grad = regroup(low(enc_sum)).astype(jnp.float32)
+
+    grad_low = low(gradient)
+    bias_out_one = jnp.sum(grad_low.astype(jnp.float32), axis=0)
+    grad_near, grad_far = spread_rows(grad_low)
+    mixed_grad = jnp.concatenate([low(product(grad_near, w_so)), low(product(grad_far, w_so))], axis=0)
+    dq, dk, dv = attend_back(
+        self_plan, self_meta, qkv, 0, qkv, pairs, 2 * pairs, mixed, mixed_grad, self_lse, pairs, 1152
+    )
+    dqkv = jnp.concatenate([dq, dk, dv], axis=1)
+    d_near, d_far = dqkv[: count // 2], dqkv[count // 2 :]
+    part, gain_one, shift_one = norm_backward(
+        sum_rows(d_near, d_far, lambda rows: product_right_t(rows, w_qkv)), hat_one, inv_one, vectors[0]
+    )
+    input_grad = regroup(low(gradient + part)).astype(jnp.float32)
+    grad_self = jnp.concatenate(
+        [
+            low(product_left_t(attn_near, d_near) + product_left_t(attn_far, d_far)),
+            low(product_left_t(grad_near, near) + product_left_t(grad_far, far)),
+        ],
+        axis=1,
+    )
+    bias_self_query = jnp.sum(dq.astype(jnp.float32), axis=0)
+    bias_self_value = jnp.sum(dv.astype(jnp.float32), axis=0)
+
+    def keep_half(values, index, axis, axis_name):
+        kept = half_of(values, index, axis).astype(jnp.float32)
+        return kept + trade(half_of(values, 1 - index, axis), axis_name).astype(jnp.float32)
+
+    def to_shards(values):
+        kept, sent = half_of(values, core, 0), half_of(values, 1 - core, 0)
+        return in_order(core, kept, trade(low(sent), "core").astype(jnp.float32), values.ndim - 1)
+
+    def hidden_shard(partial):
+        total = sum_over_chips(low(partial))
+        return to_shards(keep_half(total, zhi, 1, "zhi"))
+
+    ff_in_grad = hidden_shard(grad_w_in)
+    ff_out_grad = hidden_shard(grad_w_out).T
+    total = sum_over_chips(grad_cross).reshape(rows_of, 4, 2, -1)
+    total = low(keep_half(total, zhi, 2, "zhi")).reshape(rows_of, 4, 2, -1)
+    cross_grad = to_shards(keep_half(total, zlo, 2, "zlo").reshape(rows_of, 4, -1))
+    total = sum_over_chips(grad_self).reshape(rows_of, 4, 2, -1)
+    self_grad = to_shards(keep_half(total, zhi, 2, "zhi").reshape(rows_of, 4, -1))
+
+    vec_sums = jnp.stack(
+        [
+            gain_one,
+            gain_two,
+            gain_three,
+            shift_one,
+            shift_two,
+            shift_three,
+            bias_out_one,
+            bias_out_two,
+            bias_out_three,
+        ]
+    )
+    at_zlo = (jnp.arange(2) == zlo).astype(jnp.float32)
+    at_core = (jnp.arange(2) == core).astype(jnp.float32)
+    quarter = (at_zlo[:, None] * at_core[None, :])[:, :, None]
+    self_sums = jnp.stack([bias_self_query, bias_self_value]).reshape(2, 2, 1, 1, -1) * quarter
+    cross_sums = jnp.stack([bias_cross_query, bias_cross_value]).reshape(2, 2, 2, 1, -1) * at_core[:, None]
+    head_sums = jnp.concatenate([self_sums, cross_sums], axis=0)
+    hidden_sums = grad_hidden_bias.reshape(2, 1, 1, -1) * quarter
+    vec_sums = jnp.broadcast_to(vec_sums.reshape(9, 8, -1).transpose(1, 0, 2).reshape(8, 1, -1), (8, 4, sizes[0]))
+    head_sums = head_sums.reshape(4, 4, 8, -1).transpose(2, 1, 0, 3).reshape(8, 4, -1)
+    hidden_sums = hidden_sums.reshape(4, 8, -1).transpose(1, 0, 2)
+    sums = jnp.concatenate([vec_sums, head_sums, hidden_sums], axis=2).reshape(32, -1)
+    sums = lax.psum_scatter(sums, AXES, scatter_dimension=0, tiled=True).reshape(-1)
+    vec_grad, head_grad, ff_bias_grad = jnp.split(sums, [sizes[0], sizes[0] + sizes[1]])
+    return (
+        layer_out,
+        input_grad,
+        enc_grad,
+        self_grad[:, :3].transpose(1, 0, 2),
+        self_grad[:, 3].T,
+        cross_grad[:, :3].transpose(1, 0, 2),
+        cross_grad[:, 3].T,
+        ff_in_grad,
+        ff_out_grad,
+        head_grad.reshape(head_bias.shape),
+        ff_bias_grad,
+        vec_grad.reshape(vec_params.shape),
+    )
+
+
 def solution(mesh):
+    fast = tuple(mesh.shape[axis] for axis in ("dp", "tensor")) == (8, 4)
+    dp, tensor = (AXES[:3], AXES[3:]) if fast else (("dp",), ("tensor",))
+    both = dp + tensor
+    rows = P(both, None)
+    qkv = P(None, dp, tensor)
+    out = P(tensor, dp)
     in_specs = (
-        P(("dp", "tensor"), None),
-        P(("dp", "tensor"), None),
-        P("dp"),
-        P("dp", None),
-        P(("dp", "tensor"), None),
-        P(None, "dp", "tensor"),
-        P("tensor", "dp"),
-        P(None, "dp", "tensor"),
-        P("tensor", "dp"),
-        P("dp", "tensor"),
-        P("tensor", "dp"),
-        P(None, ("tensor", "dp")),
-        P(("tensor", "dp")),
-        P(None, "dp"),
+        rows,
+        rows,
+        P(dp),
+        P(dp, None),
+        rows,
+        qkv,
+        out,
+        qkv,
+        out,
+        P(dp, tensor),
+        out,
+        P(None, tensor + dp),
+        P(tensor + dp),
+        P(None, dp),
     )
     out_specs = (
-        P(("dp", "tensor"), None),
-        P(("dp", "tensor"), None),
-        P(("dp", "tensor"), None),
-        P(None, "dp", "tensor"),
-        P("tensor", "dp"),
-        P(None, "dp", "tensor"),
-        P("tensor", "dp"),
-        P("dp", "tensor"),
-        P("tensor", "dp"),
-        P(None, ("tensor", "dp")),
-        P(("tensor", "dp")),
-        P(None, "dp"),
-    )
-    return jax.shard_map(shards, mesh=mesh, in_specs=in_specs, out_specs=out_specs, check_vma=False)
+        rows,
+        rows,
+        rows,
+        qkv,
+        out,
+        qkv,
+        out,
+        P(dp, tensor),
+        out,
+        P(None, tensor + dp),
+        P(tensor + dp),
+        P(None, dp),
+    )
+    if fast:
+        mesh = Mesh(mesh.devices.reshape(2, 2, 2, 2, 2), AXES)
+    return jax.shard_map(
+        fast_layer if fast else shards, mesh=mesh, in_specs=in_specs, out_specs=out_specs, check_vma=False
+    )

time: 2450 us -> 986 us (0.40)
  waiting for transfers between devices: 1760 us -> 427 us
  matrix products: 380 us -> 180 us
  Pallas kernels: 0 us -> 94.7 us
  other arithmetic: 132 us -> 51.8 us
  starting transfers between devices: 1.45 us -> 69.5 us
    reduce_scatter x14 -> x4, waiting for transfers between devices: 1190 us -> 85.7 us  [sum_over_chips(): lax.psum_scatter(partial, ('y', 'x'), scatter_dimension=0, tiled=True)]
    all_gather x11 -> x4, waiting for transfers between devices: 566 us -> 0.02 us  [over_chips(): return lax.all_gather(rows, ('y', 'x'), axis=0, tiled=True)]
    ppermute x0 -> x54, waiting for transfers between devices: none -> 299 us  [the longest x47 299 us: trade(): return lax.ppermute(rows, axis, [(0, 1), (1, 0)])]
    dot_general x56 -> x0, matrix products: 197 us -> none  [the longest x8 48.9 us: back_block(): jnp.einsum('qhd,khd->hqk', grad_block, value_heads, preferred_element_typ...]
    pallas_call x0 -> x4, Pallas kernels: none -> 94.7 us  [the longest x2 56.2 us: attend_back(): pl.pallas_call(functools.partial(backward_kernel, sections), grid_spec=pl...]
    ppermute x0 -> x54, starting transfers between devices: none -> 68.3 us  [the longest x47 42.5 us: trade(): return lax.ppermute(rows, axis, [(0, 1), (1, 0)])]
    convert_element_type x15 -> x10, other arithmetic: 56 us -> 11.1 us  [the longest x6 6.95 us: low(): return values.astype(jnp.bfloat16)]
    unnamed x27 -> x10, waiting for transfers between devices: 3.98 us -> 42.2 us
  transfers between devices with their start and end apart: 26 -> 63, of which waited for: 23 -> 23; matrix products, arithmetic and copies ran while one was open for 5% -> 27% of each run, Pallas kernels for 0% -> 10%
where the time goes in v1:
time: 986 us; the launch traced here: 978 us
  waiting for transfers between devices  427 us (43%)
  matrix products  180 us (18%)
  Pallas kernels  94.7 us (10%)
  blocking collectives  84.8 us (9%)
  starting transfers between devices  69.5 us (7%)
  local copies, waits for them, and re-layouts  54 us (5%)
  other arithmetic  51.8 us (5%)
  between operations  16.5 us (2%)
    ppermute x47, waiting for transfers between devices, trade(): return lax.ppermute(rows, axis, [(0, 1), (1, 0)])  299 us
    reduce_scatter x4, waiting for transfers between devices, sum_over_chips(): lax.psum_scatter(partial, ('y', 'x'), scatter_dimension=0, tiled=True)  85.7 us
    all_gather x1, blocking collectives, fast_layer(): lax.all_gather(flat, AXES, axis=0).reshape(8, 4, -1).astype(jnp.float32)  84.8 us
    dot_general x11, matrix products, product(): return jnp.dot(left, right, preferred_element_type=jnp.float32)  72.2 us
    dot_general x24, matrix products, product_right_t(): lax.dot_general(left, right, (((1,), (1,)), ((), ())), preferred_element_...  59.3 us
    pallas_call x2, Pallas kernels, attend_back(): pl.pallas_call(functools.partial(backward_kernel, sections), grid_spec=pl...  56.2 us
    dot_general x12, matrix products, product_left_t(): lax.dot_general(left, right, (((0,), (0,)), ((), ())), preferred_element_...  48.7 us
    ppermute x47, starting transfers between devices, trade(): return lax.ppermute(rows, axis, [(0, 1), (1, 0)])  42.5 us
  transfers between devices with their start and end apart: 63, of which 23 were waited for; matrix products, arithmetic and copies ran while one was open for 27% of the time, Pallas kernels for 10%

profile of v1, /device:TPU:0, one launch (start us, length us, event | category | flops | bytes accessed | tf_op | source)
XLA Modules:
  0.0 978.1 jit_solution(5331742435192992352)
XLA Ops:
  16.3 12.2 %collective-permute-done.4 = bf16[256,4,1,128]{0,3,2,1:T(8,128)(2,1)S(1)} collective-permute-done((bf16[256,4,1,128]{0,3,2,1:T(8,128)(2,1)S(1)}, bf16[256,4,1,128]{0,3,2,1:T(8,128)(2,1)S(1)}, u32[]{:S(2)}, u32[]{:S(2)}) %collective-permute-start.4) | collective-permute-done | bytes 262176 | tf_op jit(solution)/shard_map/ppermute | solution.py:638
  30.3 7.1 collective-permute-done.11
  40.4 22.8 %collective-permute-done.12 = bf16[256,4,1,2,128]{0,4,1,3,2:T(8,128)(2,1)S(1)} collective-permute-done((bf16[256,4,1,2,128]{0,4,1,3,2:T(8,128)(2,1)S(1)}, bf16[256,4,1,2,128]{0,4,1,3,2:T(8,128)(2,1)S(1)}, u32[]{:S(2)}, u32[]{:S(2)}) %collective-permute-start.12) | collective-permute-done | bytes 524320 | tf_op jit(solution)/shard_map/ppermute | solution.py:638
  67.0 84.8 %all-gather.3 = bf16[32,1,1536]{2,1,0:T(2,128)(2,1)S(1)} all-gather(bf16[1,1,1536]{2,1,0:T(2,128)(2,1)S(1)} %reshape.356), channel_id=2, replica_groups=mesh['y'=2,'x'=2,'core'=2,'zhi'=2,'zlo'=2] {'y','x','core','zhi','zlo'}, dimensions={0}, use_global_device_ids=true | all-gather | bytes 101376 | tf_op jit(solution)/shard_map/all_gather | solution.py:707
  159.2 32.5 %collective-permute-done.5 = bf16[512,1024]{1,0:T(8,128)(2,1)} collective-permute-done((bf16[512,1024]{1,0:T(8,128)(2,1)}, bf16[512,1024]{1,0:T(8,128)(2,1)}, u32[]{:S(2)}, u32[]{:S(2)}) %collective-permute-start.5) | collective-permute-done | bytes 1048608 | tf_op jit(solution)/shard_map/ppermute | solution.py:638
  192.6 9.5 collective-permute-start.2
  218.6 23.2 %shard_map.229 = (bf16[2048,256]{1,0:T(8,128)(2,1)}, f32[2048,256]{1,0:T(8,128)}) custom-call(s32[13]{0:T(128)} %concatenate.121.meta_ref, bf16[2048,768]{1,0:T(8,128)(2,1)} %pad_maximum_fusion.1.q_ref.k_ref.v_ref, bf16[2048,768]{1,0:T(8,128)(2,1)} %pad_maximum_fusion.1.q_ref.k_ref.v_ref, bf16[2048,768]{1,0:T(8,128)(2,1)} %pad_maximum_fusion.1.q_ref.k_ref.v_ref), custom_call_target="tpu_custom_call" | custom-call | flops 19327352832 | bytes 5242880 | tf_op jit(solution)/shard_map/pallas_call | solution.py:180
  249.8 24.8 %collective-permute-done.9 = bf16[512,1024]{1,0:T(8,128)(2,1)S(1)} collective-permute-done((bf16[512,1024]{1,0:T(8,128)(2,1)S(1)}, bf16[512,1024]{1,0:T(8,128)(2,1)S(1)}, u32[]{:S(2)}, u32[]{:S(2)}) %collective-permute-start.9) | collective-permute-done | bytes 1048608 | tf_op jit(solution)/shard_map/ppermute | solution.py:638
  292.9 15.3 %shard_map.230 = (bf16[1024,512]{1,0:T(8,128)(2,1)}, f32[1024,512]{1,0:T(8,128)}) custom-call(s32[1]{0:T(128)} %slice.225.meta_ref, bf16[1024,512]{1,0:T(8,128)(2,1)} %multiply_convert_fusion.4.q_ref, bf16[512,1024]{1,0:T(8,128)(2,1)} %add_convert_fusion.8.k_ref.v_ref, bf16[512,1024]{1,0:T(8,128)(2,1)} %add_convert_fusion.8.k_ref.v_ref), custom_call_target="tpu_custom_call" | custom-call | flops 8589934592 | bytes 5242880 | tf_op jit(solution)/shard_map/pallas_call | solution.py:180
  320.8 20.0 %collective-permute-done.29 = bf16[512,1024]{1,0:T(8,128)(2,1)} collective-permute-done((bf16[512,1024]{1,0:T(8,128)(2,1)S(1)}, bf16[512,1024]{1,0:T(8,128)(2,1)}, u32[]{:S(2)}, u32[]{:S(2)}) %collective-permute-start.29) | collective-permute-done | bytes 1048608 | tf_op jit(solution)/shard_map/ppermute | solution.py:638
  340.8 21.5 %collective-permute-done.21 = bf16[512,1024]{1,0:T(8,128)(2,1)S(1)} collective-permute-done((bf16[512,1024]{1,0:T(8,128)(2,1)S(1)}, bf16[512,1024]{1,0:T(8,128)(2,1)S(1)}, u32[]{:S(2)}, u32[]{:S(2)}) %collective-permute-start.21) | collective-permute-done | bytes 1048608 | tf_op jit(solution)/shard_map/ppermute | solution.py:638
  371.8 10.7 %fusion.32 = f32[1024,2048]{1,0:T(8,128)} fusion(bf16[1024,1024]{1,0:T(8,128)(2,1)} %constant_dynamic-update-slice_fusion.2, bf16[1,1024,2048]{1,2,0:T(8,128)(2,1)} %all-gather.13.cloned.1.call-done), kind=kOutput, calls=%fused_computation.43 | convolution fusion | flops 4294967296 | bytes 14680064 | tf_op jit(solution)/shard_map/dot_general | solution.py:268
  382.6 13.2 %convert_reduce_fusion = (f32[2048]{0:T(1024)S(1)}, bf16[1024,2048]{1,0:T(8,128)(2,1)S(1)}) fusion(f32[1024,2048]{1,0:T(8,128)} %fusion.32, f32[2048]{0:T(1024)S(1)} %bitcast.223, bf16[1024,1024]{1,0:T(8,128)(2,1)} %copy-done.41, bf16[1,1024,2048]{1,2,0:T(8,128)(2,1)} %all-gather.15.cloned.1.call-done), kind=kOutput, calls=%fused_computation.18 | convolution fusion | flops 4341102592 | bytes 18890752 | tf_op jit(solution)/shard_map/dot_general | solution.py:268
  401.5 15.9 %multiply_convert_fusion.1 = (bf16[1024,2048]{1,0:T(8,128)(2,1)}, bf16[1024,2048]{1,0:T(8,128)(2,1)}, f32[1024,2048]{1,0:T(8,128)}) fusion(f32[2048]{0:T(1024)S(1)} %bitcast.224, f32[1024,2048]{1,0:T(8,128)} %fusion.32, bf16[1,1024,2048]{1,2,0:T(8,128)(2,1)S(1)} %copy-done.68, bf16[512,1024]{1,0:T(8,128)(2,1)S(1)} %collective-permute-done.17, ...), kind=kOutput, calls=%fused_computation.23 | convolution fusion | flops 4341104640 | bytes 31465472 | tf_op jit(solution)/shard_map/dot_general | solution.py:268
  417.4 11.4 %convert_reduce_fusion.1 = (f32[2048]{0:T(1024)S(1)}, bf16[1024,2048]{1,0:T(8,128)(2,1)S(1)}) fusion(f32[1024,2048]{1,0:T(8,128)} %get-tuple-element.151, f32[2048]{0:T(1024)S(1)} %bitcast.225, bf16[1024,1024]{1,0:T(8,128)(2,1)S(1)} %copy-done.44, bf16[1,1024,2048]{1,2,0:T(8,128)(2,1)S(1)} %copy-done.70), kind=kOutput, calls=%fused_computation.19 | convolution fusion | flops 4341102592 | bytes 18890752 | tf_op jit(solution)/shard_map/dot_general | solution.py:268
  446.1 7.8 add_convert_fusion.1
  472.4 17.8 %collective-permute-done.32 = bf16[512,1024]{1,0:T(8,128)(2,1)S(1)} collective-permute-done((bf16[512,1024]{1,0:T(8,128)(2,1)S(1)}, bf16[512,1024]{1,0:T(8,128)(2,1)S(1)}, u32[]{:S(2)}, u32[]{:S(2)}) %collective-permute-start.32) | collective-permute-done | bytes 1048608 | tf_op jit(solution)/shard_map/ppermute | solution.py:638
  491.4 20.9 %collective-permute-done.24 = bf16[512,1024]{1,0:T(8,128)(2,1)S(1)} collective-permute-done((bf16[512,1024]{1,0:T(8,128)(2,1)S(1)}, bf16[512,1024]{1,0:T(8,128)(2,1)S(1)}, u32[]{:S(2)}, u32[]{:S(2)}) %collective-permute-start.24) | collective-permute-done | bytes 1048608 | tf_op jit(solution)/shard_map/ppermute | solution.py:638
  521.7 18.5 %shard_map.231 = (bf16[1024,512]{1,0:T(8,128)(2,1)}, bf16[512,512]{1,0:T(8,128)(2,1)}, bf16[512,512]{1,0:T(8,128)(2,1)}) custom-call(s32[1]{0:T(128)} %slice.225.meta_ref, bf16[1024,512]{1,0:T(8,128)(2,1)} %multiply_convert_fusion.4.q_ref, bf16[512,1024]{1,0:T(8,128)(2,1)} %add_convert_fusion.8.k_ref.v_ref, bf16[512,1024]{1,0:T(8,128)(2,1)} %add_convert_fusion.8.k_ref.v_ref, ...), custom_call_target="tpu_custom_call" | custom-call | flops 21474836480 | bytes 10485760 | tf_op jit(solution)/shard_map/pallas_call | solution.py:202
  542.9 7.2 fusion.181
  564.5 16.3 %collective-permute-done.36 = bf16[512,1024]{1,0:T(8,128)(2,1)} collective-permute-done((bf16[512,1024]{1,0:T(8,128)(2,1)S(1)}, bf16[512,1024]{1,0:T(8,128)(2,1)}, u32[]{:S(2)}, u32[]{:S(2)}) %collective-permute-start.36) | collective-permute-done | bytes 1048608 | tf_op jit(solution)/shard_map/ppermute | solution.py:638
  591.4 37.7 %shard_map.232 = (bf16[2048,256]{1,0:T(8,128)(2,1)}, bf16[2048,256]{1,0:T(8,128)(2,1)}, bf16[2048,256]{1,0:T(8,128)(2,1)}) custom-call(s32[13]{0:T(128)} %concatenate.121.meta_ref, bf16[2048,768]{1,0:T(8,128)(2,1)} %pad_maximum_fusion.1.q_ref.k_ref.v_ref, bf16[2048,768]{1,0:T(8,128)(2,1)} %pad_maximum_fusion.1.q_ref.k_ref.v_ref, ...), custom_call_target="tpu_custom_call" | custom-call | flops 48318382080 | bytes 10485760 | tf_op jit(solution)/shard_map/pallas_call | solution.py:202
  656.0 15.5 %collective-permute-done.40 = bf16[512,1024]{1,0:T(8,128)(2,1)} collective-permute-done((bf16[512,1024]{1,0:T(8,128)(2,1)}, bf16[512,1024]{1,0:T(8,128)(2,1)}, u32[]{:S(2)}, u32[]{:S(2)}) %collective-permute-start.40) | collective-permute-done | bytes 1048608 | tf_op jit(solution)/shard_map/ppermute | solution.py:638
  693.5 9.6 collective-permute-start.25
  708.1 17.0 %collective-permute-done.43 = bf16[128,1024]{1,0:T(8,128)(2,1)} collective-permute-done((bf16[128,1024]{1,0:T(8,128)(2,1)S(1)}, bf16[128,1024]{1,0:T(8,128)(2,1)}, u32[]{:S(2)}, u32[]{:S(2)}) %collective-permute-start.43) | collective-permute-done | bytes 262176 | tf_op jit(solution)/shard_map/ppermute | solution.py:638
  735.5 32.3 %collective-permute-done.50 = bf16[256,1024]{1,0:T(8,128)(2,1)} collective-permute-done((bf16[256,1024]{1,0:T(8,128)(2,1)}, bf16[256,1024]{1,0:T(8,128)(2,1)}, u32[]{:S(2)}, u32[]{:S(2)}) %collective-permute-start.50) | collective-permute-done | bytes 524320 | tf_op jit(solution)/shard_map/ppermute | solution.py:638
  770.9 8.2 collective-permute-done.52
  782.7 9.6 collective-permute-start.41
  792.3 42.0 %all-reduce.4.cloned.1.call-done = f32[32,1536]{1,0:T(8,128)} async-done(((f32[32,1536]{1,0:T(8,128)}), f32[32,1536]{1,0:T(8,128)}) %all-reduce.4.cloned.1.call-update) | async-done | bytes 196624
  840.8 33.2 %reduce-scatter.5.cloned.1.call-done = bf16[256,1024]{0,1:T(8,128)(2,1)} async-done(((bf16[1024,1024]{0,1:T(8,128)(2,1)}), bf16[256,1024]{0,1:T(8,128)(2,1)}) %reduce-scatter.5.cloned.1.call-update) | async-done | bytes 524304 | tf_op jit(solution)/shard_map/reduce_scatter | solution.py:665
  877.5 52.4 %reduce-scatter.7.cloned.1.call-done = bf16[256,2048]{0,1:T(8,128)(2,1)} async-done(((bf16[1024,2048]{0,1:T(8,128)(2,1)}), bf16[256,2048]{0,1:T(8,128)(2,1)}) %reduce-scatter.7.cloned.1.call-update) | async-done | bytes 1048592 | tf_op jit(solution)/shard_map/reduce_scatter | solution.py:665
  935.8 21.2 %collective-permute-done.47 = bf16[256,4,1,256]{0,3,1,2:T(8,128)(2,1)S(1)} collective-permute-done((bf16[256,4,1,256]{0,3,1,2:T(8,128)(2,1)S(1)}, bf16[256,4,1,256]{0,3,1,2:T(8,128)(2,1)S(1)}, u32[]{:S(2)}, u32[]{:S(2)}) %collective-permute-start.47) | collective-permute-done | bytes 524320 | tf_op jit(solution)/shard_map/ppermute | solution.py:638
  (503 shorter events, 269.3 us)
Async XLA Ops:
  7.2 201.6 %all-gather.9.cloned.1.call-start = ((), (), s32[]{:S(2)}) async-start(), calls=%async_computation.4 | async-start | bytes 2621440 | tf_op jit(solution)/shard_map/all_gather | solution.py:661
  29.5 256.9 %all-gather.11.cloned.1.call-start = ((), (), s32[]{:S(2)}) async-start(), calls=%async_computation.5 | async-start | bytes 5242880 | tf_op jit(solution)/shard_map/all_gather | solution.py:661
  64.5 307.4 %all-gather.13.cloned.1.call-start = ((), (), s32[]{:S(2)}) async-start(), calls=%async_computation.10 | async-start | bytes 5242880 | tf_op jit(solution)/shard_map/all_gather | solution.py:661
  64.5 88.5 %collective-permute-start = (bf16[512,1024]{1,0:T(8,128)(2,1)}, bf16[512,1024]{1,0:T(8,128)(2,1)S(1)}, u32[]{:S(2)}, u32[]{:S(2)}) collective-permute-start(bf16[512,1024]{1,0:T(8,128)(2,1)} %param.14), channel_id=1, source_target_pairs={{0,0},{2,4},{4,2},{6,6},{1,1},{3,5},{5,3},{7,7},{8,8},{10,12},{12,... | collective-permute-start | bytes 3145736 | tf_op jit(solution)/shard_map/ppermute | solution.py:642
  66.7 88.4 %collective-permute-start.18 = (bf16[2,128,1024]{1,2,0:T(8,128)(2,1)S(1)}, bf16[2,128,1024]{1,2,0:T(8,128)(2,1)}, u32[]{:S(2)}, u32[]{:S(2)}) collective-permute-start(bf16[2,128,1024]{1,2,0:T(8,128)(2,1)S(1)} %fusion.124), channel_id=1, source_target_pairs={{0,4},{4,0},{1,5},{5,1},{2,6},{6,2},{3,7},{7,3},{8,12},{12,8},{9,1... | collective-permute-start | bytes 1572872 | tf_op jit(solution)/shard_map/ppermute | solution.py:638
  155.1 36.6 %collective-permute-start.5 = (bf16[512,1024]{1,0:T(8,128)(2,1)}, bf16[512,1024]{1,0:T(8,128)(2,1)}, u32[]{:S(2)}, u32[]{:S(2)}) collective-permute-start(bf16[512,1024]{1,0:T(8,128)(2,1)} %fusion.43), channel_id=1, source_target_pairs={{0,1},{1,0},{2,3},{3,2},{4,5},{5,4},{6,7},{7,6},{8,9},{9,8},{10,11... | collective-permute-start | bytes 3145736 | tf_op jit(solution)/shard_map/ppermute | solution.py:638
  157.5 44.7 %collective-permute-start.19 = (bf16[2,256,1024]{1,2,0:T(8,128)(2,1)}, bf16[2,256,1024]{1,2,0:T(8,128)(2,1)S(1)}, u32[]{:S(2)}, u32[]{:S(2)}) collective-permute-start(bf16[2,256,1024]{1,2,0:T(8,128)(2,1)} %pad_maximum_fusion.23), channel_id=1, source_target_pairs={{0,2},{2,0},{1,3},{3,1},{4,6},{6,4},{5,7},{7,5},{8,10},{10,8},{9,1... | collective-permute-start | bytes 3145736 | tf_op jit(solution)/shard_map/ppermute | solution.py:638
  158.2 33.5 %collective-permute-start.1 = (s32[9]{0:T(128)S(1)}, s32[9]{0:T(128)S(1)}, u32[]{:S(2)}, u32[]{:S(2)}) collective-permute-start(s32[9]{0:T(128)S(1)} %pad_add_fusion), channel_id=1, source_target_pairs={{0,0},{2,4},{4,2},{6,6},{1,1},{3,5},{5,3},{7,7},{8,8},{10,12},{12,... | collective-permute-start | bytes 116 | tf_op jit(solution)/shard_map/ppermute | solution.py:642
  204.0 178.5 %all-gather.15.cloned.1.call-start = ((), (), s32[]{:S(2)}) async-start(), calls=%async_computation.11 | async-start | bytes 5242880 | tf_op jit(solution)/shard_map/all_gather | solution.py:661
  246.5 28.1 %collective-permute-start.9 = (bf16[512,1024]{1,0:T(8,128)(2,1)S(1)}, bf16[512,1024]{1,0:T(8,128)(2,1)S(1)}, u32[]{:S(2)}, u32[]{:S(2)}) collective-permute-start(bf16[512,1024]{1,0:T(8,128)(2,1)S(1)} %add_convert_fusion.10), channel_id=1, source_target_pairs={{0,1},{1,0},{2,3},{3,2},{4,5},{5,4},{6,7},{7,6},{8,9},{9,8},{10,11... | collective-permute-start | bytes 3145736 | tf_op jit(solution)/shard_map/ppermute | solution.py:638
  247.3 32.3 %collective-permute-start.14 = (bf16[128,1024]{1,0:T(8,128)(2,1)S(1)}, bf16[128,1024]{1,0:T(8,128)(2,1)S(1)}, u32[]{:S(2)}, u32[]{:S(2)}) collective-permute-start(bf16[128,1024]{1,0:T(8,128)(2,1)S(1)} %collective-permute-done.13), channel_id=1, source_target_pairs={{0,1},{1,0},{2,3},{3,2},{4,5},{5,4},{6,7},{7,6},{8,9},{9,8},{10,11... | collective-permute-start | bytes 786440 | tf_op jit(solution)/shard_map/ppermute | solution.py:638
  281.3 33.4 %collective-permute-start.26 = (bf16[512,1024]{1,0:T(8,128)(2,1)}, bf16[512,1024]{1,0:T(8,128)(2,1)S(1)}, u32[]{:S(2)}, u32[]{:S(2)}) collective-permute-start(bf16[512,1024]{1,0:T(8,128)(2,1)} %param.18), channel_id=1, source_target_pairs={{0,0},{2,4},{4,2},{6,6},{1,1},{3,5},{5,3},{7,7},{8,8},{10,12},{12,... | collective-permute-start | bytes 3145736 | tf_op jit(solution)/shard_map/ppermute | solution.py:642
  286.3 443.2 %reduce-scatter.9.cloned.1.call-start = ((), (), s32[]{:S(2)}) async-start(), calls=%async_computation.8 | async-start | bytes 5242880 | tf_op jit(solution)/shard_map/reduce_scatter | solution.py:665
  320.5 41.8 %collective-permute-start.21 = (bf16[512,1024]{1,0:T(8,128)(2,1)S(1)}, bf16[512,1024]{1,0:T(8,128)(2,1)S(1)}, u32[]{:S(2)}, u32[]{:S(2)}) collective-permute-start(bf16[512,1024]{1,0:T(8,128)(2,1)S(1)} %add_convert_fusion.7), channel_id=1, source_target_pairs={{0,1},{1,0},{2,3},{3,2},{4,5},{5,4},{6,7},{7,6},{8,9},{9,8},{10,11... | collective-permute-start | bytes 3145736 | tf_op jit(solution)/shard_map/ppermute | solution.py:638
  320.5 44.0 %collective-permute-start.27 = (bf16[512,1024]{1,0:T(8,128)(2,1)S(1)}, bf16[512,1024]{1,0:T(8,128)(2,1)}, u32[]{:S(2)}, u32[]{:S(2)}) collective-permute-start(bf16[512,1024]{1,0:T(8,128)(2,1)S(1)} %collective-permute-done.26), channel_id=1, source_target_pairs={{0,4},{4,0},{1,5},{5,1},{2,6},{6,2},{3,7},{7,3},{8,12},{12,8},{9,1... | collective-permute-start | bytes 3145736 | tf_op jit(solution)/shard_map/ppermute | solution.py:638
  367.9 33.6 %collective-permute-start.17 = (bf16[512,1024]{1,0:T(8,128)(2,1)S(1)}, bf16[512,1024]{1,0:T(8,128)(2,1)S(1)}, u32[]{:S(2)}, u32[]{:S(2)}) collective-permute-start(bf16[512,1024]{1,0:T(8,128)(2,1)S(1)} %add_convert_fusion.7), channel_id=1, source_target_pairs={{0,4},{4,0},{1,5},{5,1},{2,6},{6,2},{3,7},{7,3},{8,12},{12,8},{9,1... | collective-permute-start | bytes 3145736 | tf_op jit(solution)/shard_map/ppermute | solution.py:638
  401.0 58.6 %collective-permute-start.31 = (bf16[512,1024]{1,0:T(8,128)(2,1)}, bf16[512,1024]{1,0:T(8,128)(2,1)}, u32[]{:S(2)}, u32[]{:S(2)}) collective-permute-start(bf16[512,1024]{1,0:T(8,128)(2,1)} %fusion.75), channel_id=1, source_target_pairs={{0,4},{4,0},{1,5},{5,1},{2,6},{6,2},{3,7},{7,3},{8,12},{12,8},{9,1... | collective-permute-start | bytes 3145736 | tf_op jit(solution)/shard_map/ppermute | solution.py:638
  434.2 38.2 %collective-permute-start.28 = (bf16[512,1024]{1,0:T(8,128)(2,1)}, bf16[512,1024]{1,0:T(8,128)(2,1)S(1)}, u32[]{:S(2)}, u32[]{:S(2)}) collective-permute-start(bf16[512,1024]{1,0:T(8,128)(2,1)} %fusion.70), channel_id=1, source_target_pairs={{0,4},{4,0},{1,5},{5,1},{2,6},{6,2},{3,7},{7,3},{8,12},{12,8},{9,1... | collective-permute-start | bytes 3145736 | tf_op jit(solution)/shard_map/ppermute | solution.py:638
  441.5 49.9 %collective-permute-start.20 = (bf16[512,1024]{1,0:T(8,128)(2,1)}, bf16[512,1024]{1,0:T(8,128)(2,1)S(1)}, u32[]{:S(2)}, u32[]{:S(2)}) collective-permute-start(bf16[512,1024]{1,0:T(8,128)(2,1)} %fusion.80), channel_id=1, source_target_pairs={{0,4},{4,0},{1,5},{5,1},{2,6},{6,2},{3,7},{7,3},{8,12},{12,8},{9,1... | collective-permute-start | bytes 3145736 | tf_op jit(solution)/shard_map/ppermute | solution.py:638
  454.0 277.4 %reduce-scatter.11.cloned.1.call-start = ((), (), s32[]{:S(2)}) async-start(), calls=%async_computation.9 | async-start | bytes 5242880 | tf_op jit(solution)/shard_map/reduce_scatter | solution.py:665
  468.1 44.1 %collective-permute-start.24 = (bf16[512,1024]{1,0:T(8,128)(2,1)S(1)}, bf16[512,1024]{1,0:T(8,128)(2,1)S(1)}, u32[]{:S(2)}, u32[]{:S(2)}) collective-permute-start(bf16[512,1024]{1,0:T(8,128)(2,1)S(1)} %add_convert_fusion.6), channel_id=1, source_target_pairs={{0,1},{1,0},{2,3},{3,2},{4,5},{5,4},{6,7},{7,6},{8,9},{9,8},{10,11... | collective-permute-start | bytes 3145736 | tf_op jit(solution)/shard_map/ppermute | solution.py:638
  555.6 27.0 %collective-permute-start.35 = (bf16[512,1024]{1,0:T(8,128)(2,1)S(1)}, bf16[512,1024]{1,0:T(8,128)(2,1)}, u32[]{:S(2)}, u32[]{:S(2)}) collective-permute-start(bf16[512,1024]{1,0:T(8,128)(2,1)S(1)} %get-tuple-element.96), channel_id=1, source_target_pairs={{0,4},{4,0},{1,5},{5,1},{2,6},{6,2},{3,7},{7,3},{8,12},{12,8},{9,1... | collective-permute-start | bytes 3145736 | tf_op jit(solution)/shard_map/ppermute | solution.py:638
  563.1 271.3 %all-reduce.4.cloned.1.call-start = ((), (), s32[]{:S(2)}) async-start(), calls=%async_computation.12 | async-start | bytes 393216
  675.2 198.9 %reduce-scatter.5.cloned.1.call-start = ((), (), s32[]{:S(2)}) async-start(), calls=%async_computation.6 | async-start | bytes 2621440 | tf_op jit(solution)/shard_map/reduce_scatter | solution.py:665
  678.3 251.7 %reduce-scatter.7.cloned.1.call-start = ((), (), s32[]{:S(2)}) async-start(), calls=%async_computation.7 | async-start | bytes 5242880 | tf_op jit(solution)/shard_map/reduce_scatter | solution.py:665
  693.5 35.1 %collective-permute-start.25 = (bf16[512,1024]{1,0:T(8,128)(2,1)}, bf16[512,1024]{1,0:T(8,128)(2,1)}, u32[]{:S(2)}, u32[]{:S(2)}) collective-permute-start(bf16[512,1024]{1,0:T(8,128)(2,1)} %get-tuple-element.102), channel_id=1, source_target_pairs={{0,0},{2,4},{4,2},{6,6},{1,1},{3,5},{5,3},{7,7},{8,8},{10,12},{12,... | collective-permute-start | bytes 3145736 | tf_op jit(solution)/shard_map/ppermute | solution.py:642
  731.3 36.5 %collective-permute-start.50 = (bf16[256,1024]{1,0:T(8,128)(2,1)}, bf16[256,1024]{1,0:T(8,128)(2,1)}, u32[]{:S(2)}, u32[]{:S(2)}) collective-permute-start(bf16[256,1024]{1,0:T(8,128)(2,1)} %constant_dynamic-slice_fusion.3), channel_id=1, source_target_pairs={{0,2},{2,0},{1,3},{3,1},{4,6},{6,4},{5,7},{7,5},{8,10},{10,8},{9,1... | collective-permute-start | bytes 1572872 | tf_op jit(solution)/shard_map/ppermute | solution.py:638
  732.5 46.6 %collective-permute-start.52 = (bf16[256,1024]{1,0:T(8,128)(2,1)S(1)}, bf16[256,1024]{1,0:T(8,128)(2,1)S(1)}, u32[]{:S(2)}, u32[]{:S(2)}) collective-permute-start(bf16[256,1024]{1,0:T(8,128)(2,1)S(1)} %constant_dynamic-slice_fusion.2), channel_id=1, source_target_pairs={{0,2},{2,0},{1,3},{3,1},{4,6},{6,4},{5,7},{7,5},{8,10},{10,8},{9,1... | collective-permute-start | bytes 1572872 | tf_op jit(solution)/shard_map/ppermute | solution.py:638
  770.9 67.6 %collective-permute-start.51 = (bf16[128,1024]{1,0:T(8,128)(2,1)}, bf16[128,1024]{1,0:T(8,128)(2,1)S(1)}, u32[]{:S(2)}, u32[]{:S(2)}) collective-permute-start(bf16[128,1024]{1,0:T(8,128)(2,1)} %dynamic-slice_convert_fusion.1), channel_id=1, source_target_pairs={{0,4},{4,0},{1,5},{5,1},{2,6},{6,2},{3,7},{7,3},{8,12},{12,8},{9,1... | collective-permute-start | bytes 786440 | tf_op jit(solution)/shard_map/ppermute | solution.py:638
  781.0 58.7 %collective-permute-start.53 = (bf16[128,1024]{1,0:T(8,128)(2,1)}, bf16[128,1024]{1,0:T(8,128)(2,1)}, u32[]{:S(2)}, u32[]{:S(2)}) collective-permute-start(bf16[128,1024]{1,0:T(8,128)(2,1)} %dynamic-slice_convert_fusion), channel_id=1, source_target_pairs={{0,4},{4,0},{1,5},{5,1},{2,6},{6,2},{3,7},{7,3},{8,12},{12,8},{9,1... | collective-permute-start | bytes 786440 | tf_op jit(solution)/shard_map/ppermute | solution.py:638
  782.7 176.4 %collective-permute-start.41 = (bf16[512,1024]{1,0:T(8,128)(2,1)}, bf16[512,1024]{1,0:T(8,128)(2,1)}, u32[]{:S(2)}, u32[]{:S(2)}) collective-permute-start(bf16[512,1024]{1,0:T(8,128)(2,1)} %fusion.48), channel_id=1, source_target_pairs={{0,0},{2,4},{4,2},{6,6},{1,1},{3,5},{5,3},{7,7},{8,8},{10,12},{12,... | collective-permute-start | bytes 3145736 | tf_op jit(solution)/shard_map/ppermute | solution.py:642
  875.1 59.6 %collective-permute-start.45 = (bf16[256,4,1,128]{0,3,1,2:T(8,128)(2,1)S(1)}, bf16[256,4,1,128]{0,3,1,2:T(8,128)(2,1)}, u32[]{:S(2)}, u32[]{:S(2)}) collective-permute-start(bf16[256,4,1,128]{0,3,1,2:T(8,128)(2,1)S(1)} %dynamic-slice_bitcast_fusion.1), channel_id=1, source_target_pairs={{0,2},{2,0},{1,3},{3,1},{4,6},{6,4},{5,7},{7,5},{8,10},{10,8},{9,1... | collective-permute-start | bytes 786440 | tf_op jit(solution)/shard_map/ppermute | solution.py:638
  (121 other events, 1478.7 us)
Sparse Core Ops, SparseCore 0:
  29.6 36.3 all-gather.8
  68.4 52.8 all-gather.10
  204.2 51.3 all-gather.12
  286.4 54.0 all-gather.14
  454.1 50.6 reduce-scatter.8
  563.2 50.2 reduce-scatter.10
  675.3 159.0 all-reduce.3
  837.9 36.0 reduce-scatter.4
  877.3 52.6 reduce-scatter.6

commit v2 on v1

--- a/solution.py
+++ b/solution.py
@@ -634,12 +634,564 @@
     )
 
 
-def trade(rows, axis):
-    return lax.ppermute(rows, axis, [(0, 1), (1, 0)])
-
-
-def regroup(rows):
-    return lax.ppermute(rows, ("core", "zhi"), [(0, 0), (1, 2), (2, 1), (3, 3)])
+MESH = pl.DeviceIdType.MESH
+LINKS = ("core", "x", "y", "zhi", "zlo")
+
+
+def start_kernel(
+    tokens,
+    enc,
+    w_self,
+    w_cross,
+    w_in,
+    w_out,
+    small,
+    token_rows,
+    attn,
+    g_self,
+    g_cross,
+    hidden,
+    enc_full,
+    small_all,
+    held,
+    normed,
+    gathered,
+    send,
+    recv,
+    local,
+):
+    y, x, core, zhi, zlo = (lax.axis_index(axis) for axis in AXES)
+    crossing = core != zhi
+    rows = tokens.shape[0]
+    part = w_self.shape[1]
+    counts = {"sent": 0, "local": 0}
+
+    def push(source, target, axis):
+        index = counts["sent"]
+        counts["sent"] += 1
+        copy = pltpu.make_async_remote_copy(
+            src_ref=source,
+            dst_ref=target,
+            send_sem=send.at[index],
+            recv_sem=recv.at[index],
+            device_id={axis: 1 - lax.axis_index(axis)},
+            device_id_type=MESH,
+        )
+        copy.start()
+        return copy
+
+    def keep(source, target):
+        index = counts["local"]
+        counts["local"] += 1
+        copy = pltpu.make_async_copy(source, target, local.at[index])
+        copy.start()
+        return copy
+
+    def moving(source, target, source_here, target_here):
+        index, index_here = counts["sent"], counts["local"]
+        counts["sent"] += 1
+        counts["local"] += 1
+
+        def remote():
+            return pltpu.make_async_remote_copy(
+                src_ref=source,
+                dst_ref=target,
+                send_sem=send.at[index],
+                recv_sem=recv.at[index],
+                device_id={"core": zhi, "zhi": core},
+                device_id_type=MESH,
+            )
+
+        def here():
+            return pltpu.make_async_copy(source_here, target_here, local.at[index_here])
+
+        @pl.when(crossing)
+        def _():
+            remote().start()
+
+        @pl.when(jnp.logical_not(crossing))
+        def _():
+            here().start()
+
+        def wait():
+            @pl.when(crossing)
+            def _():
+                remote().wait()
+
+            @pl.when(jnp.logical_not(crossing))
+            def _():
+                here().wait()
+
+        return wait
+
+    def lanes(block, size):
+        return pl.ds(pl.multiple_of(block * size, size), size)
+
+    barrier = pltpu.get_barrier_semaphore()
+    for axis in LINKS:
+        pl.semaphore_signal(barrier, inc=1, device_id={axis: 1 - lax.axis_index(axis)}, device_id_type=MESH)
+
+    @pl.when(crossing)
+    def _():
+        pl.semaphore_signal(barrier, inc=1, device_id={"core": zhi, "zhi": core}, device_id_type=MESH)
+
+    pl.semaphore_wait(barrier, len(LINKS) + crossing.astype(jnp.int32))
+
+    wait_tokens = moving(tokens, held, tokens, held)
+    own_small = keep(small, gathered.at[y, x, core, zhi, zlo])
+    own_rows = pl.ds(pl.multiple_of(core * part, part), part)
+    quarter = 2 * zhi + zlo
+
+    def from_shard(shard, target, block, size):
+        own = keep(shard.at[:, :, lanes(core, size)], target.at[:, y, x, own_rows, lanes(block, size)])
+        other = push(
+            shard.at[:, :, lanes(1 - core, size)], target.at[:, y, x, own_rows, lanes(block, size)], "core"
+        )
+        return own, other
+
+    self_width = w_self.shape[2] // 2
+    hidden_width = w_in.shape[1] // 2
+    cross_core = from_shard(w_cross, g_cross, quarter, self_width)
+    own_small.wait()
+    small_core = push(gathered.at[y, x, core, zhi, zlo], gathered.at[y, x, core, zhi, zlo], "core")
+    self_core = from_shard(w_self, g_self, zhi, self_width)
+    hidden_core = []
+    for plane, shard in enumerate((w_in, w_out)):
+        target = hidden.at[plane, own_rows, lanes(zhi, hidden_width)]
+        hidden_core.append(keep(shard.at[:, lanes(core, hidden_width)], target))
+        hidden_core.append(push(shard.at[:, lanes(1 - core, hidden_width)], target, "core"))
+    for copy in cross_core:
+        copy.wait()
+    region = g_cross.at[:, y, x, :, lanes(quarter, self_width)]
+    cross_zlo = push(region, region, "zlo")
+    small_core.wait()
+    region = gathered.at[y, x, :, zhi, zlo]
+    small_x = push(region, region, "x")
+    for copy in self_core:
+        copy.wait()
+    small_x.wait()
+    region = gathered.at[y, :, :, zhi, zlo]
+    small_y = push(region, region, "y")
+    cross_zlo.wait()
+    small_y.wait()
+
+    def over_plane(target, width):
+        first, second = pl.ds(0, width), pl.ds(width, width)
+        region_a, region_b = target.at[:, y, x, :, first], target.at[:, y, x, :, second]
+        steps = (push(region_a, region_a, "x"), push(region_b, region_b, "y"))
+
+        def second_steps():
+            steps[0].wait()
+            region_a = target.at[:, y, :, :, first]
+            step_a = push(region_a, region_a, "y")
+            steps[1].wait()
+            region_b = target.at[:, :, x, :, second]
+            return step_a, push(region_b, region_b, "x")
+
+        return second_steps
+
+    wait_tokens()
+    keep_tokens = keep(held, token_rows)
+    region = gathered.at[:, :, :, zhi, zlo]
+    small_zhi = push(region, region, "zhi")
+    region = g_self.at[:, y, x, :, lanes(zhi, self_width)]
+    self_zhi = push(region, region, "zhi")
+    gain = jnp.concatenate([gathered[d // 4, d // 2 % 2, d % 2, zhi, zlo, 0:1, :] for d in range(8)], axis=1)
+    shift = jnp.concatenate([gathered[d // 4, d // 2 % 2, d % 2, zhi, zlo, 3:4, :] for d in range(8)], axis=1)
+
+    def norm_step(step, carry):
+        block = pl.ds(pl.multiple_of(step * 64, 64), 64)
+        values = held[block, :].astype(jnp.float32)
+        centred = values - jnp.mean(values, axis=1, keepdims=True)
+        inverse = lax.rsqrt(jnp.mean(centred * centred, axis=1, keepdims=True) + EPSILON)
+        normed[block, :] = (centred * inverse * gain + shift).astype(normed.dtype)
+        return carry
+
+    lax.fori_loop(0, rows // 64, norm_step, 0)
+    attn_zlo = push(normed, attn.at[pl.ds(2 * rows, rows)], "zlo")
+    attn_core = push(normed, attn.at[pl.ds(rows, rows)], "core")
+    attn_own = keep(normed, attn.at[pl.ds(0, rows)])
+
+    self_zhi.wait()
+    region = g_cross.at[:, y, x, :, lanes(zhi, 2 * self_width)]
+    cross_zhi = push(region, region, "zhi")
+    self_second = over_plane(g_self, self_width)
+    self_last = self_second()
+    small_zhi.wait()
+    region = gathered.at[:, :, :, :, zlo]
+    small_zlo = push(region, region, "zlo")
+    for copy in hidden_core:
+        copy.wait()
+    cross_zhi.wait()
+    region = hidden.at[0, :, lanes(zhi, hidden_width)]
+    hidden_zhi = push(region, region, "zhi")
+    wait_enc = moving(enc, enc_full.at[2 * zhi + zlo], enc, enc_full.at[2 * core + zlo])
+    cross_second = over_plane(g_cross, 2 * self_width)
+    attn_zlo.wait()
+    attn_diagonal = push(attn.at[pl.ds(2 * rows, rows)], attn.at[pl.ds(3 * rows, rows)], "core")
+    cross_last = cross_second()
+    wait_enc()
+    region = enc_full.at[2 * core + zlo]
+    enc_zlo = push(region, region, "zlo")
+    enc_core = push(region, region, "core")
+    enc_zlo.wait()
+    region = enc_full.at[2 * core + 1 - zlo]
+    enc_diagonal = push(region, region, "core")
+    small_zlo.wait()
+    keep_small = keep(gathered, small_all)
+    for copy in (
+        *self_last,
+        *cross_last,
+        hidden_zhi,
+        attn_core,
+        attn_diagonal,
+        enc_core,
+        enc_diagonal,
+        attn_own,
+        keep_tokens,
+        keep_small,
+    ):
+        copy.wait()
+
+
+def start_exchange(tokens, enc, w_self, w_cross, w_in, w_out, small):
+    rows, model = tokens.shape
+    part = w_self.shape[1]
+    low_type = tokens.dtype
+    shapes = [
+        jax.ShapeDtypeStruct((rows, model), low_type),
+        jax.ShapeDtypeStruct((4 * rows, model), low_type),
+        jax.ShapeDtypeStruct((4, 2, 2, 2 * part, w_self.shape[2]), low_type),
+        jax.ShapeDtypeStruct((4, 2, 2, 2 * part, 2 * w_cross.shape[2]), low_type),
+        jax.ShapeDtypeStruct((2, 2 * part, w_in.shape[1]), low_type),
+        jax.ShapeDtypeStruct((4, enc.shape[0], model), low_type),
+        jax.ShapeDtypeStruct((2,) * 5 + small.shape, small.dtype),
+    ]
+    anywhere = pl.BlockSpec(memory_space=pl.ANY)
+    return pl.pallas_call(
+        start_kernel,
+        out_shape=shapes,
+        in_specs=[anywhere] * 7,
+        out_specs=[anywhere] * len(shapes),
+        scratch_shapes=[
+            pltpu.VMEM((rows, model), low_type),
+            pltpu.VMEM((rows, model), low_type),
+            pltpu.VMEM((2,) * 5 + small.shape, small.dtype),
+            pltpu.SemaphoreType.DMA((30,)),
+            pltpu.SemaphoreType.DMA((30,)),
+            pltpu.SemaphoreType.DMA((12,)),
+        ],
+        compiler_params=pltpu.CompilerParams(collective_id=0, has_side_effects=True),
+    )(tokens, enc, w_self, w_cross, w_in, w_out, small)
+
+
+def finish_kernel(spread, hidden, attention, small, *refs):
+    y, x, core, zhi, zlo = (lax.axis_index(axis) for axis in AXES)
+    crossing = core != zhi
+    refs = list(refs)
+
+    def take(number):
+        taken, refs[:number] = refs[:number], []
+        return taken
+
+    links = ("core", "zhi")
+    if spread or attention or small:
+        links += ("zlo",)
+    if attention or small:
+        links += ("x", "y")
+    rows_in = take(1) if spread else []
+    hidden_in = take(hidden)
+    attention_in = take(3) if attention else []
+    small_in = take(small)
+    rows_out = take(1) if spread else []
+    hidden_out = take(hidden)
+    attention_out = take(3) if attention else []
+    small_out = take(small)
+    hidden_kept = [take(3) for _ in range(hidden)]
+    if attention:
+        enc_own, enc_got, enc_sum, enc_far, enc_low = take(5)
+        kept, got, total, low_part, got_low, total_low = take(6)
+        self_own, self_got, self_low, self_got_low, self_total, self_send, self_last = take(7)
+    if small:
+        small_sum, *small_got = take(1 + len(AXES))
+    send, recv, local = take(3)
+    counts = {"sent": 0, "local": 0}
+
+    def push(source, target, axis):
+        index = counts["sent"]
+        counts["sent"] += 1
+        copy = pltpu.make_async_remote_copy(
+            src_ref=source,
+            dst_ref=target,
+            send_sem=send.at[index],
+            recv_sem=recv.at[index],
+            device_id={axis: 1 - lax.axis_index(axis)},
+            device_id_type=MESH,
+        )
+        copy.start()
+        return copy
+
+    def keep(source, target):
+        index = counts["local"]
+        counts["local"] += 1
+        copy = pltpu.make_async_copy(source, target, local.at[index])
+        copy.start()
+        return copy
+
+    def lanes(block, size):
+        return pl.ds(pl.multiple_of(block * size, size), size)
+
+    def moving(source, target, source_here, target_here):
+        index, index_here = counts["sent"], counts["local"]
+        counts["sent"] += 1
+        counts["local"] += 1
+
+        def remote():
+            return pltpu.make_async_remote_copy(
+                src_ref=source,
+                dst_ref=target,
+                send_sem=send.at[index],
+                recv_sem=recv.at[index],
+                device_id={"core": zhi, "zhi": core},
+                device_id_type=MESH,
+            )
+
+        def here():
+            return pltpu.make_async_copy(source_here, target_here, local.at[index_here])
+
+        @pl.when(crossing)
+        def _():
+            remote().start()
+
+        @pl.when(jnp.logical_not(crossing))
+        def _():
+            here().start()
+
+        def wait():
+            @pl.when(crossing)
+            def _():
+                remote().wait()
+
+            @pl.when(jnp.logical_not(crossing))
+            def _():
+                here().wait()
+
+        return wait
+
+    def add(target, left, right, columns_of=slice(None)):
+        def step(index, carry):
+            rows = pl.ds(pl.multiple_of(index * 64, 64), 64)
+            value = left[rows, columns_of].astype(jnp.float32) + right[rows, :].astype(jnp.float32)
+            target[rows, :] = value.astype(target.dtype)
+            return carry
+
+        lax.fori_loop(0, target.shape[0] // 64, step, 0)
+
+    def narrow(target, source, columns_of=slice(None)):
+        def step(index, carry):
+            rows = pl.ds(pl.multiple_of(index * 64, 64), 64)
+            target[rows, :] = source[rows, columns_of].astype(target.dtype)
+            return carry
+
+        lax.fori_loop(0, target.shape[0] // 64, step, 0)
+
+    barrier = pltpu.get_barrier_semaphore()
+    for axis in links:
+        pl.semaphore_signal(barrier, inc=1, device_id={axis: 1 - lax.axis_index(axis)}, device_id_type=MESH)
+    if attention:
+
+        @pl.when(crossing)
+        def _():
+            pl.semaphore_signal(barrier, inc=1, device_id={"core": zhi, "zhi": core}, device_id_type=MESH)
+
+        pl.semaphore_wait(barrier, len(links) + crossing.astype(jnp.int32))
+    else:
+        pl.semaphore_wait(barrier, len(links))
+
+    small_first, small_size = 0, 32
+
+    def small_send(stage):
+        half, got = small_size // 2, small_got[stage]
+        away = small_first + (1 - lax.axis_index(AXES[stage])) * half
+        return push(small_sum.at[pl.ds(away, half)], got, AXES[stage])
+
+    def small_add(stage, copy):
+        copy.wait()
+        half, got = small_size // 2, small_got[stage]
+        mine = small_first + lax.axis_index(AXES[stage]) * half
+
+        def step(index, carry):
+            small_sum[mine + index] += got[index]
+            return carry
+
+        lax.fori_loop(0, half, step, 0)
+        return mine, half
+
+    last = []
+
+    def to_cores(values, out):
+        part, width = values.shape[0] // 2, values.shape[1]
+        there = pl.ds(pl.multiple_of((1 - core) * part, part), part)
+        here = pl.ds(pl.multiple_of(core * part, part), part)
+        last.append(push(values.at[there], out.at[:, lanes(core, width)], "core"))
+        last.append(keep(values.at[here], out.at[:, lanes(core, width)]))
+
+    if spread:
+        rows = rows_in[0].shape[0]
+        out = rows_out[0]
+        spread_zlo = push(rows_in[0], out.at[pl.ds(2 * rows, rows)], "zlo")
+        last.append(push(rows_in[0], out.at[pl.ds(rows, rows)], "core"))
+        last.append(keep(rows_in[0], out.at[pl.ds(0, rows)]))
+    steps = []
+    for partial, (mine, theirs, _) in zip(hidden_in, hidden_kept):
+        width = mine.shape[1]
+        steps.append(
+            (push(partial.at[:, lanes(1 - zhi, width)], theirs, "zhi"), keep(partial.at[:, lanes(zhi, width)], mine))
+        )
+    if small:
+        keep(small_in[0], small_sum).wait()
+        for stage in range(len(AXES)):
+            small_first, small_size = small_add(stage, small_send(stage))
+        keep(small_sum.at[small_first], small_out[0]).wait()
+    if attention:
+        cross_part, self_part, enc_part = attention_in
+        width = kept.shape[1]
+        cross_zhi = push(cross_part.at[:, lanes(1 - zhi, width)], got, "zhi")
+        cross_own = keep(cross_part.at[:, lanes(zhi, width)], kept)
+        half = self_got.shape[3]
+        first, second = pl.ds(0, half), pl.ds(half, half)
+        enc_core = push(enc_part.at[1 - core], enc_got, "core")
+        enc_keep = keep(enc_part.at[core], enc_own)
+        self_x = push(self_part.at[:, 1 - x, :, first], self_got.at[0], "x")
+        self_y = push(self_part.at[1 - y, :, :, second], self_got.at[1], "y")
+        own_a = keep(self_part.at[:, x, :, first], self_own.at[0])
+        own_b = keep(self_part.at[y, :, :, second], self_own.at[1])
+        enc_core.wait()
+        enc_keep.wait()
+        add(enc_sum, enc_own.at[1 - zlo], enc_got.at[1 - zlo])
+        enc_zlo = push(enc_sum, enc_far, "zlo")
+        own_a.wait()
+        self_x.wait()
+        add(self_low, self_own.at[0, 1 - y], self_got.at[0, 1 - y])
+        a_second = push(self_low, self_got_low.at[0], "y")
+        own_b.wait()
+        self_y.wait()
+        add(self_send, self_own.at[1, 1 - x], self_got.at[1, 1 - x])
+        b_second = push(self_send, self_got_low.at[1], "x")
+        add(self_total.at[0], self_own.at[0, y], self_got.at[0, y])
+        add(self_total.at[1], self_own.at[1, x], self_got.at[1, x])
+        a_second.wait()
+        add(self_total.at[0], self_total.at[0], self_got_low.at[0])
+        b_second.wait()
+        add(self_total.at[1], self_total.at[1], self_got_low.at[1])
+        enc_zlo.wait()
+
+        def enc_step(index, carry):
+            rows = pl.ds(pl.multiple_of(index * 64, 64), 64)
+            value = enc_own[zlo, rows, :].astype(jnp.float32) + enc_got[zlo, rows, :].astype(jnp.float32)
+            enc_low[rows, :] = (value + enc_far[rows, :].astype(jnp.float32)).astype(enc_low.dtype)
+            return carry
+
+        lax.fori_loop(0, enc_low.shape[0] // 64, enc_step, 0)
+        wait_enc = moving(enc_low, attention_out[2], enc_low, attention_out[2])
+        narrow(self_low, self_total.at[1 - zhi])
+        self_zhi = push(self_low, self_last, "zhi")
+        cross_own.wait()
+        cross_zhi.wait()
+        add(total, kept, got)
+        narrow(low_part, total, lanes(1 - zlo, low_part.shape[1]))
+        cross_zlo = push(low_part, got_low, "zlo")
+        self_zhi.wait()
+        add(self_total.at[zhi], self_total.at[zhi], self_last)
+        to_cores(self_total.at[zhi], attention_out[1])
+        cross_zlo.wait()
+        add(total_low, total, got_low, lanes(zlo, low_part.shape[1]))
+        to_cores(total_low, attention_out[0])
+    if spread:
+        spread_zlo.wait()
+        last.append(push(rows_out[0].at[pl.ds(2 * rows, rows)], rows_out[0].at[pl.ds(3 * rows, rows)], "core"))
+    for copies, (mine, theirs, summed), out in zip(steps, hidden_kept, hidden_out):
+        for copy in copies:
+            copy.wait()
+        add(summed, mine, theirs)
+        to_cores(summed, out)
+    if attention:
+        wait_enc()
+    for copy in last:
+        copy.wait()
+
+
+def finish(rows, hidden, attention, small, collective_id):
+    operands, shapes, scratch = [], [], []
+    if rows is not None:
+        operands.append(rows)
+        shapes.append(jax.ShapeDtypeStruct((4 * rows.shape[0], rows.shape[1]), rows.dtype))
+    for partial in hidden:
+        count, width = partial.shape
+        operands.append(partial)
+        shapes.append(jax.ShapeDtypeStruct((count // 2, width), jnp.float32))
+        scratch += [pltpu.VMEM((count, width // 2), partial.dtype)] * 2
+        scratch.append(pltpu.VMEM((count, width // 2), jnp.float32))
+    if attention is not None:
+        cross, own, enc = attention
+        enc_shape = enc.shape[2:]
+        count, width = cross.shape
+        part, half = own.shape[2], own.shape[3] // 2
+        operands += [cross, own, enc]
+        shapes.append(jax.ShapeDtypeStruct((count // 2, width // 2), jnp.float32))
+        shapes.append(jax.ShapeDtypeStruct((part // 2, 2 * half), jnp.float32))
+        shapes.append(jax.ShapeDtypeStruct(enc_shape, enc.dtype))
+        scratch += [
+            pltpu.VMEM((2, *enc_shape), enc.dtype),
+            pltpu.VMEM((2, *enc_shape), enc.dtype),
+            pltpu.VMEM(enc_shape, enc.dtype),
+            pltpu.VMEM(enc_shape, enc.dtype),
+            pltpu.VMEM(enc_shape, enc.dtype),
+            pltpu.VMEM((count, width // 2), cross.dtype),
+            pltpu.VMEM((count, width // 2), cross.dtype),
+            pltpu.VMEM((count, width // 2), jnp.float32),
+            pltpu.VMEM((count, width // 4), cross.dtype),
+            pltpu.VMEM((count, width // 4), cross.dtype),
+            pltpu.VMEM((count, width // 4), jnp.float32),
+            pltpu.VMEM((2, 2, part, half), own.dtype),
+            pltpu.VMEM((2, 2, part, half), own.dtype),
+            pltpu.VMEM((part, half), own.dtype),
+            pltpu.VMEM((2, part, half), own.dtype),
+            pltpu.VMEM((2, part, half), jnp.float32),
+            pltpu.VMEM((part, half), own.dtype),
+            pltpu.VMEM((part, half), own.dtype),
+        ]
+    if small is not None:
+        operands.append(small)
+        shapes.append(jax.ShapeDtypeStruct(small.shape[1:], small.dtype))
+        scratch.append(pltpu.VMEM(small.shape, small.dtype))
+        scratch += [pltpu.VMEM((32 >> stage, *small.shape[1:]), small.dtype) for stage in range(1, 6)]
+    anywhere = pl.BlockSpec(memory_space=pl.ANY)
+    return pl.pallas_call(
+        functools.partial(
+            finish_kernel, rows is not None, len(hidden), attention is not None, int(small is not None)
+        ),
+        out_shape=shapes,
+        in_specs=[anywhere] * len(operands),
+        out_specs=[anywhere] * len(shapes),
+        scratch_shapes=scratch + [pltpu.SemaphoreType.DMA((16,))] * 3,
+        compiler_params=pltpu.CompilerParams(collective_id=collective_id, has_side_effects=True),
+        cost_estimate=pl.CostEstimate(flops=20_000_000_000, bytes_accessed=0, transcendentals=0),
+    )(*operands)
+
+
+def trade(rows, axis, name="trade"):
+    with jax.named_scope(name):
+        return lax.ppermute(rows, axis, [(0, 1), (1, 0)])
+
+
+def after(value, *others):
+    return lax.optimization_barrier((value, *others))[0]
+
+
+def regroup(rows, name="regroup"):
+    with jax.named_scope("re_" + name):
+        return lax.ppermute(rows, ("core", "zhi"), [(0, 0), (1, 2), (2, 1), (3, 3)])
 
 
 def in_order(index, own, other, axis):
@@ -665,19 +1217,19 @@
     return lax.psum_scatter(partial, ("y", "x"), scatter_dimension=0, tiled=True)
 
 
-def spread_rows(rows):
-    beyond = trade(rows, "zlo")
+def spread_rows(rows, name):
+    beyond = trade(rows, "zlo", name + "_z")
     return (
-        jnp.concatenate([rows, trade(rows, "core")], axis=0),
-        jnp.concatenate([beyond, trade(beyond, "core")], axis=0),
-    )
-
-
-def sum_rows(near, far, term):
+        jnp.concatenate([rows, trade(rows, "core", name + "_c")], axis=0),
+        jnp.concatenate([beyond, trade(beyond, "core", name + "_zc")], axis=0),
+    )
+
+
+def sum_rows(near, far, term, name):
     size = near.shape[0] // 2
-    far_sum = term(far[:size]) + trade(low(term(far[size:])), "core")
-    from_far = trade(low(far_sum), "zlo")
-    near_other = trade(low(term(near[size:])), "core")
+    far_sum = term(far[:size]) + trade(low(term(far[size:])), "core", name + "_zc")
+    from_far = trade(low(far_sum), "zlo", name + "_z")
+    near_other = trade(low(term(near[size:])), "core", name + "_c")
     return term(near[:size]) + near_other + from_far
 
 
@@ -702,10 +1254,33 @@
     model = tokens.shape[1]
     segments = cont_lengths.shape[1]
 
-    flat = jnp.concatenate([vec_params.reshape(-1), head_bias.reshape(-1), ff_bias])
+    flat = jnp.concatenate([vec_params.reshape(-1), head_bias.reshape(-1), ff_bias]).astype(jnp.float32)
     sizes = (vec_params.size, head_bias.size, ff_bias.size)
-    small = lax.all_gather(flat, AXES, axis=0).reshape(8, 4, -1).astype(jnp.float32)
-    vec_part, head_part, ff_part = jnp.split(small, [sizes[0], sizes[0] + sizes[1]], axis=2)
+    flat = jnp.pad(flat.reshape(-1, 128), ((0, 4), (0, 0)))
+    token_rows, attn_rows, w_self, w_cross, w_hidden, enc_full, small = start_exchange(
+        tokens,
+        enc_states,
+        jnp.concatenate([self_qkv, self_out.T[None]], axis=0),
+        jnp.concatenate([cross_qkv, cross_out.T[None]], axis=0),
+        ff_in,
+        ff_out.T,
+        flat,
+    )
+    w_self, w_cross = w_self.reshape(4, model, -1), w_cross.reshape(4, model, -1)
+    w_in = over_chips(w_hidden[0])
+    out_own = half_of(w_hidden[1], zhi, 1)
+    out_beyond = trade(out_own, "zhi", "wo_zhi")
+    w_qkv, w_so = jnp.concatenate([w_self[0], w_self[1], w_self[2]], axis=1), w_self[3]
+    w_cq, w_ckv, w_co = w_cross[0], jnp.concatenate([w_cross[1], w_cross[2]], axis=1), w_cross[3]
+    rows_of = model // 4
+    width, cross_width = w_self.shape[2], w_cross.shape[2]
+    pairs, cross_pairs = width // PAIR, cross_width // PAIR
+    enc_full = enc_full.reshape(-1, model)
+    attn_near, attn_far = attn_rows[: attn_rows.shape[0] // 2], attn_rows[attn_rows.shape[0] // 2 :]
+    small = small.reshape(8, 4, -1)
+    vec_part, head_part, ff_part = jnp.split(
+        small[:, :, : sum(sizes)], [sizes[0], sizes[0] + sizes[1]], axis=2
+    )
     vectors = vec_part[:, 0].reshape(8, 9, -1).transpose(1, 0, 2).reshape(9, model)
     heads = head_part.reshape(8, 4, 4, -1).transpose(2, 1, 0, 3).reshape(4, 2, 2, 2, -1)
     self_bias = lax.dynamic_index_in_dim(
@@ -717,8 +1292,6 @@
         lax.dynamic_index_in_dim(hidden_bias, zlo, 1, False), core, 1, False
     ).reshape(-1)
 
-    token_rows = regroup(tokens)
-    grad_rows = regroup(cotangent)
     lengths = regroup(jnp.concatenate([cont_lengths[0], enc_len]))
     places = jnp.stack(
         [512 * ((core != block // 2) + 2 * (zlo != block % 2)) for block in range(4)]
@@ -729,94 +1302,92 @@
     self_meta = jnp.concatenate([places, bounds])
     cross_meta = lengths[segments:]
 
-    attention = jnp.concatenate([self_qkv, self_out.T[None], cross_qkv, cross_out.T[None]], axis=0)
-    mine, theirs = half_of(attention, core, 2), half_of(attention, 1 - core, 2)
-    attention = in_order(core, mine, trade(theirs, "core"), 1)
-    rows_of = attention.shape[1]
-    own = attention[:4].transpose(1, 0, 2)[:, :, None]
-    own = in_order(zhi, own, trade(own, "zhi"), 2)
-    w_self = over_chips(own.reshape(rows_of, -1))
-    own = attention[4:].transpose(1, 0, 2)[:, :, None]
-    own = in_order(zlo, own, trade(own, "zlo"), 2)[:, :, None]
-    own = in_order(zhi, own, trade(own, "zhi"), 2)
-    w_cross = over_chips(own.reshape(rows_of, -1))
-    hidden = jnp.stack([ff_in, ff_out.T])
-    mine, theirs = half_of(hidden, core, 2), half_of(hidden, 1 - core, 2)
-    hidden = in_order(core, mine, trade(theirs, "core"), 1)
-    hidden = in_order(zhi, hidden, trade(hidden, "zhi"), 2)
-    w_in = over_chips(hidden[0])
-    w_out = over_chips(hidden[1])
-    width = w_self.shape[1] // 4
-    pairs = width // PAIR
-    cross_width = w_cross.shape[1] // 4
-    cross_pairs = cross_width // PAIR
-
-    enc_rows = regroup(enc_states)
-    enc_both = in_order(zlo, enc_rows, trade(enc_rows, "zlo"), 0)
-    enc_full = in_order(core, enc_both, trade(enc_both, "core"), 0)
-
     resid = token_rows.astype(jnp.float32)
-    normed_in, hat_one, inv_one = norm_forward(resid, vectors[0], vectors[3])
-    attn_near, attn_far = spread_rows(low(normed_in))
+    _, hat_one, inv_one = norm_forward(resid, vectors[0], vectors[3])
     qkv_bias = jnp.concatenate([self_bias[0], jnp.zeros((width,), jnp.float32), self_bias[1]])
     qkv_scale = jnp.concatenate([jnp.full((width,), scaling), jnp.ones((2 * width,))]).astype(jnp.float32)
-    w_qkv, w_so = w_self[:, : 3 * width], w_self[:, 3 * width :]
-
     def project(rows):
         return low((product(rows, w_qkv) + qkv_bias) * qkv_scale)
 
-    qkv = jnp.concatenate([project(attn_near), project(attn_far)], axis=0)
+    qkv = project(attn_rows)
     count = qkv.shape[0]
     self_plan = functools.partial(self_sections, segments=segments)
     mixed, self_lse = attend(self_plan, self_meta, qkv, 0, qkv, pairs, 2 * pairs, pairs, 1152)
+    mixed = after(mixed, out_beyond)
+    w_out = over_chips(in_order(zhi, out_own, after(out_beyond, mixed), 1))
     near, far = mixed[: count // 2], mixed[count // 2 :]
-    branch = sum_rows(near, far, lambda rows: product_right_t(rows, w_so))
+    so_far = low(
+        product_right_t(far[: count // 4], w_so)
+        + trade(low(product_right_t(far[count // 4 :], w_so)), "core", "so_zc")
+    )
+    so_near_other = low(product_right_t(near[count // 4 :], w_so))
+    so_near = product_right_t(near[: count // 4], w_so)
+    grad_rows = regroup(after(cotangent, attn_rows), "cotangent")
+    cross_kv = low(
+        product(after(enc_full, grad_rows, so_far), w_ckv)
+        + jnp.concatenate([jnp.zeros((cross_width,), jnp.float32), cross_bias[1]])
+    )
+    branch = so_near + trade(so_near_other, "core", "so_c") + after(trade(so_far, "zlo", "so_z"), cross_kv)
     after_one = resid + (branch + vectors[6])
+
+    cot_beyond = trade(after(grad_rows, after_one), "zlo", "cot_z")
+    cot_near = jnp.concatenate([grad_rows, trade(grad_rows, "core", "cot_c")], axis=0)
 
     normed_mid, hat_two, inv_two = norm_forward(after_one, vectors[1], vectors[4])
     cross_low = low(normed_mid)
-    cross_rows = jnp.concatenate([cross_low, trade(cross_low, "core")], axis=0)
+    cross_rows = jnp.concatenate([cross_low, trade(cross_low, "core", "cin")], axis=0)
     own_rows = cross_low.shape[0]
-    w_cq = w_cross[:, :cross_width]
-    w_ckv = w_cross[:, cross_width : 3 * cross_width]
-    w_co = w_cross[:, 3 * cross_width :]
-    cross_kv = low(
-        product(enc_full, w_ckv)
-        + jnp.concatenate([jnp.zeros((cross_width,), jnp.float32), cross_bias[1]])
-    )
     cross_q = low((product(cross_rows, w_cq) + cross_bias[0]) * scaling)
     cross_plan = functools.partial(cross_sections, blocks=cross_q.shape[0] // BLOCK)
     cross_mixed, cross_lse = attend(
         cross_plan, cross_meta, cross_q, 0, cross_kv, 0, cross_pairs, cross_pairs, ENC
     )
-    other = trade(low(product_right_t(cross_mixed[own_rows:], w_co)), "core")
+    cross_mixed = after(cross_mixed, cot_beyond)
+    other = trade(low(product_right_t(cross_mixed[own_rows:], w_co)), "core", "co_c")
     branch = product_right_t(cross_mixed[:own_rows], w_co) + other
     after_two = after_one + (branch + vectors[7])
 
     normed_out, hat_three, inv_three = norm_forward(after_two, vectors[2], vectors[5])
-    mlp_near, mlp_far = spread_rows(low(normed_out))
-    grad_near, grad_far = spread_rows(grad_rows)
+    mlp_in = low(normed_out)
+    beyond = trade(mlp_in, "zlo", "mlp_z")
+    mlp_near = jnp.concatenate([mlp_in, trade(mlp_in, "core", "mlp_c")], axis=0)
     pre_near = product(mlp_near, w_in) + hidden_bias
+    act_near = low(gelu_value(pre_near))
+    beyond = after(beyond, act_near)
+    mlp_far = jnp.concatenate([beyond, trade(beyond, "core", "mlp_zc")], axis=0)
     pre_far = product(mlp_far, w_in) + hidden_bias
-    act_near, act_far = low(gelu_value(pre_near)), low(gelu_value(pre_far))
-    dpre_near = low(product(grad_near, w_out) * gelu_slope(pre_near))
-    dpre_far = low(product(grad_far, w_out) * gelu_slope(pre_far))
+    act_far = low(gelu_value(pre_far))
+    cot_far = jnp.concatenate([cot_beyond, trade(cot_beyond, "core", "cot_zc")], axis=0)
+    out_parts = [
+        low(product_right_t(act_far[own_rows:], w_out)),
+        product_right_t(act_far[:own_rows], w_out),
+        low(product_right_t(act_near[own_rows:], w_out)),
+        product_right_t(act_near[:own_rows], w_out),
+    ]
+    out_far = trade(low(out_parts[1] + trade(out_parts[0], "core", "out_zc")), "zlo", "out_z")
+    out_branch = out_parts[3] + trade(out_parts[2], "core", "out_c")
+    dpre_near = low(product(after(cot_near, act_far, out_branch), w_out) * gelu_slope(pre_near))
+    dpre_far = low(product(after(cot_far, dpre_near), w_out) * gelu_slope(pre_far))
     gradient = grad_rows.astype(jnp.float32)
     bias_out_three = jnp.sum(gradient, axis=0)
-    mlp_term = sum_rows(dpre_near, dpre_far, lambda rows: product_right_t(rows, w_in))
-    branch = sum_rows(act_near, act_far, lambda rows: product_right_t(rows, w_out))
-    layer_out = regroup(low(after_two + (branch + vectors[8])))
-    grad_w_out = product_left_t(grad_near, act_near) + product_left_t(grad_far, act_far)
-    grad_w_in = product_left_t(mlp_near, dpre_near) + product_left_t(mlp_far, dpre_far)
-    grad_hidden_bias = jnp.sum(dpre_near.astype(jnp.float32), axis=0) + jnp.sum(
-        dpre_far.astype(jnp.float32), axis=0
-    )
+    dmlp_far = low(
+        product_right_t(dpre_far[:own_rows], w_in)
+        + trade(low(product_right_t(dpre_far[own_rows:], w_in)), "core", "dmlp_zc")
+    )
+    mlp_term = product_right_t(dpre_near[:own_rows], w_in) + trade(
+        low(product_right_t(dpre_near[own_rows:], w_in)), "core", "dmlp_c"
+    )
+    act_near, act_far = after(act_near, dmlp_far, mlp_term), after(act_far, dmlp_far, mlp_term)
+    grad_w_out = low(product_left_t(cot_near, act_near) + product_left_t(cot_far, act_far))
+    mlp_near, mlp_far = after(mlp_near, grad_w_out), after(mlp_far, grad_w_out)
+    grad_w_in = low(product_left_t(mlp_near, dpre_near) + product_left_t(mlp_far, dpre_far))
+    mlp_term = mlp_term + after(trade(dmlp_far, "zlo", "dmlp_z"), grad_w_in)
     part, gain_three, shift_three = norm_backward(mlp_term, hat_three, inv_three, vectors[2])
     gradient = gradient + part
 
     grad_low = low(gradient)
     bias_out_two = jnp.sum(grad_low.astype(jnp.float32), axis=0)
-    grad_both = jnp.concatenate([grad_low, trade(grad_low, "core")], axis=0)
+    grad_both = jnp.concatenate([grad_low, trade(grad_low, "core", "e2")], axis=0)
     cross_mixed_grad = low(product(grad_both, w_co))
     cross_dq, cross_dk, cross_dv = attend_back(
         cross_plan,
@@ -832,75 +1403,90 @@
         cross_pairs,
         ENC,
     )
-    other = trade(low(product_right_t(cross_dq[own_rows:], w_cq)), "core")
+    out_sum = sum_over_chips(grad_w_out)
+    out_sum = half_of(out_sum, zhi, 1).astype(jnp.float32) + trade(half_of(out_sum, 1 - zhi, 1), "zhi", "go_zhi").astype(
+        jnp.float32
+    )
+    cross_dq = after(cross_dq, out_sum)
+    layer_out = regroup(low(after_two + (out_branch + after(out_far, cross_dq) + vectors[8])), "out")
+    other = trade(low(product_right_t(cross_dq[own_rows:], w_cq)), "core", "dcin")
     part, gain_two, shift_two = norm_backward(
         product_right_t(cross_dq[:own_rows], w_cq) + other, hat_two, inv_two, vectors[1]
     )
     gradient = gradient + part
+
+    grad_low = low(gradient)
+    bias_out_one = jnp.sum(grad_low.astype(jnp.float32), axis=0)
+    cross_parts = [
+        low(product_left_t(cross_rows, after(cross_dq, grad_low))),
+        low(product_left_t(enc_full, cross_dk)),
+        low(product_left_t(enc_full, cross_dv)),
+        low(product_left_t(grad_both, cross_mixed)),
+    ]
     grad_cross = jnp.concatenate(
-        [
-            low(product_left_t(cross_rows, cross_dq)),
-            low(product_left_t(enc_full, cross_dk)),
-            low(product_left_t(enc_full, cross_dv)),
-            low(product_left_t(grad_both, cross_mixed)),
-        ],
-        axis=1,
-    )
+        [part[:, lo : lo + width // 2] for lo in range(0, cross_width, width // 2) for part in cross_parts], axis=1
+    )
+    e1_rows, ff_in_grad = finish(after(grad_low, grad_cross), [sum_over_chips(grad_w_in)], None, None, 1)
+    lacking = trade(half_of(after(out_sum, e1_rows), 1 - core, 0), "core", "go_core")
+    ff_out_grad = in_order(core, half_of(out_sum, core, 0), lacking, 1)
+    cross_sum = sum_over_chips(grad_cross)
+    mixed_grad = low(product(e1_rows, w_so))
+    dq, dk, dv = attend_back(
+        self_plan, self_meta, qkv, 0, qkv, pairs, 2 * pairs, mixed, mixed_grad, self_lse, pairs, 1152
+    )
+    dqkv = jnp.concatenate([dq, dk, dv], axis=1)
+    d_near, d_far = dqkv[: count // 2], dqkv[count // 2 :]
+    dx_far = low(
+        product_right_t(d_far[: count // 4], w_qkv)
+        + trade(low(product_right_t(d_far[count // 4 :], w_qkv)), "core", "dx_zc")
+    )
+    dx = product_right_t(d_near[: count // 4], w_qkv) + trade(
+        low(product_right_t(d_near[count // 4 :], w_qkv)), "core", "dx_c"
+    )
+    dq, dk, dv = after(dq, dx_far), after(dk, dx_far), after(dv, dx_far)
+    self_parts = [
+        low(product_left_t(attn_rows, dq)),
+        low(product_left_t(attn_rows, dk)),
+        low(product_left_t(attn_rows, dv)),
+        low(product_left_t(e1_rows, mixed)),
+    ]
+    grad_self = jnp.concatenate(
+        [part[:, lo : lo + width // 2] for lo in range(0, width, width // 2) for part in self_parts], axis=1
+    )
+
+    enc_part = low(
+        product_right_t(after(cross_dk, dq), w_ckv[:, :cross_width])
+        + product_right_t(after(cross_dv, dq), w_ckv[:, cross_width:])
+    )
+    cross_grad, self_grad, enc_grad = finish(
+        None,
+        [],
+        (
+            after(cross_sum, dx),
+            grad_self.reshape(2, 2, rows_of, -1),
+            enc_part.reshape(2, 2, -1, model),
+        ),
+        None,
+        2,
+    )
+    enc_grad = enc_grad.astype(jnp.float32)
+    dx = dx + after(trade(dx_far, "zlo", "dx_z"), cross_grad)
+
+    def planes(shard):
+        return shard.reshape(shard.shape[0], 2, 4, -1).transpose(2, 0, 1, 3).reshape(4, shard.shape[0], -1)
+
+    cross_grad, self_grad = planes(cross_grad), planes(self_grad)
+    part, gain_one, shift_one = norm_backward(dx, hat_one, inv_one, vectors[0])
+    input_part = low(gradient + part)
+    input_grad = regroup(input_part, "dgrad").astype(jnp.float32)
+
+    bias_self_query = jnp.sum(dq.astype(jnp.float32), axis=0)
+    bias_self_value = jnp.sum(dv.astype(jnp.float32), axis=0)
     bias_cross_query = jnp.sum(cross_dq.astype(jnp.float32), axis=0)
     bias_cross_value = jnp.sum(cross_dv.astype(jnp.float32), axis=0)
-
-    def enc_term(rows):
-        return product_right_t(half_of(cross_dk, rows, 0), w_ckv[:, :cross_width]) + product_right_t(
-            half_of(cross_dv, rows, 0), w_ckv[:, cross_width:]
-        )
-
-    enc_half = enc_term(core) + trade(low(enc_term(1 - core)), "core")
-    enc_sum = half_of(enc_half, zlo, 0) + trade(low(half_of(enc_half, 1 - zlo, 0)), "zlo")
-    enc_grad = regroup(low(enc_sum)).astype(jnp.float32)
-
-    grad_low = low(gradient)
-    bias_out_one = jnp.sum(grad_low.astype(jnp.float32), axis=0)
-    grad_near, grad_far = spread_rows(grad_low)
-    mixed_grad = jnp.concatenate([low(product(grad_near, w_so)), low(product(grad_far, w_so))], axis=0)
-    dq, dk, dv = attend_back(
-        self_plan, self_meta, qkv, 0, qkv, pairs, 2 * pairs, mixed, mixed_grad, self_lse, pairs, 1152
-    )
-    dqkv = jnp.concatenate([dq, dk, dv], axis=1)
-    d_near, d_far = dqkv[: count // 2], dqkv[count // 2 :]
-    part, gain_one, shift_one = norm_backward(
-        sum_rows(d_near, d_far, lambda rows: product_right_t(rows, w_qkv)), hat_one, inv_one, vectors[0]
-    )
-    input_grad = regroup(low(gradient + part)).astype(jnp.float32)
-    grad_self = jnp.concatenate(
-        [
-            low(product_left_t(attn_near, d_near) + product_left_t(attn_far, d_far)),
-            low(product_left_t(grad_near, near) + product_left_t(grad_far, far)),
-        ],
-        axis=1,
-    )
-    bias_self_query = jnp.sum(dq.astype(jnp.float32), axis=0)
-    bias_self_value = jnp.sum(dv.astype(jnp.float32), axis=0)
-
-    def keep_half(values, index, axis, axis_name):
-        kept = half_of(values, index, axis).astype(jnp.float32)
-        return kept + trade(half_of(values, 1 - index, axis), axis_name).astype(jnp.float32)
-
-    def to_shards(values):
-        kept, sent = half_of(values, core, 0), half_of(values, 1 - core, 0)
-        return in_order(core, kept, trade(low(sent), "core").astype(jnp.float32), values.ndim - 1)
-
-    def hidden_shard(partial):
-        total = sum_over_chips(low(partial))
-        return to_shards(keep_half(total, zhi, 1, "zhi"))
-
-    ff_in_grad = hidden_shard(grad_w_in)
-    ff_out_grad = hidden_shard(grad_w_out).T
-    total = sum_over_chips(grad_cross).reshape(rows_of, 4, 2, -1)
-    total = low(keep_half(total, zhi, 2, "zhi")).reshape(rows_of, 4, 2, -1)
-    cross_grad = to_shards(keep_half(total, zlo, 2, "zlo").reshape(rows_of, 4, -1))
-    total = sum_over_chips(grad_self).reshape(rows_of, 4, 2, -1)
-    self_grad = to_shards(keep_half(total, zhi, 2, "zhi").reshape(rows_of, 4, -1))
-
+    grad_hidden_bias = jnp.sum(dpre_near.astype(jnp.float32), axis=0) + jnp.sum(
+        dpre_far.astype(jnp.float32), axis=0
+    )
     vec_sums = jnp.stack(
         [
             gain_one,
@@ -921,22 +1507,29 @@
     cross_sums = jnp.stack([bias_cross_query, bias_cross_value]).reshape(2, 2, 2, 1, -1) * at_core[:, None]
     head_sums = jnp.concatenate([self_sums, cross_sums], axis=0)
     hidden_sums = grad_hidden_bias.reshape(2, 1, 1, -1) * quarter
-    vec_sums = jnp.broadcast_to(vec_sums.reshape(9, 8, -1).transpose(1, 0, 2).reshape(8, 1, -1), (8, 4, sizes[0]))
-    head_sums = head_sums.reshape(4, 4, 8, -1).transpose(2, 1, 0, 3).reshape(8, 4, -1)
-    hidden_sums = hidden_sums.reshape(4, 8, -1).transpose(1, 0, 2)
-    sums = jnp.concatenate([vec_sums, head_sums, hidden_sums], axis=2).reshape(32, -1)
-    sums = lax.psum_scatter(sums, AXES, scatter_dimension=0, tiled=True).reshape(-1)
+    vec_sums = vec_sums.reshape(9, 8, -1).transpose(1, 0, 2).reshape(8, 1, -1)
+    sums = jnp.concatenate(
+        [
+            jnp.broadcast_to(vec_sums, (8, 4, sizes[0])),
+            head_sums.reshape(4, 4, 8, -1).transpose(2, 1, 0, 3).reshape(8, 4, -1),
+            hidden_sums.reshape(4, 8, -1).transpose(1, 0, 2),
+        ],
+        axis=2,
+    )
+    sums = jnp.pad(after(sums, input_part).reshape(32, -1, 128), ((0, 0), (0, 4), (0, 0)))
+    (sums,) = finish(None, [], None, sums, 3)
+    sums = sums.reshape(-1)[: sum(sizes)]
     vec_grad, head_grad, ff_bias_grad = jnp.split(sums, [sizes[0], sizes[0] + sizes[1]])
     return (
         layer_out,
         input_grad,
         enc_grad,
-        self_grad[:, :3].transpose(1, 0, 2),
-        self_grad[:, 3].T,
-        cross_grad[:, :3].transpose(1, 0, 2),
-        cross_grad[:, 3].T,
+        self_grad[:3],
+        self_grad[3].T,
+        cross_grad[:3],
+        cross_grad[3].T,
         ff_in_grad,
-        ff_out_grad,
+        ff_out_grad.T,
         head_grad.reshape(head_bias.shape),
         ff_bias_grad,
         vec_grad.reshape(vec_params.shape),

time: 986 us -> 724 us (0.73)
  waiting for transfers between devices: 427 us -> 79.2 us
  Pallas kernels: 94.7 us -> 325 us
  blocking collectives: 84.8 us -> 0 us
  starting transfers between devices: 69.5 us -> 21.6 us
  other arithmetic: 51.8 us -> 36.3 us
  local copies, waits for them, and re-layouts: 54 us -> 64.8 us
    pallas_call x0 -> x4, Pallas kernels: none -> 230 us  [the longest x3 124 us: finish(): pl.pallas_call(functools.partial(finish_kernel, rows is not None, len(hid...]
    ppermute x47 -> x25, waiting for transfers between devices: 299 us -> 79.1 us  [trade(): return lax.ppermute(rows, axis, [(0, 1), (1, 0)])]
    reduce_scatter x4 -> x3, waiting for transfers between devices: 85.7 us -> 0.06 us  [sum_over_chips(): lax.psum_scatter(partial, ('y', 'x'), scatter_dimension=0, tiled=True)]
    all_gather x1 -> x0, blocking collectives: 84.8 us -> none  [fast_layer(): lax.all_gather(flat, AXES, axis=0).reshape(8, 4, -1).astype(jnp.float32)]
    unnamed x10 -> x5, waiting for transfers between devices: 42.2 us -> 0.08 us
    ppermute x47 -> x25, starting transfers between devices: 42.5 us -> 14.7 us  [trade(): return lax.ppermute(rows, axis, [(0, 1), (1, 0)])]
    ppermute x7 -> x4, starting transfers between devices: 25.8 us -> 6.71 us  [regroup(): return lax.ppermute(rows, ('core', 'zhi'), [(0, 0), (1, 2), (2, 1), (3, 3)])]
    slice x1 -> x12, local copies, waits for them, and re-layouts: 0.01 us -> 10.4 us  [the longest x1 2.74 us: fast_layer(): w_in = over_chips(w_hidden[0])]
  transfers between devices with their start and end apart: 63 -> 34, of which waited for: 23 -> 6; matrix products, arithmetic and copies ran while one was open for 27% -> 29% of each run, Pallas kernels for 10% -> 45%
where the time goes in v2:
time: 724 us; the launch traced here: 716 us
  Pallas kernels  325 us (45%)
  matrix products  173 us (24%)
  waiting for transfers between devices  79.2 us (11%)
  local copies, waits for them, and re-layouts  64.8 us (9%)
  other arithmetic  36.3 us (5%)
  starting transfers between devices  21.6 us (3%)
  between operations  16.2 us (2%)
    pallas_call x3, Pallas kernels, finish(): pl.pallas_call(functools.partial(finish_kernel, rows is not None, len(hid...  124 us
    pallas_call x1, Pallas kernels, start_exchange(): pl.pallas_call(start_kernel, out_shape=shapes, in_specs=[anywhere] * 7, o...  106 us
    ppermute x25, waiting for transfers between devices, trade(): return lax.ppermute(rows, axis, [(0, 1), (1, 0)])  79.1 us
    dot_general x9, matrix products, product(): return jnp.dot(left, right, preferred_element_type=jnp.float32)  69.5 us
    dot_general x22, matrix products, product_right_t(): lax.dot_general(left, right, (((1,), (1,)), ((), ())), preferred_element_...  60.3 us
    pallas_call x2, Pallas kernels, attend_back(): pl.pallas_call(functools.partial(backward_kernel, sections), grid_spec=pl...  56.6 us
    dot_general x12, matrix products, product_left_t(): lax.dot_general(left, right, (((0,), (0,)), ((), ())), preferred_element_...  43.1 us
    pallas_call x2, Pallas kernels, attend(): pl.pallas_call(functools.partial(forward_kernel, sections), grid_spec=plt...  38.2 us
  transfers between devices with their start and end apart: 34, of which 6 were waited for; matrix products, arithmetic and copies ran while one was open for 29% of the time, Pallas kernels for 45%

profile of v2, /device:TPU:0, one launch (start us, length us, event | category | flops | bytes accessed | tf_op | source)
XLA Modules:
  0.0 716.1 jit_solution(10364745215444808420)
XLA Ops:
  17.1 105.8 %shard_map.229 = (bf16[512,1024]{1,0:T(8,128)(2,1)}, bf16[2048,1024]{1,0:T(8,128)(2,1)}, bf16[4,2,2,256,256]{4,3,2,1,0:T(8,128)(2,1)}, bf16[4,2,2,256,512]{4,3,2...) custom-call(bf16[512,1024]{1,0:T(8,128)(2,1)} %tokens.1, ...), custom_call_target="tpu_custom_call" | custom-call | tf_op jit(solution)/shard_map/pallas_call | solution.py:871
  130.0 8.1 %multiply_convert_fusion.2.q_ref.k_ref.v_ref = bf16[2048,768]{1,0:T(8,128)(2,1)} fusion(bf16[2048,1024]{1,0:T(8,128)(2,1)} %get-tuple-element.63, f32[768]{0:T(1024)S(1)} %copy-done.87, f32[768]{0:T(1024)S(1)} %pad_maximum_fusion.12, bf16[1024,256]{1,0:T(8,128)(2,1)S(1)} %bitcast.220, bf16[1024,256]{1,0:T(8,128)(2,1)S(1)} %bitcast.225, ...), kind=kOutput, calls=%fused_computation.24 | convolution fusion | flops 3230662656 | bytes 8919040 | tf_op jit(solution)/shard_map/dot_general | solution.py:268
  139.0 23.1 %shard_map.230 = (bf16[2048,256]{1,0:T(8,128)(2,1)}, f32[2048,256]{1,0:T(8,128)}) custom-call(s32[13]{0:T(128)} %concatenate.78.meta_ref, bf16[2048,768]{1,0:T(8,128)(2,1)} %multiply_convert_fusion.2.q_ref.k_ref.v_ref, bf16[2048,768]{1,0:T(8,128)(2,1)} %multiply_convert_fusion.2.q_ref.k_ref.v_ref, bf16[2048,768]{1,0:T(8,128)(2,1)} %multiply_convert_fusion.2.q_ref.k_ref.v_ref), custom_call_target="tpu_custom_call" | custom-call | flops 19327352832 | bytes 5242880 | tf_op jit(solution)/shard_map/pallas_call | solution.py:180
  181.6 26.5 %collective-permute-done.4 = bf16[512,1024]{1,0:T(8,128)(2,1)S(1)} collective-permute-done((bf16[512,1024]{1,0:T(8,128)(2,1)S(1)}, bf16[512,1024]{1,0:T(8,128)(2,1)S(1)}, u32[]{:S(2)}, u32[]{:S(2)}) %collective-permute-start.4) | collective-permute-done | bytes 1048608 | tf_op jit(solution)/shard_map/so_z/ppermute | solution.py:1185
  217.5 15.1 %shard_map.231 = (bf16[1024,512]{1,0:T(8,128)(2,1)}, f32[1024,512]{1,0:T(8,128)}) custom-call(s32[1]{0:T(128)} %slice.307.meta_ref, bf16[1024,512]{1,0:T(8,128)(2,1)} %multiply_convert_fusion.3.q_ref, bf16[512,1024]{1,0:T(8,128)(2,1)} %add_convert_fusion.9.k_ref.v_ref, bf16[512,1024]{1,0:T(8,128)(2,1)} %add_convert_fusion.9.k_ref.v_ref), custom_call_target="tpu_custom_call" | custom-call | flops 8589934592 | bytes 5242880 | tf_op jit(solution)/shard_map/pallas_call | solution.py:180
  232.6 6.6 collective-permute-done.7
  252.7 13.3 %multiply_convert_fusion.1 = (bf16[1024,2048]{1,0:T(8,128)(2,1)}, f32[1024,2048]{1,0:T(8,128)}) fusion(f32[2048]{0:T(1024)S(1)} %bitcast.241, bf16[1,1024,2048]{2,1,0:T(8,128)(2,1)} %all-gather.6.cloned.1.call-done, bf16[512,1024]{1,0:T(8,128)(2,1)} %collective-permute-done.9, bf16[512,1024]{1,0:T(8,128)(2,1)} %add_convert_fusion.7), kind=kOutput, calls=%fused_computation.23 | convolution fusion | flops 4320133120 | bytes 18882560 | tf_op jit(solution)/shard_map/dot_general | solution.py:268
  266.1 12.3 %collective-permute-done.11 = bf16[512,1024]{1,0:T(8,128)(2,1)} collective-permute-done((bf16[512,1024]{1,0:T(8,128)(2,1)}, bf16[512,1024]{1,0:T(8,128)(2,1)}, u32[]{:S(2)}, u32[]{:S(2)}) %collective-permute-start.11) | collective-permute-done | bytes 1048608 | tf_op jit(solution)/shard_map/mlp_z/ppermute | solution.py:1185
  285.2 5.3 fusion.56
  292.4 8.5 %multiply_convert_fusion = (bf16[1024,2048]{1,0:T(8,128)(2,1)S(1)}, f32[1024,2048]{1,0:T(8,128)}) fusion(f32[2048]{0:T(1024)S(1)} %bitcast.242, bf16[1024,1024]{1,0:T(8,128)(2,1)S(1)} %constant_dynamic-update-slice_fusion, bf16[1,1024,2048]{2,1,0:T(8,128)(2,1)S(1)} %copy-done.82), kind=kOutput, calls=%fused_computation.22 | convolution fusion | flops 4315938816 | bytes 18882560 | tf_op jit(solution)/shard_map/dot_general | solution.py:268
  304.7 12.0 %convert_reduce_fusion.1 = (f32[2048]{0:T(1024)S(1)}, bf16[1024,2048]{1,0:T(8,128)(2,1)S(1)}) fusion(f32[1024,2048]{1,0:T(8,128)} %get-tuple-element.201, f32[2048]{0:T(1024)S(1)} %bitcast.243, bf16[1024,1024]{1,0:T(8,128)(2,1)} %constant_dynamic-update-slice_fusion.2, bf16[1024,2048]{1,0:T(8,128)(2,1)S(1)} %copy-done.83), kind=kOutput, calls=%fused_computation.19 | convolution fusion | flops 4341102592 | bytes 18890752 | tf_op jit(solution)/shard_map/dot_general | solution.py:268
  316.6 13.7 %convert_reduce_fusion = (f32[2048]{0:T(1024)S(1)}, bf16[1024,2048]{1,0:T(8,128)(2,1)S(1)}) fusion(f32[1024,2048]{1,0:T(8,128)} %get-tuple-element.203, f32[2048]{0:T(1024)S(1)} %bitcast.244, bf16[1024,1024]{1,0:T(8,128)(2,1)} %constant_dynamic-update-slice_fusion.4, bf16[1024,2048]{1,0:T(8,128)(2,1)S(1)} %copy-done.83), kind=kOutput, calls=%fused_computation.18 | convolution fusion | flops 4341102592 | bytes 18890752 | tf_op jit(solution)/shard_map/dot_general | solution.py:268
  342.8 6.6 fusion.107
  349.4 7.8 %add_convert_fusion.1 = bf16[1024,2048]{1,0:T(8,128)(2,1)} fusion(f32[1024,2048]{1,0:T(8,128)S(1)} %fusion.107, bf16[1024,1024]{1,0:T(8,128)(2,1)} %constant_dynamic-update-slice_fusion.2, bf16[1024,2048]{1,0:T(8,128)(2,1)S(1)} %copy-done.92), kind=kOutput, calls=%fused_computation.21 | convolution fusion | flops 4299161600 | bytes 18874368 | tf_op jit(solution)/shard_map/dot_general | solution.py:272
  360.6 5.2 fusion.59
  366.1 4.6 fusion.108
  370.8 6.4 add_convert_fusion
  377.1 14.5 %collective-permute-done.19 = bf16[512,1024]{1,0:T(8,128)(2,1)} collective-permute-done((bf16[512,1024]{1,0:T(8,128)(2,1)}, bf16[512,1024]{1,0:T(8,128)(2,1)}, u32[]{:S(2)}, u32[]{:S(2)}) %collective-permute-start.19) | collective-permute-done | bytes 1048608 | tf_op jit(solution)/shard_map/dmlp_z/ppermute | solution.py:1185
  395.2 4.3 convert_reduce_fusion.7
  400.9 6.4 add_convert_fusion.6
  408.5 3.8 convolution_convert_fusion.5.do_ref
  412.3 18.6 %shard_map.232 = (bf16[1024,512]{1,0:T(8,128)(2,1)}, bf16[512,512]{1,0:T(8,128)(2,1)}, bf16[512,512]{1,0:T(8,128)(2,1)}) custom-call(s32[1]{0:T(128)} %slice.307.meta_ref, bf16[1024,512]{1,0:T(8,128)(2,1)} %multiply_convert_fusion.3.q_ref, bf16[512,1024]{1,0:T(8,128)(2,1)} %add_convert_fusion.9.k_ref.v_ref, bf16[512,1024]{1,0:T(8,128)(2,1)} %add_convert_fusion.9.k_ref.v_ref, ...), custom_call_target="tpu_custom_call" | custom-call | flops 21474836480 | bytes 10485760 | tf_op jit(solution)/shard_map/pallas_call | solution.py:202
  432.2 4.2 collective-permute-start.21
  439.7 4.0 convolution_convert_fusion.3
  443.7 16.3 %collective-permute-done.21 = bf16[256,1024]{1,0:T(8,128)(2,1)S(1)} collective-permute-done((bf16[256,1024]{1,0:T(8,128)(2,1)S(1)}, bf16[256,1024]{1,0:T(8,128)(2,1)S(1)}, u32[]{:S(2)}, u32[]{:S(2)}) %collective-permute-start.21) | collective-permute-done | bytes 524320 | tf_op jit(solution)/shard_map/go_zhi/ppermute | solution.py:1185
  490.4 44.1 %shard_map.233 = (bf16[2048,1024]{1,0:T(8,128)(2,1)}, f32[128,2048]{1,0:T(8,128)}) custom-call(bf16[512,1024]{1,0:T(8,128)(2,1)} %get-tuple-element.93.refs_0_, bf16[256,2048]{1,0:T(8,128)(2,1)} %reduce-scatter.6.cloned.1.call-done.refs_1_), custom_call_target="tpu_custom_call" | custom-call | flops 20000000000 | tf_op jit(solution)/shard_map/pallas_call | solution.py:1170
  534.5 4.4 convolution_convert_fusion.do_ref
  538.9 37.9 %shard_map.234 = (bf16[2048,256]{1,0:T(8,128)(2,1)}, bf16[2048,256]{1,0:T(8,128)(2,1)}, bf16[2048,256]{1,0:T(8,128)(2,1)}) custom-call(s32[13]{0:T(128)} %concatenate.78.meta_ref, bf16[2048,768]{1,0:T(8,128)(2,1)} %multiply_convert_fusion.2.q_ref.k_ref.v_ref, bf16[2048,768]{1,0:T(8,128)(2,1)} %multiply_convert_fusion.2.q_ref.k_ref.v_ref, ...), custom_call_target="tpu_custom_call" | custom-call | flops 48318382080 | bytes 10485760 | tf_op jit(solution)/shard_map/pallas_call | solution.py:202
  588.9 3.8 add_convert_fusion.3
  598.8 4.1 copy.69
  608.5 51.1 %shard_map.235 = (f32[128,1024]{1,0:T(8,128)}, f32[128,1024]{1,0:T(8,128)}, bf16[128,1024]{1,0:T(8,128)(2,1)}) custom-call(bf16[256,2048]{1,0:T(8,128)(2,1)} %reduce-scatter.8.cloned.1.call-done.refs_0_, bf16[2,2,256,1024]{3,2,1,0:T(8,128)(2,1)} %bitcast.209, bf16[2,2,128,1024]{3,2,1,0:T(8,128)(2,1)} %bitcast.211), custom_call_target="tpu_custom_call" | custom-call | flops 20000000000 | tf_op jit(solution)/shard_map/pallas_call | solution.py:1170
  668.3 29.3 %shard_map.236 = f32[16,128]{1,0:T(8,128)} custom-call(f32[32,16,128]{2,1,0:T(8,128)} %pad.13.refs_0_), custom_call_target="tpu_custom_call" | custom-call | flops 20000000000 | tf_op jit(solution)/shard_map/pallas_call | solution.py:1170
  (445 shorter events, 172.2 us)
Async XLA Ops:
  7.2 245.6 %all-gather.6.cloned.1.call-start = ((), (), s32[]{:S(2)}) async-start(), calls=%async_computation.7 | async-start | bytes 5242880 | tf_op jit(solution)/shard_map/all_gather | solution.py:1213
  8.6 129.5 %collective-permute-start = (s32[9]{0:T(128)S(1)}, s32[9]{0:T(128)S(1)}, u32[]{:S(2)}, u32[]{:S(2)}) collective-permute-start(s32[9]{0:T(128)S(1)} %pad_add_fusion), channel_id=1, source_target_pairs={{0,0},{2,4},{4,2},{6,6},{1,1},{3,5},{5,3},{7,7},{8,8},{10,12},{12,... | collective-permute-start | bytes 116 | tf_op jit(solution)/shard_map/re_regroup/ppermute | solution.py:1194
  125.7 36.4 %collective-permute-start.1 = (bf16[256,1024]{1,0:T(8,128)(2,1)S(1)}, bf16[256,1024]{1,0:T(8,128)(2,1)}, u32[]{:S(2)}, u32[]{:S(2)}) collective-permute-start(bf16[256,1024]{1,0:T(8,128)(2,1)S(1)} %dynamic-slice_bitcast_fusion), channel_id=1, source_target_pairs={{0,2},{2,0},{1,3},{3,1},{4,6},{6,4},{5,7},{7,5},{8,10},{10,8},{9,1... | collective-permute-start | bytes 1572872 | tf_op jit(solution)/shard_map/wo_zhi/ppermute | solution.py:1185
  127.8 157.3 %all-gather.4.cloned.1.call-start = ((), (), s32[]{:S(2)}) async-start(), calls=%async_computation.3 | async-start | bytes 5242880 | tf_op jit(solution)/shard_map/all_gather | solution.py:1213
  164.6 6.4 collective-permute-start.3
  164.7 13.2 %collective-permute-start.5 = (bf16[512,1024]{1,0:T(8,128)(2,1)}, bf16[512,1024]{1,0:T(8,128)(2,1)S(1)}, u32[]{:S(2)}, u32[]{:S(2)}) collective-permute-start(bf16[512,1024]{1,0:T(8,128)(2,1)} %param.18), channel_id=1, source_target_pairs={{0,0},{2,4},{4,2},{6,6},{1,1},{3,5},{5,3},{7,7},{8,8},{10,12},{12,... | collective-permute-start | bytes 3145736 | tf_op jit(solution)/shard_map/re_cotangent/ppermute | solution.py:1194
  169.6 38.5 %collective-permute-start.2 = (bf16[512,1024]{1,0:T(8,128)(2,1)S(1)}, bf16[512,1024]{1,0:T(8,128)(2,1)S(1)}, u32[]{:S(2)}, u32[]{:S(2)}) collective-permute-start(bf16[512,1024]{1,0:T(8,128)(2,1)S(1)} %convolution_convert_fusion.7), channel_id=1, source_target_pairs={{0,4},{4,0},{1,5},{5,1},{2,6},{6,2},{3,7},{7,3},{8,12},{12,8},{9,1... | collective-permute-start | bytes 3145736 | tf_op jit(solution)/shard_map/so_c/ppermute | solution.py:1185
  172.7 35.4 %collective-permute-start.4 = (bf16[512,1024]{1,0:T(8,128)(2,1)S(1)}, bf16[512,1024]{1,0:T(8,128)(2,1)S(1)}, u32[]{:S(2)}, u32[]{:S(2)}) collective-permute-start(bf16[512,1024]{1,0:T(8,128)(2,1)S(1)} %add_convert_fusion.10), channel_id=1, source_target_pairs={{0,1},{1,0},{2,3},{3,2},{4,5},{5,4},{6,7},{7,6},{8,9},{9,8},{10,11... | collective-permute-start | bytes 3145736 | tf_op jit(solution)/shard_map/so_z/ppermute | solution.py:1185
  213.5 217.5 %reduce-scatter.4.cloned.1.call-start = ((), (), s32[]{:S(2)}) async-start(), calls=%async_computation.4 | async-start | bytes 5242880 | tf_op jit(solution)/shard_map/reduce_scatter | solution.py:1217
  213.6 25.7 %collective-permute-start.7 = (bf16[512,1024]{1,0:T(8,128)(2,1)S(1)}, bf16[512,1024]{1,0:T(8,128)(2,1)}, u32[]{:S(2)}, u32[]{:S(2)}) collective-permute-start(bf16[512,1024]{1,0:T(8,128)(2,1)S(1)} %collective-permute-done.5), channel_id=1, source_target_pairs={{0,1},{1,0},{2,3},{3,2},{4,5},{5,4},{6,7},{7,6},{8,9},{9,8},{10,11... | collective-permute-start | bytes 3145736 | tf_op jit(solution)/shard_map/cot_z/ppermute | solution.py:1185
  241.0 3.4 collective-permute-start.8
  241.1 9.1 %collective-permute-start.15 = (bf16[512,1024]{1,0:T(8,128)(2,1)S(1)}, bf16[512,1024]{1,0:T(8,128)(2,1)}, u32[]{:S(2)}, u32[]{:S(2)}) collective-permute-start(bf16[512,1024]{1,0:T(8,128)(2,1)S(1)} %collective-permute-done.5), channel_id=1, source_target_pairs={{0,4},{4,0},{1,5},{5,1},{2,6},{6,2},{3,7},{7,3},{8,12},{12,8},{9,1... | collective-permute-start | bytes 3145736 | tf_op jit(solution)/shard_map/cot_c/ppermute | solution.py:1185
  248.8 3.9 collective-permute-start.9
  252.5 28.2 %collective-permute-start.17 = (bf16[512,1024]{1,0:T(8,128)(2,1)}, bf16[512,1024]{1,0:T(8,128)(2,1)}, u32[]{:S(2)}, u32[]{:S(2)}) collective-permute-start(bf16[512,1024]{1,0:T(8,128)(2,1)} %collective-permute-done.7), channel_id=1, source_target_pairs={{0,4},{4,0},{1,5},{5,1},{2,6},{6,2},{3,7},{7,3},{8,12},{12,8},{9,1... | collective-permute-start | bytes 3145736 | tf_op jit(solution)/shard_map/cot_zc/ppermute | solution.py:1185
  252.7 25.6 %collective-permute-start.11 = (bf16[512,1024]{1,0:T(8,128)(2,1)}, bf16[512,1024]{1,0:T(8,128)(2,1)}, u32[]{:S(2)}, u32[]{:S(2)}) collective-permute-start(bf16[512,1024]{1,0:T(8,128)(2,1)} %add_convert_fusion.7), channel_id=1, source_target_pairs={{0,1},{1,0},{2,3},{3,2},{4,5},{5,4},{6,7},{7,6},{8,9},{9,8},{10,11... | collective-permute-start | bytes 3145736 | tf_op jit(solution)/shard_map/mlp_z/ppermute | solution.py:1185
  278.4 12.7 %collective-permute-start.12 = (bf16[512,1024]{1,0:T(8,128)(2,1)}, bf16[512,1024]{1,0:T(8,128)(2,1)}, u32[]{:S(2)}, u32[]{:S(2)}) collective-permute-start(bf16[512,1024]{1,0:T(8,128)(2,1)} %collective-permute-done.11), channel_id=1, source_target_pairs={{0,4},{4,0},{1,5},{5,1},{2,6},{6,2},{3,7},{7,3},{8,12},{12,8},{9,1... | collective-permute-start | bytes 3145736 | tf_op jit(solution)/shard_map/mlp_zc/ppermute | solution.py:1185
  290.5 10.4 %collective-permute-start.10 = (bf16[512,1024]{1,0:T(8,128)(2,1)S(1)}, bf16[512,1024]{1,0:T(8,128)(2,1)S(1)}, u32[]{:S(2)}, u32[]{:S(2)}) collective-permute-start(bf16[512,1024]{1,0:T(8,128)(2,1)S(1)} %fusion.56), channel_id=1, source_target_pairs={{0,4},{4,0},{1,5},{5,1},{2,6},{6,2},{3,7},{7,3},{8,12},{12,8},{9,1... | collective-permute-start | bytes 3145736 | tf_op jit(solution)/shard_map/out_c/ppermute | solution.py:1185
  335.2 3.9 collective-permute-start.16
  357.3 133.1 %reduce-scatter.6.cloned.1.call-start = ((), (), s32[]{:S(2)}) async-start(), calls=%async_computation.5 | async-start | bytes 5242880 | tf_op jit(solution)/shard_map/reduce_scatter | solution.py:1217
  365.8 35.1 %collective-permute-start.13 = (bf16[512,1024]{1,0:T(8,128)(2,1)}, bf16[512,1024]{1,0:T(8,128)(2,1)}, u32[]{:S(2)}, u32[]{:S(2)}) collective-permute-start(bf16[512,1024]{1,0:T(8,128)(2,1)} %fusion.59), channel_id=1, source_target_pairs={{0,4},{4,0},{1,5},{5,1},{2,6},{6,2},{3,7},{7,3},{8,12},{12,8},{9,1... | collective-permute-start | bytes 3145736 | tf_op jit(solution)/shard_map/out_zc/ppermute | solution.py:1185
  365.8 25.9 %collective-permute-start.19 = (bf16[512,1024]{1,0:T(8,128)(2,1)}, bf16[512,1024]{1,0:T(8,128)(2,1)}, u32[]{:S(2)}, u32[]{:S(2)}) collective-permute-start(bf16[512,1024]{1,0:T(8,128)(2,1)} %add_convert_fusion.5), channel_id=1, source_target_pairs={{0,1},{1,0},{2,3},{3,2},{4,5},{5,4},{6,7},{7,6},{8,9},{9,8},{10,11... | collective-permute-start | bytes 3145736 | tf_op jit(solution)/shard_map/dmlp_z/ppermute | solution.py:1185
  399.5 8.1 %collective-permute-start.20 = (bf16[512,1024]{1,0:T(8,128)(2,1)}, bf16[512,1024]{1,0:T(8,128)(2,1)}, u32[]{:S(2)}, u32[]{:S(2)}) collective-permute-start(bf16[512,1024]{1,0:T(8,128)(2,1)} %get-tuple-element.161), channel_id=1, source_target_pairs={{0,4},{4,0},{1,5},{5,1},{2,6},{6,2},{3,7},{7,3},{8,12},{12,8},{9,1... | collective-permute-start | bytes 3145736 | tf_op jit(solution)/shard_map/e2/ppermute | solution.py:1185
  407.3 56.9 %collective-permute-start.14 = (bf16[512,1024]{1,0:T(8,128)(2,1)}, bf16[512,1024]{1,0:T(8,128)(2,1)}, u32[]{:S(2)}, u32[]{:S(2)}) collective-permute-start(bf16[512,1024]{1,0:T(8,128)(2,1)} %add_convert_fusion.6), channel_id=1, source_target_pairs={{0,1},{1,0},{2,3},{3,2},{4,5},{5,4},{6,7},{7,6},{8,9},{9,8},{10,11... | collective-permute-start | bytes 3145736 | tf_op jit(solution)/shard_map/out_z/ppermute | solution.py:1185
  407.6 200.9 %reduce-scatter.8.cloned.1.call-start = ((), (), s32[]{:S(2)}) async-start(), calls=%async_computation.6 | async-start | bytes 5242880 | tf_op jit(solution)/shard_map/reduce_scatter | solution.py:1217
  432.2 27.8 %collective-permute-start.21 = (bf16[256,1024]{1,0:T(8,128)(2,1)S(1)}, bf16[256,1024]{1,0:T(8,128)(2,1)S(1)}, u32[]{:S(2)}, u32[]{:S(2)}) collective-permute-start(bf16[256,1024]{1,0:T(8,128)(2,1)S(1)} %constant_dynamic-slice_fusion.3), channel_id=1, source_target_pairs={{0,2},{2,0},{1,3},{3,1},{4,6},{6,4},{5,7},{7,5},{8,10},{10,8},{9,1... | collective-permute-start | bytes 1572872 | tf_op jit(solution)/shard_map/go_zhi/ppermute | solution.py:1185
  462.0 7.9 %collective-permute-start.23 = (bf16[512,1024]{1,0:T(8,128)(2,1)}, bf16[512,1024]{1,0:T(8,128)(2,1)}, u32[]{:S(2)}, u32[]{:S(2)}) collective-permute-start(bf16[512,1024]{1,0:T(8,128)(2,1)} %convolution_convert_fusion.10), channel_id=1, source_target_pairs={{0,4},{4,0},{1,5},{5,1},{2,6},{6,2},{3,7},{7,3},{8,12},{12,8},{9,1... | collective-permute-start | bytes 3145736 | tf_op jit(solution)/shard_map/dcin/ppermute | solution.py:1185
  468.0 117.0 %collective-permute-start.22 = (bf16[512,1024]{1,0:T(8,128)(2,1)}, bf16[512,1024]{1,0:T(8,128)(2,1)S(1)}, u32[]{:S(2)}, u32[]{:S(2)}) collective-permute-start(bf16[512,1024]{1,0:T(8,128)(2,1)} %add_convert_fusion.4), channel_id=1, source_target_pairs={{0,0},{2,4},{4,2},{6,6},{1,1},{3,5},{5,3},{7,7},{8,8},{10,12},{12,... | collective-permute-start | bytes 3145736 | tf_op jit(solution)/shard_map/re_out/ppermute | solution.py:1194
  581.8 7.1 collective-permute-start.25
  582.4 5.0 collective-permute-start.28
  584.4 21.5 %collective-permute-start.24 = (bf16[512,1024]{1,0:T(8,128)(2,1)}, bf16[512,1024]{1,0:T(8,128)(2,1)}, u32[]{:S(2)}, u32[]{:S(2)}) collective-permute-start(bf16[512,1024]{1,0:T(8,128)(2,1)} %convolution_convert_fusion.2), channel_id=1, source_target_pairs={{0,4},{4,0},{1,5},{5,1},{2,6},{6,2},{3,7},{7,3},{8,12},{12,8},{9,1... | collective-permute-start | bytes 3145736 | tf_op jit(solution)/shard_map/dx_c/ppermute | solution.py:1185
  592.7 67.0 %collective-permute-start.26 = (bf16[512,1024]{1,0:T(8,128)(2,1)}, bf16[512,1024]{1,0:T(8,128)(2,1)}, u32[]{:S(2)}, u32[]{:S(2)}) collective-permute-start(bf16[512,1024]{1,0:T(8,128)(2,1)} %add_convert_fusion.3), channel_id=1, source_target_pairs={{0,1},{1,0},{2,3},{3,2},{4,5},{5,4},{6,7},{7,6},{8,9},{9,8},{10,11... | collective-permute-start | bytes 3145736 | tf_op jit(solution)/shard_map/dx_z/ppermute | solution.py:1185
  665.3 39.9 %collective-permute-start.27 = (bf16[512,1024]{1,0:T(8,128)(2,1)}, bf16[512,1024]{1,0:T(8,128)(2,1)S(1)}, u32[]{:S(2)}, u32[]{:S(2)}) collective-permute-start(bf16[512,1024]{1,0:T(8,128)(2,1)} %fusion.35), channel_id=1, source_target_pairs={{0,0},{2,4},{4,2},{6,6},{1,1},{3,5},{5,3},{7,7},{8,8},{10,12},{12,... | collective-permute-start | bytes 3145736 | tf_op jit(solution)/shard_map/re_dgrad/ppermute | solution.py:1194
  (97 other events, 942.1 us)
Sparse Core Ops, SparseCore 0:
  127.9 53.0 all-gather.5
  213.6 55.5 all-gather.3
  357.4 55.1 reduce-scatter.3
  415.7 52.6 reduce-scatter.5
  490.5 54.2 reduce-scatter.7

commit v3 on v2

--- a/solution.py
+++ b/solution.py
@@ -632,6 +632,52 @@
         results[7],
         vector_total,
     )
+
+
+def hidden_kernel(x_ref, e_ref, w_in_ref, w_out_ref, bias_ref, act_ref, grad_ref, sum_ref):
+    chunk = 256
+    sum_ref[...] = jnp.zeros_like(sum_ref)
+
+    def step(index, carry):
+        rows = pl.ds(pl.multiple_of(index * chunk, chunk), chunk)
+        value = dot_nn(x_ref[rows, :], w_in_ref[...]) + bias_ref[...]
+        upper = dot_nn(e_ref[rows, :], w_out_ref[...])
+        square = value * value
+        inner = jnp.tanh(value * (GELU_C + (GELU_C * GELU_A) * square))
+        half = 0.5 + 0.5 * inner
+        act_ref[rows, :] = (value * half).astype(act_ref.dtype)
+        slope = half + (value * (half * (1.0 - inner))) * (GELU_C + (3.0 * GELU_C * GELU_A) * square)
+        grad = (upper * slope).astype(grad_ref.dtype)
+        grad_ref[rows, :] = grad
+        sum_ref[...] += jnp.sum(grad.astype(jnp.float32), axis=0, keepdims=True)
+        return carry
+
+    lax.fori_loop(0, x_ref.shape[0] // chunk, step, 0, unroll=2)
+
+
+def hidden_units(rows, grads, w_in, w_out, bias, tile=512):
+    count, model = rows.shape
+    width = w_in.shape[1]
+    whole = pl.BlockSpec((count, model), lambda i: (0, 0))
+    weight = pl.BlockSpec((model, tile), lambda i: (0, i))
+    line = pl.BlockSpec((1, tile), lambda i: (0, i))
+    out = pl.BlockSpec((count, tile), lambda i: (0, i))
+    return pl.pallas_call(
+        hidden_kernel,
+        grid=(width // tile,),
+        in_specs=[whole, whole, weight, weight, line],
+        out_specs=[out, out, line],
+        out_shape=[
+            jax.ShapeDtypeStruct((count, width), jnp.bfloat16),
+            jax.ShapeDtypeStruct((count, width), jnp.bfloat16),
+            jax.ShapeDtypeStruct((1, width), jnp.float32),
+        ],
+        cost_estimate=pl.CostEstimate(
+            flops=4 * count * model * width,
+            bytes_accessed=4 * (count * model + model * width + count * width),
+            transcendentals=count * width,
+        ),
+    )(rows, grads, w_in, w_out, bias)
 
 
 MESH = pl.DeviceIdType.MESH
@@ -885,36 +931,54 @@
     )(tokens, enc, w_self, w_cross, w_in, w_out, small)
 
 
-def finish_kernel(spread, hidden, attention, small, *refs):
+def finish_kernel(
+    ff_in,
+    ff_out,
+    cross,
+    self_q,
+    self_k,
+    self_v,
+    self_o,
+    enc_part,
+    small,
+    ff_in_out,
+    ff_out_out,
+    cross_qkv_out,
+    cross_out_out,
+    self_qkv_out,
+    self_out_out,
+    enc_out,
+    small_out,
+    cross_own,
+    cross_got,
+    cross_low,
+    cross_got_low,
+    cross_total,
+    enc_own,
+    enc_got,
+    enc_sum,
+    enc_far,
+    enc_low,
+    self_own,
+    self_got,
+    low_a,
+    low_b,
+    self_got_low,
+    self_total,
+    self_last,
+    small_sum,
+    small_got_0,
+    small_got_1,
+    small_got_2,
+    small_got_3,
+    small_got_4,
+    send,
+    recv,
+    local,
+):
     y, x, core, zhi, zlo = (lax.axis_index(axis) for axis in AXES)
     crossing = core != zhi
-    refs = list(refs)
-
-    def take(number):
-        taken, refs[:number] = refs[:number], []
-        return taken
-
-    links = ("core", "zhi")
-    if spread or attention or small:
-        links += ("zlo",)
-    if attention or small:
-        links += ("x", "y")
-    rows_in = take(1) if spread else []
-    hidden_in = take(hidden)
-    attention_in = take(3) if attention else []
-    small_in = take(small)
-    rows_out = take(1) if spread else []
-    hidden_out = take(hidden)
-    attention_out = take(3) if attention else []
-    small_out = take(small)
-    hidden_kept = [take(3) for _ in range(hidden)]
-    if attention:
-        enc_own, enc_got, enc_sum, enc_far, enc_low = take(5)
-        kept, got, total, low_part, got_low, total_low = take(6)
-        self_own, self_got, self_low, self_got_low, self_total, self_send, self_last = take(7)
-    if small:
-        small_sum, *small_got = take(1 + len(AXES))
-    send, recv, local = take(3)
+    small_got = (small_got_0, small_got_1, small_got_2, small_got_3, small_got_4)
     counts = {"sent": 0, "local": 0}
 
     def push(source, target, axis):
@@ -938,9 +1002,6 @@
         copy.start()
         return copy
 
-    def lanes(block, size):
-        return pl.ds(pl.multiple_of(block * size, size), size)
-
     def moving(source, target, source_here, target_here):
         index, index_here = counts["sent"], counts["local"]
         counts["sent"] += 1
@@ -978,206 +1039,203 @@
 
         return wait
 
-    def add(target, left, right, columns_of=slice(None)):
+    def lanes(block, size):
+        return pl.ds(pl.multiple_of(block * size, size), size)
+
+    def add(target, *terms):
         def step(index, carry):
             rows = pl.ds(pl.multiple_of(index * 64, 64), 64)
-            value = left[rows, columns_of].astype(jnp.float32) + right[rows, :].astype(jnp.float32)
+            value = sum(term[rows, :].astype(jnp.float32) for term in terms)
             target[rows, :] = value.astype(target.dtype)
             return carry
 
         lax.fori_loop(0, target.shape[0] // 64, step, 0)
 
-    def narrow(target, source, columns_of=slice(None)):
-        def step(index, carry):
-            rows = pl.ds(pl.multiple_of(index * 64, 64), 64)
-            target[rows, :] = source[rows, columns_of].astype(target.dtype)
-            return carry
-
-        lax.fori_loop(0, target.shape[0] // 64, step, 0)
-
     barrier = pltpu.get_barrier_semaphore()
-    for axis in links:
+    for axis in LINKS:
         pl.semaphore_signal(barrier, inc=1, device_id={axis: 1 - lax.axis_index(axis)}, device_id_type=MESH)
-    if attention:
-
-        @pl.when(crossing)
-        def _():
-            pl.semaphore_signal(barrier, inc=1, device_id={"core": zhi, "zhi": core}, device_id_type=MESH)
-
-        pl.semaphore_wait(barrier, len(links) + crossing.astype(jnp.int32))
-    else:
-        pl.semaphore_wait(barrier, len(links))
+
+    @pl.when(crossing)
+    def _():
+        pl.semaphore_signal(barrier, inc=1, device_id={"core": zhi, "zhi": core}, device_id_type=MESH)
+
+    pl.semaphore_wait(barrier, len(LINKS) + crossing.astype(jnp.int32))
+
+    last = []
+    half = self_q.shape[3] // 2
+
+    def to_cores(values, out):
+        part, width = values.shape[0] // 2, values.shape[1]
+        there, here = lanes(1 - core, part), lanes(core, part)
+        last.append(push(values.at[there], out.at[:, lanes(core, width)], "core"))
+        last.append(keep(values.at[here], out.at[:, lanes(core, width)]))
+
+    def planes_to_cores(values, qkv_out, out_out):
+        part = values.shape[0] // 2
+        there, here = lanes(1 - core, part), lanes(core, part)
+        for plane in range(4):
+            columns_of = pl.ds(plane * half, half)
+            out = qkv_out.at[plane, :, lanes(core, half)] if plane < 3 else out_out.at[:, lanes(core, half)]
+            last.append(push(values.at[there, columns_of], out, "core"))
+            last.append(keep(values.at[here, columns_of], out))
+
+    cross_zhi, cross_keep = [], []
+    for plane in range(4):
+        columns_of = pl.ds(plane * 2 * half, 2 * half)
+        there = pl.ds(pl.multiple_of((2 * plane + 1 - zhi) * 2 * half, 2 * half), 2 * half)
+        here = pl.ds(pl.multiple_of((2 * plane + zhi) * 2 * half, 2 * half), 2 * half)
+        cross_zhi.append(push(cross.at[:, there], cross_got.at[:, columns_of], "zhi"))
+        cross_keep.append(keep(cross.at[:, here], cross_own.at[:, columns_of]))
+
+    first, second = pl.ds(0, half), pl.ds(half, half)
+    parts = (self_q, self_k, self_v, self_o)
+    self_x, self_y, own_a, own_b = [], [], [], []
+    for plane, partial in enumerate(parts):
+        columns_of = pl.ds(plane * half, half)
+        self_x.append(push(partial.at[:, 1 - x, :, first], self_got.at[0, :, :, columns_of], "x"))
+        self_y.append(push(partial.at[1 - y, :, :, second], self_got.at[1, :, :, columns_of], "y"))
+        own_a.append(keep(partial.at[:, x, :, first], self_own.at[0, :, :, columns_of]))
+        own_b.append(keep(partial.at[y, :, :, second], self_own.at[1, :, :, columns_of]))
+    enc_core = push(enc_part.at[1 - core], enc_got, "core")
+    enc_keep = keep(enc_part.at[core], enc_own)
+
+    to_cores(ff_in, ff_in_out)
+    to_cores(ff_out, ff_out_out)
 
     small_first, small_size = 0, 32
 
     def small_send(stage):
-        half, got = small_size // 2, small_got[stage]
-        away = small_first + (1 - lax.axis_index(AXES[stage])) * half
-        return push(small_sum.at[pl.ds(away, half)], got, AXES[stage])
+        rows = small_size // 2
+        away = small_first + (1 - lax.axis_index(AXES[stage])) * rows
+        return push(small_sum.at[pl.ds(away, rows)], small_got[stage], AXES[stage])
 
     def small_add(stage, copy):
         copy.wait()
-        half, got = small_size // 2, small_got[stage]
-        mine = small_first + lax.axis_index(AXES[stage]) * half
+        rows, got = small_size // 2, small_got[stage]
+        mine = small_first + lax.axis_index(AXES[stage]) * rows
 
         def step(index, carry):
             small_sum[mine + index] += got[index]
             return carry
 
-        lax.fori_loop(0, half, step, 0)
-        return mine, half
-
-    last = []
-
-    def to_cores(values, out):
-        part, width = values.shape[0] // 2, values.shape[1]
-        there = pl.ds(pl.multiple_of((1 - core) * part, part), part)
-        here = pl.ds(pl.multiple_of(core * part, part), part)
-        last.append(push(values.at[there], out.at[:, lanes(core, width)], "core"))
-        last.append(keep(values.at[here], out.at[:, lanes(core, width)]))
-
-    if spread:
-        rows = rows_in[0].shape[0]
-        out = rows_out[0]
-        spread_zlo = push(rows_in[0], out.at[pl.ds(2 * rows, rows)], "zlo")
-        last.append(push(rows_in[0], out.at[pl.ds(rows, rows)], "core"))
-        last.append(keep(rows_in[0], out.at[pl.ds(0, rows)]))
-    steps = []
-    for partial, (mine, theirs, _) in zip(hidden_in, hidden_kept):
-        width = mine.shape[1]
-        steps.append(
-            (push(partial.at[:, lanes(1 - zhi, width)], theirs, "zhi"), keep(partial.at[:, lanes(zhi, width)], mine))
-        )
-    if small:
-        keep(small_in[0], small_sum).wait()
-        for stage in range(len(AXES)):
-            small_first, small_size = small_add(stage, small_send(stage))
-        keep(small_sum.at[small_first], small_out[0]).wait()
-    if attention:
-        cross_part, self_part, enc_part = attention_in
-        width = kept.shape[1]
-        cross_zhi = push(cross_part.at[:, lanes(1 - zhi, width)], got, "zhi")
-        cross_own = keep(cross_part.at[:, lanes(zhi, width)], kept)
-        half = self_got.shape[3]
-        first, second = pl.ds(0, half), pl.ds(half, half)
-        enc_core = push(enc_part.at[1 - core], enc_got, "core")
-        enc_keep = keep(enc_part.at[core], enc_own)
-        self_x = push(self_part.at[:, 1 - x, :, first], self_got.at[0], "x")
-        self_y = push(self_part.at[1 - y, :, :, second], self_got.at[1], "y")
-        own_a = keep(self_part.at[:, x, :, first], self_own.at[0])
-        own_b = keep(self_part.at[y, :, :, second], self_own.at[1])
-        enc_core.wait()
-        enc_keep.wait()
-        add(enc_sum, enc_own.at[1 - zlo], enc_got.at[1 - zlo])
-        enc_zlo = push(enc_sum, enc_far, "zlo")
-        own_a.wait()
-        self_x.wait()
-        add(self_low, self_own.at[0, 1 - y], self_got.at[0, 1 - y])
-        a_second = push(self_low, self_got_low.at[0], "y")
-        own_b.wait()
-        self_y.wait()
-        add(self_send, self_own.at[1, 1 - x], self_got.at[1, 1 - x])
-        b_second = push(self_send, self_got_low.at[1], "x")
-        add(self_total.at[0], self_own.at[0, y], self_got.at[0, y])
-        add(self_total.at[1], self_own.at[1, x], self_got.at[1, x])
-        a_second.wait()
-        add(self_total.at[0], self_total.at[0], self_got_low.at[0])
-        b_second.wait()
-        add(self_total.at[1], self_total.at[1], self_got_low.at[1])
-        enc_zlo.wait()
-
-        def enc_step(index, carry):
+        lax.fori_loop(0, rows, step, 0)
+        return mine, rows
+
+    keep(small, small_sum).wait()
+    small_copy = small_send(0)
+    enc_core.wait()
+    enc_keep.wait()
+    add(enc_sum, enc_own.at[1 - zlo], enc_got.at[1 - zlo])
+    enc_zlo = push(enc_sum, enc_far, "zlo")
+    small_first, small_size = small_add(0, small_copy)
+    small_copy = small_send(1)
+    for copy in own_a + self_x:
+        copy.wait()
+    add(low_a, self_own.at[0, 1 - y], self_got.at[0, 1 - y])
+    a_second = push(low_a, self_got_low.at[0], "y")
+    for copy in own_b + self_y:
+        copy.wait()
+    add(low_b, self_own.at[1, 1 - x], self_got.at[1, 1 - x])
+    b_second = push(low_b, self_got_low.at[1], "x")
+    small_first, small_size = small_add(1, small_copy)
+    small_copy = small_send(2)
+    add(self_total.at[0], self_own.at[0, y], self_got.at[0, y])
+    add(self_total.at[1], self_own.at[1, x], self_got.at[1, x])
+    enc_zlo.wait()
+    add(enc_low, enc_own.at[zlo], enc_got.at[zlo], enc_far)
+    small_first, small_size = small_add(2, small_copy)
+    small_copy = small_send(3)
+    a_second.wait()
+    add(self_total.at[0], self_total.at[0], self_got_low.at[0])
+    b_second.wait()
+    add(self_total.at[1], self_total.at[1], self_got_low.at[1])
+    add(low_a, self_total.at[1 - zhi])
+    self_zhi = push(low_a, self_last, "zhi")
+    for copy in cross_zhi + cross_keep:
+        copy.wait()
+
+    def cross_step(target, which, *others):
+        def step(index, carry):
             rows = pl.ds(pl.multiple_of(index * 64, 64), 64)
-            value = enc_own[zlo, rows, :].astype(jnp.float32) + enc_got[zlo, rows, :].astype(jnp.float32)
-            enc_low[rows, :] = (value + enc_far[rows, :].astype(jnp.float32)).astype(enc_low.dtype)
+            for plane in range(4):
+                source = pl.ds(pl.multiple_of((2 * plane + which) * half, half), half)
+                columns_of = pl.ds(plane * half, half)
+                value = cross_own[rows, source].astype(jnp.float32) + cross_got[rows, source].astype(jnp.float32)
+                for other in others:
+                    value += other[rows, columns_of].astype(jnp.float32)
+                target[rows, columns_of] = value.astype(target.dtype)
             return carry
 
-        lax.fori_loop(0, enc_low.shape[0] // 64, enc_step, 0)
-        wait_enc = moving(enc_low, attention_out[2], enc_low, attention_out[2])
-        narrow(self_low, self_total.at[1 - zhi])
-        self_zhi = push(self_low, self_last, "zhi")
-        cross_own.wait()
-        cross_zhi.wait()
-        add(total, kept, got)
-        narrow(low_part, total, lanes(1 - zlo, low_part.shape[1]))
-        cross_zlo = push(low_part, got_low, "zlo")
-        self_zhi.wait()
-        add(self_total.at[zhi], self_total.at[zhi], self_last)
-        to_cores(self_total.at[zhi], attention_out[1])
-        cross_zlo.wait()
-        add(total_low, total, got_low, lanes(zlo, low_part.shape[1]))
-        to_cores(total_low, attention_out[0])
-    if spread:
-        spread_zlo.wait()
-        last.append(push(rows_out[0].at[pl.ds(2 * rows, rows)], rows_out[0].at[pl.ds(3 * rows, rows)], "core"))
-    for copies, (mine, theirs, summed), out in zip(steps, hidden_kept, hidden_out):
-        for copy in copies:
-            copy.wait()
-        add(summed, mine, theirs)
-        to_cores(summed, out)
-    if attention:
-        wait_enc()
+        lax.fori_loop(0, target.shape[0] // 64, step, 0)
+
+    cross_step(cross_low, 1 - zlo)
+    cross_zlo = push(cross_low, cross_got_low, "zlo")
+    wait_enc = moving(enc_low, enc_out, enc_low, enc_out)
+    cross_zlo.wait()
+    cross_step(cross_total, zlo, cross_got_low)
+    planes_to_cores(cross_total, cross_qkv_out, cross_out_out)
+    small_first, small_size = small_add(3, small_copy)
+    small_copy = small_send(4)
+    self_zhi.wait()
+    add(self_total.at[zhi], self_total.at[zhi], self_last)
+    planes_to_cores(self_total.at[zhi], self_qkv_out, self_out_out)
+    small_first, small_size = small_add(4, small_copy)
+    keep(small_sum.at[small_first], small_out).wait()
+    wait_enc()
     for copy in last:
         copy.wait()
 
 
-def finish(rows, hidden, attention, small, collective_id):
-    operands, shapes, scratch = [], [], []
-    if rows is not None:
-        operands.append(rows)
-        shapes.append(jax.ShapeDtypeStruct((4 * rows.shape[0], rows.shape[1]), rows.dtype))
-    for partial in hidden:
-        count, width = partial.shape
-        operands.append(partial)
-        shapes.append(jax.ShapeDtypeStruct((count // 2, width), jnp.float32))
-        scratch += [pltpu.VMEM((count, width // 2), partial.dtype)] * 2
-        scratch.append(pltpu.VMEM((count, width // 2), jnp.float32))
-    if attention is not None:
-        cross, own, enc = attention
-        enc_shape = enc.shape[2:]
-        count, width = cross.shape
-        part, half = own.shape[2], own.shape[3] // 2
-        operands += [cross, own, enc]
-        shapes.append(jax.ShapeDtypeStruct((count // 2, width // 2), jnp.float32))
-        shapes.append(jax.ShapeDtypeStruct((part // 2, 2 * half), jnp.float32))
-        shapes.append(jax.ShapeDtypeStruct(enc_shape, enc.dtype))
-        scratch += [
-            pltpu.VMEM((2, *enc_shape), enc.dtype),
-            pltpu.VMEM((2, *enc_shape), enc.dtype),
-            pltpu.VMEM(enc_shape, enc.dtype),
-            pltpu.VMEM(enc_shape, enc.dtype),
-            pltpu.VMEM(enc_shape, enc.dtype),
-            pltpu.VMEM((count, width // 2), cross.dtype),
-            pltpu.VMEM((count, width // 2), cross.dtype),
-            pltpu.VMEM((count, width // 2), jnp.float32),
-            pltpu.VMEM((count, width // 4), cross.dtype),
-            pltpu.VMEM((count, width // 4), cross.dtype),
-            pltpu.VMEM((count, width // 4), jnp.float32),
-            pltpu.VMEM((2, 2, part, half), own.dtype),
-            pltpu.VMEM((2, 2, part, half), own.dtype),
-            pltpu.VMEM((part, half), own.dtype),
-            pltpu.VMEM((2, part, half), own.dtype),
-            pltpu.VMEM((2, part, half), jnp.float32),
-            pltpu.VMEM((part, half), own.dtype),
-            pltpu.VMEM((part, half), own.dtype),
-        ]
-    if small is not None:
-        operands.append(small)
-        shapes.append(jax.ShapeDtypeStruct(small.shape[1:], small.dtype))
-        scratch.append(pltpu.VMEM(small.shape, small.dtype))
-        scratch += [pltpu.VMEM((32 >> stage, *small.shape[1:]), small.dtype) for stage in range(1, 6)]
+def finish(ff_in, ff_out, cross, self_parts, enc, small):
+    rows, width = ff_in.shape
+    part, half = self_parts[0].shape[2], self_parts[0].shape[3] // 2
+    low_type, enc_shape = enc.dtype, enc.shape[2:]
+    wide = 4 * half
+
+    def full(*shape):
+        return jax.ShapeDtypeStruct(shape, jnp.float32)
+
+    shapes = [
+        full(rows // 2, 2 * width),
+        full(rows // 2, 2 * width),
+        full(3, part // 2, 2 * half),
+        full(part // 2, 2 * half),
+        full(3, part // 2, 2 * half),
+        full(part // 2, 2 * half),
+        jax.ShapeDtypeStruct(enc_shape, low_type),
+        jax.ShapeDtypeStruct(small.shape[1:], small.dtype),
+    ]
     anywhere = pl.BlockSpec(memory_space=pl.ANY)
     return pl.pallas_call(
-        functools.partial(
-            finish_kernel, rows is not None, len(hidden), attention is not None, int(small is not None)
-        ),
+        finish_kernel,
         out_shape=shapes,
-        in_specs=[anywhere] * len(operands),
+        in_specs=[anywhere] * 9,
         out_specs=[anywhere] * len(shapes),
-        scratch_shapes=scratch + [pltpu.SemaphoreType.DMA((16,))] * 3,
-        compiler_params=pltpu.CompilerParams(collective_id=collective_id, has_side_effects=True),
-        cost_estimate=pl.CostEstimate(flops=20_000_000_000, bytes_accessed=0, transcendentals=0),
-    )(*operands)
+        scratch_shapes=[
+            pltpu.VMEM((part, 2 * wide), low_type),
+            pltpu.VMEM((part, 2 * wide), low_type),
+            pltpu.VMEM((part, wide), low_type),
+            pltpu.VMEM((part, wide), low_type),
+            pltpu.VMEM((part, wide), jnp.float32),
+            pltpu.VMEM((2, *enc_shape), low_type),
+            pltpu.VMEM((2, *enc_shape), low_type),
+            pltpu.VMEM(enc_shape, low_type),
+            pltpu.VMEM(enc_shape, low_type),
+            pltpu.VMEM(enc_shape, low_type),
+            pltpu.VMEM((2, 2, part, wide), low_type),
+            pltpu.VMEM((2, 2, part, wide), low_type),
+            pltpu.VMEM((part, wide), low_type),
+            pltpu.VMEM((part, wide), low_type),
+            pltpu.VMEM((2, part, wide), low_type),
+            pltpu.VMEM((2, part, wide), jnp.float32),
+            pltpu.VMEM((part, wide), low_type),
+            pltpu.VMEM(small.shape, small.dtype),
+        ]
+        + [pltpu.VMEM((32 >> stage, *small.shape[1:]), small.dtype) for stage in range(1, 6)]
+        + [pltpu.SemaphoreType.DMA((40,))] * 3,
+        compiler_params=pltpu.CompilerParams(collective_id=1, has_side_effects=True),
+        cost_estimate=pl.CostEstimate(flops=40_000_000_000, bytes_accessed=0, transcendentals=0),
+    )(ff_in, ff_out, cross, *self_parts, enc, small)
 
 
 def trade(rows, axis, name="trade"):
@@ -1191,7 +1249,8 @@
 
 def regroup(rows, name="regroup"):
     with jax.named_scope("re_" + name):
-        return lax.ppermute(rows, ("core", "zhi"), [(0, 0), (1, 2), (2, 1), (3, 3)])
+        moved = lax.ppermute(rows, ("core", "zhi"), [(1, 2), (2, 1)])
+        return jnp.where(lax.axis_index("core") == lax.axis_index("zhi"), rows, moved)
 
 
 def in_order(index, own, other, axis):
@@ -1351,37 +1410,34 @@
     mlp_in = low(normed_out)
     beyond = trade(mlp_in, "zlo", "mlp_z")
     mlp_near = jnp.concatenate([mlp_in, trade(mlp_in, "core", "mlp_c")], axis=0)
-    pre_near = product(mlp_near, w_in) + hidden_bias
-    act_near = low(gelu_value(pre_near))
+    act_near, dpre_near, sum_near = hidden_units(mlp_near, cot_near, w_in, w_out, hidden_bias[None])
     beyond = after(beyond, act_near)
     mlp_far = jnp.concatenate([beyond, trade(beyond, "core", "mlp_zc")], axis=0)
-    pre_far = product(mlp_far, w_in) + hidden_bias
-    act_far = low(gelu_value(pre_far))
     cot_far = jnp.concatenate([cot_beyond, trade(cot_beyond, "core", "cot_zc")], axis=0)
+    act_far, dpre_far, sum_far = hidden_units(mlp_far, cot_far, w_in, w_out, hidden_bias[None])
+    gradient = grad_rows.astype(jnp.float32)
+    bias_out_three = jnp.sum(gradient, axis=0)
+    dmlp_far = low(
+        product_right_t(dpre_far[:own_rows], w_in)
+        + trade(low(product_right_t(dpre_far[own_rows:], w_in)), "core", "dmlp_zc")
+    )
+    mlp_term = product_right_t(dpre_near[:own_rows], w_in) + trade(
+        low(product_right_t(dpre_near[own_rows:], w_in)), "core", "dmlp_c"
+    )
+    act_near, act_far = after(act_near, dmlp_far, mlp_term), after(act_far, dmlp_far, mlp_term)
     out_parts = [
         low(product_right_t(act_far[own_rows:], w_out)),
         product_right_t(act_far[:own_rows], w_out),
         low(product_right_t(act_near[own_rows:], w_out)),
         product_right_t(act_near[:own_rows], w_out),
     ]
-    out_far = trade(low(out_parts[1] + trade(out_parts[0], "core", "out_zc")), "zlo", "out_z")
+    out_far = low(out_parts[1] + trade(out_parts[0], "core", "out_zc"))
     out_branch = out_parts[3] + trade(out_parts[2], "core", "out_c")
-    dpre_near = low(product(after(cot_near, act_far, out_branch), w_out) * gelu_slope(pre_near))
-    dpre_far = low(product(after(cot_far, dpre_near), w_out) * gelu_slope(pre_far))
-    gradient = grad_rows.astype(jnp.float32)
-    bias_out_three = jnp.sum(gradient, axis=0)
-    dmlp_far = low(
-        product_right_t(dpre_far[:own_rows], w_in)
-        + trade(low(product_right_t(dpre_far[own_rows:], w_in)), "core", "dmlp_zc")
-    )
-    mlp_term = product_right_t(dpre_near[:own_rows], w_in) + trade(
-        low(product_right_t(dpre_near[own_rows:], w_in)), "core", "dmlp_c"
-    )
-    act_near, act_far = after(act_near, dmlp_far, mlp_term), after(act_far, dmlp_far, mlp_term)
     grad_w_out = low(product_left_t(cot_near, act_near) + product_left_t(cot_far, act_far))
     mlp_near, mlp_far = after(mlp_near, grad_w_out), after(mlp_far, grad_w_out)
     grad_w_in = low(product_left_t(mlp_near, dpre_near) + product_left_t(mlp_far, dpre_far))
-    mlp_term = mlp_term + after(trade(dmlp_far, "zlo", "dmlp_z"), grad_w_in)
+    mlp_term = mlp_term + after(trade(dmlp_far, "zlo", "dmlp_z"), grad_w_in, grad_w_out)
+    out_far = trade(after(out_far, mlp_term), "zlo", "out_z")
     part, gain_three, shift_three = norm_backward(mlp_term, hat_three, inv_three, vectors[2])
     gradient = gradient + part
 
@@ -1403,11 +1459,7 @@
         cross_pairs,
         ENC,
     )
-    out_sum = sum_over_chips(grad_w_out)
-    out_sum = half_of(out_sum, zhi, 1).astype(jnp.float32) + trade(half_of(out_sum, 1 - zhi, 1), "zhi", "go_zhi").astype(
-        jnp.float32
-    )
-    cross_dq = after(cross_dq, out_sum)
+    cross_dq = after(cross_dq, out_far)
     layer_out = regroup(low(after_two + (out_branch + after(out_far, cross_dq) + vectors[8])), "out")
     other = trade(low(product_right_t(cross_dq[own_rows:], w_cq)), "core", "dcin")
     part, gain_two, shift_two = norm_backward(
@@ -1417,23 +1469,31 @@
 
     grad_low = low(gradient)
     bias_out_one = jnp.sum(grad_low.astype(jnp.float32), axis=0)
+    def zhi_sum(partial, axis, name):
+        mine, theirs = half_of(partial, zhi, axis), half_of(partial, 1 - zhi, axis)
+        return mine.astype(jnp.float32) + trade(theirs, "zhi", name).astype(jnp.float32)
+
+    beyond = trade(grad_low, "zlo", "e1_z")
+    grad_near = jnp.concatenate([grad_low, trade(grad_low, "core", "e1_c")], axis=0)
+    mixed_grad = low(product(grad_near, w_so))
     cross_parts = [
         low(product_left_t(cross_rows, after(cross_dq, grad_low))),
-        low(product_left_t(enc_full, cross_dk)),
-        low(product_left_t(enc_full, cross_dv)),
-        low(product_left_t(grad_both, cross_mixed)),
+        low(product_left_t(enc_full, after(cross_dk, grad_low))),
+        low(product_left_t(enc_full, after(cross_dv, grad_low))),
+        low(product_left_t(after(grad_both, grad_low), cross_mixed)),
     ]
-    grad_cross = jnp.concatenate(
-        [part[:, lo : lo + width // 2] for lo in range(0, cross_width, width // 2) for part in cross_parts], axis=1
-    )
-    e1_rows, ff_in_grad = finish(after(grad_low, grad_cross), [sum_over_chips(grad_w_in)], None, None, 1)
-    lacking = trade(half_of(after(out_sum, e1_rows), 1 - core, 0), "core", "go_core")
-    ff_out_grad = in_order(core, half_of(out_sum, core, 0), lacking, 1)
+    grad_cross = jnp.concatenate(cross_parts, axis=1)
+    beyond = after(beyond, mixed_grad, grad_cross, layer_out)
     cross_sum = sum_over_chips(grad_cross)
-    mixed_grad = low(product(e1_rows, w_so))
+    grad_far = jnp.concatenate([beyond, trade(beyond, "core", "e1_zc")], axis=0)
+    mixed_grad = jnp.concatenate([mixed_grad, low(product(grad_far, w_so))], axis=0)
+
+    out_sum = zhi_sum(sum_over_chips(grad_w_out), 1, "go_zhi")
+    in_sum = zhi_sum(sum_over_chips(grad_w_in), 1, "gi_zhi")
     dq, dk, dv = attend_back(
         self_plan, self_meta, qkv, 0, qkv, pairs, 2 * pairs, mixed, mixed_grad, self_lse, pairs, 1152
     )
+    dq, dk, dv = after(dq, in_sum, out_sum), after(dk, in_sum, out_sum), after(dv, in_sum, out_sum)
     dqkv = jnp.concatenate([dq, dk, dv], axis=1)
     d_near, d_far = dqkv[: count // 2], dqkv[count // 2 :]
     dx_far = low(
@@ -1448,34 +1508,13 @@
         low(product_left_t(attn_rows, dq)),
         low(product_left_t(attn_rows, dk)),
         low(product_left_t(attn_rows, dv)),
-        low(product_left_t(e1_rows, mixed)),
+        low(product_left_t(grad_near, near) + product_left_t(grad_far, far)),
     ]
-    grad_self = jnp.concatenate(
-        [part[:, lo : lo + width // 2] for lo in range(0, width, width // 2) for part in self_parts], axis=1
-    )
-
     enc_part = low(
         product_right_t(after(cross_dk, dq), w_ckv[:, :cross_width])
         + product_right_t(after(cross_dv, dq), w_ckv[:, cross_width:])
     )
-    cross_grad, self_grad, enc_grad = finish(
-        None,
-        [],
-        (
-            after(cross_sum, dx),
-            grad_self.reshape(2, 2, rows_of, -1),
-            enc_part.reshape(2, 2, -1, model),
-        ),
-        None,
-        2,
-    )
-    enc_grad = enc_grad.astype(jnp.float32)
-    dx = dx + after(trade(dx_far, "zlo", "dx_z"), cross_grad)
-
-    def planes(shard):
-        return shard.reshape(shard.shape[0], 2, 4, -1).transpose(2, 0, 1, 3).reshape(4, shard.shape[0], -1)
-
-    cross_grad, self_grad = planes(cross_grad), planes(self_grad)
+    dx = dx + after(trade(dx_far, "zlo", "dx_z"), enc_part, *self_parts)
     part, gain_one, shift_one = norm_backward(dx, hat_one, inv_one, vectors[0])
     input_part = low(gradient + part)
     input_grad = regroup(input_part, "dgrad").astype(jnp.float32)
@@ -1484,9 +1523,7 @@
     bias_self_value = jnp.sum(dv.astype(jnp.float32), axis=0)
     bias_cross_query = jnp.sum(cross_dq.astype(jnp.float32), axis=0)
     bias_cross_value = jnp.sum(cross_dv.astype(jnp.float32), axis=0)
-    grad_hidden_bias = jnp.sum(dpre_near.astype(jnp.float32), axis=0) + jnp.sum(
-        dpre_far.astype(jnp.float32), axis=0
-    )
+    grad_hidden_bias = (sum_near + sum_far)[0]
     vec_sums = jnp.stack(
         [
             gain_one,
@@ -1517,17 +1554,24 @@
         axis=2,
     )
     sums = jnp.pad(after(sums, input_part).reshape(32, -1, 128), ((0, 0), (0, 4), (0, 0)))
-    (sums,) = finish(None, [], None, sums, 3)
+    ff_in_grad, ff_out_grad, cross_qkv_grad, cross_out_grad, self_qkv_grad, self_out_grad, enc_grad, sums = finish(
+        in_sum,
+        out_sum,
+        cross_sum,
+        [part.reshape(2, 2, rows_of, -1) for part in self_parts],
+        enc_part.reshape(2, 2, -1, model),
+        sums,
+    )
     sums = sums.reshape(-1)[: sum(sizes)]
     vec_grad, head_grad, ff_bias_grad = jnp.split(sums, [sizes[0], sizes[0] + sizes[1]])
     return (
         layer_out,
         input_grad,
-        enc_grad,
-        self_grad[:3],
-        self_grad[3].T,
-        cross_grad[:3],
-        cross_grad[3].T,
+        enc_grad.astype(jnp.float32),
+        self_qkv_grad,
+        self_out_grad.T,
+        cross_qkv_grad,
+        cross_out_grad.T,
         ff_in_grad,
         ff_out_grad.T,
         head_grad.reshape(head_bias.shape),

time: 724 us -> 669 us (0.924)
  matrix products: 173 us -> 127 us
  Pallas kernels: 325 us -> 306 us
  other arithmetic: 36.3 us -> 53.8 us
  local copies, waits for them, and re-layouts: 64.8 us -> 53.7 us
    dot_general x9 -> x6, matrix products: 69.5 us -> 16.9 us  [product(): return jnp.dot(left, right, preferred_element_type=jnp.float32)]
    pallas_call x3, Pallas kernels: 124 us -> 106 us  [the longest x1 72.2 us: finish(): pl.pallas_call(finish_kernel, out_shape=shapes, in_specs=[anywhere] * 9,...]
    concatenate x0 -> x4, other arithmetic: none -> 8.37 us  [the longest x1 2.75 us: fast_layer(): jnp.concatenate([grad_rows, trade(grad_rows, 'core', 'cot_c')], axis=0)]
    ppermute x25 -> x28, waiting for transfers between devices: 79.1 us -> 85.1 us  [trade(): return lax.ppermute(rows, axis, [(0, 1), (1, 0)])]
    unnamed x235 -> x174, local copies, waits for them, and re-layouts: 34.5 us -> 28.9 us
    dot_general x12 -> x13, matrix products: 43.1 us -> 43.8 us  [product_left_t(): lax.dot_general(left, right, (((0,), (0,)), ((), ())), preferred_element_...]
    ppermute x25 -> x28, starting transfers between devices: 14.7 us -> 15.1 us  [trade(): return lax.ppermute(rows, axis, [(0, 1), (1, 0)])]
  transfers between devices with their start and end apart: 34 -> 37, of which waited for: 6 -> 11; matrix products, arithmetic and copies ran while one was open for 29% -> 30% of each run, Pallas kernels for 45% -> 46%
where the time goes in v3:
time: 669 us; the launch traced here: 661 us
  Pallas kernels  306 us (46%)
  matrix products  127 us (19%)
  waiting for transfers between devices  85.2 us (13%)
  other arithmetic  53.8 us (8%)
  local copies, waits for them, and re-layouts  53.7 us (8%)
  starting transfers between devices  19.4 us (3%)
  between operations  15.9 us (2%)
    pallas_call x1, Pallas kernels, start_exchange(): pl.pallas_call(start_kernel, out_shape=shapes, in_specs=[anywhere] * 7, o...  106 us
    ppermute x28, waiting for transfers between devices, trade(): return lax.ppermute(rows, axis, [(0, 1), (1, 0)])  85.1 us
    pallas_call x1, Pallas kernels, finish(): pl.pallas_call(finish_kernel, out_shape=shapes, in_specs=[anywhere] * 9,...  72.2 us
    dot_general x22, matrix products, product_right_t(): lax.dot_general(left, right, (((1,), (1,)), ((), ())), preferred_element_...  65.9 us
    pallas_call x2, Pallas kernels, attend_back(): pl.pallas_call(functools.partial(backward_kernel, sections), grid_spec=pl...  56.3 us
    dot_general x13, matrix products, product_left_t(): lax.dot_general(left, right, (((0,), (0,)), ((), ())), preferred_element_...  43.8 us
    pallas_call x2, Pallas kernels, attend(): pl.pallas_call(functools.partial(forward_kernel, sections), grid_spec=plt...  38.2 us
    pallas_call x2, Pallas kernels, hidden_units(): pl.pallas_call(hidden_kernel, grid=(width // tile,), in_specs=[whole, who...  33.7 us
  transfers between devices with their start and end apart: 37, of which 11 were waited for; matrix products, arithmetic and copies ran while one was open for 30% of the time, Pallas kernels for 46%

profile of v3, /device:TPU:0, one launch (start us, length us, event | category | flops | bytes accessed | tf_op | source)
XLA Modules:
  0.0 660.7 jit_solution(17351393955209221360)
XLA Ops:
  17.1 105.8 %shard_map.229 = (bf16[512,1024]{1,0:T(8,128)(2,1)}, bf16[2048,1024]{1,0:T(8,128)(2,1)}, bf16[4,2,2,256,256]{4,3,2,1,0:T(8,128)(2,1)}, bf16[4,2,2,256,512]{4,3,2...) custom-call(bf16[512,1024]{1,0:T(8,128)(2,1)} %tokens.1, ...), custom_call_target="tpu_custom_call" | custom-call | tf_op jit(solution)/shard_map/pallas_call | solution.py:917
  134.8 4.8 multiply_convert_fusion.q_ref.k_ref.v_ref
  140.6 23.1 %shard_map.230 = (bf16[2048,256]{1,0:T(8,128)(2,1)}, f32[2048,256]{1,0:T(8,128)}) custom-call(s32[13]{0:T(128)} %concatenate.81.meta_ref, bf16[2048,768]{1,0:T(8,128)(2,1)} %multiply_convert_fusion.q_ref.k_ref.v_ref, bf16[2048,768]{1,0:T(8,128)(2,1)} %multiply_convert_fusion.q_ref.k_ref.v_ref, bf16[2048,768]{1,0:T(8,128)(2,1)} %multiply_convert_fusion.q_ref.k_ref.v_ref), custom_call_target="tpu_custom_call" | custom-call | flops 19327352832 | bytes 5242880 | tf_op jit(solution)/shard_map/pallas_call | solution.py:180
  163.7 10.6 %collective-permute-done.1 = bf16[256,1024]{1,0:T(8,128)(2,1)} collective-permute-done((bf16[256,1024]{1,0:T(8,128)(2,1)S(1)}, bf16[256,1024]{1,0:T(8,128)(2,1)}, u32[]{:S(2)}, u32[]{:S(2)}) %collective-permute-start.1) | collective-permute-done | bytes 524320 | tf_op jit(solution)/shard_map/wo_zhi/ppermute | solution.py:1243
  175.8 4.3 fusion.86
  192.2 18.0 %collective-permute-done.4 = bf16[512,1024]{1,0:T(8,128)(2,1)} collective-permute-done((bf16[512,1024]{1,0:T(8,128)(2,1)}, bf16[512,1024]{1,0:T(8,128)(2,1)}, u32[]{:S(2)}, u32[]{:S(2)}) %collective-permute-start.4) | collective-permute-done | bytes 1048608 | tf_op jit(solution)/shard_map/so_z/ppermute | solution.py:1243
  220.0 15.1 %shard_map.231 = (bf16[1024,512]{1,0:T(8,128)(2,1)}, f32[1024,512]{1,0:T(8,128)}) custom-call(s32[1]{0:T(128)} %slice.219.meta_ref, bf16[1024,512]{1,0:T(8,128)(2,1)} %multiply_convert_fusion.1.q_ref, bf16[512,1024]{1,0:T(8,128)(2,1)} %add_convert_fusion.9.k_ref.v_ref, bf16[512,1024]{1,0:T(8,128)(2,1)} %add_convert_fusion.9.k_ref.v_ref), custom_call_target="tpu_custom_call" | custom-call | flops 8589934592 | bytes 5242880 | tf_op jit(solution)/shard_map/pallas_call | solution.py:180
  235.1 5.3 collective-permute-done.7
  256.7 16.7 %shard_map.232 = (bf16[1024,2048]{1,0:T(8,128)(2,1)}, bf16[1024,2048]{1,0:T(8,128)(2,1)}, f32[1,2048]{1,0:T(1,128)}) custom-call(bf16[1024,1024]{1,0:T(8,128)(2,1)} %pad_maximum_fusion.2.x_ref, bf16[1024,1024]{1,0:T(8,128)(2,1)} %pad_maximum_fusion.3.e_ref, bf16[1024,2048]{1,0:T(8,128)(2,1)} %bitcast.222, ...), custom_call_target="tpu_custom_call" | custom-call | flops 8589934592 | bytes 20971520 | tf_op jit(solution)/shard_map/pallas_call | solution.py:665
  281.0 5.0 fusion.39
  290.0 17.0 %shard_map.233 = (bf16[1024,2048]{1,0:T(8,128)(2,1)}, bf16[1024,2048]{1,0:T(8,128)(2,1)}, f32[1,2048]{1,0:T(1,128)}) custom-call(bf16[1024,1024]{1,0:T(8,128)(2,1)} %constant_dynamic-update-slice_fusion.x_ref, bf16[1024,1024]{1,0:T(8,128)(2,1)} %constant_dynamic-update-slice_fusion.2.e_ref, bf16[1024,2048]{1,0:T(8,128)(2,1)} %bitcast.223, ...), custom_call_target="tpu_custom_call" | custom-call | flops 8589934592 | bytes 20971520 | tf_op jit(solution)/shard_map/pallas_call | solution.py:665
  307.0 5.3 fusion.36
  312.5 5.1 convert_add_fusion.5
  317.5 3.4 add_convert_fusion.6
  320.9 5.9 fusion.84
  326.9 8.2 %add_convert_fusion.1 = bf16[1024,2048]{1,0:T(8,128)(2,1)} fusion(f32[1024,2048]{1,0:T(8,128)S(1)} %fusion.84, bf16[1024,1024]{1,0:T(8,128)(2,1)} %constant_dynamic-update-slice_fusion.2.e_ref, bf16[1024,2048]{1,0:T(8,128)(2,1)S(1)} %copy-done.71), kind=kOutput, calls=%fused_computation.1 | convolution fusion | flops 4299161600 | bytes 18874368 | tf_op jit(solution)/shard_map/dot_general | solution.py:272
  336.4 6.3 fusion.45
  343.1 4.7 fusion.91
  347.8 8.0 %add_convert_fusion = bf16[1024,2048]{1,0:T(8,128)(2,1)} fusion(f32[1024,2048]{1,0:T(8,128)S(1)} %fusion.91, bf16[1024,1024]{1,0:T(8,128)(2,1)} %constant_dynamic-update-slice_fusion.x_ref, bf16[1024,2048]{1,0:T(8,128)(2,1)S(1)} %copy-done.73), kind=kOutput, calls=%fused_computation | convolution fusion | flops 4299161600 | bytes 18874368 | tf_op jit(solution)/shard_map/dot_general | solution.py:272
  355.7 6.4 collective-permute-done.18
  362.1 3.4 multiply_reduce_fusion
  373.6 6.5 add_convert_fusion.5
  380.9 3.9 convolution_convert_fusion.4.do_ref
  384.7 18.7 %shard_map.234 = (bf16[1024,512]{1,0:T(8,128)(2,1)}, bf16[512,512]{1,0:T(8,128)(2,1)}, bf16[512,512]{1,0:T(8,128)(2,1)}) custom-call(s32[1]{0:T(128)} %slice.219.meta_ref, bf16[1024,512]{1,0:T(8,128)(2,1)} %multiply_convert_fusion.1.q_ref, bf16[512,1024]{1,0:T(8,128)(2,1)} %add_convert_fusion.9.k_ref.v_ref, bf16[512,1024]{1,0:T(8,128)(2,1)} %add_convert_fusion.9.k_ref.v_ref, ...), custom_call_target="tpu_custom_call" | custom-call | flops 21474836480 | bytes 10485760 | tf_op jit(solution)/shard_map/pallas_call | solution.py:202
  408.0 5.5 fusion.22
  422.1 3.7 collective-permute-start.23
  437.5 20.7 %collective-permute-done.24 = bf16[512,1024]{1,0:T(8,128)(2,1)} collective-permute-done((bf16[512,1024]{1,0:T(8,128)(2,1)}, bf16[512,1024]{1,0:T(8,128)(2,1)}, u32[]{:S(2)}, u32[]{:S(2)}) %collective-permute-start.24) | collective-permute-done | bytes 1048608 | tf_op jit(solution)/shard_map/e1_z/ppermute | solution.py:1243
  473.9 37.6 %shard_map.235 = (bf16[2048,256]{1,0:T(8,128)(2,1)}, bf16[2048,256]{1,0:T(8,128)(2,1)}, bf16[2048,256]{1,0:T(8,128)(2,1)}) custom-call(s32[13]{0:T(128)} %concatenate.81.meta_ref, bf16[2048,768]{1,0:T(8,128)(2,1)} %multiply_convert_fusion.q_ref.k_ref.v_ref, bf16[2048,768]{1,0:T(8,128)(2,1)} %multiply_convert_fusion.q_ref.k_ref.v_ref, ...), custom_call_target="tpu_custom_call" | custom-call | flops 48318382080 | bytes 10485760 | tf_op jit(solution)/shard_map/pallas_call | solution.py:202
  513.9 3.8 collective-permute-done.26
  542.2 4.8 convolution_convert_fusion.12
  549.3 10.4 %collective-permute-done.30 = bf16[512,1024]{1,0:T(8,128)(2,1)} collective-permute-done((bf16[512,1024]{1,0:T(8,128)(2,1)}, bf16[512,1024]{1,0:T(8,128)(2,1)}, u32[]{:S(2)}, u32[]{:S(2)}) %collective-permute-start.30) | collective-permute-done | bytes 1048608 | tf_op jit(solution)/shard_map/dx_z/ppermute | solution.py:1243
  566.2 72.2 %shard_map.236 = (f32[128,2048]{1,0:T(8,128)}, f32[128,2048]{1,0:T(8,128)}, f32[3,128,256]{2,1,0:T(8,128)}, f32[128,256]{1,0:T(8,128)}, f32[3,128,256]{2,1,0:T(8...) custom-call(f32[256,1024]{1,0:T(8,128)} %convert_add_fusion.7.ff_in, ...), custom_call_target="tpu_custom_call" | custom-call | flops 40000000000 | tf_op jit(solution)/shard_map/pallas_call | solution.py:1209
  (381 shorter events, 174.8 us)
Async XLA Ops:
  7.2 249.5 %all-gather.6.cloned.1.call-start = ((), (), s32[]{:S(2)}) async-start(), calls=%async_computation.7 | async-start | bytes 5242880 | tf_op jit(solution)/shard_map/all_gather | solution.py:1272
  8.6 131.0 %collective-permute-start = (s32[9]{0:T(128)S(1)}, s32[9]{0:T(128)S(1)}, u32[]{:S(2)}, u32[]{:S(2)}) collective-permute-start(s32[9]{0:T(128)S(1)} %pad_add_fusion), channel_id=1, source_target_pairs={{2,4},{4,2},{3,5},{5,3},{10,12},{12,10},{11,13},{13,11},{18,20},{2... | collective-permute-start | bytes 116 | tf_op jit(solution)/shard_map/re_regroup/ppermute | solution.py:1252
  122.9 64.6 %collective-permute-start.5 = (bf16[512,1024]{1,0:T(8,128)(2,1)}, bf16[512,1024]{1,0:T(8,128)(2,1)}, u32[]{:S(2)}, u32[]{:S(2)}) collective-permute-start(bf16[512,1024]{1,0:T(8,128)(2,1)} %param.18), channel_id=1, source_target_pairs={{2,4},{4,2},{3,5},{5,3},{10,12},{12,10},{11,13},{13,11},{18,20},{2... | collective-permute-start | bytes 3145736 | tf_op jit(solution)/shard_map/re_cotangent/ppermute | solution.py:1252
  127.3 129.3 %all-gather.4.cloned.1.call-start = ((), (), s32[]{:S(2)}) async-start(), calls=%async_computation.3 | async-start | bytes 5242880 | tf_op jit(solution)/shard_map/all_gather | solution.py:1272
  127.4 46.9 %collective-permute-start.1 = (bf16[256,1024]{1,0:T(8,128)(2,1)S(1)}, bf16[256,1024]{1,0:T(8,128)(2,1)}, u32[]{:S(2)}, u32[]{:S(2)}) collective-permute-start(bf16[256,1024]{1,0:T(8,128)(2,1)S(1)} %dynamic-slice_bitcast_fusion), channel_id=1, source_target_pairs={{0,2},{2,0},{1,3},{3,1},{4,6},{6,4},{5,7},{7,5},{8,10},{10,8},{9,1... | collective-permute-start | bytes 1572872 | tf_op jit(solution)/shard_map/wo_zhi/ppermute | solution.py:1243
  175.7 7.6 %collective-permute-start.3 = (bf16[512,1024]{1,0:T(8,128)(2,1)S(1)}, bf16[512,1024]{1,0:T(8,128)(2,1)S(1)}, u32[]{:S(2)}, u32[]{:S(2)}) collective-permute-start(bf16[512,1024]{1,0:T(8,128)(2,1)S(1)} %convolution_convert_fusion.5), channel_id=1, source_target_pairs={{0,4},{4,0},{1,5},{5,1},{2,6},{6,2},{3,7},{7,3},{8,12},{12,8},{9,1... | collective-permute-start | bytes 3145736 | tf_op jit(solution)/shard_map/so_zc/ppermute | solution.py:1243
  181.6 28.6 %collective-permute-start.2 = (bf16[512,1024]{1,0:T(8,128)(2,1)}, bf16[512,1024]{1,0:T(8,128)(2,1)}, u32[]{:S(2)}, u32[]{:S(2)}) collective-permute-start(bf16[512,1024]{1,0:T(8,128)(2,1)} %convolution_convert_fusion.6), channel_id=1, source_target_pairs={{0,4},{4,0},{1,5},{5,1},{2,6},{6,2},{3,7},{7,3},{8,12},{12,8},{9,1... | collective-permute-start | bytes 3145736 | tf_op jit(solution)/shard_map/so_c/ppermute | solution.py:1243
  184.8 25.4 %collective-permute-start.4 = (bf16[512,1024]{1,0:T(8,128)(2,1)}, bf16[512,1024]{1,0:T(8,128)(2,1)}, u32[]{:S(2)}, u32[]{:S(2)}) collective-permute-start(bf16[512,1024]{1,0:T(8,128)(2,1)} %add_convert_fusion.10), channel_id=1, source_target_pairs={{0,1},{1,0},{2,3},{3,2},{4,5},{5,4},{6,7},{7,6},{8,9},{9,8},{10,11... | collective-permute-start | bytes 3145736 | tf_op jit(solution)/shard_map/so_z/ppermute | solution.py:1243
  185.9 281.2 %reduce-scatter.6.cloned.1.call-start = ((), (), s32[]{:S(2)}) async-start(), calls=%async_computation.5 | async-start | bytes 5242880 | tf_op jit(solution)/shard_map/reduce_scatter | solution.py:1276
  214.7 25.7 %collective-permute-start.7 = (bf16[512,1024]{1,0:T(8,128)(2,1)S(1)}, bf16[512,1024]{1,0:T(8,128)(2,1)}, u32[]{:S(2)}, u32[]{:S(2)}) collective-permute-start(bf16[512,1024]{1,0:T(8,128)(2,1)S(1)} %get-tuple-element.87), channel_id=1, source_target_pairs={{0,1},{1,0},{2,3},{3,2},{4,5},{5,4},{6,7},{7,6},{8,9},{9,8},{10,11... | collective-permute-start | bytes 3145736 | tf_op jit(solution)/shard_map/cot_z/ppermute | solution.py:1243
  242.3 8.5 %collective-permute-start.10 = (bf16[512,1024]{1,0:T(8,128)(2,1)S(1)}, bf16[512,1024]{1,0:T(8,128)(2,1)}, u32[]{:S(2)}, u32[]{:S(2)}) collective-permute-start(bf16[512,1024]{1,0:T(8,128)(2,1)S(1)} %get-tuple-element.87), channel_id=1, source_target_pairs={{0,4},{4,0},{1,5},{5,1},{2,6},{6,2},{3,7},{7,3},{8,12},{12,8},{9,1... | collective-permute-start | bytes 3145736 | tf_op jit(solution)/shard_map/cot_c/ppermute | solution.py:1243
  250.5 25.8 %collective-permute-start.11 = (bf16[512,1024]{1,0:T(8,128)(2,1)}, bf16[512,1024]{1,0:T(8,128)(2,1)}, u32[]{:S(2)}, u32[]{:S(2)}) collective-permute-start(bf16[512,1024]{1,0:T(8,128)(2,1)} %add_convert_fusion.7), channel_id=1, source_target_pairs={{0,1},{1,0},{2,3},{3,2},{4,5},{5,4},{6,7},{7,6},{8,9},{9,8},{10,11... | collective-permute-start | bytes 3145736 | tf_op jit(solution)/shard_map/mlp_z/ppermute | solution.py:1243
  253.5 25.1 %collective-permute-start.13 = (bf16[512,1024]{1,0:T(8,128)(2,1)}, bf16[512,1024]{1,0:T(8,128)(2,1)}, u32[]{:S(2)}, u32[]{:S(2)}) collective-permute-start(bf16[512,1024]{1,0:T(8,128)(2,1)} %collective-permute-done.7), channel_id=1, source_target_pairs={{0,4},{4,0},{1,5},{5,1},{2,6},{6,2},{3,7},{7,3},{8,12},{12,8},{9,1... | collective-permute-start | bytes 3145736 | tf_op jit(solution)/shard_map/cot_zc/ppermute | solution.py:1243
  276.2 12.7 %collective-permute-start.12 = (bf16[512,1024]{1,0:T(8,128)(2,1)}, bf16[512,1024]{1,0:T(8,128)(2,1)S(1)}, u32[]{:S(2)}, u32[]{:S(2)}) collective-permute-start(bf16[512,1024]{1,0:T(8,128)(2,1)} %collective-permute-done.11), channel_id=1, source_target_pairs={{0,4},{4,0},{1,5},{5,1},{2,6},{6,2},{3,7},{7,3},{8,12},{12,8},{9,1... | collective-permute-start | bytes 3145736 | tf_op jit(solution)/shard_map/mlp_zc/ppermute | solution.py:1243
  286.0 26.4 %collective-permute-start.15 = (bf16[512,1024]{1,0:T(8,128)(2,1)}, bf16[512,1024]{1,0:T(8,128)(2,1)}, u32[]{:S(2)}, u32[]{:S(2)}) collective-permute-start(bf16[512,1024]{1,0:T(8,128)(2,1)} %fusion.39), channel_id=1, source_target_pairs={{0,4},{4,0},{1,5},{5,1},{2,6},{6,2},{3,7},{7,3},{8,12},{12,8},{9,1... | collective-permute-start | bytes 3145736 | tf_op jit(solution)/shard_map/dmlp_c/ppermute | solution.py:1243
  335.1 134.1 %reduce-scatter.4.cloned.1.call-start = ((), (), s32[]{:S(2)}) async-start(), calls=%async_computation.4 | async-start | bytes 5242880 | tf_op jit(solution)/shard_map/reduce_scatter | solution.py:1276
  336.1 26.0 %collective-permute-start.18 = (bf16[512,1024]{1,0:T(8,128)(2,1)}, bf16[512,1024]{1,0:T(8,128)(2,1)}, u32[]{:S(2)}, u32[]{:S(2)}) collective-permute-start(bf16[512,1024]{1,0:T(8,128)(2,1)} %add_convert_fusion.6), channel_id=1, source_target_pairs={{0,1},{1,0},{2,3},{3,2},{4,5},{5,4},{6,7},{7,6},{8,9},{9,8},{10,11... | collective-permute-start | bytes 3145736 | tf_op jit(solution)/shard_map/dmlp_z/ppermute | solution.py:1243
  342.8 30.9 %collective-permute-start.17 = (bf16[512,1024]{1,0:T(8,128)(2,1)}, bf16[512,1024]{1,0:T(8,128)(2,1)}, u32[]{:S(2)}, u32[]{:S(2)}) collective-permute-start(bf16[512,1024]{1,0:T(8,128)(2,1)} %fusion.45), channel_id=1, source_target_pairs={{0,4},{4,0},{1,5},{5,1},{2,6},{6,2},{3,7},{7,3},{8,12},{12,8},{9,1... | collective-permute-start | bytes 3145736 | tf_op jit(solution)/shard_map/out_zc/ppermute | solution.py:1243
  368.1 12.8 %collective-permute-start.20 = (bf16[512,1024]{1,0:T(8,128)(2,1)}, bf16[512,1024]{1,0:T(8,128)(2,1)}, u32[]{:S(2)}, u32[]{:S(2)}) collective-permute-start(bf16[512,1024]{1,0:T(8,128)(2,1)} %get-tuple-element.187), channel_id=1, source_target_pairs={{0,4},{4,0},{1,5},{5,1},{2,6},{6,2},{3,7},{7,3},{8,12},{12,8},{9,1... | collective-permute-start | bytes 3145736 | tf_op jit(solution)/shard_map/e2/ppermute | solution.py:1243
  373.5 39.9 %collective-permute-start.16 = (bf16[512,1024]{1,0:T(8,128)(2,1)}, bf16[512,1024]{1,0:T(8,128)(2,1)}, u32[]{:S(2)}, u32[]{:S(2)}) collective-permute-start(bf16[512,1024]{1,0:T(8,128)(2,1)} %fusion.42), channel_id=1, source_target_pairs={{0,4},{4,0},{1,5},{5,1},{2,6},{6,2},{3,7},{7,3},{8,12},{12,8},{9,1... | collective-permute-start | bytes 3145736 | tf_op jit(solution)/shard_map/out_c/ppermute | solution.py:1243
  373.6 192.6 %reduce-scatter.8.cloned.1.call-start = ((), (), s32[]{:S(2)}) async-start(), calls=%async_computation.6 | async-start | bytes 5242880 | tf_op jit(solution)/shard_map/reduce_scatter | solution.py:1276
  380.1 25.9 %collective-permute-start.19 = (bf16[512,1024]{1,0:T(8,128)(2,1)}, bf16[512,1024]{1,0:T(8,128)(2,1)}, u32[]{:S(2)}, u32[]{:S(2)}) collective-permute-start(bf16[512,1024]{1,0:T(8,128)(2,1)} %add_convert_fusion.5), channel_id=1, source_target_pairs={{0,1},{1,0},{2,3},{3,2},{4,5},{5,4},{6,7},{7,6},{8,9},{9,8},{10,11... | collective-permute-start | bytes 3145736 | tf_op jit(solution)/shard_map/out_z/ppermute | solution.py:1243
  407.9 10.6 %collective-permute-start.22 = (bf16[512,1024]{1,0:T(8,128)(2,1)S(1)}, bf16[512,1024]{1,0:T(8,128)(2,1)S(1)}, u32[]{:S(2)}, u32[]{:S(2)}) collective-permute-start(bf16[512,1024]{1,0:T(8,128)(2,1)S(1)} %convolution_convert_fusion.9), channel_id=1, source_target_pairs={{0,4},{4,0},{1,5},{5,1},{2,6},{6,2},{3,7},{7,3},{8,12},{12,8},{9,1... | collective-permute-start | bytes 3145736 | tf_op jit(solution)/shard_map/dcin/ppermute | solution.py:1243
  415.7 10.1 %collective-permute-start.21 = (bf16[512,1024]{1,0:T(8,128)(2,1)S(1)}, bf16[512,1024]{1,0:T(8,128)(2,1)S(1)}, u32[]{:S(2)}, u32[]{:S(2)}) collective-permute-start(bf16[512,1024]{1,0:T(8,128)(2,1)S(1)} %add_convert_fusion.4), channel_id=1, source_target_pairs={{2,4},{4,2},{3,5},{5,3},{10,12},{12,10},{11,13},{13,11},{18,20},{2... | collective-permute-start | bytes 3145736 | tf_op jit(solution)/shard_map/re_out/ppermute | solution.py:1252
  421.8 36.4 %collective-permute-start.24 = (bf16[512,1024]{1,0:T(8,128)(2,1)}, bf16[512,1024]{1,0:T(8,128)(2,1)}, u32[]{:S(2)}, u32[]{:S(2)}) collective-permute-start(bf16[512,1024]{1,0:T(8,128)(2,1)} %get-tuple-element.190), channel_id=1, source_target_pairs={{0,1},{1,0},{2,3},{3,2},{4,5},{5,4},{6,7},{7,6},{8,9},{9,8},{10,11... | collective-permute-start | bytes 3145736 | tf_op jit(solution)/shard_map/e1_z/ppermute | solution.py:1243
  422.1 12.3 %collective-permute-start.23 = (bf16[512,1024]{1,0:T(8,128)(2,1)}, bf16[512,1024]{1,0:T(8,128)(2,1)}, u32[]{:S(2)}, u32[]{:S(2)}) collective-permute-start(bf16[512,1024]{1,0:T(8,128)(2,1)} %get-tuple-element.190), channel_id=1, source_target_pairs={{0,4},{4,0},{1,5},{5,1},{2,6},{6,2},{3,7},{7,3},{8,12},{12,8},{9,1... | collective-permute-start | bytes 3145736 | tf_op jit(solution)/shard_map/e1_c/ppermute | solution.py:1243
  469.1 42.4 %collective-permute-start.27 = (bf16[256,1024]{1,0:T(8,128)(2,1)}, bf16[256,1024]{1,0:T(8,128)(2,1)S(1)}, u32[]{:S(2)}, u32[]{:S(2)}) collective-permute-start(bf16[256,1024]{1,0:T(8,128)(2,1)} %constant_dynamic-slice_fusion.2), channel_id=1, source_target_pairs={{0,2},{2,0},{1,3},{3,1},{4,6},{6,4},{5,7},{7,5},{8,10},{10,8},{9,1... | collective-permute-start | bytes 1572872 | tf_op jit(solution)/shard_map/go_zhi/ppermute | solution.py:1243
  471.1 46.6 %collective-permute-start.26 = (bf16[256,1024]{1,0:T(8,128)(2,1)}, bf16[256,1024]{1,0:T(8,128)(2,1)}, u32[]{:S(2)}, u32[]{:S(2)}) collective-permute-start(bf16[256,1024]{1,0:T(8,128)(2,1)} %constant_dynamic-slice_fusion.3), channel_id=1, source_target_pairs={{0,2},{2,0},{1,3},{3,1},{4,6},{6,4},{5,7},{7,5},{8,10},{10,8},{9,1... | collective-permute-start | bytes 1572872 | tf_op jit(solution)/shard_map/gi_zhi/ppermute | solution.py:1243
  522.6 9.1 %collective-permute-start.29 = (bf16[512,1024]{1,0:T(8,128)(2,1)S(1)}, bf16[512,1024]{1,0:T(8,128)(2,1)S(1)}, u32[]{:S(2)}, u32[]{:S(2)}) collective-permute-start(bf16[512,1024]{1,0:T(8,128)(2,1)S(1)} %convolution_convert_fusion), channel_id=1, source_target_pairs={{0,4},{4,0},{1,5},{5,1},{2,6},{6,2},{3,7},{7,3},{8,12},{12,8},{9,1... | collective-permute-start | bytes 3145736 | tf_op jit(solution)/shard_map/dx_zc/ppermute | solution.py:1243
  529.4 30.2 %collective-permute-start.28 = (bf16[512,1024]{1,0:T(8,128)(2,1)}, bf16[512,1024]{1,0:T(8,128)(2,1)}, u32[]{:S(2)}, u32[]{:S(2)}) collective-permute-start(bf16[512,1024]{1,0:T(8,128)(2,1)} %convolution_convert_fusion.1), channel_id=1, source_target_pairs={{0,4},{4,0},{1,5},{5,1},{2,6},{6,2},{3,7},{7,3},{8,12},{12,8},{9,1... | collective-permute-start | bytes 3145736 | tf_op jit(solution)/shard_map/dx_c/ppermute | solution.py:1243
  533.7 25.9 %collective-permute-start.30 = (bf16[512,1024]{1,0:T(8,128)(2,1)}, bf16[512,1024]{1,0:T(8,128)(2,1)}, u32[]{:S(2)}, u32[]{:S(2)}) collective-permute-start(bf16[512,1024]{1,0:T(8,128)(2,1)} %add_convert_fusion.3), channel_id=1, source_target_pairs={{0,1},{1,0},{2,3},{3,2},{4,5},{5,4},{6,7},{7,6},{8,9},{9,8},{10,11... | collective-permute-start | bytes 3145736 | tf_op jit(solution)/shard_map/dx_z/ppermute | solution.py:1243
  564.4 83.6 %collective-permute-start.31 = (bf16[512,1024]{1,0:T(8,128)(2,1)}, bf16[512,1024]{1,0:T(8,128)(2,1)S(1)}, u32[]{:S(2)}, u32[]{:S(2)}) collective-permute-start(bf16[512,1024]{1,0:T(8,128)(2,1)} %fusion.9), channel_id=1, source_target_pairs={{2,4},{4,2},{3,5},{5,3},{10,12},{12,10},{11,13},{13,11},{18,20},{2... | collective-permute-start | bytes 3145736 | tf_op jit(solution)/shard_map/re_dgrad/ppermute | solution.py:1252
  (79 other events, 500.4 us)
Sparse Core Ops, SparseCore 0:
  127.4 55.0 all-gather.5
  186.0 52.6 all-gather.3
  335.2 52.1 reduce-scatter.5
  390.5 52.6 reduce-scatter.3
  461.2 52.3 reduce-scatter.7

commit v4 on v3

--- a/solution.py
+++ b/solution.py
@@ -655,17 +655,19 @@
     lax.fori_loop(0, x_ref.shape[0] // chunk, step, 0, unroll=2)
 
 
-def hidden_units(rows, grads, w_in, w_out, bias, tile=512):
+def hidden_units(rows, grads, weights, bias, tile=512):
     count, model = rows.shape
-    width = w_in.shape[1]
+    width = weights.shape[1] // 2
+    tiles = width // tile
     whole = pl.BlockSpec((count, model), lambda i: (0, 0))
     weight = pl.BlockSpec((model, tile), lambda i: (0, i))
+    weight_out = pl.BlockSpec((model, tile), lambda i: (0, tiles + i))
     line = pl.BlockSpec((1, tile), lambda i: (0, i))
     out = pl.BlockSpec((count, tile), lambda i: (0, i))
     return pl.pallas_call(
         hidden_kernel,
         grid=(width // tile,),
-        in_specs=[whole, whole, weight, weight, line],
+        in_specs=[whole, whole, weight, weight_out, line],
         out_specs=[out, out, line],
         out_shape=[
             jax.ShapeDtypeStruct((count, width), jnp.bfloat16),
@@ -677,7 +679,7 @@
             bytes_accessed=4 * (count * model + model * width + count * width),
             transcendentals=count * width,
         ),
-    )(rows, grads, w_in, w_out, bias)
+    )(rows, grads, weights, weights, bias)
 
 
 MESH = pl.DeviceIdType.MESH
@@ -695,7 +697,7 @@
     token_rows,
     attn,
     g_self,
-    g_cross,
+    cross_rows,
     hidden,
     enc_full,
     small_all,
@@ -797,19 +799,23 @@
 
     self_width = w_self.shape[2] // 2
     hidden_width = w_in.shape[1] // 2
-    cross_core = from_shard(w_cross, g_cross, quarter, self_width)
+    cross_core = []
+    for plane in range(4):
+        target = cross_rows.at[own_rows, lanes(4 * plane + quarter, self_width)]
+        cross_core.append(keep(w_cross.at[plane, :, lanes(core, self_width)], target))
+        cross_core.append(push(w_cross.at[plane, :, lanes(1 - core, self_width)], target, "core"))
     own_small.wait()
     small_core = push(gathered.at[y, x, core, zhi, zlo], gathered.at[y, x, core, zhi, zlo], "core")
     self_core = from_shard(w_self, g_self, zhi, self_width)
     hidden_core = []
     for plane, shard in enumerate((w_in, w_out)):
-        target = hidden.at[plane, own_rows, lanes(zhi, hidden_width)]
+        target = hidden.at[plane, own_rows]
         hidden_core.append(keep(shard.at[:, lanes(core, hidden_width)], target))
         hidden_core.append(push(shard.at[:, lanes(1 - core, hidden_width)], target, "core"))
     for copy in cross_core:
         copy.wait()
-    region = g_cross.at[:, y, x, :, lanes(quarter, self_width)]
-    cross_zlo = push(region, region, "zlo")
+    regions = [cross_rows.at[:, lanes(4 * plane + quarter, self_width)] for plane in range(4)]
+    cross_zlo = [push(region, region, "zlo") for region in regions]
     small_core.wait()
     region = gathered.at[y, x, :, zhi, zlo]
     small_x = push(region, region, "x")
@@ -818,7 +824,8 @@
     small_x.wait()
     region = gathered.at[y, :, :, zhi, zlo]
     small_y = push(region, region, "y")
-    cross_zlo.wait()
+    for copy in cross_zlo:
+        copy.wait()
     small_y.wait()
 
     def over_plane(target, width):
@@ -842,6 +849,9 @@
     small_zhi = push(region, region, "zhi")
     region = g_self.at[:, y, x, :, lanes(zhi, self_width)]
     self_zhi = push(region, region, "zhi")
+    wait_enc = moving(enc, enc_full.at[2 * zhi + zlo], enc, enc_full.at[2 * core + zlo])
+    regions = [cross_rows.at[:, lanes(2 * plane + zhi, 2 * self_width)] for plane in range(4)]
+    cross_zhi = [push(region, region, "zhi") for region in regions]
     gain = jnp.concatenate([gathered[d // 4, d // 2 % 2, d % 2, zhi, zlo, 0:1, :] for d in range(8)], axis=1)
     shift = jnp.concatenate([gathered[d // 4, d // 2 % 2, d % 2, zhi, zlo, 3:4, :] for d in range(8)], axis=1)
 
@@ -858,37 +868,27 @@
     attn_core = push(normed, attn.at[pl.ds(rows, rows)], "core")
     attn_own = keep(normed, attn.at[pl.ds(0, rows)])
 
+    wait_enc()
+    region = enc_full.at[2 * core + zlo]
+    enc_zlo = push(region, region, "zlo")
+    enc_core = push(region, region, "core")
     self_zhi.wait()
-    region = g_cross.at[:, y, x, :, lanes(zhi, 2 * self_width)]
-    cross_zhi = push(region, region, "zhi")
     self_second = over_plane(g_self, self_width)
     self_last = self_second()
     small_zhi.wait()
     region = gathered.at[:, :, :, :, zlo]
     small_zlo = push(region, region, "zlo")
-    for copy in hidden_core:
-        copy.wait()
-    cross_zhi.wait()
-    region = hidden.at[0, :, lanes(zhi, hidden_width)]
-    hidden_zhi = push(region, region, "zhi")
-    wait_enc = moving(enc, enc_full.at[2 * zhi + zlo], enc, enc_full.at[2 * core + zlo])
-    cross_second = over_plane(g_cross, 2 * self_width)
-    attn_zlo.wait()
-    attn_diagonal = push(attn.at[pl.ds(2 * rows, rows)], attn.at[pl.ds(3 * rows, rows)], "core")
-    cross_last = cross_second()
-    wait_enc()
-    region = enc_full.at[2 * core + zlo]
-    enc_zlo = push(region, region, "zlo")
-    enc_core = push(region, region, "core")
     enc_zlo.wait()
     region = enc_full.at[2 * core + 1 - zlo]
     enc_diagonal = push(region, region, "core")
+    attn_zlo.wait()
+    attn_diagonal = push(attn.at[pl.ds(2 * rows, rows)], attn.at[pl.ds(3 * rows, rows)], "core")
     small_zlo.wait()
     keep_small = keep(gathered, small_all)
     for copy in (
         *self_last,
-        *cross_last,
-        hidden_zhi,
+        *cross_zhi,
+        *hidden_core,
         attn_core,
         attn_diagonal,
         enc_core,
@@ -908,8 +908,8 @@
         jax.ShapeDtypeStruct((rows, model), low_type),
         jax.ShapeDtypeStruct((4 * rows, model), low_type),
         jax.ShapeDtypeStruct((4, 2, 2, 2 * part, w_self.shape[2]), low_type),
-        jax.ShapeDtypeStruct((4, 2, 2, 2 * part, 2 * w_cross.shape[2]), low_type),
-        jax.ShapeDtypeStruct((2, 2 * part, w_in.shape[1]), low_type),
+        jax.ShapeDtypeStruct((2 * part, 8 * w_cross.shape[2]), low_type),
+        jax.ShapeDtypeStruct((2, 2 * part, w_in.shape[1] // 2), low_type),
         jax.ShapeDtypeStruct((4, enc.shape[0], model), low_type),
         jax.ShapeDtypeStruct((2,) * 5 + small.shape, small.dtype),
     ]
@@ -923,9 +923,9 @@
             pltpu.VMEM((rows, model), low_type),
             pltpu.VMEM((rows, model), low_type),
             pltpu.VMEM((2,) * 5 + small.shape, small.dtype),
-            pltpu.SemaphoreType.DMA((30,)),
-            pltpu.SemaphoreType.DMA((30,)),
-            pltpu.SemaphoreType.DMA((12,)),
+            pltpu.SemaphoreType.DMA((40,)),
+            pltpu.SemaphoreType.DMA((40,)),
+            pltpu.SemaphoreType.DMA((20,)),
         ],
         compiler_params=pltpu.CompilerParams(collective_id=0, has_side_effects=True),
     )(tokens, enc, w_self, w_cross, w_in, w_out, small)
@@ -935,6 +935,7 @@
     ff_in,
     ff_out,
     cross,
+    cross_beyond,
     self_q,
     self_k,
     self_v,
@@ -1079,13 +1080,7 @@
             last.append(push(values.at[there, columns_of], out, "core"))
             last.append(keep(values.at[here, columns_of], out))
 
-    cross_zhi, cross_keep = [], []
-    for plane in range(4):
-        columns_of = pl.ds(plane * 2 * half, 2 * half)
-        there = pl.ds(pl.multiple_of((2 * plane + 1 - zhi) * 2 * half, 2 * half), 2 * half)
-        here = pl.ds(pl.multiple_of((2 * plane + zhi) * 2 * half, 2 * half), 2 * half)
-        cross_zhi.append(push(cross.at[:, there], cross_got.at[:, columns_of], "zhi"))
-        cross_keep.append(keep(cross.at[:, here], cross_own.at[:, columns_of]))
+    cross_keep = [keep(cross, cross_own), keep(cross_beyond, cross_got)]
 
     first, second = pl.ds(0, half), pl.ds(half, half)
     parts = (self_q, self_k, self_v, self_o)
@@ -1123,6 +1118,25 @@
 
     keep(small, small_sum).wait()
     small_copy = small_send(0)
+    for copy in cross_keep:
+        copy.wait()
+
+    def cross_step(target, which, *others):
+        def step(index, carry):
+            rows = pl.ds(pl.multiple_of(index * 64, 64), 64)
+            for plane in range(4):
+                source = pl.ds(pl.multiple_of((2 * plane + which) * half, half), half)
+                columns_of = pl.ds(plane * half, half)
+                value = cross_own[rows, source].astype(jnp.float32) + cross_got[rows, source].astype(jnp.float32)
+                for other in others:
+                    value += other[rows, columns_of].astype(jnp.float32)
+                target[rows, columns_of] = value.astype(target.dtype)
+            return carry
+
+        lax.fori_loop(0, target.shape[0] // 64, step, 0)
+
+    cross_step(cross_low, 1 - zlo)
+    cross_zlo = push(cross_low, cross_got_low, "zlo")
     enc_core.wait()
     enc_keep.wait()
     add(enc_sum, enc_own.at[1 - zlo], enc_got.at[1 - zlo])
@@ -1151,25 +1165,6 @@
     add(self_total.at[1], self_total.at[1], self_got_low.at[1])
     add(low_a, self_total.at[1 - zhi])
     self_zhi = push(low_a, self_last, "zhi")
-    for copy in cross_zhi + cross_keep:
-        copy.wait()
-
-    def cross_step(target, which, *others):
-        def step(index, carry):
-            rows = pl.ds(pl.multiple_of(index * 64, 64), 64)
-            for plane in range(4):
-                source = pl.ds(pl.multiple_of((2 * plane + which) * half, half), half)
-                columns_of = pl.ds(plane * half, half)
-                value = cross_own[rows, source].astype(jnp.float32) + cross_got[rows, source].astype(jnp.float32)
-                for other in others:
-                    value += other[rows, columns_of].astype(jnp.float32)
-                target[rows, columns_of] = value.astype(target.dtype)
-            return carry
-
-        lax.fori_loop(0, target.shape[0] // 64, step, 0)
-
-    cross_step(cross_low, 1 - zlo)
-    cross_zlo = push(cross_low, cross_got_low, "zlo")
     wait_enc = moving(enc_low, enc_out, enc_low, enc_out)
     cross_zlo.wait()
     cross_step(cross_total, zlo, cross_got_low)
@@ -1186,7 +1181,7 @@
         copy.wait()
 
 
-def finish(ff_in, ff_out, cross, self_parts, enc, small):
+def finish(ff_in, ff_out, cross, cross_beyond, self_parts, enc, small):
     rows, width = ff_in.shape
     part, half = self_parts[0].shape[2], self_parts[0].shape[3] // 2
     low_type, enc_shape = enc.dtype, enc.shape[2:]
@@ -1209,7 +1204,7 @@
     return pl.pallas_call(
         finish_kernel,
         out_shape=shapes,
-        in_specs=[anywhere] * 9,
+        in_specs=[anywhere] * 10,
         out_specs=[anywhere] * len(shapes),
         scratch_shapes=[
             pltpu.VMEM((part, 2 * wide), low_type),
@@ -1235,7 +1230,7 @@
         + [pltpu.SemaphoreType.DMA((40,))] * 3,
         compiler_params=pltpu.CompilerParams(collective_id=1, has_side_effects=True),
         cost_estimate=pl.CostEstimate(flops=40_000_000_000, bytes_accessed=0, transcendentals=0),
-    )(ff_in, ff_out, cross, *self_parts, enc, small)
+    )(ff_in, ff_out, cross, cross_beyond, *self_parts, enc, small)
 
 
 def trade(rows, axis, name="trade"):
@@ -1316,7 +1311,7 @@
     flat = jnp.concatenate([vec_params.reshape(-1), head_bias.reshape(-1), ff_bias]).astype(jnp.float32)
     sizes = (vec_params.size, head_bias.size, ff_bias.size)
     flat = jnp.pad(flat.reshape(-1, 128), ((0, 4), (0, 0)))
-    token_rows, attn_rows, w_self, w_cross, w_hidden, enc_full, small = start_exchange(
+    token_rows, attn_rows, w_self, w_cross, hidden, enc_full, small = start_exchange(
         tokens,
         enc_states,
         jnp.concatenate([self_qkv, self_out.T[None]], axis=0),
@@ -1325,14 +1320,14 @@
         ff_out.T,
         flat,
     )
-    w_self, w_cross = w_self.reshape(4, model, -1), w_cross.reshape(4, model, -1)
-    w_in = over_chips(w_hidden[0])
-    out_own = half_of(w_hidden[1], zhi, 1)
-    out_beyond = trade(out_own, "zhi", "wo_zhi")
+    w_self = w_self.reshape(4, model, -1)
+    w_cross = over_chips(w_cross)
+    cross_width = w_cross.shape[1] // 4
+    hidden_beyond = trade(hidden, "zhi", "wh_zhi")
     w_qkv, w_so = jnp.concatenate([w_self[0], w_self[1], w_self[2]], axis=1), w_self[3]
-    w_cq, w_ckv, w_co = w_cross[0], jnp.concatenate([w_cross[1], w_cross[2]], axis=1), w_cross[3]
+    w_cq, w_ckv, w_co = jnp.split(w_cross, [cross_width, 3 * cross_width], axis=1)
     rows_of = model // 4
-    width, cross_width = w_self.shape[2], w_cross.shape[2]
+    width = w_self.shape[2]
     pairs, cross_pairs = width // PAIR, cross_width // PAIR
     enc_full = enc_full.reshape(-1, model)
     attn_near, attn_far = attn_rows[: attn_rows.shape[0] // 2], attn_rows[attn_rows.shape[0] // 2 :]
@@ -1372,8 +1367,10 @@
     count = qkv.shape[0]
     self_plan = functools.partial(self_sections, segments=segments)
     mixed, self_lse = attend(self_plan, self_meta, qkv, 0, qkv, pairs, 2 * pairs, pairs, 1152)
-    mixed = after(mixed, out_beyond)
-    w_out = over_chips(in_order(zhi, out_own, after(out_beyond, mixed), 1))
+    mixed = after(mixed, hidden_beyond)
+    hidden = in_order(zhi, hidden, after(hidden_beyond, mixed), 2).transpose(1, 0, 2)
+    w_hidden = over_chips(hidden.reshape(hidden.shape[0], -1))
+    w_in, w_out = jnp.split(w_hidden, 2, axis=1)
     near, far = mixed[: count // 2], mixed[count // 2 :]
     so_far = low(
         product_right_t(far[: count // 4], w_so)
@@ -1381,7 +1378,7 @@
     )
     so_near_other = low(product_right_t(near[count // 4 :], w_so))
     so_near = product_right_t(near[: count // 4], w_so)
-    grad_rows = regroup(after(cotangent, attn_rows), "cotangent")
+    grad_rows = regroup(after(cotangent, mixed), "cotangent")
     cross_kv = low(
         product(after(enc_full, grad_rows, so_far), w_ckv)
         + jnp.concatenate([jnp.zeros((cross_width,), jnp.float32), cross_bias[1]])
@@ -1410,11 +1407,11 @@
     mlp_in = low(normed_out)
     beyond = trade(mlp_in, "zlo", "mlp_z")
     mlp_near = jnp.concatenate([mlp_in, trade(mlp_in, "core", "mlp_c")], axis=0)
-    act_near, dpre_near, sum_near = hidden_units(mlp_near, cot_near, w_in, w_out, hidden_bias[None])
+    act_near, dpre_near, sum_near = hidden_units(mlp_near, cot_near, w_hidden, hidden_bias[None])
     beyond = after(beyond, act_near)
     mlp_far = jnp.concatenate([beyond, trade(beyond, "core", "mlp_zc")], axis=0)
     cot_far = jnp.concatenate([cot_beyond, trade(cot_beyond, "core", "cot_zc")], axis=0)
-    act_far, dpre_far, sum_far = hidden_units(mlp_far, cot_far, w_in, w_out, hidden_bias[None])
+    act_far, dpre_far, sum_far = hidden_units(mlp_far, cot_far, w_hidden, hidden_bias[None])
     gradient = grad_rows.astype(jnp.float32)
     bias_out_three = jnp.sum(gradient, axis=0)
     dmlp_far = low(
@@ -1460,7 +1457,6 @@
         ENC,
     )
     cross_dq = after(cross_dq, out_far)
-    layer_out = regroup(low(after_two + (out_branch + after(out_far, cross_dq) + vectors[8])), "out")
     other = trade(low(product_right_t(cross_dq[own_rows:], w_cq)), "core", "dcin")
     part, gain_two, shift_two = norm_backward(
         product_right_t(cross_dq[:own_rows], w_cq) + other, hat_two, inv_two, vectors[1]
@@ -1483,6 +1479,7 @@
         low(product_left_t(after(grad_both, grad_low), cross_mixed)),
     ]
     grad_cross = jnp.concatenate(cross_parts, axis=1)
+    layer_out = low(after_two + (out_branch + after(out_far, grad_low) + vectors[8]))
     beyond = after(beyond, mixed_grad, grad_cross, layer_out)
     cross_sum = sum_over_chips(grad_cross)
     grad_far = jnp.concatenate([beyond, trade(beyond, "core", "e1_zc")], axis=0)
@@ -1494,6 +1491,7 @@
         self_plan, self_meta, qkv, 0, qkv, pairs, 2 * pairs, mixed, mixed_grad, self_lse, pairs, 1152
     )
     dq, dk, dv = after(dq, in_sum, out_sum), after(dk, in_sum, out_sum), after(dv, in_sum, out_sum)
+    layer_out = regroup(after(layer_out, dq), "out")
     dqkv = jnp.concatenate([dq, dk, dv], axis=1)
     d_near, d_far = dqkv[: count // 2], dqkv[count // 2 :]
     dx_far = low(
@@ -1514,7 +1512,10 @@
         product_right_t(after(cross_dk, dq), w_ckv[:, :cross_width])
         + product_right_t(after(cross_dv, dq), w_ckv[:, cross_width:])
     )
-    dx = dx + after(trade(dx_far, "zlo", "dx_z"), enc_part, *self_parts)
+    cross_sum = after(cross_sum, dq).reshape(rows_of, 4, 2, -1)
+    cross_kept = half_of(cross_sum, zhi, 2).reshape(rows_of, -1)
+    cross_beyond = trade(half_of(cross_sum, 1 - zhi, 2).reshape(rows_of, -1), "zhi", "gc_zhi")
+    dx = dx + after(trade(dx_far, "zlo", "dx_z"), enc_part, layer_out, cross_beyond, *self_parts)
     part, gain_one, shift_one = norm_backward(dx, hat_one, inv_one, vectors[0])
     input_part = low(gradient + part)
     input_grad = regroup(input_part, "dgrad").astype(jnp.float32)
@@ -1557,7 +1558,8 @@
     ff_in_grad, ff_out_grad, cross_qkv_grad, cross_out_grad, self_qkv_grad, self_out_grad, enc_grad, sums = finish(
         in_sum,
         out_sum,
-        cross_sum,
+        cross_kept,
+        cross_beyond,
         [part.reshape(2, 2, rows_of, -1) for part in self_parts],
         enc_part.reshape(2, 2, -1, model),
         sums,

time: 669 us -> 646 us (0.966)
  Pallas kernels: 306 us -> 260 us
  matrix products: 127 us -> 142 us
  starting transfers between devices: 19.4 us -> 28.3 us
  waiting for transfers between devices: 85.2 us -> 93.5 us
  other arithmetic: 53.8 us -> 47.1 us
    pallas_call x1, Pallas kernels: 72.2 us -> 46.2 us  [finish(): pl.pallas_call(finish_kernel, out_shape=shapes, in_specs=[anywhere] * 10,...]
    pallas_call x1, Pallas kernels: 106 us -> 85.2 us  [start_exchange(): pl.pallas_call(start_kernel, out_shape=shapes, in_specs=[anywhere] * 7, o...]
    dot_general x22, matrix products: 65.9 us -> 75.2 us  [product_right_t(): lax.dot_general(left, right, (((1,), (1,)), ((), ())), preferred_element_...]
    ppermute x28 -> x29, waiting for transfers between devices: 85.1 us -> 93.4 us  [trade(): return lax.ppermute(rows, axis, [(0, 1), (1, 0)])]
    ppermute x28 -> x29, starting transfers between devices: 15.1 us -> 23 us  [trade(): return lax.ppermute(rows, axis, [(0, 1), (1, 0)])]
    slice x2 -> x0, local copies, waits for them, and re-layouts: 7.03 us -> none  [the longest x1 4.31 us: fast_layer(): w_cross[0]]
    unnamed x174 -> x172, local copies, waits for them, and re-layouts: 28.9 us -> 26.9 us
  transfers between devices with their start and end apart: 37 -> 38, of which waited for: 11 -> 12; matrix products, arithmetic and copies ran while one was open for 30% -> 31% of each run, Pallas kernels for 46% -> 28%
where the time goes in v4:
time: 646 us; the launch traced here: 636 us
  Pallas kernels  260 us (40%)
  matrix products  142 us (22%)
  waiting for transfers between devices  93.5 us (14%)
  local copies, waits for them, and re-layouts  49.5 us (8%)
  other arithmetic  47.1 us (7%)
  starting transfers between devices  28.3 us (4%)
  between operations  15.9 us (2%)
    ppermute x29, waiting for transfers between devices, trade(): return lax.ppermute(rows, axis, [(0, 1), (1, 0)])  93.4 us
    pallas_call x1, Pallas kernels, start_exchange(): pl.pallas_call(start_kernel, out_shape=shapes, in_specs=[anywhere] * 7, o...  85.2 us
    dot_general x22, matrix products, product_right_t(): lax.dot_general(left, right, (((1,), (1,)), ((), ())), preferred_element_...  75.2 us
    pallas_call x2, Pallas kernels, attend_back(): pl.pallas_call(functools.partial(backward_kernel, sections), grid_spec=pl...  56.3 us
    pallas_call x1, Pallas kernels, finish(): pl.pallas_call(finish_kernel, out_shape=shapes, in_specs=[anywhere] * 10,...  46.2 us
    dot_general x13, matrix products, product_left_t(): lax.dot_general(left, right, (((0,), (0,)), ((), ())), preferred_element_...  46.1 us
    pallas_call x2, Pallas kernels, attend(): pl.pallas_call(functools.partial(forward_kernel, sections), grid_spec=plt...  38.7 us
    pallas_call x2, Pallas kernels, hidden_units(): pl.pallas_call(hidden_kernel, grid=(width // tile,), in_specs=[whole, who...  33.8 us
  transfers between devices with their start and end apart: 38, of which 12 were waited for; matrix products, arithmetic and copies ran while one was open for 31% of the time, Pallas kernels for 28%

profile of v4, /device:TPU:0, one launch (start us, length us, event | category | flops | bytes accessed | tf_op | source)
XLA Modules:
  0.0 636.3 jit_solution(16734724382693166797)
XLA Ops:
  15.1 85.2 %shard_map.229 = (bf16[512,1024]{1,0:T(8,128)(2,1)}, bf16[2048,1024]{1,0:T(8,128)(2,1)}, bf16[4,2,2,256,256]{4,3,2,1,0:T(8,128)(2,1)}, bf16[256,2048]{1,0:T(8,12...) custom-call(bf16[512,1024]{1,0:T(8,128)(2,1)} %tokens.1, ...), custom_call_target="tpu_custom_call" | custom-call | tf_op jit(solution)/shard_map/pallas_call | solution.py:917
  101.8 5.0 collective-permute-start.1
  111.3 4.8 multiply_convert_fusion.q_ref.k_ref.v_ref
  117.1 23.2 %shard_map.230 = (bf16[2048,256]{1,0:T(8,128)(2,1)}, f32[2048,256]{1,0:T(8,128)}) custom-call(s32[13]{0:T(128)} %concatenate.78.meta_ref, bf16[2048,768]{1,0:T(8,128)(2,1)} %multiply_convert_fusion.q_ref.k_ref.v_ref, bf16[2048,768]{1,0:T(8,128)(2,1)} %multiply_convert_fusion.q_ref.k_ref.v_ref, bf16[2048,768]{1,0:T(8,128)(2,1)} %multiply_convert_fusion.q_ref.k_ref.v_ref), custom_call_target="tpu_custom_call" | custom-call | flops 19327352832 | bytes 5242880 | tf_op jit(solution)/shard_map/pallas_call | solution.py:180
  140.3 11.1 %collective-permute-done.1 = bf16[2,256,1024]{2,1,0:T(8,128)(2,1)S(1)} collective-permute-done((bf16[2,256,1024]{2,1,0:T(8,128)(2,1)}, bf16[2,256,1024]{2,1,0:T(8,128)(2,1)S(1)}, u32[]{:S(2)}, u32[]{:S(2)}) %collective-permute-start.1) | collective-permute-done | bytes 1048608 | tf_op jit(solution)/shard_map/wh_zhi/ppermute | solution.py:1238
  170.3 4.3 add_convert_fusion.9.k_ref.v_ref
  174.6 26.7 %collective-permute-done.4 = bf16[512,1024]{1,0:T(8,128)(2,1)} collective-permute-done((bf16[512,1024]{1,0:T(8,128)(2,1)}, bf16[512,1024]{1,0:T(8,128)(2,1)}, u32[]{:S(2)}, u32[]{:S(2)}) %collective-permute-start.4) | collective-permute-done | bytes 1048608 | tf_op jit(solution)/shard_map/so_z/ppermute | solution.py:1238
  212.3 15.5 %shard_map.231 = (bf16[1024,512]{1,0:T(8,128)(2,1)}, f32[1024,512]{1,0:T(8,128)}) custom-call(s32[1]{0:T(128)} %slice.202.meta_ref, bf16[1024,512]{1,0:T(8,128)(2,1)} %multiply_convert_fusion.1.q_ref, bf16[512,1024]{1,0:T(8,128)(2,1)} %add_convert_fusion.9.k_ref.v_ref, bf16[512,1024]{1,0:T(8,128)(2,1)} %add_convert_fusion.9.k_ref.v_ref), custom_call_target="tpu_custom_call" | custom-call | flops 8589934592 | bytes 5242880 | tf_op jit(solution)/shard_map/pallas_call | solution.py:180
  248.0 16.9 %shard_map.232 = (bf16[1024,2048]{1,0:T(8,128)(2,1)}, bf16[1024,2048]{1,0:T(8,128)(2,1)}, f32[1,2048]{1,0:T(1,128)}) custom-call(bf16[1024,1024]{1,0:T(8,128)(2,1)} %pad_maximum_fusion.2.x_ref, bf16[1024,1024]{1,0:T(8,128)(2,1)} %pad_maximum_fusion.3.e_ref, bf16[1024,4096]{1,0:T(8,128)(2,1)} %all-gather.5.cloned.1.call-done.w_in_ref.w_out_ref, ...), custom_call_target="tpu_custom_call" | custom-call | flops 8589934592 | bytes 20971520 | tf_op jit(solution)/shard_map/pallas_call | solution.py:667
  272.2 5.5 fusion.49
  281.8 17.0 %shard_map.233 = (bf16[1024,2048]{1,0:T(8,128)(2,1)}, bf16[1024,2048]{1,0:T(8,128)(2,1)}, f32[1,2048]{1,0:T(1,128)}) custom-call(bf16[1024,1024]{1,0:T(8,128)(2,1)} %constant_dynamic-update-slice_fusion.x_ref, bf16[1024,1024]{1,0:T(8,128)(2,1)} %constant_dynamic-update-slice_fusion.2.e_ref, ...), custom_call_target="tpu_custom_call" | custom-call | flops 8589934592 | bytes 20971520 | tf_op jit(solution)/shard_map/pallas_call | solution.py:667
  298.8 5.3 fusion.44
  304.3 6.3 convert_add_fusion.5
  314.0 5.9 fusion.108
  320.0 8.0 %add_convert_fusion.1 = bf16[1024,2048]{1,0:T(8,128)(2,1)} fusion(f32[1024,2048]{1,0:T(8,128)S(1)} %fusion.108, bf16[1024,1024]{1,0:T(8,128)(2,1)} %constant_dynamic-update-slice_fusion.2.e_ref, bf16[1024,2048]{1,0:T(8,128)(2,1)S(1)} %copy-done.66), kind=kOutput, calls=%fused_computation.1 | convolution fusion | flops 4299161600 | bytes 18874368 | tf_op jit(solution)/shard_map/dot_general | solution.py:272
  328.6 6.3 fusion.59
  335.2 4.7 fusion.113
  339.9 8.4 %add_convert_fusion = bf16[1024,2048]{1,0:T(8,128)(2,1)} fusion(f32[1024,2048]{1,0:T(8,128)S(1)} %fusion.113, bf16[1024,1024]{1,0:T(8,128)(2,1)} %constant_dynamic-update-slice_fusion.x_ref, bf16[1024,2048]{1,0:T(8,128)(2,1)S(1)} %copy-done.68), kind=kOutput, calls=%fused_computation | convolution fusion | flops 4299161600 | bytes 18874368 | tf_op jit(solution)/shard_map/dot_general | solution.py:272
  348.3 6.0 collective-permute-done.18
  361.3 6.5 %add_convert_fusion.5 = bf16[512,1024]{1,0:T(8,128)(2,1)} fusion(bf16[512,1024]{1,0:T(8,128)(2,1)} %collective-permute-done.17, bf16[1024,4096]{1,0:T(8,128)(2,1)} %all-gather.5.cloned.1.call-done.w_in_ref.w_out_ref, bf16[1024,2048]{1,0:T(8,128)(2,1)} %get-tuple-element.98), kind=kOutput, calls=%fused_computation.61 | convolution fusion | flops 2149056512 | bytes 8388608 | tf_op jit(solution)/shard_map/dot_general | solution.py:278
  368.0 4.1 convolution_convert_fusion.4.do_ref
  372.1 18.6 %shard_map.234 = (bf16[1024,512]{1,0:T(8,128)(2,1)}, bf16[512,512]{1,0:T(8,128)(2,1)}, bf16[512,512]{1,0:T(8,128)(2,1)}) custom-call(s32[1]{0:T(128)} %slice.202.meta_ref, bf16[1024,512]{1,0:T(8,128)(2,1)} %multiply_convert_fusion.1.q_ref, bf16[512,1024]{1,0:T(8,128)(2,1)} %add_convert_fusion.9.k_ref.v_ref, bf16[512,1024]{1,0:T(8,128)(2,1)} %add_convert_fusion.9.k_ref.v_ref, ...), custom_call_target="tpu_custom_call" | custom-call | flops 21474836480 | bytes 10485760 | tf_op jit(solution)/shard_map/pallas_call | solution.py:202
  396.2 6.5 %fusion.54 = bf16[512,1024]{1,0:T(8,128)(2,1)} fusion(bf16[1024,4096]{1,0:T(8,128)(2,1)} %all-gather.5.cloned.1.call-done.w_in_ref.w_out_ref, bf16[1024,2048]{1,0:T(8,128)(2,1)} %get-tuple-element.96), kind=kOutput, calls=%fused_computation.99 | convolution fusion | flops 2148007936 | bytes 7340032 | tf_op jit(solution)/shard_map/dot_general | solution.py:278
  422.6 3.9 add_convert_fusion.4
  429.6 10.8 %collective-permute-done.23 = bf16[512,1024]{1,0:T(8,128)(2,1)} collective-permute-done((bf16[512,1024]{1,0:T(8,128)(2,1)}, bf16[512,1024]{1,0:T(8,128)(2,1)}, u32[]{:S(2)}, u32[]{:S(2)}) %collective-permute-start.23) | collective-permute-done | bytes 1048608 | tf_op jit(solution)/shard_map/e1_z/ppermute | solution.py:1238
  453.7 37.7 %shard_map.235 = (bf16[2048,256]{1,0:T(8,128)(2,1)}, bf16[2048,256]{1,0:T(8,128)(2,1)}, bf16[2048,256]{1,0:T(8,128)(2,1)}) custom-call(s32[13]{0:T(128)} %concatenate.78.meta_ref, bf16[2048,768]{1,0:T(8,128)(2,1)} %multiply_convert_fusion.q_ref.k_ref.v_ref, bf16[2048,768]{1,0:T(8,128)(2,1)} %multiply_convert_fusion.q_ref.k_ref.v_ref, ...), custom_call_target="tpu_custom_call" | custom-call | flops 48318382080 | bytes 10485760 | tf_op jit(solution)/shard_map/pallas_call | solution.py:202
  492.5 4.7 collective-permute-done.25
  519.7 4.4 convolution_convert_fusion.14
  532.8 5.2 collective-permute-start.31
  538.2 4.4 convolution_convert_fusion.13
  543.7 19.3 %collective-permute-done.30 = bf16[512,1024]{1,0:T(8,128)(2,1)} collective-permute-done((bf16[512,1024]{1,0:T(8,128)(2,1)}, bf16[512,1024]{1,0:T(8,128)(2,1)}, u32[]{:S(2)}, u32[]{:S(2)}) %collective-permute-start.30) | collective-permute-done | bytes 1048608 | tf_op jit(solution)/shard_map/dx_z/ppermute | solution.py:1238
  569.2 46.2 %shard_map.236 = (f32[128,2048]{1,0:T(8,128)}, f32[128,2048]{1,0:T(8,128)}, f32[3,128,256]{2,1,0:T(8,128)}, f32[128,256]{1,0:T(8,128)}, f32[3,128,256]{2,1,0:T(8...) custom-call(f32[256,1024]{1,0:T(8,128)} %convert_add_fusion.7.ff_in, ...), custom_call_target="tpu_custom_call" | custom-call | flops 40000000000 | tf_op jit(solution)/shard_map/pallas_call | solution.py:1204
  (384 shorter events, 182.1 us)
Async XLA Ops:
  7.2 163.1 %all-gather.3.cloned.1.call-start = ((), (), s32[]{:S(2)}) async-start(), calls=%async_computation.3 | async-start | bytes 5242880 | tf_op jit(solution)/shard_map/all_gather | solution.py:1267
  100.4 147.6 %all-gather.5.cloned.1.call-start = ((), (), s32[]{:S(2)}) async-start(), calls=%async_computation.4 | async-start | bytes 10485760 | tf_op jit(solution)/shard_map/all_gather | solution.py:1267
  101.2 14.9 %collective-permute-start = (s32[9]{0:T(128)S(1)}, s32[9]{0:T(128)S(1)}, u32[]{:S(2)}, u32[]{:S(2)}) collective-permute-start(s32[9]{0:T(128)S(1)} %pad_add_fusion), channel_id=1, source_target_pairs={{2,4},{4,2},{3,5},{5,3},{10,12},{12,10},{11,13},{13,11},{18,20},{2... | collective-permute-start | bytes 116 | tf_op jit(solution)/shard_map/re_regroup/ppermute | solution.py:1247
  101.8 49.6 %collective-permute-start.1 = (bf16[2,256,1024]{2,1,0:T(8,128)(2,1)}, bf16[2,256,1024]{2,1,0:T(8,128)(2,1)S(1)}, u32[]{:S(2)}, u32[]{:S(2)}) collective-permute-start(bf16[2,256,1024]{2,1,0:T(8,128)(2,1)} %get-tuple-element.81), channel_id=1, source_target_pairs={{0,2},{2,0},{1,3},{3,1},{4,6},{6,4},{5,7},{7,5},{8,10},{10,8},{9,1... | collective-permute-start | bytes 3145736 | tf_op jit(solution)/shard_map/wh_zhi/ppermute | solution.py:1238
  153.4 293.4 %reduce-scatter.6.cloned.1.call-start = ((), (), s32[]{:S(2)}) async-start(), calls=%async_computation.6 | async-start | bytes 5242880 | tf_op jit(solution)/shard_map/reduce_scatter | solution.py:1271
  155.9 13.4 %collective-permute-start.5 = (bf16[512,1024]{1,0:T(8,128)(2,1)}, bf16[512,1024]{1,0:T(8,128)(2,1)}, u32[]{:S(2)}, u32[]{:S(2)}) collective-permute-start(bf16[512,1024]{1,0:T(8,128)(2,1)} %param.18), channel_id=1, source_target_pairs={{2,4},{4,2},{3,5},{5,3},{10,12},{12,10},{11,13},{13,11},{18,20},{2... | collective-permute-start | bytes 3145736 | tf_op jit(solution)/shard_map/re_cotangent/ppermute | solution.py:1247
  160.4 40.9 %collective-permute-start.2 = (bf16[512,1024]{1,0:T(8,128)(2,1)}, bf16[512,1024]{1,0:T(8,128)(2,1)}, u32[]{:S(2)}, u32[]{:S(2)}) collective-permute-start(bf16[512,1024]{1,0:T(8,128)(2,1)} %convolution_convert_fusion.6), channel_id=1, source_target_pairs={{0,4},{4,0},{1,5},{5,1},{2,6},{6,2},{3,7},{7,3},{8,12},{12,8},{9,1... | collective-permute-start | bytes 3145736 | tf_op jit(solution)/shard_map/so_c/ppermute | solution.py:1238
  164.1 37.2 %collective-permute-start.4 = (bf16[512,1024]{1,0:T(8,128)(2,1)}, bf16[512,1024]{1,0:T(8,128)(2,1)}, u32[]{:S(2)}, u32[]{:S(2)}) collective-permute-start(bf16[512,1024]{1,0:T(8,128)(2,1)} %add_convert_fusion.10), channel_id=1, source_target_pairs={{0,1},{1,0},{2,3},{3,2},{4,5},{5,4},{6,7},{7,6},{8,9},{9,8},{10,11... | collective-permute-start | bytes 3145736 | tf_op jit(solution)/shard_map/so_z/ppermute | solution.py:1238
  205.9 25.6 %collective-permute-start.7 = (bf16[512,1024]{1,0:T(8,128)(2,1)S(1)}, bf16[512,1024]{1,0:T(8,128)(2,1)}, u32[]{:S(2)}, u32[]{:S(2)}) collective-permute-start(bf16[512,1024]{1,0:T(8,128)(2,1)S(1)} %get-tuple-element.89), channel_id=1, source_target_pairs={{0,1},{1,0},{2,3},{3,2},{4,5},{5,4},{6,7},{7,6},{8,9},{9,8},{10,11... | collective-permute-start | bytes 3145736 | tf_op jit(solution)/shard_map/cot_z/ppermute | solution.py:1238
  233.7 8.3 %collective-permute-start.10 = (bf16[512,1024]{1,0:T(8,128)(2,1)S(1)}, bf16[512,1024]{1,0:T(8,128)(2,1)}, u32[]{:S(2)}, u32[]{:S(2)}) collective-permute-start(bf16[512,1024]{1,0:T(8,128)(2,1)S(1)} %get-tuple-element.89), channel_id=1, source_target_pairs={{0,4},{4,0},{1,5},{5,1},{2,6},{6,2},{3,7},{7,3},{8,12},{12,8},{9,1... | collective-permute-start | bytes 3145736 | tf_op jit(solution)/shard_map/cot_c/ppermute | solution.py:1238
  241.8 25.8 %collective-permute-start.11 = (bf16[512,1024]{1,0:T(8,128)(2,1)}, bf16[512,1024]{1,0:T(8,128)(2,1)}, u32[]{:S(2)}, u32[]{:S(2)}) collective-permute-start(bf16[512,1024]{1,0:T(8,128)(2,1)} %add_convert_fusion.7), channel_id=1, source_target_pairs={{0,1},{1,0},{2,3},{3,2},{4,5},{5,4},{6,7},{7,6},{8,9},{9,8},{10,11... | collective-permute-start | bytes 3145736 | tf_op jit(solution)/shard_map/mlp_z/ppermute | solution.py:1238
  244.8 25.1 %collective-permute-start.13 = (bf16[512,1024]{1,0:T(8,128)(2,1)}, bf16[512,1024]{1,0:T(8,128)(2,1)}, u32[]{:S(2)}, u32[]{:S(2)}) collective-permute-start(bf16[512,1024]{1,0:T(8,128)(2,1)} %collective-permute-done.7), channel_id=1, source_target_pairs={{0,4},{4,0},{1,5},{5,1},{2,6},{6,2},{3,7},{7,3},{8,12},{12,8},{9,1... | collective-permute-start | bytes 3145736 | tf_op jit(solution)/shard_map/cot_zc/ppermute | solution.py:1238
  267.5 13.2 %collective-permute-start.12 = (bf16[512,1024]{1,0:T(8,128)(2,1)}, bf16[512,1024]{1,0:T(8,128)(2,1)S(1)}, u32[]{:S(2)}, u32[]{:S(2)}) collective-permute-start(bf16[512,1024]{1,0:T(8,128)(2,1)} %collective-permute-done.11), channel_id=1, source_target_pairs={{0,4},{4,0},{1,5},{5,1},{2,6},{6,2},{3,7},{7,3},{8,12},{12,8},{9,1... | collective-permute-start | bytes 3145736 | tf_op jit(solution)/shard_map/mlp_zc/ppermute | solution.py:1238
  277.8 26.5 %collective-permute-start.15 = (bf16[512,1024]{1,0:T(8,128)(2,1)}, bf16[512,1024]{1,0:T(8,128)(2,1)}, u32[]{:S(2)}, u32[]{:S(2)}) collective-permute-start(bf16[512,1024]{1,0:T(8,128)(2,1)} %fusion.49), channel_id=1, source_target_pairs={{0,4},{4,0},{1,5},{5,1},{2,6},{6,2},{3,7},{7,3},{8,12},{12,8},{9,1... | collective-permute-start | bytes 3145736 | tf_op jit(solution)/shard_map/dmlp_c/ppermute | solution.py:1238
  328.1 121.3 %reduce-scatter.4.cloned.1.call-start = ((), (), s32[]{:S(2)}) async-start(), calls=%async_computation.5 | async-start | bytes 5242880 | tf_op jit(solution)/shard_map/reduce_scatter | solution.py:1271
  328.3 26.0 %collective-permute-start.18 = (bf16[512,1024]{1,0:T(8,128)(2,1)}, bf16[512,1024]{1,0:T(8,128)(2,1)}, u32[]{:S(2)}, u32[]{:S(2)}) collective-permute-start(bf16[512,1024]{1,0:T(8,128)(2,1)} %add_convert_fusion.6), channel_id=1, source_target_pairs={{0,1},{1,0},{2,3},{3,2},{4,5},{5,4},{6,7},{7,6},{8,9},{9,8},{10,11... | collective-permute-start | bytes 3145736 | tf_op jit(solution)/shard_map/dmlp_z/ppermute | solution.py:1238
  334.9 26.4 %collective-permute-start.17 = (bf16[512,1024]{1,0:T(8,128)(2,1)}, bf16[512,1024]{1,0:T(8,128)(2,1)}, u32[]{:S(2)}, u32[]{:S(2)}) collective-permute-start(bf16[512,1024]{1,0:T(8,128)(2,1)} %fusion.59), channel_id=1, source_target_pairs={{0,4},{4,0},{1,5},{5,1},{2,6},{6,2},{3,7},{7,3},{8,12},{12,8},{9,1... | collective-permute-start | bytes 3145736 | tf_op jit(solution)/shard_map/out_zc/ppermute | solution.py:1238
  360.9 7.1 %collective-permute-start.20 = (bf16[512,1024]{1,0:T(8,128)(2,1)}, bf16[512,1024]{1,0:T(8,128)(2,1)}, u32[]{:S(2)}, u32[]{:S(2)}) collective-permute-start(bf16[512,1024]{1,0:T(8,128)(2,1)} %get-tuple-element.191), channel_id=1, source_target_pairs={{0,4},{4,0},{1,5},{5,1},{2,6},{6,2},{3,7},{7,3},{8,12},{12,8},{9,1... | collective-permute-start | bytes 3145736 | tf_op jit(solution)/shard_map/e2/ppermute | solution.py:1238
  361.2 169.3 %reduce-scatter.8.cloned.1.call-start = ((), (), s32[]{:S(2)}) async-start(), calls=%async_computation.7 | async-start | bytes 5242880 | tf_op jit(solution)/shard_map/reduce_scatter | solution.py:1271
  367.7 25.8 %collective-permute-start.19 = (bf16[512,1024]{1,0:T(8,128)(2,1)}, bf16[512,1024]{1,0:T(8,128)(2,1)S(1)}, u32[]{:S(2)}, u32[]{:S(2)}) collective-permute-start(bf16[512,1024]{1,0:T(8,128)(2,1)} %add_convert_fusion.5), channel_id=1, source_target_pairs={{0,1},{1,0},{2,3},{3,2},{4,5},{5,4},{6,7},{7,6},{8,9},{9,8},{10,11... | collective-permute-start | bytes 3145736 | tf_op jit(solution)/shard_map/out_z/ppermute | solution.py:1238
  396.1 13.2 %collective-permute-start.21 = (bf16[512,1024]{1,0:T(8,128)(2,1)S(1)}, bf16[512,1024]{1,0:T(8,128)(2,1)S(1)}, u32[]{:S(2)}, u32[]{:S(2)}) collective-permute-start(bf16[512,1024]{1,0:T(8,128)(2,1)S(1)} %convolution_convert_fusion.9), channel_id=1, source_target_pairs={{0,4},{4,0},{1,5},{5,1},{2,6},{6,2},{3,7},{7,3},{8,12},{12,8},{9,1... | collective-permute-start | bytes 3145736 | tf_op jit(solution)/shard_map/dcin/ppermute | solution.py:1238
  402.7 19.9 %collective-permute-start.16 = (bf16[512,1024]{1,0:T(8,128)(2,1)}, bf16[512,1024]{1,0:T(8,128)(2,1)}, u32[]{:S(2)}, u32[]{:S(2)}) collective-permute-start(bf16[512,1024]{1,0:T(8,128)(2,1)} %fusion.54), channel_id=1, source_target_pairs={{0,4},{4,0},{1,5},{5,1},{2,6},{6,2},{3,7},{7,3},{8,12},{12,8},{9,1... | collective-permute-start | bytes 3145736 | tf_op jit(solution)/shard_map/out_c/ppermute | solution.py:1238
  415.0 25.4 %collective-permute-start.23 = (bf16[512,1024]{1,0:T(8,128)(2,1)}, bf16[512,1024]{1,0:T(8,128)(2,1)}, u32[]{:S(2)}, u32[]{:S(2)}) collective-permute-start(bf16[512,1024]{1,0:T(8,128)(2,1)} %get-tuple-element.194), channel_id=1, source_target_pairs={{0,1},{1,0},{2,3},{3,2},{4,5},{5,4},{6,7},{7,6},{8,9},{9,8},{10,11... | collective-permute-start | bytes 3145736 | tf_op jit(solution)/shard_map/e1_z/ppermute | solution.py:1238
  415.0 11.4 %collective-permute-start.22 = (bf16[512,1024]{1,0:T(8,128)(2,1)}, bf16[512,1024]{1,0:T(8,128)(2,1)}, u32[]{:S(2)}, u32[]{:S(2)}) collective-permute-start(bf16[512,1024]{1,0:T(8,128)(2,1)} %get-tuple-element.194), channel_id=1, source_target_pairs={{0,4},{4,0},{1,5},{5,1},{2,6},{6,2},{3,7},{7,3},{8,12},{12,8},{9,1... | collective-permute-start | bytes 3145736 | tf_op jit(solution)/shard_map/e1_c/ppermute | solution.py:1238
  448.8 42.5 %collective-permute-start.26 = (bf16[256,1024]{1,0:T(8,128)(2,1)}, bf16[256,1024]{1,0:T(8,128)(2,1)S(1)}, u32[]{:S(2)}, u32[]{:S(2)}) collective-permute-start(bf16[256,1024]{1,0:T(8,128)(2,1)} %constant_dynamic-slice_fusion.4), channel_id=1, source_target_pairs={{0,2},{2,0},{1,3},{3,1},{4,6},{6,4},{5,7},{7,5},{8,10},{10,8},{9,1... | collective-permute-start | bytes 1572872 | tf_op jit(solution)/shard_map/go_zhi/ppermute | solution.py:1238
  451.3 45.9 %collective-permute-start.25 = (bf16[256,1024]{1,0:T(8,128)(2,1)}, bf16[256,1024]{1,0:T(8,128)(2,1)S(1)}, u32[]{:S(2)}, u32[]{:S(2)}) collective-permute-start(bf16[256,1024]{1,0:T(8,128)(2,1)} %constant_dynamic-slice_fusion.5), channel_id=1, source_target_pairs={{0,2},{2,0},{1,3},{3,1},{4,6},{6,4},{5,7},{7,5},{8,10},{10,8},{9,1... | collective-permute-start | bytes 1572872 | tf_op jit(solution)/shard_map/gi_zhi/ppermute | solution.py:1238
  501.1 11.3 %collective-permute-start.29 = (bf16[512,1024]{1,0:T(8,128)(2,1)S(1)}, bf16[512,1024]{1,0:T(8,128)(2,1)S(1)}, u32[]{:S(2)}, u32[]{:S(2)}) collective-permute-start(bf16[512,1024]{1,0:T(8,128)(2,1)S(1)} %convolution_convert_fusion), channel_id=1, source_target_pairs={{0,4},{4,0},{1,5},{5,1},{2,6},{6,2},{3,7},{7,3},{8,12},{12,8},{9,1... | collective-permute-start | bytes 3145736 | tf_op jit(solution)/shard_map/dx_zc/ppermute | solution.py:1238
  506.0 23.4 %collective-permute-start.27 = (bf16[512,1024]{1,0:T(8,128)(2,1)S(1)}, bf16[512,1024]{1,0:T(8,128)(2,1)}, u32[]{:S(2)}, u32[]{:S(2)}) collective-permute-start(bf16[512,1024]{1,0:T(8,128)(2,1)S(1)} %copy-done.10), channel_id=1, source_target_pairs={{2,4},{4,2},{3,5},{5,3},{10,12},{12,10},{11,13},{13,11},{18,20},{2... | collective-permute-start | bytes 3145736 | tf_op jit(solution)/shard_map/re_out/ppermute | solution.py:1247
  509.8 53.2 %collective-permute-start.28 = (bf16[512,1024]{1,0:T(8,128)(2,1)}, bf16[512,1024]{1,0:T(8,128)(2,1)}, u32[]{:S(2)}, u32[]{:S(2)}) collective-permute-start(bf16[512,1024]{1,0:T(8,128)(2,1)} %convolution_convert_fusion.1), channel_id=1, source_target_pairs={{0,4},{4,0},{1,5},{5,1},{2,6},{6,2},{3,7},{7,3},{8,12},{12,8},{9,1... | collective-permute-start | bytes 3145736 | tf_op jit(solution)/shard_map/dx_c/ppermute | solution.py:1238
  514.4 48.5 %collective-permute-start.30 = (bf16[512,1024]{1,0:T(8,128)(2,1)}, bf16[512,1024]{1,0:T(8,128)(2,1)}, u32[]{:S(2)}, u32[]{:S(2)}) collective-permute-start(bf16[512,1024]{1,0:T(8,128)(2,1)} %add_convert_fusion.3), channel_id=1, source_target_pairs={{0,1},{1,0},{2,3},{3,2},{4,5},{5,4},{6,7},{7,6},{8,9},{9,8},{10,11... | collective-permute-start | bytes 3145736 | tf_op jit(solution)/shard_map/dx_z/ppermute | solution.py:1238
  532.8 30.1 %collective-permute-start.31 = (bf16[256,1024]{1,0:T(8,128)(2,1)}, bf16[256,1024]{1,0:T(8,128)(2,1)}, u32[]{:S(2)}, u32[]{:S(2)}) collective-permute-start(bf16[256,1024]{1,0:T(8,128)(2,1)} %copy.73), channel_id=1, source_target_pairs={{0,2},{2,0},{1,3},{3,1},{4,6},{6,4},{5,7},{7,5},{8,10},{10,8},{9,1... | collective-permute-start | bytes 1572872 | tf_op jit(solution)/shard_map/gc_zhi/ppermute | solution.py:1238
  567.4 57.6 %collective-permute-start.32 = (bf16[512,1024]{1,0:T(8,128)(2,1)S(1)}, bf16[512,1024]{1,0:T(8,128)(2,1)S(1)}, u32[]{:S(2)}, u32[]{:S(2)}) collective-permute-start(bf16[512,1024]{1,0:T(8,128)(2,1)S(1)} %fusion.25), channel_id=1, source_target_pairs={{2,4},{4,2},{3,5},{5,3},{10,12},{12,10},{11,13},{13,11},{18,20},{2... | collective-permute-start | bytes 3145736 | tf_op jit(solution)/shard_map/re_dgrad/ppermute | solution.py:1247
  (79 other events, 681.8 us)
Sparse Core Ops, SparseCore 0:
  100.5 51.2 all-gather.2
  153.6 87.6 all-gather.4
  328.2 52.6 reduce-scatter.5
  383.9 52.6 reduce-scatter.3
  441.2 52.3 reduce-scatter.7

commit v5 on v4

--- a/solution.py
+++ b/solution.py
@@ -634,55 +634,138 @@
     )
 
 
-def hidden_kernel(x_ref, e_ref, w_in_ref, w_out_ref, bias_ref, act_ref, grad_ref, sum_ref):
+def hidden_kernel(x0_ref, x1_ref, e0_ref, e1_ref, w_in_ref, w_out_ref, bias_ref, act_ref, grad_ref, sum_ref):
     chunk = 256
     sum_ref[...] = jnp.zeros_like(sum_ref)
-
-    def step(index, carry):
-        rows = pl.ds(pl.multiple_of(index * chunk, chunk), chunk)
-        value = dot_nn(x_ref[rows, :], w_in_ref[...]) + bias_ref[...]
-        upper = dot_nn(e_ref[rows, :], w_out_ref[...])
-        square = value * value
-        inner = jnp.tanh(value * (GELU_C + (GELU_C * GELU_A) * square))
-        half = 0.5 + 0.5 * inner
-        act_ref[rows, :] = (value * half).astype(act_ref.dtype)
-        slope = half + (value * (half * (1.0 - inner))) * (GELU_C + (3.0 * GELU_C * GELU_A) * square)
-        grad = (upper * slope).astype(grad_ref.dtype)
-        grad_ref[rows, :] = grad
-        sum_ref[...] += jnp.sum(grad.astype(jnp.float32), axis=0, keepdims=True)
-        return carry
-
-    lax.fori_loop(0, x_ref.shape[0] // chunk, step, 0, unroll=2)
+    count = x0_ref.shape[0]
+
+    for which, (x_ref, e_ref) in enumerate(((x0_ref, e0_ref), (x1_ref, e1_ref))):
+
+        def step(index, carry, which=which, x_ref=x_ref, e_ref=e_ref):
+            rows = pl.ds(pl.multiple_of(index * chunk, chunk), chunk)
+            out_rows = pl.ds(pl.multiple_of(which * count + index * chunk, chunk), chunk)
+            value = dot_nn(x_ref[rows, :], w_in_ref[...]) + bias_ref[...]
+            upper = dot_nn(e_ref[rows, :], w_out_ref[...])
+            square = value * value
+            inner = jnp.tanh(value * (GELU_C + (GELU_C * GELU_A) * square))
+            half = 0.5 + 0.5 * inner
+            act_ref[out_rows, :] = (value * half).astype(act_ref.dtype)
+            slope = half + (value * (half * (1.0 - inner))) * (GELU_C + (3.0 * GELU_C * GELU_A) * square)
+            grad = (upper * slope).astype(grad_ref.dtype)
+            grad_ref[out_rows, :] = grad
+            sum_ref[...] += jnp.sum(grad.astype(jnp.float32), axis=0, keepdims=True)
+            return carry
+
+        lax.fori_loop(0, count // chunk, step, 0, unroll=2)
 
 
 def hidden_units(rows, grads, weights, bias, tile=512):
-    count, model = rows.shape
+    count, model = rows[0].shape
     width = weights.shape[1] // 2
     tiles = width // tile
     whole = pl.BlockSpec((count, model), lambda i: (0, 0))
     weight = pl.BlockSpec((model, tile), lambda i: (0, i))
     weight_out = pl.BlockSpec((model, tile), lambda i: (0, tiles + i))
     line = pl.BlockSpec((1, tile), lambda i: (0, i))
-    out = pl.BlockSpec((count, tile), lambda i: (0, i))
+    out = pl.BlockSpec((2 * count, tile), lambda i: (0, i))
     return pl.pallas_call(
         hidden_kernel,
-        grid=(width // tile,),
-        in_specs=[whole, whole, weight, weight_out, line],
+        grid=(tiles,),
+        in_specs=[whole] * 4 + [weight, weight_out, line],
         out_specs=[out, out, line],
         out_shape=[
-            jax.ShapeDtypeStruct((count, width), jnp.bfloat16),
-            jax.ShapeDtypeStruct((count, width), jnp.bfloat16),
+            jax.ShapeDtypeStruct((2 * count, width), jnp.bfloat16),
+            jax.ShapeDtypeStruct((2 * count, width), jnp.bfloat16),
             jax.ShapeDtypeStruct((1, width), jnp.float32),
         ],
         cost_estimate=pl.CostEstimate(
-            flops=4 * count * model * width,
-            bytes_accessed=4 * (count * model + model * width + count * width),
-            transcendentals=count * width,
+            flops=8 * count * model * width,
+            bytes_accessed=4 * (2 * count * model + model * width + 2 * count * width),
+            transcendentals=2 * count * width,
         ),
-    )(rows, grads, weights, weights, bias)
+    )(*rows, *grads, weights, weights, bias)
 
 
 MESH = pl.DeviceIdType.MESH
+
+
+def weight_grad_kernel(*refs):
+    rows_ref, refs = refs[0], refs[1:]
+    sides, (rows_out, *outs, turned, send, recv) = (refs[:6], refs[6:12]), refs[12:]
+    count, depth = sides[0][0].shape[0], sides[0][4].shape[0]
+    step_of, tiles = pl.program_id(0), pl.num_programs(0) // 2
+
+    def copy():
+        return pltpu.make_async_remote_copy(
+            src_ref=rows_ref,
+            dst_ref=rows_out,
+            send_sem=send,
+            recv_sem=recv,
+            device_id={"zlo": 1 - lax.axis_index("zlo")},
+            device_id_type=MESH,
+        )
+
+    @pl.when(step_of == 0)
+    def _():
+        barrier = pltpu.get_barrier_semaphore()
+        pl.semaphore_signal(
+            barrier, inc=1, device_id={"zlo": 1 - lax.axis_index("zlo")}, device_id_type=MESH
+        )
+        pl.semaphore_wait(barrier, 1)
+        copy().start()
+
+    for half, ((x0_ref, x1_ref, x2_ref, x3_ref, near_ref, far_ref), out_ref) in enumerate(zip(sides, outs)):
+
+        @pl.when(step_of == half * tiles)
+        def _(blocks=(x0_ref, x1_ref, x2_ref, x3_ref)):
+            for which, x_ref in enumerate(blocks):
+                turned[:, which * count : (which + 1) * count] = jnp.transpose(x_ref[...])
+
+        @pl.when(step_of // tiles == half)
+        def _(near_ref=near_ref, far_ref=far_ref, out_ref=out_ref):
+            def step(index, carry):
+                rows = pl.ds(pl.multiple_of(index * 256, 256), 256)
+                total = dot_nn(turned[rows, :depth], near_ref[...]) + dot_nn(turned[rows, depth:], far_ref[...])
+                out_ref[rows, :] = total.astype(out_ref.dtype)
+                return carry
+
+            lax.fori_loop(0, out_ref.shape[0] // 256, step, 0, unroll=2)
+
+    @pl.when(step_of == 2 * tiles - 1)
+    def _():
+        copy().wait()
+
+
+def weight_grads(rows, first, second, collective_id, tile=512):
+    blocks, near, _ = first
+    (count, model), (depth, width) = blocks[0].shape, near.shape
+    tiles = width // tile
+    anywhere = pl.BlockSpec(memory_space=pl.ANY)
+    whole = pl.BlockSpec((count, model), lambda i: (0, 0))
+
+    def early(size):
+        return pl.BlockSpec((size, tile), lambda i: (0, jnp.minimum(i, tiles - 1)))
+
+    def late(size):
+        return pl.BlockSpec((size, tile), lambda i: (0, jnp.maximum(i - tiles, 0)))
+
+    shape = jax.ShapeDtypeStruct((model, width), near.dtype)
+    return pl.pallas_call(
+        weight_grad_kernel,
+        grid=(2 * tiles,),
+        in_specs=[anywhere] + [whole] * 4 + [early(depth)] * 2 + [whole] * 4 + [late(depth)] * 2,
+        out_specs=[anywhere, early(model), late(model)],
+        out_shape=[jax.ShapeDtypeStruct(rows.shape, rows.dtype), shape, shape],
+        scratch_shapes=[
+            pltpu.VMEM((model, 4 * count), near.dtype),
+            pltpu.SemaphoreType.DMA,
+            pltpu.SemaphoreType.DMA,
+        ],
+        compiler_params=pltpu.CompilerParams(collective_id=collective_id, has_side_effects=True),
+        cost_estimate=pl.CostEstimate(flops=16 * count * model * width, bytes_accessed=0, transcendentals=0),
+    )(rows, *first[0], *first[1:], *second[0], *second[1:])
+
+
 LINKS = ("core", "x", "y", "zhi", "zlo")
 
 
@@ -1387,7 +1470,7 @@
     after_one = resid + (branch + vectors[6])
 
     cot_beyond = trade(after(grad_rows, after_one), "zlo", "cot_z")
-    cot_near = jnp.concatenate([grad_rows, trade(grad_rows, "core", "cot_c")], axis=0)
+    cot_near = [grad_rows, trade(grad_rows, "core", "cot_c")]
 
     normed_mid, hat_two, inv_two = norm_forward(after_one, vectors[1], vectors[4])
     cross_low = low(normed_mid)
@@ -1406,11 +1489,11 @@
     normed_out, hat_three, inv_three = norm_forward(after_two, vectors[2], vectors[5])
     mlp_in = low(normed_out)
     beyond = trade(mlp_in, "zlo", "mlp_z")
-    mlp_near = jnp.concatenate([mlp_in, trade(mlp_in, "core", "mlp_c")], axis=0)
+    mlp_near = [mlp_in, trade(mlp_in, "core", "mlp_c")]
     act_near, dpre_near, sum_near = hidden_units(mlp_near, cot_near, w_hidden, hidden_bias[None])
     beyond = after(beyond, act_near)
-    mlp_far = jnp.concatenate([beyond, trade(beyond, "core", "mlp_zc")], axis=0)
-    cot_far = jnp.concatenate([cot_beyond, trade(cot_beyond, "core", "cot_zc")], axis=0)
+    mlp_far = [beyond, trade(beyond, "core", "mlp_zc")]
+    cot_far = [cot_beyond, trade(cot_beyond, "core", "cot_zc")]
     act_far, dpre_far, sum_far = hidden_units(mlp_far, cot_far, w_hidden, hidden_bias[None])
     gradient = grad_rows.astype(jnp.float32)
     bias_out_three = jnp.sum(gradient, axis=0)
@@ -1430,10 +1513,10 @@
     ]
     out_far = low(out_parts[1] + trade(out_parts[0], "core", "out_zc"))
     out_branch = out_parts[3] + trade(out_parts[2], "core", "out_c")
-    grad_w_out = low(product_left_t(cot_near, act_near) + product_left_t(cot_far, act_far))
-    mlp_near, mlp_far = after(mlp_near, grad_w_out), after(mlp_far, grad_w_out)
-    grad_w_in = low(product_left_t(mlp_near, dpre_near) + product_left_t(mlp_far, dpre_far))
-    mlp_term = mlp_term + after(trade(dmlp_far, "zlo", "dmlp_z"), grad_w_in, grad_w_out)
+    dmlp_beyond, grad_w_out, grad_w_in = weight_grads(
+        dmlp_far, (cot_near + cot_far, act_near, act_far), (mlp_near + mlp_far, dpre_near, dpre_far), 2
+    )
+    mlp_term = mlp_term + dmlp_beyond
     out_far = trade(after(out_far, mlp_term), "zlo", "out_z")
     part, gain_three, shift_three = norm_backward(mlp_term, hat_three, inv_three, vectors[2])
     gradient = gradient + part

time: 646 us -> 638 us (0.988)
  Pallas kernels: 260 us -> 293 us
  matrix products: 142 us -> 116 us
  local copies, waits for them, and re-layouts: 49.5 us -> 42.1 us
    pallas_call x2 -> x3, Pallas kernels: 33.8 us -> 66.1 us  [the longest x2 33.6 us: hidden_units(): pl.pallas_call(hidden_kernel, grid=(tiles,), in_specs=[whole] * 4 + [weig...]
    dot_general x13 -> x9, matrix products: 46.1 us -> 19.2 us  [product_left_t(): lax.dot_general(left, right, (((0,), (0,)), ((), ())), preferred_element_...]
    ppermute x29 -> x28, waiting for transfers between devices: 93.4 us -> 82.1 us  [trade(): return lax.ppermute(rows, axis, [(0, 1), (1, 0)])]
    unnamed x172 -> x162, local copies, waits for them, and re-layouts: 26.9 us -> 22.3 us
    ppermute x29 -> x28, starting transfers between devices: 23 us -> 25.5 us  [trade(): return lax.ppermute(rows, axis, [(0, 1), (1, 0)])]
  transfers between devices with their start and end apart: 38 -> 37, of which waited for: 12 -> 13; matrix products, arithmetic and copies ran while one was open for 31% -> 27% of each run, Pallas kernels for 28% -> 28%
where the time goes in v5:
time: 638 us; the launch traced here: 628 us
  Pallas kernels  293 us (46%)
  matrix products  116 us (18%)
  waiting for transfers between devices  88.4 us (14%)
  local copies, waits for them, and re-layouts  42.1 us (7%)
  other arithmetic  41.2 us (6%)
  starting transfers between devices  31.4 us (5%)
  between operations  15.8 us (2%)
    pallas_call x1, Pallas kernels, start_exchange(): pl.pallas_call(start_kernel, out_shape=shapes, in_specs=[anywhere] * 7, o...  85.2 us
    ppermute x28, waiting for transfers between devices, trade(): return lax.ppermute(rows, axis, [(0, 1), (1, 0)])  82.1 us
    dot_general x22, matrix products, product_right_t(): lax.dot_general(left, right, (((1,), (1,)), ((), ())), preferred_element_...  75.7 us
    pallas_call x2, Pallas kernels, attend_back(): pl.pallas_call(functools.partial(backward_kernel, sections), grid_spec=pl...  56.3 us
    pallas_call x1, Pallas kernels, finish(): pl.pallas_call(finish_kernel, out_shape=shapes, in_specs=[anywhere] * 10,...  47.3 us
    pallas_call x2, Pallas kernels, attend(): pl.pallas_call(functools.partial(forward_kernel, sections), grid_spec=plt...  38.4 us
    pallas_call x2, Pallas kernels, hidden_units(): pl.pallas_call(hidden_kernel, grid=(tiles,), in_specs=[whole] * 4 + [weig...  33.6 us
    pallas_call x1, Pallas kernels, weight_grads(): pl.pallas_call(weight_grad_kernel, grid=(2 * tiles,), in_specs=[anywhere]...  32.5 us
  transfers between devices with their start and end apart: 37, of which 13 were waited for; matrix products, arithmetic and copies ran while one was open for 27% of the time, Pallas kernels for 28%

profile of v5, /device:TPU:0, one launch (start us, length us, event | category | flops | bytes accessed | tf_op | source)
XLA Modules:
  0.0 627.9 jit_solution(14921984655316975401)
XLA Ops:
  15.1 85.2 %shard_map.229 = (bf16[512,1024]{1,0:T(8,128)(2,1)}, bf16[2048,1024]{1,0:T(8,128)(2,1)}, bf16[4,2,2,256,256]{4,3,2,1,0:T(8,128)(2,1)}, bf16[256,2048]{1,0:T(8,12...) custom-call(bf16[512,1024]{1,0:T(8,128)(2,1)} %tokens.1, ...), custom_call_target="tpu_custom_call" | custom-call | tf_op jit(solution)/shard_map/pallas_call | solution.py:1000
  101.8 5.0 collective-permute-start.1
  111.3 4.8 multiply_convert_fusion.q_ref.k_ref.v_ref
  117.0 23.2 %shard_map.230 = (bf16[2048,256]{1,0:T(8,128)(2,1)}, f32[2048,256]{1,0:T(8,128)}) custom-call(s32[13]{0:T(128)} %concatenate.66.meta_ref, bf16[2048,768]{1,0:T(8,128)(2,1)} %multiply_convert_fusion.q_ref.k_ref.v_ref, bf16[2048,768]{1,0:T(8,128)(2,1)} %multiply_convert_fusion.q_ref.k_ref.v_ref, bf16[2048,768]{1,0:T(8,128)(2,1)} %multiply_convert_fusion.q_ref.k_ref.v_ref), custom_call_target="tpu_custom_call" | custom-call | flops 19327352832 | bytes 5242880 | tf_op jit(solution)/shard_map/pallas_call | solution.py:180
  140.2 11.2 %collective-permute-done.1 = bf16[2,256,1024]{2,1,0:T(8,128)(2,1)S(1)} collective-permute-done((bf16[2,256,1024]{2,1,0:T(8,128)(2,1)}, bf16[2,256,1024]{2,1,0:T(8,128)(2,1)S(1)}, u32[]{:S(2)}, u32[]{:S(2)}) %collective-permute-start.1) | collective-permute-done | bytes 1048608 | tf_op jit(solution)/shard_map/wh_zhi/ppermute | solution.py:1321
  172.7 4.3 add_convert_fusion.7.k_ref.v_ref
  177.0 24.5 %collective-permute-done.4 = bf16[512,1024]{1,0:T(8,128)(2,1)} collective-permute-done((bf16[512,1024]{1,0:T(8,128)(2,1)}, bf16[512,1024]{1,0:T(8,128)(2,1)}, u32[]{:S(2)}, u32[]{:S(2)}) %collective-permute-start.4) | collective-permute-done | bytes 1048608 | tf_op jit(solution)/shard_map/so_z/ppermute | solution.py:1321
  212.2 15.2 %shard_map.231 = (bf16[1024,512]{1,0:T(8,128)(2,1)}, f32[1024,512]{1,0:T(8,128)}) custom-call(s32[1]{0:T(128)} %slice.202.meta_ref, bf16[1024,512]{1,0:T(8,128)(2,1)} %multiply_convert_fusion.1.q_ref, bf16[512,1024]{1,0:T(8,128)(2,1)} %add_convert_fusion.7.k_ref.v_ref, bf16[512,1024]{1,0:T(8,128)(2,1)} %add_convert_fusion.7.k_ref.v_ref), custom_call_target="tpu_custom_call" | custom-call | flops 8589934592 | bytes 5242880 | tf_op jit(solution)/shard_map/pallas_call | solution.py:180
  227.3 4.1 collective-permute-done.7.e0_ref.refs_3_
  244.4 16.7 %shard_map.232 = (bf16[1024,2048]{1,0:T(8,128)(2,1)}, bf16[1024,2048]{1,0:T(8,128)(2,1)}, f32[1,2048]{1,0:T(1,128)}) custom-call(bf16[512,1024]{1,0:T(8,128)(2,1)} %add_convert_fusion.5.x0_ref.refs_7_, bf16[512,1024]{1,0:T(8,128)(2,1)} %collective-permute-done.9.x1_ref.refs_8_, bf16[512,1024]{1,0:T(8,128)(2,1)} %get-tuple-element.89.e0_ref.refs_1_, ...), custom_call_target="tpu_custom_call" | custom-call | flops 8589934592 | bytes 20971520 | tf_op jit(solution)/shard_map/pallas_call | solution.py:671
  261.1 6.1 collective-permute-done.11.x0_ref.refs_9_
  267.2 6.2 fusion.49
  273.9 16.9 %shard_map.233 = (bf16[1024,2048]{1,0:T(8,128)(2,1)}, bf16[1024,2048]{1,0:T(8,128)(2,1)}, f32[1,2048]{1,0:T(1,128)}) custom-call(bf16[512,1024]{1,0:T(8,128)(2,1)} %collective-permute-done.11.x0_ref.refs_9_, bf16[512,1024]{1,0:T(8,128)(2,1)} %collective-permute-done.12.x1_ref.refs_10_, bf16[512,1024]{1,0:T(8,128)(2,1)} %copy-done.60, ...), custom_call_target="tpu_custom_call" | custom-call | flops 8589934592 | bytes 20971520 | tf_op jit(solution)/shard_map/pallas_call | solution.py:671
  290.8 5.3 fusion.44
  296.3 6.3 %convert_add_fusion.5 = f32[512,1024]{1,0:T(8,128)} fusion(bf16[512,1024]{1,0:T(8,128)(2,1)} %collective-permute-done.15, bf16[1024,4096]{1,0:T(8,128)(2,1)} %all-gather.5.cloned.1.call-done.w_in_ref.w_out_ref, bf16[1024,2048]{1,0:T(8,128)(2,1)S(1)} %copy-done.62), kind=kOutput, calls=%fused_computation.62 | convolution fusion | flops 2148532224 | bytes 9437184 | tf_op jit(solution)/shard_map/dot_general | solution.py:278
  306.0 32.5 %shard_map.234 = (bf16[512,1024]{1,0:T(8,128)(2,1)}, bf16[1024,2048]{1,0:T(8,128)(2,1)}, bf16[1024,2048]{1,0:T(8,128)(2,1)}) custom-call(bf16[512,1024]{1,0:T(8,128)(2,1)} %add_convert_fusion.4.refs_0_, bf16[512,1024]{1,0:T(8,128)(2,1)} %get-tuple-element.89.e0_ref.refs_1_, bf16[512,1024]{1,0:T(8,128)(2,1)} %collective-permute-done.10.e1_ref.refs_2_, ...), custom_call_target="tpu_custom_call" | custom-call | flops 17179869184 | tf_op jit(solution)/shard_map/pallas_call | solution.py:753
  338.9 6.3 %fusion.59 = bf16[512,1024]{1,0:T(8,128)(2,1)} fusion(bf16[1024,4096]{1,0:T(8,128)(2,1)} %all-gather.5.cloned.1.call-done.w_in_ref.w_out_ref, bf16[1024,2048]{1,0:T(8,128)(2,1)} %get-tuple-element.98.refs_6_), kind=kOutput, calls=%fused_computation.96 | convolution fusion | flops 2148007936 | bytes 7340032 | tf_op jit(solution)/shard_map/dot_general | solution.py:278
  347.0 4.3 convert_reduce_fusion.5
  352.3 6.7 %add_convert_fusion.3 = bf16[512,1024]{1,0:T(8,128)(2,1)} fusion(bf16[512,1024]{1,0:T(8,128)(2,1)} %collective-permute-done.17, bf16[1024,4096]{1,0:T(8,128)(2,1)} %all-gather.5.cloned.1.call-done.w_in_ref.w_out_ref, bf16[1024,2048]{1,0:T(8,128)(2,1)} %get-tuple-element.98.refs_6_), kind=kOutput, calls=%fused_computation.57 | convolution fusion | flops 2149056512 | bytes 8388608 | tf_op jit(solution)/shard_map/dot_general | solution.py:278
  359.1 4.4 convolution_convert_fusion.4.do_ref
  363.4 18.7 %shard_map.235 = (bf16[1024,512]{1,0:T(8,128)(2,1)}, bf16[512,512]{1,0:T(8,128)(2,1)}, bf16[512,512]{1,0:T(8,128)(2,1)}) custom-call(s32[1]{0:T(128)} %slice.202.meta_ref, bf16[1024,512]{1,0:T(8,128)(2,1)} %multiply_convert_fusion.1.q_ref, bf16[512,1024]{1,0:T(8,128)(2,1)} %add_convert_fusion.7.k_ref.v_ref, bf16[512,1024]{1,0:T(8,128)(2,1)} %add_convert_fusion.7.k_ref.v_ref, ...), custom_call_target="tpu_custom_call" | custom-call | flops 21474836480 | bytes 10485760 | tf_op jit(solution)/shard_map/pallas_call | solution.py:202
  386.8 6.4 %fusion.54 = bf16[512,1024]{1,0:T(8,128)(2,1)} fusion(bf16[1024,4096]{1,0:T(8,128)(2,1)} %all-gather.5.cloned.1.call-done.w_in_ref.w_out_ref, bf16[1024,2048]{1,0:T(8,128)(2,1)} %get-tuple-element.96.refs_5_), kind=kOutput, calls=%fused_computation.95 | convolution fusion | flops 2148007936 | bytes 7340032 | tf_op jit(solution)/shard_map/dot_general | solution.py:278
  414.0 4.0 add_convert_fusion.2
  421.2 10.9 %collective-permute-done.22 = bf16[512,1024]{1,0:T(8,128)(2,1)} collective-permute-done((bf16[512,1024]{1,0:T(8,128)(2,1)}, bf16[512,1024]{1,0:T(8,128)(2,1)}, u32[]{:S(2)}, u32[]{:S(2)}) %collective-permute-start.22) | collective-permute-done | bytes 1048608 | tf_op jit(solution)/shard_map/e1_z/ppermute | solution.py:1321
  440.7 6.1 reduce-scatter.4.cloned.1.call-done
  451.1 37.6 %shard_map.236 = (bf16[2048,256]{1,0:T(8,128)(2,1)}, bf16[2048,256]{1,0:T(8,128)(2,1)}, bf16[2048,256]{1,0:T(8,128)(2,1)}) custom-call(s32[13]{0:T(128)} %concatenate.66.meta_ref, bf16[2048,768]{1,0:T(8,128)(2,1)} %multiply_convert_fusion.q_ref.k_ref.v_ref, bf16[2048,768]{1,0:T(8,128)(2,1)} %multiply_convert_fusion.q_ref.k_ref.v_ref, ...), custom_call_target="tpu_custom_call" | custom-call | flops 48318382080 | bytes 10485760 | tf_op jit(solution)/shard_map/pallas_call | solution.py:202
  511.5 4.3 convolution_convert_fusion.12
  525.3 9.6 %collective-permute-start.30 = (bf16[256,1024]{1,0:T(8,128)(2,1)}, bf16[256,1024]{1,0:T(8,128)(2,1)}, u32[]{:S(2)}, u32[]{:S(2)}) collective-permute-start(bf16[256,1024]{1,0:T(8,128)(2,1)} %copy.73), channel_id=1, source_target_pairs={{0,2},{2,0},{1,3},{3,1},{4,6},{6,4},{5,7},{7,5},{8,10},{10,8},{9,1... | collective-permute-start | bytes 1572872 | tf_op jit(solution)/shard_map/gc_zhi/ppermute | solution.py:1321
  535.1 4.7 convolution_convert_fusion.13
  541.9 7.2 %collective-permute-done.29 = bf16[512,1024]{1,0:T(8,128)(2,1)} collective-permute-done((bf16[512,1024]{1,0:T(8,128)(2,1)}, bf16[512,1024]{1,0:T(8,128)(2,1)}, u32[]{:S(2)}, u32[]{:S(2)}) %collective-permute-start.29) | collective-permute-done | bytes 1048608 | tf_op jit(solution)/shard_map/dx_z/ppermute | solution.py:1321
  549.1 8.3 %collective-permute-done.30.cross_beyond = bf16[256,1024]{1,0:T(8,128)(2,1)} collective-permute-done((bf16[256,1024]{1,0:T(8,128)(2,1)}, bf16[256,1024]{1,0:T(8,128)(2,1)}, u32[]{:S(2)}, u32[]{:S(2)}) %collective-permute-start.30) | collective-permute-done | bytes 524320 | tf_op jit(solution)/shard_map/gc_zhi/ppermute | solution.py:1321
  563.0 47.3 %shard_map.237 = (f32[128,2048]{1,0:T(8,128)}, f32[128,2048]{1,0:T(8,128)}, f32[3,128,256]{2,1,0:T(8,128)}, f32[128,256]{1,0:T(8,128)}, f32[3,128,256]{2,1,0:T(8...) custom-call(f32[256,1024]{1,0:T(8,128)} %convert_add_fusion.7.ff_in, ...), custom_call_target="tpu_custom_call" | custom-call | flops 40000000000 | tf_op jit(solution)/shard_map/pallas_call | solution.py:1287
  (365 shorter events, 157.5 us)
Async XLA Ops:
  7.2 165.5 %all-gather.3.cloned.1.call-start = ((), (), s32[]{:S(2)}) async-start(), calls=%async_computation.3 | async-start | bytes 5242880 | tf_op jit(solution)/shard_map/all_gather | solution.py:1350
  100.4 144.0 %all-gather.5.cloned.1.call-start = ((), (), s32[]{:S(2)}) async-start(), calls=%async_computation.4 | async-start | bytes 10485760 | tf_op jit(solution)/shard_map/all_gather | solution.py:1350
  101.2 14.9 %collective-permute-start = (s32[9]{0:T(128)S(1)}, s32[9]{0:T(128)S(1)}, u32[]{:S(2)}, u32[]{:S(2)}) collective-permute-start(s32[9]{0:T(128)S(1)} %pad_add_fusion), channel_id=1, source_target_pairs={{2,4},{4,2},{3,5},{5,3},{10,12},{12,10},{11,13},{13,11},{18,20},{2... | collective-permute-start | bytes 116 | tf_op jit(solution)/shard_map/re_regroup/ppermute | solution.py:1330
  101.8 49.6 %collective-permute-start.1 = (bf16[2,256,1024]{2,1,0:T(8,128)(2,1)}, bf16[2,256,1024]{2,1,0:T(8,128)(2,1)S(1)}, u32[]{:S(2)}, u32[]{:S(2)}) collective-permute-start(bf16[2,256,1024]{2,1,0:T(8,128)(2,1)} %get-tuple-element.81), channel_id=1, source_target_pairs={{0,2},{2,0},{1,3},{3,1},{4,6},{6,4},{5,7},{7,5},{8,10},{10,8},{9,1... | collective-permute-start | bytes 3145736 | tf_op jit(solution)/shard_map/wh_zhi/ppermute | solution.py:1321
  153.3 285.2 %reduce-scatter.6.cloned.1.call-start = ((), (), s32[]{:S(2)}) async-start(), calls=%async_computation.6 | async-start | bytes 5242880 | tf_op jit(solution)/shard_map/reduce_scatter | solution.py:1354
  156.9 12.5 %collective-permute-start.5 = (bf16[512,1024]{1,0:T(8,128)(2,1)}, bf16[512,1024]{1,0:T(8,128)(2,1)}, u32[]{:S(2)}, u32[]{:S(2)}) collective-permute-start(bf16[512,1024]{1,0:T(8,128)(2,1)} %param.18), channel_id=1, source_target_pairs={{2,4},{4,2},{3,5},{5,3},{10,12},{12,10},{11,13},{13,11},{18,20},{2... | collective-permute-start | bytes 3145736 | tf_op jit(solution)/shard_map/re_cotangent/ppermute | solution.py:1330
  160.6 40.8 %collective-permute-start.2 = (bf16[512,1024]{1,0:T(8,128)(2,1)}, bf16[512,1024]{1,0:T(8,128)(2,1)S(1)}, u32[]{:S(2)}, u32[]{:S(2)}) collective-permute-start(bf16[512,1024]{1,0:T(8,128)(2,1)} %convolution_convert_fusion.6), channel_id=1, source_target_pairs={{0,4},{4,0},{1,5},{5,1},{2,6},{6,2},{3,7},{7,3},{8,12},{12,8},{9,1... | collective-permute-start | bytes 3145736 | tf_op jit(solution)/shard_map/so_c/ppermute | solution.py:1321
  164.3 37.1 %collective-permute-start.4 = (bf16[512,1024]{1,0:T(8,128)(2,1)}, bf16[512,1024]{1,0:T(8,128)(2,1)}, u32[]{:S(2)}, u32[]{:S(2)}) collective-permute-start(bf16[512,1024]{1,0:T(8,128)(2,1)} %add_convert_fusion.8), channel_id=1, source_target_pairs={{0,1},{1,0},{2,3},{3,2},{4,5},{5,4},{6,7},{7,6},{8,9},{9,8},{10,11... | collective-permute-start | bytes 3145736 | tf_op jit(solution)/shard_map/so_z/ppermute | solution.py:1321
  205.8 25.7 %collective-permute-start.7 = (bf16[512,1024]{1,0:T(8,128)(2,1)}, bf16[512,1024]{1,0:T(8,128)(2,1)S(1)}, u32[]{:S(2)}, u32[]{:S(2)}) collective-permute-start(bf16[512,1024]{1,0:T(8,128)(2,1)} %get-tuple-element.89.e0_ref.refs_1_), channel_id=1, source_target_pairs={{0,1},{1,0},{2,3},{3,2},{4,5},{5,4},{6,7},{7,6},{8,9},{9,8},{10,11... | collective-permute-start | bytes 3145736 | tf_op jit(solution)/shard_map/cot_z/ppermute | solution.py:1321
  234.1 8.5 %collective-permute-start.10 = (bf16[512,1024]{1,0:T(8,128)(2,1)}, bf16[512,1024]{1,0:T(8,128)(2,1)}, u32[]{:S(2)}, u32[]{:S(2)}) collective-permute-start(bf16[512,1024]{1,0:T(8,128)(2,1)} %get-tuple-element.89.e0_ref.refs_1_), channel_id=1, source_target_pairs={{0,4},{4,0},{1,5},{5,1},{2,6},{6,2},{3,7},{7,3},{8,12},{12,8},{9,1... | collective-permute-start | bytes 3145736 | tf_op jit(solution)/shard_map/cot_c/ppermute | solution.py:1321
  241.5 25.8 %collective-permute-start.11 = (bf16[512,1024]{1,0:T(8,128)(2,1)}, bf16[512,1024]{1,0:T(8,128)(2,1)}, u32[]{:S(2)}, u32[]{:S(2)}) collective-permute-start(bf16[512,1024]{1,0:T(8,128)(2,1)} %add_convert_fusion.5.x0_ref.refs_7_), channel_id=1, source_target_pairs={{0,1},{1,0},{2,3},{3,2},{4,5},{5,4},{6,7},{7,6},{8,9},{9,8},{10,11... | collective-permute-start | bytes 3145736 | tf_op jit(solution)/shard_map/mlp_z/ppermute | solution.py:1321
  242.4 31.5 %collective-permute-start.13 = (bf16[512,1024]{1,0:T(8,128)(2,1)}, bf16[512,1024]{1,0:T(8,128)(2,1)}, u32[]{:S(2)}, u32[]{:S(2)}) collective-permute-start(bf16[512,1024]{1,0:T(8,128)(2,1)} %copy-done.60), channel_id=1, source_target_pairs={{0,4},{4,0},{1,5},{5,1},{2,6},{6,2},{3,7},{7,3},{8,12},{12,8},{9,1... | collective-permute-start | bytes 3145736 | tf_op jit(solution)/shard_map/cot_zc/ppermute | solution.py:1321
  267.2 6.7 %collective-permute-start.12 = (bf16[512,1024]{1,0:T(8,128)(2,1)}, bf16[512,1024]{1,0:T(8,128)(2,1)}, u32[]{:S(2)}, u32[]{:S(2)}) collective-permute-start(bf16[512,1024]{1,0:T(8,128)(2,1)} %collective-permute-done.11.x0_ref.refs_9_), channel_id=1, source_target_pairs={{0,4},{4,0},{1,5},{5,1},{2,6},{6,2},{3,7},{7,3},{8,12},{12,8},{9,1... | collective-permute-start | bytes 3145736 | tf_op jit(solution)/shard_map/mlp_zc/ppermute | solution.py:1321
  273.4 22.9 %collective-permute-start.15 = (bf16[512,1024]{1,0:T(8,128)(2,1)}, bf16[512,1024]{1,0:T(8,128)(2,1)}, u32[]{:S(2)}, u32[]{:S(2)}) collective-permute-start(bf16[512,1024]{1,0:T(8,128)(2,1)} %fusion.49), channel_id=1, source_target_pairs={{0,4},{4,0},{1,5},{5,1},{2,6},{6,2},{3,7},{7,3},{8,12},{12,8},{9,1... | collective-permute-start | bytes 3145736 | tf_op jit(solution)/shard_map/dmlp_c/ppermute | solution.py:1321
  296.2 6.4 %collective-permute-start.14 = (bf16[512,1024]{1,0:T(8,128)(2,1)S(1)}, bf16[512,1024]{1,0:T(8,128)(2,1)S(1)}, u32[]{:S(2)}, u32[]{:S(2)}) collective-permute-start(bf16[512,1024]{1,0:T(8,128)(2,1)S(1)} %fusion.44), channel_id=1, source_target_pairs={{0,4},{4,0},{1,5},{5,1},{2,6},{6,2},{3,7},{7,3},{8,12},{12,8},{9,1... | collective-permute-start | bytes 3145736 | tf_op jit(solution)/shard_map/dmlp_zc/ppermute | solution.py:1321
  338.5 108.4 %reduce-scatter.4.cloned.1.call-start = ((), (), s32[]{:S(2)}) async-start(), calls=%async_computation.5 | async-start | bytes 5242880 | tf_op jit(solution)/shard_map/reduce_scatter | solution.py:1354
  345.2 7.0 %collective-permute-start.17 = (bf16[512,1024]{1,0:T(8,128)(2,1)}, bf16[512,1024]{1,0:T(8,128)(2,1)}, u32[]{:S(2)}, u32[]{:S(2)}) collective-permute-start(bf16[512,1024]{1,0:T(8,128)(2,1)} %fusion.59), channel_id=1, source_target_pairs={{0,4},{4,0},{1,5},{5,1},{2,6},{6,2},{3,7},{7,3},{8,12},{12,8},{9,1... | collective-permute-start | bytes 3145736 | tf_op jit(solution)/shard_map/out_zc/ppermute | solution.py:1321
  351.3 7.8 %collective-permute-start.19 = (bf16[512,1024]{1,0:T(8,128)(2,1)}, bf16[512,1024]{1,0:T(8,128)(2,1)}, u32[]{:S(2)}, u32[]{:S(2)}) collective-permute-start(bf16[512,1024]{1,0:T(8,128)(2,1)} %get-tuple-element.191), channel_id=1, source_target_pairs={{0,4},{4,0},{1,5},{5,1},{2,6},{6,2},{3,7},{7,3},{8,12},{12,8},{9,1... | collective-permute-start | bytes 3145736 | tf_op jit(solution)/shard_map/e2/ppermute | solution.py:1321
  352.2 170.0 %reduce-scatter.8.cloned.1.call-start = ((), (), s32[]{:S(2)}) async-start(), calls=%async_computation.7 | async-start | bytes 5242880 | tf_op jit(solution)/shard_map/reduce_scatter | solution.py:1354
  358.9 25.4 %collective-permute-start.18 = (bf16[512,1024]{1,0:T(8,128)(2,1)}, bf16[512,1024]{1,0:T(8,128)(2,1)}, u32[]{:S(2)}, u32[]{:S(2)}) collective-permute-start(bf16[512,1024]{1,0:T(8,128)(2,1)} %add_convert_fusion.3), channel_id=1, source_target_pairs={{0,1},{1,0},{2,3},{3,2},{4,5},{5,4},{6,7},{7,6},{8,9},{9,8},{10,11... | collective-permute-start | bytes 3145736 | tf_op jit(solution)/shard_map/out_z/ppermute | solution.py:1321
  386.7 13.1 %collective-permute-start.20 = (bf16[512,1024]{1,0:T(8,128)(2,1)S(1)}, bf16[512,1024]{1,0:T(8,128)(2,1)S(1)}, u32[]{:S(2)}, u32[]{:S(2)}) collective-permute-start(bf16[512,1024]{1,0:T(8,128)(2,1)S(1)} %convolution_convert_fusion.9), channel_id=1, source_target_pairs={{0,4},{4,0},{1,5},{5,1},{2,6},{6,2},{3,7},{7,3},{8,12},{12,8},{9,1... | collective-permute-start | bytes 3145736 | tf_op jit(solution)/shard_map/dcin/ppermute | solution.py:1321
  393.2 20.8 %collective-permute-start.16 = (bf16[512,1024]{1,0:T(8,128)(2,1)}, bf16[512,1024]{1,0:T(8,128)(2,1)}, u32[]{:S(2)}, u32[]{:S(2)}) collective-permute-start(bf16[512,1024]{1,0:T(8,128)(2,1)} %fusion.54), channel_id=1, source_target_pairs={{0,4},{4,0},{1,5},{5,1},{2,6},{6,2},{3,7},{7,3},{8,12},{12,8},{9,1... | collective-permute-start | bytes 3145736 | tf_op jit(solution)/shard_map/out_c/ppermute | solution.py:1321
  406.2 11.8 %collective-permute-start.21 = (bf16[512,1024]{1,0:T(8,128)(2,1)}, bf16[512,1024]{1,0:T(8,128)(2,1)}, u32[]{:S(2)}, u32[]{:S(2)}) collective-permute-start(bf16[512,1024]{1,0:T(8,128)(2,1)} %get-tuple-element.194), channel_id=1, source_target_pairs={{0,4},{4,0},{1,5},{5,1},{2,6},{6,2},{3,7},{7,3},{8,12},{12,8},{9,1... | collective-permute-start | bytes 3145736 | tf_op jit(solution)/shard_map/e1_c/ppermute | solution.py:1321
  406.3 25.8 %collective-permute-start.22 = (bf16[512,1024]{1,0:T(8,128)(2,1)}, bf16[512,1024]{1,0:T(8,128)(2,1)}, u32[]{:S(2)}, u32[]{:S(2)}) collective-permute-start(bf16[512,1024]{1,0:T(8,128)(2,1)} %get-tuple-element.194), channel_id=1, source_target_pairs={{0,1},{1,0},{2,3},{3,2},{4,5},{5,4},{6,7},{7,6},{8,9},{9,8},{10,11... | collective-permute-start | bytes 3145736 | tf_op jit(solution)/shard_map/e1_z/ppermute | solution.py:1321
  440.4 48.3 %collective-permute-start.25 = (bf16[256,1024]{1,0:T(8,128)(2,1)}, bf16[256,1024]{1,0:T(8,128)(2,1)S(1)}, u32[]{:S(2)}, u32[]{:S(2)}) collective-permute-start(bf16[256,1024]{1,0:T(8,128)(2,1)} %constant_dynamic-slice_fusion.4), channel_id=1, source_target_pairs={{0,2},{2,0},{1,3},{3,1},{4,6},{6,4},{5,7},{7,5},{8,10},{10,8},{9,1... | collective-permute-start | bytes 1572872 | tf_op jit(solution)/shard_map/go_zhi/ppermute | solution.py:1321
  448.7 41.2 %collective-permute-start.24 = (bf16[256,1024]{1,0:T(8,128)(2,1)}, bf16[256,1024]{1,0:T(8,128)(2,1)S(1)}, u32[]{:S(2)}, u32[]{:S(2)}) collective-permute-start(bf16[256,1024]{1,0:T(8,128)(2,1)} %constant_dynamic-slice_fusion.5), channel_id=1, source_target_pairs={{0,2},{2,0},{1,3},{3,1},{4,6},{6,4},{5,7},{7,5},{8,10},{10,8},{9,1... | collective-permute-start | bytes 1572872 | tf_op jit(solution)/shard_map/gi_zhi/ppermute | solution.py:1321
  494.0 11.1 %collective-permute-start.28 = (bf16[512,1024]{1,0:T(8,128)(2,1)S(1)}, bf16[512,1024]{1,0:T(8,128)(2,1)S(1)}, u32[]{:S(2)}, u32[]{:S(2)}) collective-permute-start(bf16[512,1024]{1,0:T(8,128)(2,1)S(1)} %convolution_convert_fusion), channel_id=1, source_target_pairs={{0,4},{4,0},{1,5},{5,1},{2,6},{6,2},{3,7},{7,3},{8,12},{12,8},{9,1... | collective-permute-start | bytes 3145736 | tf_op jit(solution)/shard_map/dx_zc/ppermute | solution.py:1321
  501.0 56.4 %collective-permute-start.27 = (bf16[512,1024]{1,0:T(8,128)(2,1)}, bf16[512,1024]{1,0:T(8,128)(2,1)}, u32[]{:S(2)}, u32[]{:S(2)}) collective-permute-start(bf16[512,1024]{1,0:T(8,128)(2,1)} %convolution_convert_fusion.1), channel_id=1, source_target_pairs={{0,4},{4,0},{1,5},{5,1},{2,6},{6,2},{3,7},{7,3},{8,12},{12,8},{9,1... | collective-permute-start | bytes 3145736 | tf_op jit(solution)/shard_map/dx_c/ppermute | solution.py:1321
  501.0 20.1 %collective-permute-start.26 = (bf16[512,1024]{1,0:T(8,128)(2,1)S(1)}, bf16[512,1024]{1,0:T(8,128)(2,1)}, u32[]{:S(2)}, u32[]{:S(2)}) collective-permute-start(bf16[512,1024]{1,0:T(8,128)(2,1)S(1)} %copy-done.8), channel_id=1, source_target_pairs={{2,4},{4,2},{3,5},{5,3},{10,12},{12,10},{11,13},{13,11},{18,20},{2... | collective-permute-start | bytes 3145736 | tf_op jit(solution)/shard_map/re_out/ppermute | solution.py:1330
  507.2 41.9 %collective-permute-start.29 = (bf16[512,1024]{1,0:T(8,128)(2,1)}, bf16[512,1024]{1,0:T(8,128)(2,1)}, u32[]{:S(2)}, u32[]{:S(2)}) collective-permute-start(bf16[512,1024]{1,0:T(8,128)(2,1)} %add_convert_fusion.1), channel_id=1, source_target_pairs={{0,1},{1,0},{2,3},{3,2},{4,5},{5,4},{6,7},{7,6},{8,9},{9,8},{10,11... | collective-permute-start | bytes 3145736 | tf_op jit(solution)/shard_map/dx_z/ppermute | solution.py:1321
  525.3 32.2 %collective-permute-start.30 = (bf16[256,1024]{1,0:T(8,128)(2,1)}, bf16[256,1024]{1,0:T(8,128)(2,1)}, u32[]{:S(2)}, u32[]{:S(2)}) collective-permute-start(bf16[256,1024]{1,0:T(8,128)(2,1)} %copy.73), channel_id=1, source_target_pairs={{0,2},{2,0},{1,3},{3,1},{4,6},{6,4},{5,7},{7,5},{8,10},{10,8},{9,1... | collective-permute-start | bytes 1572872 | tf_op jit(solution)/shard_map/gc_zhi/ppermute | solution.py:1321
  561.3 55.4 %collective-permute-start.31 = (bf16[512,1024]{1,0:T(8,128)(2,1)S(1)}, bf16[512,1024]{1,0:T(8,128)(2,1)S(1)}, u32[]{:S(2)}, u32[]{:S(2)}) collective-permute-start(bf16[512,1024]{1,0:T(8,128)(2,1)S(1)} %fusion.25), channel_id=1, source_target_pairs={{2,4},{4,2},{3,5},{5,3},{10,12},{12,10},{11,13},{13,11},{18,20},{2... | collective-permute-start | bytes 3145736 | tf_op jit(solution)/shard_map/re_dgrad/ppermute | solution.py:1330
  (74 other events, 582.2 us)
Sparse Core Ops, SparseCore 0:
  100.5 51.2 all-gather.2
  153.6 87.5 all-gather.4
  338.6 52.3 reduce-scatter.5
  394.1 52.6 reduce-scatter.3
  449.6 52.6 reduce-scatter.7

commit v6 on v5

--- a/solution.py
+++ b/solution.py
@@ -691,7 +691,7 @@
 
 def weight_grad_kernel(*refs):
     rows_ref, refs = refs[0], refs[1:]
-    sides, (rows_out, *outs, turned, send, recv) = (refs[:6], refs[6:12]), refs[12:]
+    sides, (rows_out, out_ref, turned, send, recv) = (refs[:6], refs[6:12]), refs[12:]
     count, depth = sides[0][0].shape[0], sides[0][4].shape[0]
     step_of, tiles = pl.program_id(0), pl.num_programs(0) // 2
 
@@ -714,7 +714,7 @@
         pl.semaphore_wait(barrier, 1)
         copy().start()
 
-    for half, ((x0_ref, x1_ref, x2_ref, x3_ref, near_ref, far_ref), out_ref) in enumerate(zip(sides, outs)):
+    for half, (x0_ref, x1_ref, x2_ref, x3_ref, near_ref, far_ref) in enumerate(sides):
 
         @pl.when(step_of == half * tiles)
         def _(blocks=(x0_ref, x1_ref, x2_ref, x3_ref)):
@@ -722,7 +722,7 @@
                 turned[:, which * count : (which + 1) * count] = jnp.transpose(x_ref[...])
 
         @pl.when(step_of // tiles == half)
-        def _(near_ref=near_ref, far_ref=far_ref, out_ref=out_ref):
+        def _(near_ref=near_ref, far_ref=far_ref):
             def step(index, carry):
                 rows = pl.ds(pl.multiple_of(index * 256, 256), 256)
                 total = dot_nn(turned[rows, :depth], near_ref[...]) + dot_nn(turned[rows, depth:], far_ref[...])
@@ -749,13 +749,15 @@
     def late(size):
         return pl.BlockSpec((size, tile), lambda i: (0, jnp.maximum(i - tiles, 0)))
 
-    shape = jax.ShapeDtypeStruct((model, width), near.dtype)
     return pl.pallas_call(
         weight_grad_kernel,
         grid=(2 * tiles,),
         in_specs=[anywhere] + [whole] * 4 + [early(depth)] * 2 + [whole] * 4 + [late(depth)] * 2,
-        out_specs=[anywhere, early(model), late(model)],
-        out_shape=[jax.ShapeDtypeStruct(rows.shape, rows.dtype), shape, shape],
+        out_specs=[anywhere, pl.BlockSpec((model, tile), lambda i: (0, i))],
+        out_shape=[
+            jax.ShapeDtypeStruct(rows.shape, rows.dtype),
+            jax.ShapeDtypeStruct((model, 2 * width), near.dtype),
+        ],
         scratch_shapes=[
             pltpu.VMEM((model, 4 * count), near.dtype),
             pltpu.SemaphoreType.DMA,
@@ -772,8 +774,10 @@
 def start_kernel(
     tokens,
     enc,
-    w_self,
-    w_cross,
+    self_qkv,
+    self_out,
+    cross_qkv,
+    cross_out,
     w_in,
     w_out,
     small,
@@ -794,7 +798,7 @@
     y, x, core, zhi, zlo = (lax.axis_index(axis) for axis in AXES)
     crossing = core != zhi
     rows = tokens.shape[0]
-    part = w_self.shape[1]
+    part = self_out.shape[0]
     counts = {"sent": 0, "local": 0}
 
     def push(source, target, axis):
@@ -873,23 +877,24 @@
     own_rows = pl.ds(pl.multiple_of(core * part, part), part)
     quarter = 2 * zhi + zlo
 
-    def from_shard(shard, target, block, size):
-        own = keep(shard.at[:, :, lanes(core, size)], target.at[:, y, x, own_rows, lanes(block, size)])
-        other = push(
-            shard.at[:, :, lanes(1 - core, size)], target.at[:, y, x, own_rows, lanes(block, size)], "core"
-        )
-        return own, other
-
-    self_width = w_self.shape[2] // 2
+    self_width = self_out.shape[1] // 2
     hidden_width = w_in.shape[1] // 2
     cross_core = []
     for plane in range(4):
         target = cross_rows.at[own_rows, lanes(4 * plane + quarter, self_width)]
-        cross_core.append(keep(w_cross.at[plane, :, lanes(core, self_width)], target))
-        cross_core.append(push(w_cross.at[plane, :, lanes(1 - core, self_width)], target, "core"))
+        shard = cross_qkv.at[plane] if plane < 3 else cross_out
+        cross_core.append(keep(shard.at[:, lanes(core, self_width)], target))
+        cross_core.append(push(shard.at[:, lanes(1 - core, self_width)], target, "core"))
     own_small.wait()
     small_core = push(gathered.at[y, x, core, zhi, zlo], gathered.at[y, x, core, zhi, zlo], "core")
-    self_core = from_shard(w_self, g_self, zhi, self_width)
+    target = g_self.at[pl.ds(0, 3), y, x, own_rows, lanes(zhi, self_width)]
+    target_out = g_self.at[3, y, x, own_rows, lanes(zhi, self_width)]
+    self_core = [
+        keep(self_qkv.at[:, :, lanes(core, self_width)], target),
+        push(self_qkv.at[:, :, lanes(1 - core, self_width)], target, "core"),
+        keep(self_out.at[:, lanes(core, self_width)], target_out),
+        push(self_out.at[:, lanes(1 - core, self_width)], target_out, "core"),
+    ]
     hidden_core = []
     for plane, shard in enumerate((w_in, w_out)):
         target = hidden.at[plane, own_rows]
@@ -983,15 +988,15 @@
         copy.wait()
 
 
-def start_exchange(tokens, enc, w_self, w_cross, w_in, w_out, small):
+def start_exchange(tokens, enc, self_qkv, self_out, cross_qkv, cross_out, w_in, w_out, small):
     rows, model = tokens.shape
-    part = w_self.shape[1]
+    part, shard = self_out.shape
     low_type = tokens.dtype
     shapes = [
         jax.ShapeDtypeStruct((rows, model), low_type),
         jax.ShapeDtypeStruct((4 * rows, model), low_type),
-        jax.ShapeDtypeStruct((4, 2, 2, 2 * part, w_self.shape[2]), low_type),
-        jax.ShapeDtypeStruct((2 * part, 8 * w_cross.shape[2]), low_type),
+        jax.ShapeDtypeStruct((4, 2, 2, 2 * part, shard), low_type),
+        jax.ShapeDtypeStruct((2 * part, 8 * shard), low_type),
         jax.ShapeDtypeStruct((2, 2 * part, w_in.shape[1] // 2), low_type),
         jax.ShapeDtypeStruct((4, enc.shape[0], model), low_type),
         jax.ShapeDtypeStruct((2,) * 5 + small.shape, small.dtype),
@@ -1000,7 +1005,7 @@
     return pl.pallas_call(
         start_kernel,
         out_shape=shapes,
-        in_specs=[anywhere] * 7,
+        in_specs=[anywhere] * 9,
         out_specs=[anywhere] * len(shapes),
         scratch_shapes=[
             pltpu.VMEM((rows, model), low_type),
@@ -1011,7 +1016,7 @@
             pltpu.SemaphoreType.DMA((20,)),
         ],
         compiler_params=pltpu.CompilerParams(collective_id=0, has_side_effects=True),
-    )(tokens, enc, w_self, w_cross, w_in, w_out, small)
+    )(tokens, enc, self_qkv, self_out, cross_qkv, cross_out, w_in, w_out, small)
 
 
 def finish_kernel(
@@ -1325,10 +1330,17 @@
     return lax.optimization_barrier((value, *others))[0]
 
 
+def regroup_sent(rows, name):
+    with jax.named_scope("re_" + name):
+        return lax.ppermute(rows, ("core", "zhi"), [(1, 2), (2, 1)])
+
+
+def regroup_done(rows, moved):
+    return jnp.where(lax.axis_index("core") == lax.axis_index("zhi"), rows, moved)
+
+
 def regroup(rows, name="regroup"):
-    with jax.named_scope("re_" + name):
-        moved = lax.ppermute(rows, ("core", "zhi"), [(1, 2), (2, 1)])
-        return jnp.where(lax.axis_index("core") == lax.axis_index("zhi"), rows, moved)
+    return regroup_done(rows, regroup_sent(rows, name))
 
 
 def in_order(index, own, other, axis):
@@ -1397,8 +1409,10 @@
     token_rows, attn_rows, w_self, w_cross, hidden, enc_full, small = start_exchange(
         tokens,
         enc_states,
-        jnp.concatenate([self_qkv, self_out.T[None]], axis=0),
-        jnp.concatenate([cross_qkv, cross_out.T[None]], axis=0),
+        self_qkv,
+        self_out.T,
+        cross_qkv,
+        cross_out.T,
         ff_in,
         ff_out.T,
         flat,
@@ -1491,12 +1505,12 @@
     beyond = trade(mlp_in, "zlo", "mlp_z")
     mlp_near = [mlp_in, trade(mlp_in, "core", "mlp_c")]
     act_near, dpre_near, sum_near = hidden_units(mlp_near, cot_near, w_hidden, hidden_bias[None])
-    beyond = after(beyond, act_near)
+    bias_out_three = jnp.sum(grad_rows.astype(jnp.float32), axis=0)
+    beyond = after(beyond, act_near, bias_out_three)
     mlp_far = [beyond, trade(beyond, "core", "mlp_zc")]
     cot_far = [cot_beyond, trade(cot_beyond, "core", "cot_zc")]
     act_far, dpre_far, sum_far = hidden_units(mlp_far, cot_far, w_hidden, hidden_bias[None])
     gradient = grad_rows.astype(jnp.float32)
-    bias_out_three = jnp.sum(gradient, axis=0)
     dmlp_far = low(
         product_right_t(dpre_far[:own_rows], w_in)
         + trade(low(product_right_t(dpre_far[own_rows:], w_in)), "core", "dmlp_zc")
@@ -1508,12 +1522,9 @@
     out_parts = [
         low(product_right_t(act_far[own_rows:], w_out)),
         product_right_t(act_far[:own_rows], w_out),
-        low(product_right_t(act_near[own_rows:], w_out)),
-        product_right_t(act_near[:own_rows], w_out),
     ]
     out_far = low(out_parts[1] + trade(out_parts[0], "core", "out_zc"))
-    out_branch = out_parts[3] + trade(out_parts[2], "core", "out_c")
-    dmlp_beyond, grad_w_out, grad_w_in = weight_grads(
+    dmlp_beyond, grad_hidden = weight_grads(
         dmlp_far, (cot_near + cot_far, act_near, act_far), (mlp_near + mlp_far, dpre_near, dpre_far), 2
     )
     mlp_term = mlp_term + dmlp_beyond
@@ -1548,10 +1559,6 @@
 
     grad_low = low(gradient)
     bias_out_one = jnp.sum(grad_low.astype(jnp.float32), axis=0)
-    def zhi_sum(partial, axis, name):
-        mine, theirs = half_of(partial, zhi, axis), half_of(partial, 1 - zhi, axis)
-        return mine.astype(jnp.float32) + trade(theirs, "zhi", name).astype(jnp.float32)
-
     beyond = trade(grad_low, "zlo", "e1_z")
     grad_near = jnp.concatenate([grad_low, trade(grad_low, "core", "e1_c")], axis=0)
     mixed_grad = low(product(grad_near, w_so))
@@ -1562,19 +1569,29 @@
         low(product_left_t(after(grad_both, grad_low), cross_mixed)),
     ]
     grad_cross = jnp.concatenate(cross_parts, axis=1)
+    act_near = after(act_near, grad_low)
+    out_branch = product_right_t(act_near[:own_rows], w_out) + trade(
+        low(product_right_t(act_near[own_rows:], w_out)), "core", "out_c"
+    )
     layer_out = low(after_two + (out_branch + after(out_far, grad_low) + vectors[8]))
     beyond = after(beyond, mixed_grad, grad_cross, layer_out)
     cross_sum = sum_over_chips(grad_cross)
     grad_far = jnp.concatenate([beyond, trade(beyond, "core", "e1_zc")], axis=0)
     mixed_grad = jnp.concatenate([mixed_grad, low(product(grad_far, w_so))], axis=0)
 
-    out_sum = zhi_sum(sum_over_chips(grad_w_out), 1, "go_zhi")
-    in_sum = zhi_sum(sum_over_chips(grad_w_in), 1, "gi_zhi")
+    hidden_sum = sum_over_chips(grad_hidden)
+    sides = [hidden_sum[:, : hidden_sum.shape[1] // 2], hidden_sum[:, hidden_sum.shape[1] // 2 :]]
+    sent = jnp.concatenate([half_of(side, 1 - zhi, 1) for side in sides], axis=1)
+    hidden_beyond = jnp.split(trade(sent, "zhi", "gf_zhi"), 2, axis=1)
+    out_sum, in_sum = (
+        half_of(side, zhi, 1).astype(jnp.float32) + beyond.astype(jnp.float32)
+        for side, beyond in zip(sides, hidden_beyond)
+    )
     dq, dk, dv = attend_back(
         self_plan, self_meta, qkv, 0, qkv, pairs, 2 * pairs, mixed, mixed_grad, self_lse, pairs, 1152
     )
     dq, dk, dv = after(dq, in_sum, out_sum), after(dk, in_sum, out_sum), after(dv, in_sum, out_sum)
-    layer_out = regroup(after(layer_out, dq), "out")
+    layer_moved = regroup_sent(after(layer_out, dq), "out")
     dqkv = jnp.concatenate([dq, dk, dv], axis=1)
     d_near, d_far = dqkv[: count // 2], dqkv[count // 2 :]
     dx_far = low(
@@ -1584,7 +1601,11 @@
     dx = product_right_t(d_near[: count // 4], w_qkv) + trade(
         low(product_right_t(d_near[count // 4 :], w_qkv)), "core", "dx_c"
     )
-    dq, dk, dv = after(dq, dx_far), after(dk, dx_far), after(dv, dx_far)
+    cross_sum = after(cross_sum, dx_far).reshape(rows_of, 4, 2, -1)
+    cross_kept = half_of(cross_sum, zhi, 2).reshape(rows_of, -1)
+    cross_sent = half_of(cross_sum, 1 - zhi, 2).reshape(rows_of, -1)
+    cross_beyond = trade(cross_sent, "zhi", "gc_zhi")
+    dq, dk, dv = (after(part, dx_far, cross_sent, cross_kept) for part in (dq, dk, dv))
     self_parts = [
         low(product_left_t(attn_rows, dq)),
         low(product_left_t(attn_rows, dk)),
@@ -1595,9 +1616,7 @@
         product_right_t(after(cross_dk, dq), w_ckv[:, :cross_width])
         + product_right_t(after(cross_dv, dq), w_ckv[:, cross_width:])
     )
-    cross_sum = after(cross_sum, dq).reshape(rows_of, 4, 2, -1)
-    cross_kept = half_of(cross_sum, zhi, 2).reshape(rows_of, -1)
-    cross_beyond = trade(half_of(cross_sum, 1 - zhi, 2).reshape(rows_of, -1), "zhi", "gc_zhi")
+    layer_out = regroup_done(layer_out, after(layer_moved, *self_parts))
     dx = dx + after(trade(dx_far, "zlo", "dx_z"), enc_part, layer_out, cross_beyond, *self_parts)
     part, gain_one, shift_one = norm_backward(dx, hat_one, inv_one, vectors[0])
     input_part = low(gradient + part)

time: 638 us -> 628 us (0.984)
  matrix products: 116 us -> 106 us
  waiting for transfers between devices: 88.4 us -> 97.8 us
  starting transfers between devices: 31.4 us -> 24.9 us
    ppermute x28 -> x27, waiting for transfers between devices: 82.1 us -> 97.3 us  [trade(): return lax.ppermute(rows, axis, [(0, 1), (1, 0)])]
    dot_general x22, matrix products: 75.7 us -> 68.8 us  [product_right_t(): lax.dot_general(left, right, (((1,), (1,)), ((), ())), preferred_element_...]
    ppermute x28 -> x27, starting transfers between devices: 25.5 us -> 19.1 us  [trade(): return lax.ppermute(rows, axis, [(0, 1), (1, 0)])]
    unnamed x162 -> x170, local copies, waits for them, and re-layouts: 22.3 us -> 24.9 us
  transfers between devices with their start and end apart: 37 -> 35, of which waited for: 13 -> 14; matrix products, arithmetic and copies ran while one was open for 27% -> 26% of each run, Pallas kernels for 28% -> 28%
where the time goes in v6:
time: 628 us; the launch traced here: 619 us
  Pallas kernels  291 us (46%)
  matrix products  106 us (17%)
  waiting for transfers between devices  97.8 us (16%)
  local copies, waits for them, and re-layouts  44.1 us (7%)
  other arithmetic  40.5 us (6%)
  starting transfers between devices  24.9 us (4%)
  between operations  15.7 us (2%)
    ppermute x27, waiting for transfers between devices, trade(): return lax.ppermute(rows, axis, [(0, 1), (1, 0)])  97.3 us
    pallas_call x1, Pallas kernels, start_exchange(): pl.pallas_call(start_kernel, out_shape=shapes, in_specs=[anywhere] * 9, o...  85.2 us
    dot_general x22, matrix products, product_right_t(): lax.dot_general(left, right, (((1,), (1,)), ((), ())), preferred_element_...  68.8 us
    pallas_call x2, Pallas kernels, attend_back(): pl.pallas_call(functools.partial(backward_kernel, sections), grid_spec=pl...  56.2 us
    pallas_call x1, Pallas kernels, finish(): pl.pallas_call(finish_kernel, out_shape=shapes, in_specs=[anywhere] * 10,...  45.1 us
    pallas_call x2, Pallas kernels, attend(): pl.pallas_call(functools.partial(forward_kernel, sections), grid_spec=plt...  38.4 us
    pallas_call x2, Pallas kernels, hidden_units(): pl.pallas_call(hidden_kernel, grid=(tiles,), in_specs=[whole] * 4 + [weig...  33.6 us
    pallas_call x1, Pallas kernels, weight_grads(): pl.pallas_call(weight_grad_kernel, grid=(2 * tiles,), in_specs=[anywhere]...  32.1 us
  transfers between devices with their start and end apart: 35, of which 14 were waited for; matrix products, arithmetic and copies ran while one was open for 26% of the time, Pallas kernels for 28%

profile of v6, /device:TPU:0, one launch (start us, length us, event | category | flops | bytes accessed | tf_op | source)
XLA Modules:
  0.0 619.4 jit_solution(6708325884706151966)
XLA Ops:
  14.5 85.2 %shard_map.229 = (bf16[512,1024]{1,0:T(8,128)(2,1)}, bf16[2048,1024]{1,0:T(8,128)(2,1)}, bf16[4,2,2,256,256]{4,3,2,1,0:T(8,128)(2,1)}, bf16[256,2048]{1,0:T(8,12...) custom-call(bf16[512,1024]{1,0:T(8,128)(2,1)} %tokens.1, ...), custom_call_target="tpu_custom_call" | custom-call | tf_op jit(solution)/shard_map/pallas_call | solution.py:1005
  101.2 5.0 collective-permute-start.1
  110.7 4.8 multiply_convert_fusion.q_ref.k_ref.v_ref
  116.5 23.2 %shard_map.230 = (bf16[2048,256]{1,0:T(8,128)(2,1)}, f32[2048,256]{1,0:T(8,128)}) custom-call(s32[13]{0:T(128)} %concatenate.61.meta_ref, bf16[2048,768]{1,0:T(8,128)(2,1)} %multiply_convert_fusion.q_ref.k_ref.v_ref, bf16[2048,768]{1,0:T(8,128)(2,1)} %multiply_convert_fusion.q_ref.k_ref.v_ref, bf16[2048,768]{1,0:T(8,128)(2,1)} %multiply_convert_fusion.q_ref.k_ref.v_ref), custom_call_target="tpu_custom_call" | custom-call | flops 19327352832 | bytes 5242880 | tf_op jit(solution)/shard_map/pallas_call | solution.py:180
  139.7 11.1 %collective-permute-done.1 = bf16[2,256,1024]{2,1,0:T(8,128)(2,1)S(1)} collective-permute-done((bf16[2,256,1024]{2,1,0:T(8,128)(2,1)}, bf16[2,256,1024]{2,1,0:T(8,128)(2,1)S(1)}, u32[]{:S(2)}, u32[]{:S(2)}) %collective-permute-start.1) | collective-permute-done | bytes 1048608 | tf_op jit(solution)/shard_map/wh_zhi/ppermute | solution.py:1326
  172.1 4.3 add_convert_fusion.7.k_ref.v_ref
  176.4 24.4 %collective-permute-done.4 = bf16[512,1024]{1,0:T(8,128)(2,1)} collective-permute-done((bf16[512,1024]{1,0:T(8,128)(2,1)}, bf16[512,1024]{1,0:T(8,128)(2,1)}, u32[]{:S(2)}, u32[]{:S(2)}) %collective-permute-start.4) | collective-permute-done | bytes 1048608 | tf_op jit(solution)/shard_map/so_z/ppermute | solution.py:1326
  208.1 3.4 multiply_convert_fusion.1.q_ref
  211.6 15.2 %shard_map.231 = (bf16[1024,512]{1,0:T(8,128)(2,1)}, f32[1024,512]{1,0:T(8,128)}) custom-call(s32[1]{0:T(128)} %slice.208.meta_ref, bf16[1024,512]{1,0:T(8,128)(2,1)} %multiply_convert_fusion.1.q_ref, bf16[512,1024]{1,0:T(8,128)(2,1)} %add_convert_fusion.7.k_ref.v_ref, bf16[512,1024]{1,0:T(8,128)(2,1)} %add_convert_fusion.7.k_ref.v_ref), custom_call_target="tpu_custom_call" | custom-call | flops 8589934592 | bytes 5242880 | tf_op jit(solution)/shard_map/pallas_call | solution.py:180
  226.7 4.2 collective-permute-done.7.e0_ref.refs_3_
  243.7 16.7 %shard_map.232 = (bf16[1024,2048]{1,0:T(8,128)(2,1)}, bf16[1024,2048]{1,0:T(8,128)(2,1)}, f32[1,2048]{1,0:T(1,128)}) custom-call(bf16[512,1024]{1,0:T(8,128)(2,1)} %add_convert_fusion.5.x0_ref.refs_7_, bf16[512,1024]{1,0:T(8,128)(2,1)} %collective-permute-done.9.x1_ref.refs_8_, bf16[512,1024]{1,0:T(8,128)(2,1)} %get-tuple-element.90.e0_ref.refs_1_, ...), custom_call_target="tpu_custom_call" | custom-call | flops 8589934592 | bytes 20971520 | tf_op jit(solution)/shard_map/pallas_call | solution.py:671
  260.4 6.2 collective-permute-done.11.x0_ref.refs_9_
  266.6 6.2 fusion.49
  273.3 16.9 %shard_map.233 = (bf16[1024,2048]{1,0:T(8,128)(2,1)}, bf16[1024,2048]{1,0:T(8,128)(2,1)}, f32[1,2048]{1,0:T(1,128)}) custom-call(bf16[512,1024]{1,0:T(8,128)(2,1)} %collective-permute-done.11.x0_ref.refs_9_, bf16[512,1024]{1,0:T(8,128)(2,1)} %collective-permute-done.12.x1_ref.refs_10_, bf16[512,1024]{1,0:T(8,128)(2,1)} %copy-done.61, ...), custom_call_target="tpu_custom_call" | custom-call | flops 8589934592 | bytes 20971520 | tf_op jit(solution)/shard_map/pallas_call | solution.py:671
  290.2 5.3 fusion.44
  295.7 6.3 %convert_add_fusion.5 = f32[512,1024]{1,0:T(8,128)} fusion(bf16[512,1024]{1,0:T(8,128)(2,1)} %collective-permute-done.15, bf16[1024,4096]{1,0:T(8,128)(2,1)} %all-gather.5.cloned.1.call-done.w_in_ref.w_out_ref, bf16[1024,2048]{1,0:T(8,128)(2,1)S(1)} %copy-done.63), kind=kOutput, calls=%fused_computation.62 | convolution fusion | flops 2148532224 | bytes 9437184 | tf_op jit(solution)/shard_map/dot_general | solution.py:278
  302.0 3.4 add_convert_fusion.4.refs_0_
  305.4 32.1 %shard_map.234 = (bf16[512,1024]{1,0:T(8,128)(2,1)}, bf16[1024,4096]{1,0:T(8,128)(2,1)}) custom-call(bf16[512,1024]{1,0:T(8,128)(2,1)} %add_convert_fusion.4.refs_0_, bf16[512,1024]{1,0:T(8,128)(2,1)} %get-tuple-element.90.e0_ref.refs_1_, bf16[512,1024]{1,0:T(8,128)(2,1)} %collective-permute-done.10.e1_ref.refs_2_, bf16[512,1024]{1,0:T(8,128)(2,1)} %copy-done.61, ...), custom_call_target="tpu_custom_call" | custom-call | flops 17179869184 | tf_op jit(solution)/shard_map/pallas_call | solution.py:752
  338.0 5.3 fusion.54
  345.1 3.5 convert_reduce_fusion.5
  349.8 3.4 add_convert_fusion.3
  353.7 3.8 convolution_convert_fusion.4.do_ref
  357.5 18.7 %shard_map.235 = (bf16[1024,512]{1,0:T(8,128)(2,1)}, bf16[512,512]{1,0:T(8,128)(2,1)}, bf16[512,512]{1,0:T(8,128)(2,1)}) custom-call(s32[1]{0:T(128)} %slice.208.meta_ref, bf16[1024,512]{1,0:T(8,128)(2,1)} %multiply_convert_fusion.1.q_ref, bf16[512,1024]{1,0:T(8,128)(2,1)} %add_convert_fusion.7.k_ref.v_ref, bf16[512,1024]{1,0:T(8,128)(2,1)} %add_convert_fusion.7.k_ref.v_ref, ...), custom_call_target="tpu_custom_call" | custom-call | flops 21474836480 | bytes 10485760 | tf_op jit(solution)/shard_map/pallas_call | solution.py:202
  392.9 3.4 fusion.59
  398.1 3.7 fusion.2
  428.9 37.5 %shard_map.236 = (bf16[2048,256]{1,0:T(8,128)(2,1)}, bf16[2048,256]{1,0:T(8,128)(2,1)}, bf16[2048,256]{1,0:T(8,128)(2,1)}) custom-call(s32[13]{0:T(128)} %concatenate.61.meta_ref, bf16[2048,768]{1,0:T(8,128)(2,1)} %multiply_convert_fusion.q_ref.k_ref.v_ref, bf16[2048,768]{1,0:T(8,128)(2,1)} %multiply_convert_fusion.q_ref.k_ref.v_ref, ...), custom_call_target="tpu_custom_call" | custom-call | flops 48318382080 | bytes 10485760 | tf_op jit(solution)/shard_map/pallas_call | solution.py:202
  466.4 8.9 %collective-permute-done.24 = bf16[256,2048]{1,0:T(8,128)(2,1)} collective-permute-done((bf16[256,2048]{1,0:T(8,128)(2,1)}, bf16[256,2048]{1,0:T(8,128)(2,1)}, u32[]{:S(2)}, u32[]{:S(2)}) %collective-permute-start.24) | collective-permute-done | bytes 1048608 | tf_op jit(solution)/shard_map/gf_zhi/ppermute | solution.py:1326
  501.2 3.3 collective-permute-start.29
  505.1 4.4 convolution_convert_fusion.12
  520.9 19.4 %collective-permute-done.29.cross_beyond = bf16[256,1024]{1,0:T(8,128)(2,1)} collective-permute-done((bf16[256,1024]{1,0:T(8,128)(2,1)}, bf16[256,1024]{1,0:T(8,128)(2,1)}, u32[]{:S(2)}, u32[]{:S(2)}) %collective-permute-start.29) | collective-permute-done | bytes 524320 | tf_op jit(solution)/shard_map/gc_zhi/ppermute | solution.py:1326
  540.3 10.8 %collective-permute-done.28 = bf16[512,1024]{1,0:T(8,128)(2,1)} collective-permute-done((bf16[512,1024]{1,0:T(8,128)(2,1)}, bf16[512,1024]{1,0:T(8,128)(2,1)}, u32[]{:S(2)}, u32[]{:S(2)}) %collective-permute-start.28) | collective-permute-done | bytes 1048608 | tf_op jit(solution)/shard_map/dx_z/ppermute | solution.py:1326
  556.8 45.1 %shard_map.237 = (f32[128,2048]{1,0:T(8,128)}, f32[128,2048]{1,0:T(8,128)}, f32[3,128,256]{2,1,0:T(8,128)}, f32[128,256]{1,0:T(8,128)}, f32[3,128,256]{2,1,0:T(8...) custom-call(f32[256,1024]{1,0:T(8,128)} %get-tuple-element.214.ff_in, ...), custom_call_target="tpu_custom_call" | custom-call | flops 40000000000 | tf_op jit(solution)/shard_map/pallas_call | solution.py:1292
  (367 shorter events, 158.4 us)
Async XLA Ops:
  7.2 164.9 %all-gather.3.cloned.1.call-start = ((), (), s32[]{:S(2)}) async-start(), calls=%async_computation.2 | async-start | bytes 5242880 | tf_op jit(solution)/shard_map/all_gather | solution.py:1362
  99.8 143.9 %all-gather.5.cloned.1.call-start = ((), (), s32[]{:S(2)}) async-start(), calls=%async_computation.3 | async-start | bytes 10485760 | tf_op jit(solution)/shard_map/all_gather | solution.py:1362
  100.6 14.9 %collective-permute-start = (s32[9]{0:T(128)S(1)}, s32[9]{0:T(128)S(1)}, u32[]{:S(2)}, u32[]{:S(2)}) collective-permute-start(s32[9]{0:T(128)S(1)} %pad_add_fusion), channel_id=1, source_target_pairs={{2,4},{4,2},{3,5},{5,3},{10,12},{12,10},{11,13},{13,11},{18,20},{2... | collective-permute-start | bytes 116 | tf_op jit(solution)/shard_map/re_regroup/ppermute | solution.py:1335
  101.2 49.6 %collective-permute-start.1 = (bf16[2,256,1024]{2,1,0:T(8,128)(2,1)}, bf16[2,256,1024]{2,1,0:T(8,128)(2,1)S(1)}, u32[]{:S(2)}, u32[]{:S(2)}) collective-permute-start(bf16[2,256,1024]{2,1,0:T(8,128)(2,1)} %get-tuple-element.82), channel_id=1, source_target_pairs={{0,2},{2,0},{1,3},{3,1},{4,6},{6,4},{5,7},{7,5},{8,10},{10,8},{9,1... | collective-permute-start | bytes 3145736 | tf_op jit(solution)/shard_map/wh_zhi/ppermute | solution.py:1326
  152.7 270.9 %reduce-scatter.3.cloned.1.call-start = ((), (), s32[]{:S(2)}) async-start(), calls=%async_computation.4 | async-start | bytes 10485760 | tf_op jit(solution)/shard_map/reduce_scatter | solution.py:1366
  155.4 5.3 collective-permute-start.3
  156.3 12.6 %collective-permute-start.5 = (bf16[512,1024]{1,0:T(8,128)(2,1)}, bf16[512,1024]{1,0:T(8,128)(2,1)}, u32[]{:S(2)}, u32[]{:S(2)}) collective-permute-start(bf16[512,1024]{1,0:T(8,128)(2,1)} %param.18), channel_id=1, source_target_pairs={{2,4},{4,2},{3,5},{5,3},{10,12},{12,10},{11,13},{13,11},{18,20},{2... | collective-permute-start | bytes 3145736 | tf_op jit(solution)/shard_map/re_cotangent/ppermute | solution.py:1335
  160.0 40.8 %collective-permute-start.2 = (bf16[512,1024]{1,0:T(8,128)(2,1)}, bf16[512,1024]{1,0:T(8,128)(2,1)S(1)}, u32[]{:S(2)}, u32[]{:S(2)}) collective-permute-start(bf16[512,1024]{1,0:T(8,128)(2,1)} %convolution_convert_fusion.6), channel_id=1, source_target_pairs={{0,4},{4,0},{1,5},{5,1},{2,6},{6,2},{3,7},{7,3},{8,12},{12,8},{9,1... | collective-permute-start | bytes 3145736 | tf_op jit(solution)/shard_map/so_c/ppermute | solution.py:1326
  163.7 37.1 %collective-permute-start.4 = (bf16[512,1024]{1,0:T(8,128)(2,1)}, bf16[512,1024]{1,0:T(8,128)(2,1)}, u32[]{:S(2)}, u32[]{:S(2)}) collective-permute-start(bf16[512,1024]{1,0:T(8,128)(2,1)} %add_convert_fusion.8), channel_id=1, source_target_pairs={{0,1},{1,0},{2,3},{3,2},{4,5},{5,4},{6,7},{7,6},{8,9},{9,8},{10,11... | collective-permute-start | bytes 3145736 | tf_op jit(solution)/shard_map/so_z/ppermute | solution.py:1326
  205.2 25.7 %collective-permute-start.7 = (bf16[512,1024]{1,0:T(8,128)(2,1)}, bf16[512,1024]{1,0:T(8,128)(2,1)S(1)}, u32[]{:S(2)}, u32[]{:S(2)}) collective-permute-start(bf16[512,1024]{1,0:T(8,128)(2,1)} %get-tuple-element.90.e0_ref.refs_1_), channel_id=1, source_target_pairs={{0,1},{1,0},{2,3},{3,2},{4,5},{5,4},{6,7},{7,6},{8,9},{9,8},{10,11... | collective-permute-start | bytes 3145736 | tf_op jit(solution)/shard_map/cot_z/ppermute | solution.py:1326
  233.4 3.4 collective-permute-start.8
  233.5 8.4 %collective-permute-start.10 = (bf16[512,1024]{1,0:T(8,128)(2,1)}, bf16[512,1024]{1,0:T(8,128)(2,1)}, u32[]{:S(2)}, u32[]{:S(2)}) collective-permute-start(bf16[512,1024]{1,0:T(8,128)(2,1)} %get-tuple-element.90.e0_ref.refs_1_), channel_id=1, source_target_pairs={{0,4},{4,0},{1,5},{5,1},{2,6},{6,2},{3,7},{7,3},{8,12},{12,8},{9,1... | collective-permute-start | bytes 3145736 | tf_op jit(solution)/shard_map/cot_c/ppermute | solution.py:1326
  240.8 25.8 %collective-permute-start.11 = (bf16[512,1024]{1,0:T(8,128)(2,1)}, bf16[512,1024]{1,0:T(8,128)(2,1)}, u32[]{:S(2)}, u32[]{:S(2)}) collective-permute-start(bf16[512,1024]{1,0:T(8,128)(2,1)} %add_convert_fusion.5.x0_ref.refs_7_), channel_id=1, source_target_pairs={{0,1},{1,0},{2,3},{3,2},{4,5},{5,4},{6,7},{7,6},{8,9},{9,8},{10,11... | collective-permute-start | bytes 3145736 | tf_op jit(solution)/shard_map/mlp_z/ppermute | solution.py:1326
  241.8 31.5 %collective-permute-start.13 = (bf16[512,1024]{1,0:T(8,128)(2,1)}, bf16[512,1024]{1,0:T(8,128)(2,1)}, u32[]{:S(2)}, u32[]{:S(2)}) collective-permute-start(bf16[512,1024]{1,0:T(8,128)(2,1)} %copy-done.61), channel_id=1, source_target_pairs={{0,4},{4,0},{1,5},{5,1},{2,6},{6,2},{3,7},{7,3},{8,12},{12,8},{9,1... | collective-permute-start | bytes 3145736 | tf_op jit(solution)/shard_map/cot_zc/ppermute | solution.py:1326
  266.6 6.7 %collective-permute-start.12 = (bf16[512,1024]{1,0:T(8,128)(2,1)}, bf16[512,1024]{1,0:T(8,128)(2,1)}, u32[]{:S(2)}, u32[]{:S(2)}) collective-permute-start(bf16[512,1024]{1,0:T(8,128)(2,1)} %collective-permute-done.11.x0_ref.refs_9_), channel_id=1, source_target_pairs={{0,4},{4,0},{1,5},{5,1},{2,6},{6,2},{3,7},{7,3},{8,12},{12,8},{9,1... | collective-permute-start | bytes 3145736 | tf_op jit(solution)/shard_map/mlp_zc/ppermute | solution.py:1326
  272.8 22.9 %collective-permute-start.15 = (bf16[512,1024]{1,0:T(8,128)(2,1)}, bf16[512,1024]{1,0:T(8,128)(2,1)}, u32[]{:S(2)}, u32[]{:S(2)}) collective-permute-start(bf16[512,1024]{1,0:T(8,128)(2,1)} %fusion.49), channel_id=1, source_target_pairs={{0,4},{4,0},{1,5},{5,1},{2,6},{6,2},{3,7},{7,3},{8,12},{12,8},{9,1... | collective-permute-start | bytes 3145736 | tf_op jit(solution)/shard_map/dmlp_c/ppermute | solution.py:1326
  295.6 6.4 %collective-permute-start.14 = (bf16[512,1024]{1,0:T(8,128)(2,1)S(1)}, bf16[512,1024]{1,0:T(8,128)(2,1)S(1)}, u32[]{:S(2)}, u32[]{:S(2)}) collective-permute-start(bf16[512,1024]{1,0:T(8,128)(2,1)S(1)} %fusion.44), channel_id=1, source_target_pairs={{0,4},{4,0},{1,5},{5,1},{2,6},{6,2},{3,7},{7,3},{8,12},{12,8},{9,1... | collective-permute-start | bytes 3145736 | tf_op jit(solution)/shard_map/dmlp_zc/ppermute | solution.py:1326
  337.5 157.4 %reduce-scatter.5.cloned.1.call-start = ((), (), s32[]{:S(2)}) async-start(), calls=%async_computation.5 | async-start | bytes 5242880 | tf_op jit(solution)/shard_map/reduce_scatter | solution.py:1366
  343.3 5.8 collective-permute-start.17
  348.7 5.0 collective-permute-start.16
  353.1 25.8 %collective-permute-start.18 = (bf16[512,1024]{1,0:T(8,128)(2,1)}, bf16[512,1024]{1,0:T(8,128)(2,1)}, u32[]{:S(2)}, u32[]{:S(2)}) collective-permute-start(bf16[512,1024]{1,0:T(8,128)(2,1)} %add_convert_fusion.3), channel_id=1, source_target_pairs={{0,1},{1,0},{2,3},{3,2},{4,5},{5,4},{6,7},{7,6},{8,9},{9,8},{10,11... | collective-permute-start | bytes 3145736 | tf_op jit(solution)/shard_map/out_z/ppermute | solution.py:1326
  390.6 17.3 %collective-permute-start.21 = (bf16[512,1024]{1,0:T(8,128)(2,1)}, bf16[512,1024]{1,0:T(8,128)(2,1)}, u32[]{:S(2)}, u32[]{:S(2)}) collective-permute-start(bf16[512,1024]{1,0:T(8,128)(2,1)} %get-tuple-element.194), channel_id=1, source_target_pairs={{0,4},{4,0},{1,5},{5,1},{2,6},{6,2},{3,7},{7,3},{8,12},{12,8},{9,1... | collective-permute-start | bytes 3145736 | tf_op jit(solution)/shard_map/e1_c/ppermute | solution.py:1326
  391.1 25.4 %collective-permute-start.22 = (bf16[512,1024]{1,0:T(8,128)(2,1)}, bf16[512,1024]{1,0:T(8,128)(2,1)}, u32[]{:S(2)}, u32[]{:S(2)}) collective-permute-start(bf16[512,1024]{1,0:T(8,128)(2,1)} %get-tuple-element.194), channel_id=1, source_target_pairs={{0,1},{1,0},{2,3},{3,2},{4,5},{5,4},{6,7},{7,6},{8,9},{9,8},{10,11... | collective-permute-start | bytes 3145736 | tf_op jit(solution)/shard_map/e1_z/ppermute | solution.py:1326
  396.2 14.9 %collective-permute-start.20 = (bf16[512,1024]{1,0:T(8,128)(2,1)}, bf16[512,1024]{1,0:T(8,128)(2,1)}, u32[]{:S(2)}, u32[]{:S(2)}) collective-permute-start(bf16[512,1024]{1,0:T(8,128)(2,1)} %fusion.59), channel_id=1, source_target_pairs={{0,4},{4,0},{1,5},{5,1},{2,6},{6,2},{3,7},{7,3},{8,12},{12,8},{9,1... | collective-permute-start | bytes 3145736 | tf_op jit(solution)/shard_map/out_c/ppermute | solution.py:1326
  416.5 3.3 collective-permute-start.23
  426.5 48.9 %collective-permute-start.24 = (bf16[256,2048]{1,0:T(8,128)(2,1)}, bf16[256,2048]{1,0:T(8,128)(2,1)}, u32[]{:S(2)}, u32[]{:S(2)}) collective-permute-start(bf16[256,2048]{1,0:T(8,128)(2,1)} %pad_maximum_fusion.14), channel_id=1, source_target_pairs={{0,2},{2,0},{1,3},{3,1},{4,6},{6,4},{5,7},{7,5},{8,10},{10,8},{9,1... | collective-permute-start | bytes 3145736 | tf_op jit(solution)/shard_map/gf_zhi/ppermute | solution.py:1326
  482.0 10.9 %collective-permute-start.26 = (bf16[512,1024]{1,0:T(8,128)(2,1)S(1)}, bf16[512,1024]{1,0:T(8,128)(2,1)S(1)}, u32[]{:S(2)}, u32[]{:S(2)}) collective-permute-start(bf16[512,1024]{1,0:T(8,128)(2,1)S(1)} %convolution_convert_fusion.1), channel_id=1, source_target_pairs={{0,4},{4,0},{1,5},{5,1},{2,6},{6,2},{3,7},{7,3},{8,12},{12,8},{9,1... | collective-permute-start | bytes 3145736 | tf_op jit(solution)/shard_map/dx_zc/ppermute | solution.py:1326
  488.7 62.5 %collective-permute-start.27 = (bf16[512,1024]{1,0:T(8,128)(2,1)}, bf16[512,1024]{1,0:T(8,128)(2,1)}, u32[]{:S(2)}, u32[]{:S(2)}) collective-permute-start(bf16[512,1024]{1,0:T(8,128)(2,1)} %convolution_convert_fusion), channel_id=1, source_target_pairs={{0,4},{4,0},{1,5},{5,1},{2,6},{6,2},{3,7},{7,3},{8,12},{12,8},{9,1... | collective-permute-start | bytes 3145736 | tf_op jit(solution)/shard_map/dx_c/ppermute | solution.py:1326
  488.7 25.6 %collective-permute-start.25 = (bf16[512,1024]{1,0:T(8,128)(2,1)S(1)}, bf16[512,1024]{1,0:T(8,128)(2,1)}, u32[]{:S(2)}, u32[]{:S(2)}) collective-permute-start(bf16[512,1024]{1,0:T(8,128)(2,1)S(1)} %copy-done.8), channel_id=1, source_target_pairs={{2,4},{4,2},{3,5},{5,3},{10,12},{12,10},{11,13},{13,11},{18,20},{2... | collective-permute-start | bytes 3145736 | tf_op jit(solution)/shard_map/re_out/ppermute | solution.py:1335
  501.2 39.2 %collective-permute-start.29 = (bf16[256,1024]{1,0:T(8,128)(2,1)}, bf16[256,1024]{1,0:T(8,128)(2,1)}, u32[]{:S(2)}, u32[]{:S(2)}) collective-permute-start(bf16[256,1024]{1,0:T(8,128)(2,1)} %copy.73), channel_id=1, source_target_pairs={{0,2},{2,0},{1,3},{3,1},{4,6},{6,4},{5,7},{7,5},{8,10},{10,8},{9,1... | collective-permute-start | bytes 1572872 | tf_op jit(solution)/shard_map/gc_zhi/ppermute | solution.py:1326
  504.5 46.7 %collective-permute-start.28 = (bf16[512,1024]{1,0:T(8,128)(2,1)}, bf16[512,1024]{1,0:T(8,128)(2,1)}, u32[]{:S(2)}, u32[]{:S(2)}) collective-permute-start(bf16[512,1024]{1,0:T(8,128)(2,1)} %add_convert_fusion.1), channel_id=1, source_target_pairs={{0,1},{1,0},{2,3},{3,2},{4,5},{5,4},{6,7},{7,6},{8,9},{9,8},{10,11... | collective-permute-start | bytes 3145736 | tf_op jit(solution)/shard_map/dx_z/ppermute | solution.py:1326
  555.2 53.0 %collective-permute-start.30 = (bf16[512,1024]{1,0:T(8,128)(2,1)S(1)}, bf16[512,1024]{1,0:T(8,128)(2,1)S(1)}, u32[]{:S(2)}, u32[]{:S(2)}) collective-permute-start(bf16[512,1024]{1,0:T(8,128)(2,1)S(1)} %fusion.25), channel_id=1, source_target_pairs={{2,4},{4,2},{3,5},{5,3},{10,12},{12,10},{11,13},{13,11},{18,20},{2... | collective-permute-start | bytes 3145736 | tf_op jit(solution)/shard_map/re_dgrad/ppermute | solution.py:1335
  (76 other events, 589.3 us)
Sparse Core Ops, SparseCore 0:
  99.9 51.2 all-gather.2
  153.0 87.5 all-gather.4
  337.6 86.0 reduce-scatter.2
  426.8 52.6 reduce-scatter.4

commit v7 on v6

--- a/solution.py
+++ b/solution.py
@@ -1590,7 +1590,7 @@
     dq, dk, dv = attend_back(
         self_plan, self_meta, qkv, 0, qkv, pairs, 2 * pairs, mixed, mixed_grad, self_lse, pairs, 1152
     )
-    dq, dk, dv = after(dq, in_sum, out_sum), after(dk, in_sum, out_sum), after(dv, in_sum, out_sum)
+    dq, dk, dv = (after(part, *hidden_beyond) for part in (dq, dk, dv))
     layer_moved = regroup_sent(after(layer_out, dq), "out")
     dqkv = jnp.concatenate([dq, dk, dv], axis=1)
     d_near, d_far = dqkv[: count // 2], dqkv[count // 2 :]

time: 628 us -> 624 us (level)
    unnamed x170 -> x180, local copies, waits for them, and re-layouts: 24.9 us -> 24.8 us
where the time goes in v7:
time: 624 us; the launch traced here: 614 us
  Pallas kernels  289 us (46%)
  matrix products  108 us (17%)
  waiting for transfers between devices  93.3 us (15%)
  local copies, waits for them, and re-layouts  43.9 us (7%)
  other arithmetic  38.4 us (6%)
  starting transfers between devices  25.2 us (4%)
  between operations  15.8 us (3%)
    ppermute x27, waiting for transfers between devices, trade(): return lax.ppermute(rows, axis, [(0, 1), (1, 0)])  92.9 us
    pallas_call x1, Pallas kernels, start_exchange(): pl.pallas_call(start_kernel, out_shape=shapes, in_specs=[anywhere] * 9, o...  85.2 us
    dot_general x22, matrix products, product_right_t(): lax.dot_general(left, right, (((1,), (1,)), ((), ())), preferred_element_...  68.9 us
    pallas_call x2, Pallas kernels, attend_back(): pl.pallas_call(functools.partial(backward_kernel, sections), grid_spec=pl...  56.2 us
    pallas_call x1, Pallas kernels, finish(): pl.pallas_call(finish_kernel, out_shape=shapes, in_specs=[anywhere] * 10,...  43.9 us
    pallas_call x2, Pallas kernels, attend(): pl.pallas_call(functools.partial(forward_kernel, sections), grid_spec=plt...  38.4 us
    pallas_call x2, Pallas kernels, hidden_units(): pl.pallas_call(hidden_kernel, grid=(tiles,), in_specs=[whole] * 4 + [weig...  33.6 us
    pallas_call x1, Pallas kernels, weight_grads(): pl.pallas_call(weight_grad_kernel, grid=(2 * tiles,), in_specs=[anywhere]...  32 us
  transfers between devices with their start and end apart: 35, of which 14 were waited for; matrix products, arithmetic and copies ran while one was open for 26% of the time, Pallas kernels for 28%

profile of v7, /device:TPU:0, one launch (start us, length us, event | category | flops | bytes accessed | tf_op | source)
XLA Modules:
  0.0 613.6 jit_solution(7642626181875251930)
XLA Ops:
  14.5 85.2 %shard_map.229 = (bf16[512,1024]{1,0:T(8,128)(2,1)}, bf16[2048,1024]{1,0:T(8,128)(2,1)}, bf16[4,2,2,256,256]{4,3,2,1,0:T(8,128)(2,1)}, bf16[256,2048]{1,0:T(8,12...) custom-call(bf16[512,1024]{1,0:T(8,128)(2,1)} %tokens.1, ...), custom_call_target="tpu_custom_call" | custom-call | tf_op jit(solution)/shard_map/pallas_call | solution.py:1005
  101.2 5.0 collective-permute-start.1
  110.7 4.7 multiply_convert_fusion.q_ref.k_ref.v_ref
  116.5 23.2 %shard_map.230 = (bf16[2048,256]{1,0:T(8,128)(2,1)}, f32[2048,256]{1,0:T(8,128)}) custom-call(s32[13]{0:T(128)} %concatenate.61.meta_ref, bf16[2048,768]{1,0:T(8,128)(2,1)} %multiply_convert_fusion.q_ref.k_ref.v_ref, bf16[2048,768]{1,0:T(8,128)(2,1)} %multiply_convert_fusion.q_ref.k_ref.v_ref, bf16[2048,768]{1,0:T(8,128)(2,1)} %multiply_convert_fusion.q_ref.k_ref.v_ref), custom_call_target="tpu_custom_call" | custom-call | flops 19327352832 | bytes 5242880 | tf_op jit(solution)/shard_map/pallas_call | solution.py:180
  139.7 11.1 %collective-permute-done.1 = bf16[2,256,1024]{2,1,0:T(8,128)(2,1)S(1)} collective-permute-done((bf16[2,256,1024]{2,1,0:T(8,128)(2,1)}, bf16[2,256,1024]{2,1,0:T(8,128)(2,1)S(1)}, u32[]{:S(2)}, u32[]{:S(2)}) %collective-permute-start.1) | collective-permute-done | bytes 1048608 | tf_op jit(solution)/shard_map/wh_zhi/ppermute | solution.py:1326
  172.2 4.3 add_convert_fusion.7.k_ref.v_ref
  176.5 24.4 %collective-permute-done.4 = bf16[512,1024]{1,0:T(8,128)(2,1)} collective-permute-done((bf16[512,1024]{1,0:T(8,128)(2,1)}, bf16[512,1024]{1,0:T(8,128)(2,1)}, u32[]{:S(2)}, u32[]{:S(2)}) %collective-permute-start.4) | collective-permute-done | bytes 1048608 | tf_op jit(solution)/shard_map/so_z/ppermute | solution.py:1326
  208.1 3.4 multiply_convert_fusion.1.q_ref
  211.6 15.2 %shard_map.231 = (bf16[1024,512]{1,0:T(8,128)(2,1)}, f32[1024,512]{1,0:T(8,128)}) custom-call(s32[1]{0:T(128)} %slice.208.meta_ref, bf16[1024,512]{1,0:T(8,128)(2,1)} %multiply_convert_fusion.1.q_ref, bf16[512,1024]{1,0:T(8,128)(2,1)} %add_convert_fusion.7.k_ref.v_ref, bf16[512,1024]{1,0:T(8,128)(2,1)} %add_convert_fusion.7.k_ref.v_ref), custom_call_target="tpu_custom_call" | custom-call | flops 8589934592 | bytes 5242880 | tf_op jit(solution)/shard_map/pallas_call | solution.py:180
  226.7 4.1 collective-permute-done.7.e0_ref.refs_3_
  243.7 16.7 %shard_map.232 = (bf16[1024,2048]{1,0:T(8,128)(2,1)}, bf16[1024,2048]{1,0:T(8,128)(2,1)}, f32[1,2048]{1,0:T(1,128)}) custom-call(bf16[512,1024]{1,0:T(8,128)(2,1)} %add_convert_fusion.5.x0_ref.refs_7_, bf16[512,1024]{1,0:T(8,128)(2,1)} %collective-permute-done.9.x1_ref.refs_8_, bf16[512,1024]{1,0:T(8,128)(2,1)} %get-tuple-element.90.e0_ref.refs_1_, ...), custom_call_target="tpu_custom_call" | custom-call | flops 8589934592 | bytes 20971520 | tf_op jit(solution)/shard_map/pallas_call | solution.py:671
  260.4 6.2 %collective-permute-done.11.x0_ref.refs_9_ = bf16[512,1024]{1,0:T(8,128)(2,1)} collective-permute-done((bf16[512,1024]{1,0:T(8,128)(2,1)}, bf16[512,1024]{1,0:T(8,128)(2,1)}, u32[]{:S(2)}, u32[]{:S(2)}) %collective-permute-start.11) | collective-permute-done | bytes 1048608 | tf_op jit(solution)/shard_map/mlp_z/ppermute | solution.py:1326
  266.6 6.2 %fusion.49 = bf16[512,1024]{1,0:T(8,128)(2,1)} fusion(bf16[1024,4096]{1,0:T(8,128)(2,1)} %all-gather.5.cloned.1.call-done.w_in_ref.w_out_ref, bf16[1024,2048]{1,0:T(8,128)(2,1)} %get-tuple-element.96.refs_11_), kind=kOutput, calls=%fused_computation.94 | convolution fusion | flops 2148007936 | bytes 7340032 | tf_op jit(solution)/shard_map/dot_general | solution.py:278
  273.3 16.8 %shard_map.233 = (bf16[1024,2048]{1,0:T(8,128)(2,1)}, bf16[1024,2048]{1,0:T(8,128)(2,1)}, f32[1,2048]{1,0:T(1,128)}) custom-call(bf16[512,1024]{1,0:T(8,128)(2,1)} %collective-permute-done.11.x0_ref.refs_9_, bf16[512,1024]{1,0:T(8,128)(2,1)} %collective-permute-done.12.x1_ref.refs_10_, bf16[512,1024]{1,0:T(8,128)(2,1)} %copy-done.66, ...), custom_call_target="tpu_custom_call" | custom-call | flops 8589934592 | bytes 20971520 | tf_op jit(solution)/shard_map/pallas_call | solution.py:671
  290.2 5.3 fusion.44
  295.7 6.3 %convert_add_fusion.5 = f32[512,1024]{1,0:T(8,128)} fusion(bf16[512,1024]{1,0:T(8,128)(2,1)} %collective-permute-done.15, bf16[1024,4096]{1,0:T(8,128)(2,1)} %all-gather.5.cloned.1.call-done.w_in_ref.w_out_ref, bf16[1024,2048]{1,0:T(8,128)(2,1)S(1)} %copy-done.68), kind=kOutput, calls=%fused_computation.62 | convolution fusion | flops 2148532224 | bytes 9437184 | tf_op jit(solution)/shard_map/dot_general | solution.py:278
  302.0 3.4 add_convert_fusion.4.refs_0_
  305.4 32.0 %shard_map.234 = (bf16[512,1024]{1,0:T(8,128)(2,1)}, bf16[1024,4096]{1,0:T(8,128)(2,1)}) custom-call(bf16[512,1024]{1,0:T(8,128)(2,1)} %add_convert_fusion.4.refs_0_, bf16[512,1024]{1,0:T(8,128)(2,1)} %get-tuple-element.90.e0_ref.refs_1_, bf16[512,1024]{1,0:T(8,128)(2,1)} %collective-permute-done.10.e1_ref.refs_2_, bf16[512,1024]{1,0:T(8,128)(2,1)} %copy-done.66, ...), custom_call_target="tpu_custom_call" | custom-call | flops 17179869184 | tf_op jit(solution)/shard_map/pallas_call | solution.py:752
  337.9 5.3 fusion.54
  345.0 3.5 convert_reduce_fusion.5
  349.7 3.4 add_convert_fusion.3
  353.6 3.8 convolution_convert_fusion.4.do_ref
  357.4 18.7 %shard_map.235 = (bf16[1024,512]{1,0:T(8,128)(2,1)}, bf16[512,512]{1,0:T(8,128)(2,1)}, bf16[512,512]{1,0:T(8,128)(2,1)}) custom-call(s32[1]{0:T(128)} %slice.208.meta_ref, bf16[1024,512]{1,0:T(8,128)(2,1)} %multiply_convert_fusion.1.q_ref, bf16[512,1024]{1,0:T(8,128)(2,1)} %add_convert_fusion.7.k_ref.v_ref, bf16[512,1024]{1,0:T(8,128)(2,1)} %add_convert_fusion.7.k_ref.v_ref, ...), custom_call_target="tpu_custom_call" | custom-call | flops 21474836480 | bytes 10485760 | tf_op jit(solution)/shard_map/pallas_call | solution.py:202
  392.8 3.4 fusion.59
  398.1 3.7 fusion.2
  411.1 3.3 add_convert_fusion.2
  428.9 37.5 %shard_map.236 = (bf16[2048,256]{1,0:T(8,128)(2,1)}, bf16[2048,256]{1,0:T(8,128)(2,1)}, bf16[2048,256]{1,0:T(8,128)(2,1)}) custom-call(s32[13]{0:T(128)} %concatenate.61.meta_ref, bf16[2048,768]{1,0:T(8,128)(2,1)} %multiply_convert_fusion.q_ref.k_ref.v_ref, bf16[2048,768]{1,0:T(8,128)(2,1)} %multiply_convert_fusion.q_ref.k_ref.v_ref, ...), custom_call_target="tpu_custom_call" | custom-call | flops 48318382080 | bytes 10485760 | tf_op jit(solution)/shard_map/pallas_call | solution.py:202
  469.0 6.2 %collective-permute-done.24 = bf16[256,2048]{1,0:T(8,128)(2,1)S(1)} collective-permute-done((bf16[256,2048]{1,0:T(8,128)(2,1)S(1)}, bf16[256,2048]{1,0:T(8,128)(2,1)S(1)}, u32[]{:S(2)}, u32[]{:S(2)}) %collective-permute-start.24) | collective-permute-done | bytes 1048608 | tf_op jit(solution)/shard_map/gf_zhi/ppermute | solution.py:1326
  502.0 4.4 convolution_convert_fusion.12
  517.8 17.5 %collective-permute-done.29.cross_beyond = bf16[256,1024]{1,0:T(8,128)(2,1)} collective-permute-done((bf16[256,1024]{1,0:T(8,128)(2,1)}, bf16[256,1024]{1,0:T(8,128)(2,1)}, u32[]{:S(2)}, u32[]{:S(2)}) %collective-permute-start.29) | collective-permute-done | bytes 524320 | tf_op jit(solution)/shard_map/gc_zhi/ppermute | solution.py:1326
  535.4 11.1 %collective-permute-done.28 = bf16[512,1024]{1,0:T(8,128)(2,1)} collective-permute-done((bf16[512,1024]{1,0:T(8,128)(2,1)}, bf16[512,1024]{1,0:T(8,128)(2,1)}, u32[]{:S(2)}, u32[]{:S(2)}) %collective-permute-start.28) | collective-permute-done | bytes 1048608 | tf_op jit(solution)/shard_map/dx_z/ppermute | solution.py:1326
  552.1 43.9 %shard_map.237 = (f32[128,2048]{1,0:T(8,128)}, f32[128,2048]{1,0:T(8,128)}, f32[3,128,256]{2,1,0:T(8,128)}, f32[128,256]{1,0:T(8,128)}, f32[3,128,256]{2,1,0:T(8...) custom-call(f32[256,1024]{1,0:T(8,128)} %get-tuple-element.211.ff_in, ...), custom_call_target="tpu_custom_call" | custom-call | flops 40000000000 | tf_op jit(solution)/shard_map/pallas_call | solution.py:1292
  (377 shorter events, 158.2 us)
Async XLA Ops:
  7.2 165.0 %all-gather.3.cloned.1.call-start = ((), (), s32[]{:S(2)}) async-start(), calls=%async_computation.2 | async-start | bytes 5242880 | tf_op jit(solution)/shard_map/all_gather | solution.py:1362
  99.8 143.9 %all-gather.5.cloned.1.call-start = ((), (), s32[]{:S(2)}) async-start(), calls=%async_computation.3 | async-start | bytes 10485760 | tf_op jit(solution)/shard_map/all_gather | solution.py:1362
  100.6 14.9 %collective-permute-start = (s32[9]{0:T(128)S(1)}, s32[9]{0:T(128)S(1)}, u32[]{:S(2)}, u32[]{:S(2)}) collective-permute-start(s32[9]{0:T(128)S(1)} %pad_add_fusion), channel_id=1, source_target_pairs={{2,4},{4,2},{3,5},{5,3},{10,12},{12,10},{11,13},{13,11},{18,20},{2... | collective-permute-start | bytes 116 | tf_op jit(solution)/shard_map/re_regroup/ppermute | solution.py:1335
  101.2 49.6 %collective-permute-start.1 = (bf16[2,256,1024]{2,1,0:T(8,128)(2,1)}, bf16[2,256,1024]{2,1,0:T(8,128)(2,1)S(1)}, u32[]{:S(2)}, u32[]{:S(2)}) collective-permute-start(bf16[2,256,1024]{2,1,0:T(8,128)(2,1)} %get-tuple-element.82), channel_id=1, source_target_pairs={{0,2},{2,0},{1,3},{3,1},{4,6},{6,4},{5,7},{7,5},{8,10},{10,8},{9,1... | collective-permute-start | bytes 3145736 | tf_op jit(solution)/shard_map/wh_zhi/ppermute | solution.py:1326
  152.7 270.8 %reduce-scatter.3.cloned.1.call-start = ((), (), s32[]{:S(2)}) async-start(), calls=%async_computation.4 | async-start | bytes 10485760 | tf_op jit(solution)/shard_map/reduce_scatter | solution.py:1366
  155.4 5.3 collective-permute-start.3
  156.3 12.6 %collective-permute-start.5 = (bf16[512,1024]{1,0:T(8,128)(2,1)}, bf16[512,1024]{1,0:T(8,128)(2,1)}, u32[]{:S(2)}, u32[]{:S(2)}) collective-permute-start(bf16[512,1024]{1,0:T(8,128)(2,1)} %param.18), channel_id=1, source_target_pairs={{2,4},{4,2},{3,5},{5,3},{10,12},{12,10},{11,13},{13,11},{18,20},{2... | collective-permute-start | bytes 3145736 | tf_op jit(solution)/shard_map/re_cotangent/ppermute | solution.py:1335
  160.0 40.9 %collective-permute-start.2 = (bf16[512,1024]{1,0:T(8,128)(2,1)}, bf16[512,1024]{1,0:T(8,128)(2,1)S(1)}, u32[]{:S(2)}, u32[]{:S(2)}) collective-permute-start(bf16[512,1024]{1,0:T(8,128)(2,1)} %convolution_convert_fusion.6), channel_id=1, source_target_pairs={{0,4},{4,0},{1,5},{5,1},{2,6},{6,2},{3,7},{7,3},{8,12},{12,8},{9,1... | collective-permute-start | bytes 3145736 | tf_op jit(solution)/shard_map/so_c/ppermute | solution.py:1326
  163.7 37.1 %collective-permute-start.4 = (bf16[512,1024]{1,0:T(8,128)(2,1)}, bf16[512,1024]{1,0:T(8,128)(2,1)}, u32[]{:S(2)}, u32[]{:S(2)}) collective-permute-start(bf16[512,1024]{1,0:T(8,128)(2,1)} %add_convert_fusion.8), channel_id=1, source_target_pairs={{0,1},{1,0},{2,3},{3,2},{4,5},{5,4},{6,7},{7,6},{8,9},{9,8},{10,11... | collective-permute-start | bytes 3145736 | tf_op jit(solution)/shard_map/so_z/ppermute | solution.py:1326
  205.2 25.7 %collective-permute-start.7 = (bf16[512,1024]{1,0:T(8,128)(2,1)}, bf16[512,1024]{1,0:T(8,128)(2,1)S(1)}, u32[]{:S(2)}, u32[]{:S(2)}) collective-permute-start(bf16[512,1024]{1,0:T(8,128)(2,1)} %get-tuple-element.90.e0_ref.refs_1_), channel_id=1, source_target_pairs={{0,1},{1,0},{2,3},{3,2},{4,5},{5,4},{6,7},{7,6},{8,9},{9,8},{10,11... | collective-permute-start | bytes 3145736 | tf_op jit(solution)/shard_map/cot_z/ppermute | solution.py:1326
  233.4 3.4 collective-permute-start.8
  233.5 8.4 %collective-permute-start.10 = (bf16[512,1024]{1,0:T(8,128)(2,1)}, bf16[512,1024]{1,0:T(8,128)(2,1)}, u32[]{:S(2)}, u32[]{:S(2)}) collective-permute-start(bf16[512,1024]{1,0:T(8,128)(2,1)} %get-tuple-element.90.e0_ref.refs_1_), channel_id=1, source_target_pairs={{0,4},{4,0},{1,5},{5,1},{2,6},{6,2},{3,7},{7,3},{8,12},{12,8},{9,1... | collective-permute-start | bytes 3145736 | tf_op jit(solution)/shard_map/cot_c/ppermute | solution.py:1326
  240.9 25.8 %collective-permute-start.11 = (bf16[512,1024]{1,0:T(8,128)(2,1)}, bf16[512,1024]{1,0:T(8,128)(2,1)}, u32[]{:S(2)}, u32[]{:S(2)}) collective-permute-start(bf16[512,1024]{1,0:T(8,128)(2,1)} %add_convert_fusion.5.x0_ref.refs_7_), channel_id=1, source_target_pairs={{0,1},{1,0},{2,3},{3,2},{4,5},{5,4},{6,7},{7,6},{8,9},{9,8},{10,11... | collective-permute-start | bytes 3145736 | tf_op jit(solution)/shard_map/mlp_z/ppermute | solution.py:1326
  241.8 31.5 %collective-permute-start.13 = (bf16[512,1024]{1,0:T(8,128)(2,1)}, bf16[512,1024]{1,0:T(8,128)(2,1)}, u32[]{:S(2)}, u32[]{:S(2)}) collective-permute-start(bf16[512,1024]{1,0:T(8,128)(2,1)} %copy-done.66), channel_id=1, source_target_pairs={{0,4},{4,0},{1,5},{5,1},{2,6},{6,2},{3,7},{7,3},{8,12},{12,8},{9,1... | collective-permute-start | bytes 3145736 | tf_op jit(solution)/shard_map/cot_zc/ppermute | solution.py:1326
  266.6 6.7 %collective-permute-start.12 = (bf16[512,1024]{1,0:T(8,128)(2,1)}, bf16[512,1024]{1,0:T(8,128)(2,1)}, u32[]{:S(2)}, u32[]{:S(2)}) collective-permute-start(bf16[512,1024]{1,0:T(8,128)(2,1)} %collective-permute-done.11.x0_ref.refs_9_), channel_id=1, source_target_pairs={{0,4},{4,0},{1,5},{5,1},{2,6},{6,2},{3,7},{7,3},{8,12},{12,8},{9,1... | collective-permute-start | bytes 3145736 | tf_op jit(solution)/shard_map/mlp_zc/ppermute | solution.py:1326
  272.8 22.8 %collective-permute-start.15 = (bf16[512,1024]{1,0:T(8,128)(2,1)}, bf16[512,1024]{1,0:T(8,128)(2,1)}, u32[]{:S(2)}, u32[]{:S(2)}) collective-permute-start(bf16[512,1024]{1,0:T(8,128)(2,1)} %fusion.49), channel_id=1, source_target_pairs={{0,4},{4,0},{1,5},{5,1},{2,6},{6,2},{3,7},{7,3},{8,12},{12,8},{9,1... | collective-permute-start | bytes 3145736 | tf_op jit(solution)/shard_map/dmlp_c/ppermute | solution.py:1326
  295.6 6.4 %collective-permute-start.14 = (bf16[512,1024]{1,0:T(8,128)(2,1)S(1)}, bf16[512,1024]{1,0:T(8,128)(2,1)S(1)}, u32[]{:S(2)}, u32[]{:S(2)}) collective-permute-start(bf16[512,1024]{1,0:T(8,128)(2,1)S(1)} %fusion.44), channel_id=1, source_target_pairs={{0,4},{4,0},{1,5},{5,1},{2,6},{6,2},{3,7},{7,3},{8,12},{12,8},{9,1... | collective-permute-start | bytes 3145736 | tf_op jit(solution)/shard_map/dmlp_zc/ppermute | solution.py:1326
  337.4 154.5 %reduce-scatter.5.cloned.1.call-start = ((), (), s32[]{:S(2)}) async-start(), calls=%async_computation.5 | async-start | bytes 5242880 | tf_op jit(solution)/shard_map/reduce_scatter | solution.py:1366
  343.2 5.8 collective-permute-start.17
  348.6 5.0 collective-permute-start.16
  353.0 25.8 %collective-permute-start.18 = (bf16[512,1024]{1,0:T(8,128)(2,1)}, bf16[512,1024]{1,0:T(8,128)(2,1)}, u32[]{:S(2)}, u32[]{:S(2)}) collective-permute-start(bf16[512,1024]{1,0:T(8,128)(2,1)} %add_convert_fusion.3), channel_id=1, source_target_pairs={{0,1},{1,0},{2,3},{3,2},{4,5},{5,4},{6,7},{7,6},{8,9},{9,8},{10,11... | collective-permute-start | bytes 3145736 | tf_op jit(solution)/shard_map/out_z/ppermute | solution.py:1326
  390.6 17.3 %collective-permute-start.21 = (bf16[512,1024]{1,0:T(8,128)(2,1)}, bf16[512,1024]{1,0:T(8,128)(2,1)}, u32[]{:S(2)}, u32[]{:S(2)}) collective-permute-start(bf16[512,1024]{1,0:T(8,128)(2,1)} %get-tuple-element.194), channel_id=1, source_target_pairs={{0,4},{4,0},{1,5},{5,1},{2,6},{6,2},{3,7},{7,3},{8,12},{12,8},{9,1... | collective-permute-start | bytes 3145736 | tf_op jit(solution)/shard_map/e1_c/ppermute | solution.py:1326
  391.1 25.4 %collective-permute-start.22 = (bf16[512,1024]{1,0:T(8,128)(2,1)}, bf16[512,1024]{1,0:T(8,128)(2,1)}, u32[]{:S(2)}, u32[]{:S(2)}) collective-permute-start(bf16[512,1024]{1,0:T(8,128)(2,1)} %get-tuple-element.194), channel_id=1, source_target_pairs={{0,1},{1,0},{2,3},{3,2},{4,5},{5,4},{6,7},{7,6},{8,9},{9,8},{10,11... | collective-permute-start | bytes 3145736 | tf_op jit(solution)/shard_map/e1_z/ppermute | solution.py:1326
  396.2 14.9 %collective-permute-start.20 = (bf16[512,1024]{1,0:T(8,128)(2,1)}, bf16[512,1024]{1,0:T(8,128)(2,1)}, u32[]{:S(2)}, u32[]{:S(2)}) collective-permute-start(bf16[512,1024]{1,0:T(8,128)(2,1)} %fusion.59), channel_id=1, source_target_pairs={{0,4},{4,0},{1,5},{5,1},{2,6},{6,2},{3,7},{7,3},{8,12},{12,8},{9,1... | collective-permute-start | bytes 3145736 | tf_op jit(solution)/shard_map/out_c/ppermute | solution.py:1326
  416.4 3.3 collective-permute-start.23
  426.5 48.6 %collective-permute-start.24 = (bf16[256,2048]{1,0:T(8,128)(2,1)S(1)}, bf16[256,2048]{1,0:T(8,128)(2,1)S(1)}, u32[]{:S(2)}, u32[]{:S(2)}) collective-permute-start(bf16[256,2048]{1,0:T(8,128)(2,1)S(1)} %pad_maximum_fusion.14), channel_id=1, source_target_pairs={{0,2},{2,0},{1,3},{3,1},{4,6},{6,4},{5,7},{7,5},{8,10},{10,8},{9,1... | collective-permute-start | bytes 3145736 | tf_op jit(solution)/shard_map/gf_zhi/ppermute | solution.py:1326
  478.3 11.6 %collective-permute-start.26 = (bf16[512,1024]{1,0:T(8,128)(2,1)S(1)}, bf16[512,1024]{1,0:T(8,128)(2,1)S(1)}, u32[]{:S(2)}, u32[]{:S(2)}) collective-permute-start(bf16[512,1024]{1,0:T(8,128)(2,1)S(1)} %convolution_convert_fusion.1), channel_id=1, source_target_pairs={{0,4},{4,0},{1,5},{5,1},{2,6},{6,2},{3,7},{7,3},{8,12},{12,8},{9,1... | collective-permute-start | bytes 3145736 | tf_op jit(solution)/shard_map/dx_zc/ppermute | solution.py:1326
  483.7 62.7 %collective-permute-start.27 = (bf16[512,1024]{1,0:T(8,128)(2,1)}, bf16[512,1024]{1,0:T(8,128)(2,1)}, u32[]{:S(2)}, u32[]{:S(2)}) collective-permute-start(bf16[512,1024]{1,0:T(8,128)(2,1)} %convolution_convert_fusion), channel_id=1, source_target_pairs={{0,4},{4,0},{1,5},{5,1},{2,6},{6,2},{3,7},{7,3},{8,12},{12,8},{9,1... | collective-permute-start | bytes 3145736 | tf_op jit(solution)/shard_map/dx_c/ppermute | solution.py:1326
  484.0 27.2 %collective-permute-start.25 = (bf16[512,1024]{1,0:T(8,128)(2,1)S(1)}, bf16[512,1024]{1,0:T(8,128)(2,1)}, u32[]{:S(2)}, u32[]{:S(2)}) collective-permute-start(bf16[512,1024]{1,0:T(8,128)(2,1)S(1)} %copy-done.8), channel_id=1, source_target_pairs={{2,4},{4,2},{3,5},{5,3},{10,12},{12,10},{11,13},{13,11},{18,20},{2... | collective-permute-start | bytes 3145736 | tf_op jit(solution)/shard_map/re_out/ppermute | solution.py:1335
  498.2 37.1 %collective-permute-start.29 = (bf16[256,1024]{1,0:T(8,128)(2,1)}, bf16[256,1024]{1,0:T(8,128)(2,1)}, u32[]{:S(2)}, u32[]{:S(2)}) collective-permute-start(bf16[256,1024]{1,0:T(8,128)(2,1)} %copy.73), channel_id=1, source_target_pairs={{0,2},{2,0},{1,3},{3,1},{4,6},{6,4},{5,7},{7,5},{8,10},{10,8},{9,1... | collective-permute-start | bytes 1572872 | tf_op jit(solution)/shard_map/gc_zhi/ppermute | solution.py:1326
  501.2 45.2 %collective-permute-start.28 = (bf16[512,1024]{1,0:T(8,128)(2,1)}, bf16[512,1024]{1,0:T(8,128)(2,1)}, u32[]{:S(2)}, u32[]{:S(2)}) collective-permute-start(bf16[512,1024]{1,0:T(8,128)(2,1)} %add_convert_fusion.1), channel_id=1, source_target_pairs={{0,1},{1,0},{2,3},{3,2},{4,5},{5,4},{6,7},{7,6},{8,9},{9,8},{10,11... | collective-permute-start | bytes 3145736 | tf_op jit(solution)/shard_map/dx_z/ppermute | solution.py:1326
  550.5 51.8 %collective-permute-start.30 = (bf16[512,1024]{1,0:T(8,128)(2,1)S(1)}, bf16[512,1024]{1,0:T(8,128)(2,1)S(1)}, u32[]{:S(2)}, u32[]{:S(2)}) collective-permute-start(bf16[512,1024]{1,0:T(8,128)(2,1)S(1)} %fusion.25), channel_id=1, source_target_pairs={{2,4},{4,2},{3,5},{5,3},{10,12},{12,10},{11,13},{13,11},{18,20},{2... | collective-permute-start | bytes 3145736 | tf_op jit(solution)/shard_map/re_dgrad/ppermute | solution.py:1335
  (81 other events, 600.5 us)
Sparse Core Ops, SparseCore 0:
  99.9 51.2 all-gather.2
  153.0 87.5 all-gather.4
  337.5 85.9 reduce-scatter.2
  426.6 52.6 reduce-scatter.4
